TPU v7x, 32 devices: a whole 2x2x4 slice. The times are simulated.
32 devices in a mesh: ctx: 16 (over z, y, x), fsdp: 2 (over core).
Axes of the slice: x: 2, y: 2, z: 4, core: 2. Of those that a mesh axis runs over, the one named last changes fastest.
Arguments:
- rotated_query_rows: bfloat16 [3072, 1024], P('ctx', 'fsdp'), may hold values from -6 to 6
- rotated_key_rows: bfloat16 [3072, 1024], P('ctx', 'fsdp'), may hold values from -6 to 6
- saved_value_rows: bfloat16 [3072, 1024], P('ctx', 'fsdp'), may hold values from -6 to 6
- projection_output_gradient: bfloat16 [3072, 5120], P('ctx', 'fsdp'), may hold values from -6 to 6
- frozen_weight_codes: int32 [5120, 1024], P('ctx', 'fsdp'), may hold values from 0 to 15
- block_scale_index: int32 [5120, 16], P('ctx', 'fsdp'), may hold values from 0 to 255
- block_scale_table: float32 [256], replicated, may hold values from 0.008385255 to 0.08385255
- adapter_down_matrix: bfloat16 [64, 1024], P('ctx', 'fsdp'), may hold values from -0.75 to 0.75
- adapter_up_matrix: bfloat16 [64, 5120], P('ctx', 'fsdp'), may hold values from -0.078125 to 0.078125
Outputs:
- query_grad: bfloat16 [3072, 1024], P('ctx', 'fsdp')
- key_grad: bfloat16 [3072, 1024], P('ctx', 'fsdp')
- value_grad: bfloat16 [3072, 1024], P('ctx', 'fsdp')
- down_matrix_gradient: float32 [64, 1024], P('ctx', 'fsdp')
- up_matrix_gradient: float32 [64, 5120], P('ctx', 'fsdp')
All inputs are finite; a program needn't handle non-finite values.
Results may differ from a plain program's by a relative error of at most 0.0093.
Values may be sent and summed in bfloat16 or wider, within the bound.
No kernel may reach another device: no remote copies, remote signals or barrier semaphores. Data moves between devices by JAX's collectives and lax.ppermute only.
A program may use at most 64 MiB of HBM per device.

v0:
```python
import functools

import jax
import jax.numpy as jnp
import numpy as np
from jax import lax
from jax.experimental import pallas as pl
from jax.experimental.pallas import tpu as pltpu
from jax.sharding import PartitionSpec as P

HEAD_WIDTH = 128
HALF_GROUP_DEV = 4
LANES = 128
QUERY_BLOCK = 256

nf4_values = (
    -1.0,
    -0.6961928009986877,
    -0.5250730514526367,
    -0.39491748809814453,
    -0.28444138169288635,
    -0.18477343022823334,
    -0.09105003625154495,
    0.0,
    0.07958029955625534,
    0.16093020141124725,
    0.24611230194568634,
    0.33791524171829224,
    0.44070982933044434,
    0.5626170039176941,
    0.7229568362236023,
    1.0,
)
adapter_scale = 0.25
masked = -1e30


BF = jnp.bfloat16
F32 = jnp.float32
VM = pl.BlockSpec(memory_space=pltpu.VMEM)
SM = pl.BlockSpec(memory_space=pltpu.SMEM)


def sds(shape, dtype):
    return jax.ShapeDtypeStruct(shape, dtype)


def nt(a, b):
    return lax.dot_general(a, b, (((1,), (1,)), ((), ())), preferred_element_type=F32)


def nn(a, b):
    return jnp.dot(a, b, preferred_element_type=F32)


def call(body, outs, scratch, *args, n_scalar=0):
    return pl.pallas_call(
        body,
        out_shape=outs,
        in_specs=[SM] * n_scalar + [VM] * (len(args) - n_scalar),
        out_specs=jax.tree.map(lambda _: VM, outs),
        scratch_shapes=scratch,
    )(*args)


def dequant_body(codes_ref, index_ref, table_ref, nf4_ref, out_ref):
    rows, cols = codes_ref.shape
    per_tile = index_ref.shape[1] * LANES // cols
    width = LANES // per_tile
    lane = lax.broadcasted_iota(jnp.int32, (rows, LANES), 1)
    levels = jnp.broadcast_to(nf4_ref[...], (rows, LANES))
    parts = table_ref.shape[0]
    tables = [jnp.broadcast_to(table_ref[i : i + 1, :], (rows, LANES)) for i in range(parts)]
    for b in range(cols // LANES):
        code = codes_ref[:, b * LANES : (b + 1) * LANES]
        value = jnp.take_along_axis(levels, code, axis=1)
        idx = jnp.broadcast_to(index_ref[:, b * per_tile : b * per_tile + 1], (rows, LANES))
        for i in range(1, per_tile):
            at = b * per_tile + i
            idx = jnp.where(lane >= i * width, index_ref[:, at : at + 1], idx)
        low = idx % LANES
        scale = jnp.take_along_axis(tables[0], low, axis=1)
        for i in range(1, parts):
            scale = jnp.where(
                idx >= i * LANES, jnp.take_along_axis(tables[i], low, axis=1), scale
            )
        out_ref[:, b * LANES : (b + 1) * LANES] = (value * scale).astype(BF)


def pack_grad_body(half, strips, pos_ref, g_ref, *out_refs):
    mine = pos_ref[0]
    rows = g_ref.shape[0]
    step = g_ref.shape[1] // strips
    width = step // half
    for s in range(half):
        to = mine ^ s
        for jv in range(half):

            @pl.when(to == jv)
            def _(s=s, jv=jv):
                pieces = [
                    g_ref[:, i * step + jv * width : i * step + (jv + 1) * width]
                    for i in range(strips)
                ]
                short = out_refs[s].shape[1] - strips * width
                if short:
                    pieces.append(jnp.zeros((rows, short), BF))
                out_refs[s][...] = jnp.concatenate(pieces, axis=1)


def pack_heads_body(half, pos_ref, q_ref, k_ref, v_ref, *out_refs):
    own = pos_ref[4]
    for s in range(half):
        cols = pl.ds(pl.multiple_of((own ^ s) * LANES, LANES), LANES)
        out_refs[s][0] = q_ref[:, cols]
        out_refs[s][1] = k_ref[:, cols]
        out_refs[s][2] = v_ref[:, cols]


def assemble_body(half, pos_ref, *refs):
    pieces, (q_out, kv_out) = refs[:half], refs[half:]
    mine = pos_ref[0]
    rows = pieces[0].shape[1]
    for s in range(half):
        at = pl.ds(pl.multiple_of((mine ^ s) * rows, rows), rows)
        q_out[at, :] = pieces[s][0]
        kv_out[0, at, :] = pieces[s][1]
        kv_out[1, at, :] = pieces[s][2]


def lora_body(half, fsdp, pos_ref, *refs):
    ups, grads, out_ref = refs[:fsdp], refs[fsdp:-1], refs[-1]
    mine = pos_ref[0]
    rows = grads[0].shape[0]
    for s in range(half):
        total = None
        for f in range(fsdp):
            part = nt(grads[s * fsdp + f][...], ups[f][...])
            total = part if total is None else total + part
        at = pl.ds(pl.multiple_of((mine ^ s) * rows, rows), rows)
        out_ref[at, :] = adapter_scale * total


def project_body(half, planes, fsdp, slot, targets, pos_ref, *refs):
    lora_ref, down_ref = refs[:2]
    grads = refs[2 : 2 + half * fsdp]
    weights = refs[2 + half * fsdp : 2 + half * fsdp + planes]
    outs = refs[2 + half * fsdp + planes : -2]
    w_scr, d_scr = refs[-2:]
    mine, plane, core, own = pos_ref[0], pos_ref[1], pos_ref[2], pos_ref[4]
    rows_each = weights[0].shape[0]
    tail = w_scr.shape[0] - planes * rows_each
    if tail:
        w_scr[planes * rows_each :, :] = jnp.zeros((tail, w_scr.shape[1]), BF)
    for i, t in enumerate(targets):
        cols = pl.ds(pl.multiple_of((own ^ t) * LANES, LANES), LANES)
        to = slice(i * LANES, (i + 1) * LANES)
        d_scr[:, to] = down_ref[:, cols]
        for s in range(planes):
            src = lax.rem(plane + (planes - s), planes)
            at = pl.ds(pl.multiple_of(src * rows_each, rows_each), rows_each)
            w_scr[at, to] = weights[s][:, cols]
    rows = grads[0].shape[0]
    depth = grads[0].shape[1]
    for s in range(half):
        at = pl.ds(pl.multiple_of((mine ^ s) * rows, rows), rows)
        acc = nn(lora_ref[at, :].astype(BF), d_scr[...])
        for f in range(fsdp):
            src = lax.rem(core + (fsdp - f), fsdp)
            w_at = pl.ds(pl.multiple_of(src * slot, 16), depth)
            acc = acc + nn(grads[s * fsdp + f][...], w_scr[w_at, :])
        for i in range(len(targets)):
            outs[i][at, :] = acc[:, i * LANES : (i + 1) * LANES].astype(BF)


def score_block(key, query, k0, q0):
    scores = nt(key, query) * (HEAD_WIDTH**-0.5)
    if k0 is None or k0 + key.shape[0] - 1 <= q0:
        return scores
    kpos = k0 + lax.broadcasted_iota(jnp.int32, scores.shape, 0)
    qpos = q0 + lax.broadcasted_iota(jnp.int32, scores.shape, 1)
    return jnp.where(kpos <= qpos, scores, masked)


def forward_body(pos_ref, q_ref, kv_ref, far_ref, down_ref, o_ref, lse_ref, mid_ref, vt_scr, oft_scr):
    later = pos_ref[3]
    tokens = q_ref.shape[0]
    block = min(QUERY_BLOCK, tokens)
    vt_scr[...] = kv_ref[1].T

    def finish(q0, block_out, norm):
        qs = slice(q0, q0 + block)
        out = block_out.T
        o_ref[qs, :] = out
        lse_ref[:, qs] = norm
        mid_ref[qs, :] = nt(out.astype(BF), down_ref[...])

    def near(q0):
        return score_block(kv_ref[0, : q0 + block, :], q_ref[q0 : q0 + block, :], 0, q0)

    @pl.when(later == 0)
    def _():
        for q0 in range(0, tokens, block):
            scores = near(q0)
            top = jnp.max(scores, axis=0, keepdims=True)
            prob = jnp.exp(scores - top)
            total = jnp.sum(prob, axis=0, keepdims=True)
            out = nn(vt_scr[:, : q0 + block], prob.astype(BF)) / total
            finish(q0, out, top + jnp.log(total))

    @pl.when(later != 0)
    def _():
        oft_scr[...] = far_ref[1].T
        for q0 in range(0, tokens, block):
            scores = near(q0)
            far = score_block(far_ref[0], q_ref[q0 : q0 + block, :], None, q0)
            top = jnp.maximum(
                jnp.max(scores, axis=0, keepdims=True), jnp.max(far, axis=0, keepdims=True)
            )
            prob = jnp.exp(scores - top)
            far_prob = jnp.exp(far - top)
            total = jnp.sum(prob, axis=0, keepdims=True) + jnp.sum(far_prob, axis=0, keepdims=True)
            out = nn(vt_scr[:, : q0 + block], prob.astype(BF)) + nn(
                oft_scr[...], far_prob.astype(BF)
            )
            finish(q0, out / total, top + jnp.log(total))


def grad_block(key, value, query, grad, norm, delta, k0, q0):
    prob = jnp.exp(score_block(key, query, k0, q0) - norm)
    prob_grad = nt(value, grad)
    score_grad = prob * (prob_grad - delta) * (HEAD_WIDTH**-0.5)
    return prob.astype(BF), score_grad.astype(BF)


def far_body(half, pos_ref, *refs):
    parts = refs[:half]
    q_ref, far_ref, o_ref, norm_ref = refs[half : half + 4]
    far_out, dq_ref, do_ref, delta_ref, kt_scr = refs[half + 4 :]
    later = pos_ref[3]
    tokens = q_ref.shape[0]
    block = min(QUERY_BLOCK, tokens)
    total = parts[0][...].astype(F32)
    for s in range(1, half):
        total = total + parts[s][...].astype(F32)
    grad = total.astype(BF)
    do_ref[...] = grad
    delta_ref[...] = jnp.sum((grad.astype(F32) * o_ref[...]).T, axis=0, keepdims=True)

    @pl.when(later != 0)
    def _():
        kt_scr[...] = far_ref[0].T
        for k0 in range(0, tokens, block):
            ks = slice(k0, k0 + block)
            prob, score_grad = grad_block(
                far_ref[0, ks, :],
                far_ref[1, ks, :],
                q_ref[...],
                do_ref[...],
                norm_ref[...],
                delta_ref[...],
                None,
                0,
            )
            far_out[0, ks, :] = nn(score_grad, q_ref[...]).astype(BF)
            far_out[1, ks, :] = nn(prob, do_ref[...]).astype(BF)
            part = nn(kt_scr[:, ks], score_grad)
            if k0:
                dq_ref[...] += part
            else:
                dq_ref[...] = part

    @pl.when(later == 0)
    def _():
        far_out[...] = jnp.zeros(far_out.shape, BF)
        dq_ref[...] = jnp.zeros(dq_ref.shape, F32)


def near_body(pos_ref, q_ref, kv_ref, do_ref, norm_ref, delta_ref, dq_in, dq_ref, near_ref, kt_scr):
    tokens = q_ref.shape[0]
    block = min(QUERY_BLOCK, tokens)
    kt_scr[...] = kv_ref[0].T
    for q0 in range(0, tokens, block):
        qs = slice(q0, q0 + block)
        depth = q0 + block
        prob, score_grad = grad_block(
            kv_ref[0, :depth, :],
            kv_ref[1, :depth, :],
            q_ref[qs, :],
            do_ref[qs, :],
            norm_ref[:, qs],
            delta_ref[:, qs],
            0,
            q0,
        )
        dk = nn(score_grad, q_ref[qs, :])
        dv = nn(prob, do_ref[qs, :])
        if q0:
            near_ref[0, :q0, :] += dk[:q0]
            near_ref[1, :q0, :] += dv[:q0]
        near_ref[0, qs, :] = dk[q0:]
        near_ref[1, qs, :] = dv[q0:]
        dq = dq_in[:, qs] + nn(kt_scr[:, :depth], score_grad)
        dq_ref[qs, :] = dq.T.astype(BF)


def merge_body(half, pos_ref, dq_ref, near_ref, back_ref, *out_refs):
    mine = pos_ref[0]
    rows = near_ref.shape[1] // half
    for s in range(half):
        at = pl.ds(pl.multiple_of((mine ^ s) * rows, rows), rows)
        out_refs[s][0] = dq_ref[at, :]
        for i in range(2):
            merged = near_ref[i, at, :] + back_ref[i, at, :].astype(F32)
            out_refs[s][1 + i] = merged.astype(BF)


def unpack_body(half, pos_ref, *refs):
    pieces, outs = refs[:half], refs[half:]
    own = pos_ref[4]
    for s in range(half):
        at = pl.ds(pl.multiple_of((own ^ s) * LANES, LANES), LANES)
        for i in range(3):
            outs[i][:, at] = pieces[s][i]


def adapters_body(half, pos_ref, o_ref, *refs):
    both, grads, out_ref, scr = refs[:half], refs[half : 2 * half], refs[-2], refs[-1]
    mine = pos_ref[0]
    rank = out_ref.shape[0]
    rows, wide = grads[0].shape
    total = both[0][...].astype(F32)
    for s in range(1, half):
        total = total + both[s][...].astype(F32)
    total = total.astype(BF)
    scr[...] = total
    acc = None
    for s in range(half):
        at = pl.ds(pl.multiple_of((mine ^ s) * rows, rows), rows)
        part = nn(scr[at, :].T[rank:, :], grads[s][...])
        acc = part if acc is None else acc + part
    out_ref[:, :wide] = adapter_scale * acc
    out_ref[:, wide:] = nn(total.T[:rank, :], o_ref[...].astype(BF))


def on_device(
    sizes,
    rotated_query_rows,
    rotated_key_rows,
    saved_value_rows,
    projection_output_gradient,
    frozen_weight_codes,
    block_scale_index,
    block_scale_table,
    adapter_down_matrix,
    adapter_up_matrix,
):
    n_ctx, fsdp = sizes
    half = HALF_GROUP_DEV
    planes = n_ctx // half
    rows = rotated_query_rows.shape[0]
    heads = rotated_query_rows.shape[1] // HEAD_WIDTH
    assert heads == half
    tokens = rows * half
    w_rows, w_cols = frozen_weight_codes.shape
    grad_cols = projection_output_gradient.shape[1]
    strips = grad_cols // (half * w_rows)
    slot = strips * w_rows
    wide = -(-slot // LANES) * LANES
    rank_rows = adapter_down_matrix.shape[0]
    rank = rank_rows * n_ctx

    def head_of(j, f):
        return j ^ ((f & 1) * (half // 2))

    ctx = lax.axis_index("ctx")
    core = lax.axis_index("fsdp")
    mine = ctx % half
    plane = ctx // half
    own = head_of(mine, core)
    later = jnp.where(own < heads // 2, plane % 2, 1 - plane % 2)
    pos = jnp.stack([mine, plane, core, later, own]).astype(jnp.int32)

    def in_plane(x, s):
        if s == 0:
            return x
        return lax.ppermute(x, "ctx", [(i, i ^ s) for i in range(n_ctx)])

    def along(x, s):
        if s == 0:
            return x
        return lax.ppermute(x, "ctx", [(i, (i + s * half) % n_ctx) for i in range(n_ctx)])

    def across(x, s):
        if s == 0:
            return x
        return lax.ppermute(x, "fsdp", [(i, (i + s) % fsdp) for i in range(fsdp)])

    pairs = []
    for i in range(n_ctx):
        for f in range(fsdp):
            p, j = divmod(i, half)
            if (p % 2 == 0) == (head_of(j, f) < heads // 2):
                pairs.append((i * fsdp + f, (i + half) % n_ctx * fsdp + f))

    def to_later(x):
        return lax.ppermute(x, ("ctx", "fsdp"), pairs)

    def to_earlier(x):
        return lax.ppermute(x, ("ctx", "fsdp"), [(b, a) for a, b in pairs])

    levels = np.zeros((1, LANES), np.float32)
    levels[0, : len(nf4_values)] = nf4_values
    weight = call(
        dequant_body,
        sds((w_rows, w_cols), BF),
        [],
        frozen_weight_codes,
        block_scale_index,
        block_scale_table.reshape(-1, LANES),
        jnp.asarray(levels),
    )
    weights = [along(weight, s) for s in range(planes)]

    grads = call(
        functools.partial(pack_grad_body, half, strips),
        [sds((rows, wide), BF)] * half,
        [],
        pos,
        projection_output_gradient,
        n_scalar=1,
    )
    grads = [in_plane(x, s) for s, x in enumerate(grads)]
    swapped = [across(g, f) for g in grads for f in range(fsdp)]

    packed = call(
        functools.partial(pack_heads_body, half),
        [sds((3, rows, LANES), BF)] * half,
        [],
        pos,
        rotated_query_rows,
        rotated_key_rows,
        saved_value_rows,
        n_scalar=1,
    )
    packed = [in_plane(x, s) for s, x in enumerate(packed)]
    query, key_value = call(
        functools.partial(assemble_body, half),
        [sds((tokens, LANES), BF), sds((2, tokens, LANES), BF)],
        [],
        pos,
        *packed,
        n_scalar=1,
    )
    far = to_later(key_value)

    up_chunks = adapter_up_matrix.reshape(rank_rows, strips, half, w_rows).transpose(2, 0, 1, 3)
    up_chunks = up_chunks.reshape(half, rank_rows, slot)
    up_chunks = jnp.pad(up_chunks, ((0, 0), (0, 0), (0, wide - slot)))
    down_chunks = jnp.broadcast_to(adapter_down_matrix, (half,) + adapter_down_matrix.shape)
    chunks = jnp.concatenate([up_chunks, down_chunks], axis=2)
    chunks = jnp.broadcast_to(chunks, (planes,) + chunks.shape).reshape(n_ctx * rank_rows, -1)
    adapters = lax.all_to_all(chunks, "ctx", split_axis=0, concat_axis=0, tiled=True)
    up = adapters[:, :wide]
    down = adapters[:, wide:]
    down_head = lax.dynamic_slice_in_dim(down, own * HEAD_WIDTH, HEAD_WIDTH, 1)
    ups = [across(up, f) for f in range(fsdp)]
    lora = call(
        functools.partial(lora_body, half, fsdp),
        sds((tokens, rank), F32),
        [],
        pos,
        *ups,
        *swapped,
        n_scalar=1,
    )

    def project(targets):
        return call(
            functools.partial(project_body, half, planes, fsdp, slot, targets),
            [sds((tokens, LANES), BF)] * len(targets),
            [
                pltpu.VMEM((planes * w_rows + wide - slot, LANES * len(targets)), BF),
                pltpu.VMEM((rank, LANES * len(targets)), BF),
            ],
            pos,
            lora,
            down,
            *swapped,
            *weights,
            n_scalar=1,
        )

    first, second = range(half // 2, half), range(half // 2)
    partial = dict(zip(first, project(tuple(first))))
    partial = {s: in_plane(x, s) for s, x in partial.items()}
    rest = dict(zip(second, project(tuple(second))))
    partial.update({s: in_plane(x, s) for s, x in rest.items()})

    out, norm, mid = call(
        forward_body,
        [sds((tokens, LANES), F32), sds((1, tokens), F32), sds((tokens, rank), F32)],
        [pltpu.VMEM((LANES, tokens), BF), pltpu.VMEM((LANES, tokens), BF)],
        pos,
        query,
        key_value,
        far,
        down_head,
        n_scalar=1,
    )
    mid = sum(across(mid, f) for f in range(fsdp))
    both = jnp.concatenate([lora, mid], axis=1).astype(BF)
    both = [in_plane(both, s) for s in range(half)]
    adapter_grads = call(
        functools.partial(adapters_body, half),
        sds((rank, wide + HEAD_WIDTH), F32),
        [pltpu.VMEM((tokens, 2 * rank), BF)],
        pos,
        out,
        *both,
        *grads,
        n_scalar=1,
    )
    reduced = lax.all_to_all(adapter_grads, "ctx", split_axis=0, concat_axis=0, tiled=True)
    reduced = jnp.sum(reduced.reshape(planes, half, rank_rows, -1), axis=0)
    up_grad = reduced[:, :, :slot].reshape(half, rank_rows, strips, w_rows)
    up_grad = up_grad.transpose(1, 2, 0, 3).reshape(rank_rows, grad_cols)
    down_grad = reduced[:, :, wide:]
    down_grad = jnp.where(core % 2 == 0, down_grad, jnp.roll(down_grad, half // 2, axis=0))
    down_grad = down_grad.transpose(1, 0, 2).reshape(rank_rows, heads * HEAD_WIDTH)

    far_part, dq_far, grad_out, delta = call(
        functools.partial(far_body, half),
        [
            sds((2, tokens, LANES), BF),
            sds((LANES, tokens), F32),
            sds((tokens, LANES), BF),
            sds((1, tokens), F32),
        ],
        [pltpu.VMEM((LANES, tokens), BF)],
        pos,
        *[partial[s] for s in range(half)],
        query,
        far,
        out,
        norm,
        n_scalar=1,
    )
    back = to_earlier(far_part)
    dq, near = call(
        near_body,
        [sds((tokens, LANES), BF), sds((2, tokens, LANES), F32)],
        [pltpu.VMEM((LANES, tokens), BF)],
        pos,
        query,
        key_value,
        grad_out,
        norm,
        delta,
        dq_far,
        n_scalar=1,
    )
    merged = call(
        functools.partial(merge_body, half),
        [sds((3, rows, LANES), BF)] * half,
        [],
        pos,
        dq,
        near,
        back,
        n_scalar=1,
    )
    merged = [in_plane(x, s) for s, x in enumerate(merged)]
    query_grad, key_grad, value_grad = call(
        functools.partial(unpack_body, half),
        [sds((rows, heads * HEAD_WIDTH), BF)] * 3,
        [],
        pos,
        *merged,
        n_scalar=1,
    )
    return query_grad, key_grad, value_grad, down_grad, up_grad


def solution(mesh):
    split = P("ctx", "fsdp")
    in_specs = (split,) * 6 + (P(),) + (split,) * 2

    def body(*args):
        return on_device((mesh.shape["ctx"], mesh.shape["fsdp"]), *args)

    return jax.shard_map(
        body, mesh=mesh, in_specs=in_specs, out_specs=(split,) * 5, check_vma=False
    )
```

profile of v0, /device:TPU:0, one launch (start us, length us, event | category | flops | bytes accessed | tf_op | source)
XLA Modules:
  0.0 134.7 jit_solution(7858860069216054815)
XLA Ops:
  0.7 0.6 stack.23.pos_ref
  1.3 2.0 %shard_map.137 = (bf16[3,192,128]{2,1,0:T(8,128)(2,1)}, bf16[3,192,128]{2,1,0:T(8,128)(2,1)}, bf16[3,192,128]{2,1,0:T(8,128)(2,1)}, bf16[3,192,128]{2,1,0:T(8,128)(2,1)}) custom-call(s32[5]{0:T(128)} %stack.23.pos_ref, bf16[192,512]{1,0:T(8,128)(2,1)} %q_ref.1, bf16[192,512]{1,0:T(8,128)(2,1)} %k_ref.1, bf16[192,512]{1,0:T(8,128)(2,1)} %v_ref.1), custom_call_target="tpu_custom_call" | custom-call | tf_op jit(solution)/shard_map/pallas_call | solution.py:57
  3.3 3.0 %collective-permute-start = (bf16[3,192,128]{2,1,0:T(8,128)(2,1)}, bf16[3,192,128]{2,1,0:T(8,128)(2,1)S(1)}, u32[]{:S(2)}, u32[]{:S(2)}) collective-permute-start(bf16[3,192,128]{2,1,0:T(8,128)(2,1)} %get-tuple-element.36), channel_id=1, source_target_pairs={{0,2},{2,0},{4,6},{6,4},{8,10},{10,8},{12,14},{14,12},{16,18},{18,... | collective-permute-start | bytes 442376 | tf_op jit(solution)/shard_map/ppermute | solution.py:387
  6.3 1.5 %collective-permute-start.1 = (bf16[3,192,128]{2,1,0:T(8,128)(2,1)}, bf16[3,192,128]{2,1,0:T(8,128)(2,1)S(1)}, u32[]{:S(2)}, u32[]{:S(2)}) collective-permute-start(bf16[3,192,128]{2,1,0:T(8,128)(2,1)} %get-tuple-element.37), channel_id=1, source_target_pairs={{0,4},{2,6},{4,0},{6,2},{8,12},{10,14},{12,8},{14,10},{16,20},{18,... | collective-permute-start | bytes 442376 | tf_op jit(solution)/shard_map/ppermute | solution.py:387
  7.8 2.7 %shard_map.139 = (bf16[192,640]{1,0:T(8,128)(2,1)}, bf16[192,640]{1,0:T(8,128)(2,1)}, bf16[192,640]{1,0:T(8,128)(2,1)}, bf16[192,640]{1,0:T(8,128)(2,1)}) custom-call(s32[5]{0:T(128)} %stack.23.pos_ref, bf16[192,2560]{1,0:T(8,128)(2,1)} %g_ref.1), custom_call_target="tpu_custom_call" | custom-call | tf_op jit(solution)/shard_map/pallas_call | solution.py:57
  10.5 2.0 %collective-permute-start.5 = (bf16[192,640]{1,0:T(8,128)(2,1)}, bf16[192,640]{1,0:T(8,128)(2,1)S(1)}, u32[]{:S(2)}, u32[]{:S(2)}) collective-permute-start(bf16[192,640]{1,0:T(8,128)(2,1)} %get-tuple-element.42), channel_id=1, source_target_pairs={{0,2},{2,0},{4,6},{6,4},{8,10},{10,8},{12,14},{14,12},{16,18},{18,... | collective-permute-start | bytes 737288 | tf_op jit(solution)/shard_map/ppermute | solution.py:387
  12.5 1.5 %collective-permute-start.7 = (bf16[192,640]{1,0:T(8,128)(2,1)}, bf16[192,640]{1,0:T(8,128)(2,1)S(1)}, u32[]{:S(2)}, u32[]{:S(2)}) collective-permute-start(bf16[192,640]{1,0:T(8,128)(2,1)} %get-tuple-element.43), channel_id=1, source_target_pairs={{0,4},{2,6},{4,0},{6,2},{8,12},{10,14},{12,8},{14,10},{16,20},{18,... | collective-permute-start | bytes 737288 | tf_op jit(solution)/shard_map/ppermute | solution.py:387
  14.2 0.6 collective-permute-done.1.refs_2_
  14.9 0.8 collective-permute-done.2.refs_3_
  15.7 0.7 copy-done.28
  16.4 2.0 %shard_map.138 = (bf16[768,128]{1,0:T(8,128)(2,1)}, bf16[2,768,128]{2,1,0:T(8,128)(2,1)}) custom-call(s32[5]{0:T(128)} %stack.23.pos_ref, bf16[3,192,128]{2,1,0:T(8,128)(2,1)} %get-tuple-element.35.refs_0_, bf16[3,192,128]{2,1,0:T(8,128)(2,1)} %copy-done.26, bf16[3,192,128]{2,1,0:T(8,128)(2,1)} %copy-done.27, bf16[3,192,128]{2,1,0:T(8,128)(2,1)} %copy-done.28), custom_call_target="tpu_custom_call" | custom-call | tf_op jit(solution)/shard_map/pallas_call | solution.py:57
  18.4 3.5 %collective-permute-start.17 = (bf16[2,768,128]{2,1,0:T(8,128)(2,1)}, bf16[2,768,128]{2,1,0:T(8,128)(2,1)S(1)}, u32[]{:S(2)}, u32[]{:S(2)}) collective-permute-start(bf16[2,768,128]{2,1,0:T(8,128)(2,1)} %get-tuple-element.40.kv_ref), channel_id=1, source_target_pairs={{0,8},{2,10},{5,13},{7,15},{9,17},{11,19},{12,20},{14,22},{16,24},... | collective-permute-start | bytes 1179656 | tf_op jit(solution)/shard_map/ppermute | solution.py:407
  22.0 0.7 broadcast_in_dim.7
  22.7 4.9 %all-to-all-start = ((bf16[16,4,1152]{2,1,0:T(4,128)(2,1)}), bf16[16,4,1152]{2,1,0:T(4,128)(2,1)S(1)}, u32[]{:S(2)}, u32[]{:S(2)}) async-start(bf16[16,4,1152]{2,1,0:T(4,128)(2,1)} %bitcast.6), calls=%async_computation | async-start | bytes 294912 | tf_op jit(solution)/shard_map/all_to_all | solution.py:463
  27.7 2.9 %collective-permute-start.9 = (bf16[192,640]{1,0:T(8,128)(2,1)S(1)}, bf16[192,640]{1,0:T(8,128)(2,1)S(1)}, u32[]{:S(2)}, u32[]{:S(2)}) collective-permute-start(bf16[192,640]{1,0:T(8,128)(2,1)S(1)} %copy-done.33), channel_id=1, source_target_pairs={{0,6},{2,4},{4,2},{6,0},{8,14},{10,12},{12,10},{14,8},{16,22},{18,... | collective-permute-start | bytes 737288 | tf_op jit(solution)/shard_map/ppermute | solution.py:387
  30.6 0.1 collective-permute-start.6
  30.7 0.4 collective-permute-start.8
  31.1 4.6 %all-to-all-done = bf16[16,4,1152]{2,1,0:T(4,128)(2,1)S(1)} async-done(((bf16[16,4,1152]{2,1,0:T(4,128)(2,1)}), bf16[16,4,1152]{2,1,0:T(4,128)(2,1)S(1)}, u32[]{:S(2)}, u32[]{:S(2)}) %all-to-all-start) | async-done | bytes 147488 | tf_op jit(solution)/shard_map/all_to_all | solution.py:463
  35.8 0.6 copy-done.31
  36.4 0.8 copy.20.index_ref
  37.2 3.8 %shard_map.141.refs_10_ = bf16[320,512]{1,0:T(8,128)(2,1)} custom-call(s32[320,512]{1,0:T(8,128)} %codes_ref.1, s32[320,8]{1,0:T(8,128)} %copy.20.index_ref, f32[2,128]{1,0:T(2,128)} %bitcast.19, f32[1,128]{1,0:T(1,128)} %constant.58.clone.nf4_ref), custom_call_target="tpu_custom_call" | custom-call | tf_op jit(solution)/shard_map/pallas_call | solution.py:57
  41.0 0.7 collective-permute-start.11
  41.7 1.1 collective-permute-start.12
  42.8 2.2 %collective-permute-start.13 = (bf16[320,512]{1,0:T(8,128)(2,1)}, bf16[320,512]{1,0:T(8,128)(2,1)S(1)}, u32[]{:S(2)}, u32[]{:S(2)}) collective-permute-start(bf16[320,512]{1,0:T(8,128)(2,1)} %shard_map.141.refs_10_), channel_id=1, source_target_pairs={{0,24},{2,26},{4,28},{6,30},{8,0},{10,2},{12,4},{14,6},{16,8},{18,... | collective-permute-start | bytes 983048 | tf_op jit(solution)/shard_map/ppermute | solution.py:392
  45.1 0.7 constant_dynamic-slice_fusion.down_ref
  45.7 3.8 %shard_map.144 = (f32[768,128]{1,0:T(8,128)}, f32[1,768]{1,0:T(1,128)}, f32[768,64]{1,0:T(8,128)}) custom-call(s32[5]{0:T(128)} %stack.23.pos_ref, bf16[768,128]{1,0:T(8,128)(2,1)} %get-tuple-element.39.q_ref.refs_4_, bf16[2,768,128]{2,1,0:T(8,128)(2,1)} %get-tuple-element.40.kv_ref, bf16[2,768,128]{2,1,0:T(8,128)(2,1)} %copy-done.8, ...), custom_call_target="tpu_custom_call" | custom-call | tf_op jit(solution)/shard_map/pallas_call | solution.py:57
  49.6 1.8 %collective-permute-start.22 = (f32[768,64]{1,0:T(8,128)}, f32[768,64]{1,0:T(8,128)S(1)}, u32[]{:S(2)}, u32[]{:S(2)}) collective-permute-start(f32[768,64]{1,0:T(8,128)} %get-tuple-element.64), channel_id=1, source_target_pairs={{0,1},{1,0},{2,3},{3,2},{4,5},{5,4},{6,7},{7,6},{8,9},{9,8},{10,11... | collective-permute-start | bytes 589832 | tf_op jit(solution)/shard_map/ppermute | solution.py:397
  51.4 0.7 copy-done.7
  52.1 3.1 %shard_map.140.refs_0_ = f32[768,64]{1,0:T(8,128)} custom-call(s32[5]{0:T(128)} %stack.23.pos_ref, bf16[64,640]{1,0:T(8,128)(2,1)} %copy-done.16, bf16[64,640]{1,0:T(8,128)(2,1)} %copy-done.29, bf16[192,640]{1,0:T(8,128)(2,1)} %get-tuple-element.41.refs_2_.refs_4_, bf16[192,640]{1,0:T(8,128)(2,1)} %copy-done.4, bf16[192,640]{1,0:T(8,128)(2,1)} %copy-done.1, ...), custom_call_target="tpu_custom_call" | custom-call | tf_op jit(solution)/shard_map/pallas_call | solution.py:57
  55.2 1.0 convert.6
  56.2 10.6 %collective-permute-done.12.refs_12_ = bf16[320,512]{1,0:T(8,128)(2,1)S(1)} collective-permute-done((bf16[320,512]{1,0:T(8,128)(2,1)}, bf16[320,512]{1,0:T(8,128)(2,1)S(1)}, u32[]{:S(2)}, u32[]{:S(2)}) %collective-permute-start.12) | collective-permute-done | bytes 327712 | tf_op jit(solution)/shard_map/ppermute | solution.py:392
  66.8 0.7 copy-done.10
  67.6 0.7 copy-done.11
  68.3 3.9 %shard_map.142 = (bf16[768,128]{1,0:T(8,128)(2,1)}, bf16[768,128]{1,0:T(8,128)(2,1)}) custom-call(s32[5]{0:T(128)} %stack.23.pos_ref, f32[768,64]{1,0:T(8,128)} %shard_map.140.refs_0_, bf16[64,512]{1,0:T(8,128)(2,1)} %copy-done.13, bf16[192,640]{1,0:T(8,128)(2,1)} %get-tuple-element.41.refs_2_.refs_4_, bf16[192,640]{1,0:T(8,128)(2,1)} %copy-done.4, ...), custom_call_target="tpu_custom_call" | custom-call | tf_op jit(solution)/shard_map/pallas_call | solution.py:57
  72.1 1.1 collective-permute-start.14
  73.3 3.9 %shard_map.143 = (bf16[768,128]{1,0:T(8,128)(2,1)}, bf16[768,128]{1,0:T(8,128)(2,1)}) custom-call(s32[5]{0:T(128)} %stack.23.pos_ref, f32[768,64]{1,0:T(8,128)} %shard_map.140.refs_0_, bf16[64,512]{1,0:T(8,128)(2,1)} %copy-done.13, bf16[192,640]{1,0:T(8,128)(2,1)} %get-tuple-element.41.refs_2_.refs_4_, bf16[192,640]{1,0:T(8,128)(2,1)} %copy-done.4, ...), custom_call_target="tpu_custom_call" | custom-call | tf_op jit(solution)/shard_map/pallas_call | solution.py:57
  77.1 0.2 collective-permute-start.15
  77.3 2.3 %collective-permute-start.16 = (bf16[768,128]{1,0:T(8,128)(2,1)}, bf16[768,128]{1,0:T(8,128)(2,1)S(1)}, u32[]{:S(2)}, u32[]{:S(2)}) collective-permute-start(bf16[768,128]{1,0:T(8,128)(2,1)} %get-tuple-element.48), channel_id=1, source_target_pairs={{0,6},{2,4},{4,2},{6,0},{8,14},{10,12},{12,10},{14,8},{16,22},{18,... | collective-permute-start | bytes 589832 | tf_op jit(solution)/shard_map/ppermute | solution.py:387
  79.6 0.1 pad_maximum_fusion.refs_0_
  79.8 1.1 collective-permute-start.23
  80.9 0.2 collective-permute-start.24
  81.1 2.3 %collective-permute-start.25 = (bf16[768,128]{1,0:T(8,128)(2,1)S(1)}, bf16[768,128]{1,0:T(8,128)(2,1)S(1)}, u32[]{:S(2)}, u32[]{:S(2)}) collective-permute-start(bf16[768,128]{1,0:T(8,128)(2,1)S(1)} %pad_maximum_fusion.refs_0_), channel_id=1, source_target_pairs={{0,6},{2,4},{4,2},{6,0},{8,14},{10,12},{12,10},{14,8},{16,22},{18,... | collective-permute-start | bytes 589832 | tf_op jit(solution)/shard_map/ppermute | solution.py:387
  83.3 9.0 %collective-permute-done.15.refs_2_ = bf16[768,128]{1,0:T(8,128)(2,1)S(1)} collective-permute-done((bf16[768,128]{1,0:T(8,128)(2,1)}, bf16[768,128]{1,0:T(8,128)(2,1)S(1)}, u32[]{:S(2)}, u32[]{:S(2)}) %collective-permute-start.15) | collective-permute-done | bytes 196640 | tf_op jit(solution)/shard_map/ppermute | solution.py:387
  92.3 0.7 copy-done.21
  93.0 2.9 %shard_map.145 = (bf16[2,768,128]{2,1,0:T(8,128)(2,1)}, f32[128,768]{1,0:T(8,128)}, bf16[768,128]{1,0:T(8,128)(2,1)}, f32[1,768]{1,0:T(1,128)}) custom-call(s32[5]{0:T(128)} %stack.23.pos_ref, bf16[768,128]{1,0:T(8,128)(2,1)} %get-tuple-element.45.refs_0_, bf16[768,128]{1,0:T(8,128)(2,1)} %copy-done.20, bf16[768,128]{1,0:T(8,128)(2,1)} %copy-done.21, ...), custom_call_target="tpu_custom_call" | custom-call | tf_op jit(solution)/shard_map/pallas_call | solution.py:57
  96.0 1.3 collective-permute-start.18
  97.3 0.6 copy-done.17
  98.0 0.7 copy-done.19
  98.7 2.9 %shard_map.149 = f32[64,768]{1,0:T(8,128)} custom-call(s32[5]{0:T(128)} %stack.23.pos_ref, f32[768,128]{1,0:T(8,128)} %get-tuple-element.49.refs_6_.o_ref, bf16[768,128]{1,0:T(8,128)(2,1)} %copy-done.12, bf16[768,128]{1,0:T(8,128)(2,1)} %copy-done.17, bf16[768,128]{1,0:T(8,128)(2,1)} %copy-done.18, bf16[768,128]{1,0:T(8,128)(2,1)} %copy-done.19, ...), custom_call_target="tpu_custom_call" | custom-call | tf_op jit(solution)/shard_map/pallas_call | solution.py:57
  101.6 1.7 %all_to_all.17 = f32[16,4,768]{2,1,0:T(4,128)} reshape(f32[64,768]{1,0:T(8,128)} %shard_map.149) | data formatting | bytes 393216 | tf_op jit(solution)/shard_map/all_to_all | solution.py:524
  103.3 11.1 %all-to-all-start.1 = ((f32[16,4,768]{2,1,0:T(4,128)}), f32[16,4,768]{2,1,0:T(4,128)S(1)}, u32[]{:S(2)}, u32[]{:S(2)}) async-start(f32[16,4,768]{2,1,0:T(4,128)} %all_to_all.17), calls=%async_computation.1 | async-start | bytes 393216 | tf_op jit(solution)/shard_map/all_to_all | solution.py:524
  114.4 3.4 %shard_map.146 = (bf16[768,128]{1,0:T(8,128)(2,1)}, f32[2,768,128]{2,1,0:T(8,128)}) custom-call(s32[5]{0:T(128)} %stack.23.pos_ref, bf16[768,128]{1,0:T(8,128)(2,1)} %get-tuple-element.39.q_ref.refs_4_, bf16[2,768,128]{2,1,0:T(8,128)(2,1)} %get-tuple-element.40.kv_ref, bf16[768,128]{1,0:T(8,128)(2,1)} %get-tuple-element.51.do_ref, ...), custom_call_target="tpu_custom_call" | custom-call | tf_op jit(solution)/shard_map/pallas_call | solution.py:57
  117.9 0.8 copy-done.15
  118.6 2.2 %shard_map.147 = (bf16[3,192,128]{2,1,0:T(8,128)(2,1)}, bf16[3,192,128]{2,1,0:T(8,128)(2,1)}, bf16[3,192,128]{2,1,0:T(8,128)(2,1)}, bf16[3,192,128]{2,1,0:T(8,128)(2,1)}) custom-call(s32[5]{0:T(128)} %stack.23.pos_ref, bf16[768,128]{1,0:T(8,128)(2,1)} %get-tuple-element.54.dq_ref, f32[2,768,128]{2,1,0:T(8,128)} %get-tuple-element.55.near_ref, ...), custom_call_target="tpu_custom_call" | custom-call | tf_op jit(solution)/shard_map/pallas_call | solution.py:57
  120.8 1.9 %collective-permute-start.19 = (bf16[3,192,128]{2,1,0:T(8,128)(2,1)}, bf16[3,192,128]{2,1,0:T(8,128)(2,1)S(1)}, u32[]{:S(2)}, u32[]{:S(2)}) collective-permute-start(bf16[3,192,128]{2,1,0:T(8,128)(2,1)} %get-tuple-element.58), channel_id=1, source_target_pairs={{0,2},{2,0},{4,6},{6,4},{8,10},{10,8},{12,14},{14,12},{16,18},{18,... | collective-permute-start | bytes 442376 | tf_op jit(solution)/shard_map/ppermute | solution.py:387
  122.7 1.5 %collective-permute-start.20 = (bf16[3,192,128]{2,1,0:T(8,128)(2,1)}, bf16[3,192,128]{2,1,0:T(8,128)(2,1)S(1)}, u32[]{:S(2)}, u32[]{:S(2)}) collective-permute-start(bf16[3,192,128]{2,1,0:T(8,128)(2,1)} %get-tuple-element.59), channel_id=1, source_target_pairs={{0,4},{2,6},{4,0},{6,2},{8,12},{10,14},{12,8},{14,10},{16,20},{18,... | collective-permute-start | bytes 442376 | tf_op jit(solution)/shard_map/ppermute | solution.py:387
  124.2 0.1 collective-permute-start.21
  124.3 1.9 %collective-permute-done.19.refs_1_ = bf16[3,192,128]{2,1,0:T(8,128)(2,1)S(1)} collective-permute-done((bf16[3,192,128]{2,1,0:T(8,128)(2,1)}, bf16[3,192,128]{2,1,0:T(8,128)(2,1)S(1)}, u32[]{:S(2)}, u32[]{:S(2)}) %collective-permute-start.19) | collective-permute-done | bytes 147488 | tf_op jit(solution)/shard_map/ppermute | solution.py:387
  126.2 1.9 %collective-permute-done.20.refs_2_ = bf16[3,192,128]{2,1,0:T(8,128)(2,1)S(1)} collective-permute-done((bf16[3,192,128]{2,1,0:T(8,128)(2,1)}, bf16[3,192,128]{2,1,0:T(8,128)(2,1)S(1)}, u32[]{:S(2)}, u32[]{:S(2)}) %collective-permute-start.20) | collective-permute-done | bytes 147488 | tf_op jit(solution)/shard_map/ppermute | solution.py:387
  128.1 2.4 %collective-permute-done.21.refs_3_ = bf16[3,192,128]{2,1,0:T(8,128)(2,1)S(1)} collective-permute-done((bf16[3,192,128]{2,1,0:T(8,128)(2,1)}, bf16[3,192,128]{2,1,0:T(8,128)(2,1)S(1)}, u32[]{:S(2)}, u32[]{:S(2)}) %collective-permute-start.21) | collective-permute-done | bytes 147488 | tf_op jit(solution)/shard_map/ppermute | solution.py:387
  130.5 0.7 copy-done.25
  131.1 2.0 %shard_map.148 = (bf16[192,512]{1,0:T(8,128)(2,1)}, bf16[192,512]{1,0:T(8,128)(2,1)}, bf16[192,512]{1,0:T(8,128)(2,1)}) custom-call(s32[5]{0:T(128)} %stack.23.pos_ref, bf16[3,192,128]{2,1,0:T(8,128)(2,1)} %get-tuple-element.57.refs_0_, bf16[3,192,128]{2,1,0:T(8,128)(2,1)} %copy-done.23, bf16[3,192,128]{2,1,0:T(8,128)(2,1)} %copy-done.24, ...), custom_call_target="tpu_custom_call" | custom-call | tf_op jit(solution)/shard_map/pallas_call | solution.py:57
  133.4 0.7 reshape.44
  134.1 0.6 fusion
  (96 shorter events, 1.0 us)
Async XLA Ops:
  3.3 10.9 %collective-permute-start = (bf16[3,192,128]{2,1,0:T(8,128)(2,1)}, bf16[3,192,128]{2,1,0:T(8,128)(2,1)S(1)}, u32[]{:S(2)}, u32[]{:S(2)}) collective-permute-start(bf16[3,192,128]{2,1,0:T(8,128)(2,1)} %get-tuple-element.36), channel_id=1, source_target_pairs={{0,2},{2,0},{4,6},{6,4},{8,10},{10,8},{12,14},{14,12},{16,18},{18,... | collective-permute-start | bytes 442376 | tf_op jit(solution)/shard_map/ppermute | solution.py:387
  6.3 8.6 %collective-permute-start.1 = (bf16[3,192,128]{2,1,0:T(8,128)(2,1)}, bf16[3,192,128]{2,1,0:T(8,128)(2,1)S(1)}, u32[]{:S(2)}, u32[]{:S(2)}) collective-permute-start(bf16[3,192,128]{2,1,0:T(8,128)(2,1)} %get-tuple-element.37), channel_id=1, source_target_pairs={{0,4},{2,6},{4,0},{6,2},{8,12},{10,14},{12,8},{14,10},{16,20},{18,... | collective-permute-start | bytes 442376 | tf_op jit(solution)/shard_map/ppermute | solution.py:387
  7.8 6.2 %copy-start.30 = (bf16[4,2560]{1,0:T(4,128)(2,1)S(1)}, bf16[4,2560]{1,0:T(4,128)(2,1)}, u32[]{:S(2)}) copy-start(bf16[4,2560]{1,0:T(4,128)(2,1)} %param.18) | copy-start | bytes 61444
  7.8 7.9 %collective-permute-start.2 = (bf16[3,192,128]{2,1,0:T(8,128)(2,1)}, bf16[3,192,128]{2,1,0:T(8,128)(2,1)S(1)}, u32[]{:S(2)}, u32[]{:S(2)}) collective-permute-start(bf16[3,192,128]{2,1,0:T(8,128)(2,1)} %get-tuple-element.38), channel_id=1, source_target_pairs={{0,6},{2,4},{4,2},{6,0},{8,14},{10,12},{12,10},{14,8},{16,22},{18,... | collective-permute-start | bytes 442376 | tf_op jit(solution)/shard_map/ppermute | solution.py:387
  10.5 20.0 %collective-permute-start.5 = (bf16[192,640]{1,0:T(8,128)(2,1)}, bf16[192,640]{1,0:T(8,128)(2,1)S(1)}, u32[]{:S(2)}, u32[]{:S(2)}) collective-permute-start(bf16[192,640]{1,0:T(8,128)(2,1)} %get-tuple-element.42), channel_id=1, source_target_pairs={{0,2},{2,0},{4,6},{6,4},{8,10},{10,8},{12,14},{14,12},{16,18},{18,... | collective-permute-start | bytes 737288 | tf_op jit(solution)/shard_map/ppermute | solution.py:387
  12.5 18.2 %collective-permute-start.7 = (bf16[192,640]{1,0:T(8,128)(2,1)}, bf16[192,640]{1,0:T(8,128)(2,1)S(1)}, u32[]{:S(2)}, u32[]{:S(2)}) collective-permute-start(bf16[192,640]{1,0:T(8,128)(2,1)} %get-tuple-element.43), channel_id=1, source_target_pairs={{0,4},{2,6},{4,0},{6,2},{8,12},{10,14},{12,8},{14,10},{16,20},{18,... | collective-permute-start | bytes 737288 | tf_op jit(solution)/shard_map/ppermute | solution.py:387
  14.2 1.5 %copy-start.26 = (bf16[3,192,128]{2,1,0:T(8,128)(2,1)}, bf16[3,192,128]{2,1,0:T(8,128)(2,1)S(1)}, u32[]{:S(2)}) copy-start(bf16[3,192,128]{2,1,0:T(8,128)(2,1)S(1)} %collective-permute-done.refs_1_) | copy-start | bytes 442372
  14.9 0.8 copy-start.27
  15.7 0.7 copy-start.28
  16.4 5.5 %copy-start.32 = (bf16[4,512]{1,0:T(4,128)(2,1)S(1)}, bf16[4,512]{1,0:T(4,128)(2,1)}, u32[]{:S(2)}) copy-start(bf16[4,512]{1,0:T(4,128)(2,1)} %param.17) | copy-start | bytes 12292
  18.4 26.6 %collective-permute-start.17 = (bf16[2,768,128]{2,1,0:T(8,128)(2,1)}, bf16[2,768,128]{2,1,0:T(8,128)(2,1)S(1)}, u32[]{:S(2)}, u32[]{:S(2)}) collective-permute-start(bf16[2,768,128]{2,1,0:T(8,128)(2,1)} %get-tuple-element.40.kv_ref), channel_id=1, source_target_pairs={{0,8},{2,10},{5,13},{7,15},{9,17},{11,19},{12,20},{14,22},{16,24},... | collective-permute-start | bytes 1179656 | tf_op jit(solution)/shard_map/ppermute | solution.py:407
  21.9 5.8 %copy-start.33 = (bf16[192,640]{1,0:T(8,128)(2,1)S(1)}, bf16[192,640]{1,0:T(8,128)(2,1)}, u32[]{:S(2)}) copy-start(bf16[192,640]{1,0:T(8,128)(2,1)} %get-tuple-element.44) | copy-start | bytes 737284
  22.0 5.6 %copy-start = (bf16[192,640]{1,0:T(8,128)(2,1)S(1)}, bf16[192,640]{1,0:T(8,128)(2,1)}, u32[]{:S(2)}) copy-start(bf16[192,640]{1,0:T(8,128)(2,1)} %get-tuple-element.41.refs_2_.refs_4_) | copy-start | bytes 737284
  22.7 13.0 %all-to-all-start = ((bf16[16,4,1152]{2,1,0:T(4,128)(2,1)}), bf16[16,4,1152]{2,1,0:T(4,128)(2,1)S(1)}, u32[]{:S(2)}, u32[]{:S(2)}) async-start(bf16[16,4,1152]{2,1,0:T(4,128)(2,1)} %bitcast.6), calls=%async_computation | async-start | bytes 294912 | tf_op jit(solution)/shard_map/all_to_all | solution.py:463
  27.6 8.1 %collective-permute-start.4 = (bf16[192,640]{1,0:T(8,128)(2,1)S(1)}, bf16[192,640]{1,0:T(8,128)(2,1)S(1)}, u32[]{:S(2)}, u32[]{:S(2)}) collective-permute-start(bf16[192,640]{1,0:T(8,128)(2,1)S(1)} %copy-done), channel_id=1, source_target_pairs={{0,1},{1,0},{2,3},{3,2},{4,5},{5,4},{6,7},{7,6},{8,9},{9,8},{10,11... | collective-permute-start | bytes 737288 | tf_op jit(solution)/shard_map/ppermute | solution.py:397
  27.7 13.3 %collective-permute-start.9 = (bf16[192,640]{1,0:T(8,128)(2,1)S(1)}, bf16[192,640]{1,0:T(8,128)(2,1)S(1)}, u32[]{:S(2)}, u32[]{:S(2)}) collective-permute-start(bf16[192,640]{1,0:T(8,128)(2,1)S(1)} %copy-done.33), channel_id=1, source_target_pairs={{0,6},{2,4},{4,2},{6,0},{8,14},{10,12},{12,10},{14,8},{16,22},{18,... | collective-permute-start | bytes 737288 | tf_op jit(solution)/shard_map/ppermute | solution.py:387
  30.6 6.6 %copy-start.1 = (bf16[192,640]{1,0:T(8,128)(2,1)}, bf16[192,640]{1,0:T(8,128)(2,1)S(1)}, u32[]{:S(2)}) copy-start(bf16[192,640]{1,0:T(8,128)(2,1)S(1)} %collective-permute-done.5.refs_4_.refs_5_) | copy-start | bytes 737284
  30.6 12.2 %collective-permute-start.6 = (bf16[192,640]{1,0:T(8,128)(2,1)S(1)}, bf16[192,640]{1,0:T(8,128)(2,1)S(1)}, u32[]{:S(2)}, u32[]{:S(2)}) collective-permute-start(bf16[192,640]{1,0:T(8,128)(2,1)S(1)} %collective-permute-done.5.refs_4_.refs_5_), channel_id=1, source_target_pairs={{0,1},{1,0},{2,3},{3,2},{4,5},{5,4},{6,7},{7,6},{8,9},{9,8},{10,11... | collective-permute-start | bytes 737288 | tf_op jit(solution)/shard_map/ppermute | solution.py:397
  30.7 6.5 %copy-start.2 = (bf16[192,640]{1,0:T(8,128)(2,1)}, bf16[192,640]{1,0:T(8,128)(2,1)S(1)}, u32[]{:S(2)}) copy-start(bf16[192,640]{1,0:T(8,128)(2,1)S(1)} %collective-permute-done.7.refs_6_) | copy-start | bytes 737284
  30.7 18.9 %collective-permute-start.8 = (bf16[192,640]{1,0:T(8,128)(2,1)S(1)}, bf16[192,640]{1,0:T(8,128)(2,1)S(1)}, u32[]{:S(2)}, u32[]{:S(2)}) collective-permute-start(bf16[192,640]{1,0:T(8,128)(2,1)S(1)} %collective-permute-done.7.refs_6_), channel_id=1, source_target_pairs={{0,1},{1,0},{2,3},{3,2},{4,5},{5,4},{6,7},{7,6},{8,9},{9,8},{10,11... | collective-permute-start | bytes 737288 | tf_op jit(solution)/shard_map/ppermute | solution.py:397
  35.7 0.7 copy-start.31
  35.7 1.5 %copy-start.16 = (bf16[64,640]{1,0:T(8,128)(2,1)}, bf16[64,640]{1,0:T(8,128)(2,1)S(1)}, u32[]{:S(2)}) copy-start(bf16[64,640]{1,0:T(8,128)(2,1)S(1)} %slice.28.refs_0_) | copy-start | bytes 245764
  35.7 5.3 %copy-start.4 = (bf16[192,640]{1,0:T(8,128)(2,1)}, bf16[192,640]{1,0:T(8,128)(2,1)S(1)}, u32[]{:S(2)}) copy-start(bf16[192,640]{1,0:T(8,128)(2,1)S(1)} %collective-permute-done.4.refs_3_) | copy-start | bytes 737284
  35.8 6.0 %collective-permute-start.3 = (bf16[64,640]{1,0:T(8,128)(2,1)S(1)}, bf16[64,640]{1,0:T(8,128)(2,1)S(1)}, u32[]{:S(2)}, u32[]{:S(2)}) collective-permute-start(bf16[64,640]{1,0:T(8,128)(2,1)S(1)} %slice.28.refs_0_), channel_id=1, source_target_pairs={{0,1},{1,0},{2,3},{3,2},{4,5},{5,4},{6,7},{7,6},{8,9},{9,8},{10,11... | collective-permute-start | bytes 245768 | tf_op jit(solution)/shard_map/ppermute | solution.py:397
  41.0 8.6 %copy-start.3 = (bf16[192,640]{1,0:T(8,128)(2,1)}, bf16[192,640]{1,0:T(8,128)(2,1)S(1)}, u32[]{:S(2)}) copy-start(bf16[192,640]{1,0:T(8,128)(2,1)S(1)} %collective-permute-done.9.refs_8_.refs_7_) | copy-start | bytes 737284
  41.0 15.2 %collective-permute-start.11 = (bf16[320,512]{1,0:T(8,128)(2,1)}, bf16[320,512]{1,0:T(8,128)(2,1)S(1)}, u32[]{:S(2)}, u32[]{:S(2)}) collective-permute-start(bf16[320,512]{1,0:T(8,128)(2,1)} %shard_map.141.refs_10_), channel_id=1, source_target_pairs={{0,8},{2,10},{4,12},{6,14},{8,16},{10,18},{12,20},{14,22},{16,24},... | collective-permute-start | bytes 983048 | tf_op jit(solution)/shard_map/ppermute | solution.py:392
  41.7 7.9 %copy-start.29 = (bf16[64,640]{1,0:T(8,128)(2,1)}, bf16[64,640]{1,0:T(8,128)(2,1)S(1)}, u32[]{:S(2)}) copy-start(bf16[64,640]{1,0:T(8,128)(2,1)S(1)} %collective-permute-done.3.refs_1_) | copy-start | bytes 245764
  41.7 25.1 %collective-permute-start.12 = (bf16[320,512]{1,0:T(8,128)(2,1)}, bf16[320,512]{1,0:T(8,128)(2,1)S(1)}, u32[]{:S(2)}, u32[]{:S(2)}) collective-permute-start(bf16[320,512]{1,0:T(8,128)(2,1)} %shard_map.141.refs_10_), channel_id=1, source_target_pairs={{0,16},{2,18},{4,20},{6,22},{8,24},{10,26},{12,28},{14,30},{16,0},... | collective-permute-start | bytes 983048 | tf_op jit(solution)/shard_map/ppermute | solution.py:392
  42.8 6.8 %copy-start.5 = (bf16[192,640]{1,0:T(8,128)(2,1)}, bf16[192,640]{1,0:T(8,128)(2,1)S(1)}, u32[]{:S(2)}) copy-start(bf16[192,640]{1,0:T(8,128)(2,1)S(1)} %collective-permute-done.6.refs_5_) | copy-start | bytes 737284
  42.8 24.0 %collective-permute-start.13 = (bf16[320,512]{1,0:T(8,128)(2,1)}, bf16[320,512]{1,0:T(8,128)(2,1)S(1)}, u32[]{:S(2)}, u32[]{:S(2)}) collective-permute-start(bf16[320,512]{1,0:T(8,128)(2,1)} %shard_map.141.refs_10_), channel_id=1, source_target_pairs={{0,24},{2,26},{4,28},{6,30},{8,0},{10,2},{12,4},{14,6},{16,8},{18,... | collective-permute-start | bytes 983048 | tf_op jit(solution)/shard_map/ppermute | solution.py:392
  45.0 4.6 %copy-start.13 = (bf16[64,512]{1,0:T(8,128)(2,1)}, bf16[64,512]{1,0:T(8,128)(2,1)S(1)}, u32[]{:S(2)}) copy-start(bf16[64,512]{1,0:T(8,128)(2,1)S(1)} %slice.29.refs_1_) | copy-start | bytes 196612
  45.0 0.8 copy-start.8
  45.0 6.4 %collective-permute-start.10 = (bf16[192,640]{1,0:T(8,128)(2,1)S(1)}, bf16[192,640]{1,0:T(8,128)(2,1)S(1)}, u32[]{:S(2)}, u32[]{:S(2)}) collective-permute-start(bf16[192,640]{1,0:T(8,128)(2,1)S(1)} %collective-permute-done.9.refs_8_.refs_7_), channel_id=1, source_target_pairs={{0,1},{1,0},{2,3},{3,2},{4,5},{5,4},{6,7},{7,6},{8,9},{9,8},{10,11... | collective-permute-start | bytes 737288 | tf_op jit(solution)/shard_map/ppermute | solution.py:397
  49.6 1.8 %copy-start.6 = (bf16[192,640]{1,0:T(8,128)(2,1)}, bf16[192,640]{1,0:T(8,128)(2,1)S(1)}, u32[]{:S(2)}) copy-start(bf16[192,640]{1,0:T(8,128)(2,1)S(1)} %collective-permute-done.8.refs_7_) | copy-start | bytes 737284
  49.6 30.0 %collective-permute-start.22 = (f32[768,64]{1,0:T(8,128)}, f32[768,64]{1,0:T(8,128)S(1)}, u32[]{:S(2)}, u32[]{:S(2)}) collective-permute-start(f32[768,64]{1,0:T(8,128)} %get-tuple-element.64), channel_id=1, source_target_pairs={{0,1},{1,0},{2,3},{3,2},{4,5},{5,4},{6,7},{7,6},{8,9},{9,8},{10,11... | collective-permute-start | bytes 589832 | tf_op jit(solution)/shard_map/ppermute | solution.py:397
  51.4 0.7 copy-start.7
  56.2 10.6 %copy-start.9 = (bf16[320,512]{1,0:T(8,128)(2,1)}, bf16[320,512]{1,0:T(8,128)(2,1)S(1)}, u32[]{:S(2)}) copy-start(bf16[320,512]{1,0:T(8,128)(2,1)S(1)} %collective-permute-done.11.refs_11_) | copy-start | bytes 983044
  66.8 0.7 copy-start.10
  67.5 0.7 copy-start.11
  72.1 7.4 %copy-start.14 = (f32[768,64]{1,0:T(8,128)S(1)}, f32[768,64]{1,0:T(8,128)}, u32[]{:S(2)}) copy-start(f32[768,64]{1,0:T(8,128)} %get-tuple-element.64) | copy-start | bytes 589828
  72.1 8.9 %collective-permute-start.14 = (bf16[768,128]{1,0:T(8,128)(2,1)}, bf16[768,128]{1,0:T(8,128)(2,1)S(1)}, u32[]{:S(2)}, u32[]{:S(2)}) collective-permute-start(bf16[768,128]{1,0:T(8,128)(2,1)} %get-tuple-element.46), channel_id=1, source_target_pairs={{0,2},{2,0},{4,6},{6,4},{8,10},{10,8},{12,14},{14,12},{16,18},{18,... | collective-permute-start | bytes 589832 | tf_op jit(solution)/shard_map/ppermute | solution.py:387
  77.1 15.2 %collective-permute-start.15 = (bf16[768,128]{1,0:T(8,128)(2,1)}, bf16[768,128]{1,0:T(8,128)(2,1)S(1)}, u32[]{:S(2)}, u32[]{:S(2)}) collective-permute-start(bf16[768,128]{1,0:T(8,128)(2,1)} %get-tuple-element.47), channel_id=1, source_target_pairs={{0,4},{2,6},{4,0},{6,2},{8,12},{10,14},{12,8},{14,10},{16,20},{18,... | collective-permute-start | bytes 589832 | tf_op jit(solution)/shard_map/ppermute | solution.py:387
  77.3 15.0 %collective-permute-start.16 = (bf16[768,128]{1,0:T(8,128)(2,1)}, bf16[768,128]{1,0:T(8,128)(2,1)S(1)}, u32[]{:S(2)}, u32[]{:S(2)}) collective-permute-start(bf16[768,128]{1,0:T(8,128)(2,1)} %get-tuple-element.48), channel_id=1, source_target_pairs={{0,6},{2,4},{4,2},{6,0},{8,14},{10,12},{12,10},{14,8},{16,22},{18,... | collective-permute-start | bytes 589832 | tf_op jit(solution)/shard_map/ppermute | solution.py:387
  79.8 16.2 %copy-start.12 = (bf16[768,128]{1,0:T(8,128)(2,1)}, bf16[768,128]{1,0:T(8,128)(2,1)S(1)}, u32[]{:S(2)}) copy-start(bf16[768,128]{1,0:T(8,128)(2,1)S(1)} %pad_maximum_fusion.refs_0_) | copy-start | bytes 589828
  79.8 17.5 %collective-permute-start.23 = (bf16[768,128]{1,0:T(8,128)(2,1)S(1)}, bf16[768,128]{1,0:T(8,128)(2,1)S(1)}, u32[]{:S(2)}, u32[]{:S(2)}) collective-permute-start(bf16[768,128]{1,0:T(8,128)(2,1)S(1)} %pad_maximum_fusion.refs_0_), channel_id=1, source_target_pairs={{0,2},{2,0},{4,6},{6,4},{8,10},{10,8},{12,14},{14,12},{16,18},{18,... | collective-permute-start | bytes 589832 | tf_op jit(solution)/shard_map/ppermute | solution.py:387
  80.9 16.4 %collective-permute-start.24 = (bf16[768,128]{1,0:T(8,128)(2,1)S(1)}, bf16[768,128]{1,0:T(8,128)(2,1)S(1)}, u32[]{:S(2)}, u32[]{:S(2)}) collective-permute-start(bf16[768,128]{1,0:T(8,128)(2,1)S(1)} %pad_maximum_fusion.refs_0_), channel_id=1, source_target_pairs={{0,4},{2,6},{4,0},{6,2},{8,12},{10,14},{12,8},{14,10},{16,20},{18,... | collective-permute-start | bytes 589832 | tf_op jit(solution)/shard_map/ppermute | solution.py:387
  81.1 11.2 %copy-start.20 = (bf16[768,128]{1,0:T(8,128)(2,1)}, bf16[768,128]{1,0:T(8,128)(2,1)S(1)}, u32[]{:S(2)}) copy-start(bf16[768,128]{1,0:T(8,128)(2,1)S(1)} %collective-permute-done.14.refs_1_) | copy-start | bytes 589828
  81.1 16.2 %collective-permute-start.25 = (bf16[768,128]{1,0:T(8,128)(2,1)S(1)}, bf16[768,128]{1,0:T(8,128)(2,1)S(1)}, u32[]{:S(2)}, u32[]{:S(2)}) collective-permute-start(bf16[768,128]{1,0:T(8,128)(2,1)S(1)} %pad_maximum_fusion.refs_0_), channel_id=1, source_target_pairs={{0,6},{2,4},{4,2},{6,0},{8,14},{10,12},{12,10},{14,8},{16,22},{18,... | collective-permute-start | bytes 589832 | tf_op jit(solution)/shard_map/ppermute | solution.py:387
  92.3 0.7 copy-start.21
  92.3 0.7 copy-start.22
  96.0 21.9 %collective-permute-start.18 = (bf16[2,768,128]{2,1,0:T(8,128)(2,1)}, bf16[2,768,128]{2,1,0:T(8,128)(2,1)S(1)}, u32[]{:S(2)}, u32[]{:S(2)}) collective-permute-start(bf16[2,768,128]{2,1,0:T(8,128)(2,1)} %get-tuple-element.56), channel_id=1, source_target_pairs={{8,0},{10,2},{13,5},{15,7},{17,9},{19,11},{20,12},{22,14},{24,16},... | collective-permute-start | bytes 1179656 | tf_op jit(solution)/shard_map/ppermute | solution.py:410
  97.3 0.7 copy-start.17
  97.3 0.7 copy-start.18
  98.0 0.7 copy-start.19
  103.3 29.9 %all-to-all-start.1 = ((f32[16,4,768]{2,1,0:T(4,128)}), f32[16,4,768]{2,1,0:T(4,128)S(1)}, u32[]{:S(2)}, u32[]{:S(2)}) async-start(f32[16,4,768]{2,1,0:T(4,128)} %all_to_all.17), calls=%async_computation.1 | async-start | bytes 393216 | tf_op jit(solution)/shard_map/all_to_all | solution.py:524
  117.8 0.8 copy-start.15
  120.8 5.4 %collective-permute-start.19 = (bf16[3,192,128]{2,1,0:T(8,128)(2,1)}, bf16[3,192,128]{2,1,0:T(8,128)(2,1)S(1)}, u32[]{:S(2)}, u32[]{:S(2)}) collective-permute-start(bf16[3,192,128]{2,1,0:T(8,128)(2,1)} %get-tuple-element.58), channel_id=1, source_target_pairs={{0,2},{2,0},{4,6},{6,4},{8,10},{10,8},{12,14},{14,12},{16,18},{18,... | collective-permute-start | bytes 442376 | tf_op jit(solution)/shard_map/ppermute | solution.py:387
  122.7 5.4 %collective-permute-start.20 = (bf16[3,192,128]{2,1,0:T(8,128)(2,1)}, bf16[3,192,128]{2,1,0:T(8,128)(2,1)S(1)}, u32[]{:S(2)}, u32[]{:S(2)}) collective-permute-start(bf16[3,192,128]{2,1,0:T(8,128)(2,1)} %get-tuple-element.59), channel_id=1, source_target_pairs={{0,4},{2,6},{4,0},{6,2},{8,12},{10,14},{12,8},{14,10},{16,20},{18,... | collective-permute-start | bytes 442376 | tf_op jit(solution)/shard_map/ppermute | solution.py:387
  124.2 6.3 %collective-permute-start.21 = (bf16[3,192,128]{2,1,0:T(8,128)(2,1)}, bf16[3,192,128]{2,1,0:T(8,128)(2,1)S(1)}, u32[]{:S(2)}, u32[]{:S(2)}) collective-permute-start(bf16[3,192,128]{2,1,0:T(8,128)(2,1)} %get-tuple-element.60), channel_id=1, source_target_pairs={{0,6},{2,4},{4,2},{6,0},{8,14},{10,12},{12,10},{14,8},{16,22},{18,... | collective-permute-start | bytes 442376 | tf_op jit(solution)/shard_map/ppermute | solution.py:387
  126.2 4.3 %copy-start.23 = (bf16[3,192,128]{2,1,0:T(8,128)(2,1)}, bf16[3,192,128]{2,1,0:T(8,128)(2,1)S(1)}, u32[]{:S(2)}) copy-start(bf16[3,192,128]{2,1,0:T(8,128)(2,1)S(1)} %collective-permute-done.19.refs_1_) | copy-start | bytes 442372
  128.1 2.4 %copy-start.24 = (bf16[3,192,128]{2,1,0:T(8,128)(2,1)}, bf16[3,192,128]{2,1,0:T(8,128)(2,1)S(1)}, u32[]{:S(2)}) copy-start(bf16[3,192,128]{2,1,0:T(8,128)(2,1)S(1)} %collective-permute-done.20.refs_2_) | copy-start | bytes 442372
  130.4 0.7 copy-start.25
where the time goes:
time: 135 us
  starting transfers between devices  48.7 us (36%)
  Pallas kernels  38.7 us (29%)
  waiting for transfers between devices  31.8 us (24%)
  local copies, waits for them, and re-layouts  12.6 us (9%)
  other arithmetic  1.85 us (1%)
    pallas_call x13, Pallas kernels, call(): pl.pallas_call(body, out_shape=outs, in_specs=[SM] * n_scalar + [VM] * (l...  38.7 us
    ppermute x15, starting transfers between devices, in_plane(): return lax.ppermute(x, 'ctx', [(i, i ^ s) for i in range(n_ctx)])  21.4 us
    ppermute x15, waiting for transfers between devices, in_plane(): return lax.ppermute(x, 'ctx', [(i, i ^ s) for i in range(n_ctx)])  16.6 us
    all_to_all x1, starting transfers between devices, on_device(): lax.all_to_all(adapter_grads, 'ctx', split_axis=0, concat_axis=0, tiled=T...  11.1 us
    ppermute x3, waiting for transfers between devices, along(): lax.ppermute(x, 'ctx', [(i, (i + s * half) % n_ctx) for i in range(n_ctx)])  10.6 us
    unnamed x69, local copies, waits for them, and re-layouts  7.83 us
    all_to_all x1, starting transfers between devices, on_device(): lax.all_to_all(chunks, 'ctx', split_axis=0, concat_axis=0, tiled=True)  4.9 us
    all_to_all x1, waiting for transfers between devices, on_device(): lax.all_to_all(chunks, 'ctx', split_axis=0, concat_axis=0, tiled=True)  4.55 us
  transfers between devices with their start and end apart: 28, of which 8 were waited for; matrix products, arithmetic and copies ran while one was open for 3% of the time, Pallas kernels for 27%

commit v1 on v0

--- a/solution.py
+++ b/solution.py
@@ -12,6 +12,7 @@
 HALF_GROUP_DEV = 4
 LANES = 128
 QUERY_BLOCK = 256
+KERNEL_VMEM = 16 << 20
 
 nf4_values = (
     -1.0,
@@ -60,31 +61,74 @@
         in_specs=[SM] * n_scalar + [VM] * (len(args) - n_scalar),
         out_specs=jax.tree.map(lambda _: VM, outs),
         scratch_shapes=scratch,
+        compiler_params=pltpu.CompilerParams(vmem_limit_bytes=KERNEL_VMEM),
     )(*args)
 
 
 def dequant_body(codes_ref, index_ref, table_ref, nf4_ref, out_ref):
     rows, cols = codes_ref.shape
-    per_tile = index_ref.shape[1] * LANES // cols
+    groups = index_ref.shape[0]
+    parts = table_ref.shape[0]
+    per_tile = groups * LANES // cols
     width = LANES // per_tile
-    lane = lax.broadcasted_iota(jnp.int32, (rows, LANES), 1)
-    levels = jnp.broadcast_to(nf4_ref[...], (rows, LANES))
-    parts = table_ref.shape[0]
-    tables = [jnp.broadcast_to(table_ref[i : i + 1, :], (rows, LANES)) for i in range(parts)]
-    for b in range(cols // LANES):
-        code = codes_ref[:, b * LANES : (b + 1) * LANES]
-        value = jnp.take_along_axis(levels, code, axis=1)
-        idx = jnp.broadcast_to(index_ref[:, b * per_tile : b * per_tile + 1], (rows, LANES))
-        for i in range(1, per_tile):
-            at = b * per_tile + i
-            idx = jnp.where(lane >= i * width, index_ref[:, at : at + 1], idx)
+    tables = [jnp.broadcast_to(table_ref[i : i + 1, :], (groups, LANES)) for i in range(parts)]
+    scales = []
+    for r0 in range(0, rows, LANES):
+        idx = index_ref[:, r0 : min(r0 + LANES, rows)]
+        short = LANES - idx.shape[1]
+        if short:
+            idx = jnp.concatenate([idx, jnp.zeros((groups, short), jnp.int32)], axis=1)
         low = idx % LANES
         scale = jnp.take_along_axis(tables[0], low, axis=1)
         for i in range(1, parts):
             scale = jnp.where(
                 idx >= i * LANES, jnp.take_along_axis(tables[i], low, axis=1), scale
             )
+        scales.append(scale)
+    scales = jnp.concatenate(scales, axis=1).T[:rows, :]
+    lane = lax.broadcasted_iota(jnp.int32, (rows, LANES), 1)
+    levels = jnp.broadcast_to(nf4_ref[...], (rows, LANES))
+    for b in range(cols // LANES):
+        code = codes_ref[:, b * LANES : (b + 1) * LANES]
+        value = jnp.take_along_axis(levels, code, axis=1)
+        at = b * per_tile
+        scale = jnp.broadcast_to(scales[:, at : at + 1], (rows, LANES))
+        for i in range(1, per_tile):
+            scale = jnp.where(lane >= i * width, scales[:, at + i : at + i + 1], scale)
         out_ref[:, b * LANES : (b + 1) * LANES] = (value * scale).astype(BF)
+
+
+def adapter_chunks_body(half, strips, wide, up_ref, down_ref, out_ref):
+    count, rank_rows = out_ref.shape[:2]
+    step = up_ref.shape[1] // strips
+    width = step // half
+    short = wide - strips * width
+    for j in range(half):
+        pieces = [
+            up_ref[:, i * step + j * width : i * step + (j + 1) * width] for i in range(strips)
+        ]
+        if short:
+            pieces.append(jnp.zeros((rank_rows, short), BF))
+        chunk = jnp.concatenate(pieces, axis=1)
+        for p in range(count // half):
+            out_ref[p * half + j, :, :wide] = chunk
+            out_ref[p * half + j, :, wide:] = down_ref[...]
+
+
+def adapter_grads_body(half, strips, slot, wide, pos_ref, in_ref, up_ref, down_ref):
+    core = pos_ref[2]
+    planes = in_ref.shape[0] // half
+    width = slot // strips
+    step = half * width
+    for j in range(half):
+        total = in_ref[j]
+        for p in range(1, planes):
+            total = total + in_ref[p * half + j]
+        for i in range(strips):
+            to = i * step + j * width
+            up_ref[:, to : to + width] = total[:, i * width : (i + 1) * width]
+        head = j ^ ((core & 1) * (half // 2))
+        down_ref[:, pl.ds(pl.multiple_of(head * LANES, LANES), LANES)] = total[:, wide:]
 
 
 def pack_grad_body(half, strips, pos_ref, g_ref, *out_refs):
@@ -131,44 +175,60 @@
 def lora_body(half, fsdp, pos_ref, *refs):
     ups, grads, out_ref = refs[:fsdp], refs[fsdp:-1], refs[-1]
     mine = pos_ref[0]
-    rows = grads[0].shape[0]
+    rows, wide = grads[0].shape
     for s in range(half):
         total = None
         for f in range(fsdp):
-            part = nt(grads[s * fsdp + f][...], ups[f][...])
+            part = nt(grads[s * fsdp + f][...], ups[f][:, :wide])
             total = part if total is None else total + part
         at = pl.ds(pl.multiple_of((mine ^ s) * rows, rows), rows)
         out_ref[at, :] = adapter_scale * total
 
 
+def join_body(lora_ref, *refs):
+    mids, out_ref = refs[:-1], refs[-1]
+    mid = mids[0][...]
+    for m in mids[1:]:
+        mid = mid + m[...]
+    out_ref[...] = jnp.concatenate([lora_ref[...], mid], axis=1).astype(BF)
+
+
 def project_body(half, planes, fsdp, slot, targets, pos_ref, *refs):
-    lora_ref, down_ref = refs[:2]
-    grads = refs[2 : 2 + half * fsdp]
-    weights = refs[2 + half * fsdp : 2 + half * fsdp + planes]
-    outs = refs[2 + half * fsdp + planes : -2]
+    ups = refs[:fsdp]
+    grads = refs[fsdp : fsdp + half * fsdp]
+    weights = refs[fsdp + half * fsdp : fsdp + half * fsdp + planes]
+    outs = refs[fsdp + half * fsdp + planes : -2]
     w_scr, d_scr = refs[-2:]
     mine, plane, core, own = pos_ref[0], pos_ref[1], pos_ref[2], pos_ref[4]
     rows_each = weights[0].shape[0]
+    rows, wide = grads[0].shape
     tail = w_scr.shape[0] - planes * rows_each
     if tail:
         w_scr[planes * rows_each :, :] = jnp.zeros((tail, w_scr.shape[1]), BF)
     for i, t in enumerate(targets):
         cols = pl.ds(pl.multiple_of((own ^ t) * LANES, LANES), LANES)
+        d_cols = pl.ds(pl.multiple_of(wide + (own ^ t) * LANES, LANES), LANES)
         to = slice(i * LANES, (i + 1) * LANES)
-        d_scr[:, to] = down_ref[:, cols]
+        d_scr[:, to] = ups[0][:, d_cols]
         for s in range(planes):
             src = lax.rem(plane + (planes - s), planes)
             at = pl.ds(pl.multiple_of(src * rows_each, rows_each), rows_each)
             w_scr[at, to] = weights[s][:, cols]
-    rows = grads[0].shape[0]
-    depth = grads[0].shape[1]
+    for f in range(fsdp):
+        src = lax.rem(core + (fsdp - f), fsdp)
+        at = pl.ds(pl.multiple_of(src * slot, 16), slot)
+        low = lax.dot_general(
+            ups[f][:, :wide], d_scr[...], (((0,), (0,)), ((), ())), preferred_element_type=F32
+        )
+        w_scr[at, :] = (w_scr[at, :].astype(F32) + adapter_scale * low[:slot]).astype(BF)
     for s in range(half):
         at = pl.ds(pl.multiple_of((mine ^ s) * rows, rows), rows)
-        acc = nn(lora_ref[at, :].astype(BF), d_scr[...])
+        acc = None
         for f in range(fsdp):
             src = lax.rem(core + (fsdp - f), fsdp)
-            w_at = pl.ds(pl.multiple_of(src * slot, 16), depth)
-            acc = acc + nn(grads[s * fsdp + f][...], w_scr[w_at, :])
+            w_at = pl.ds(pl.multiple_of(src * slot, 16), wide)
+            part = nn(grads[s * fsdp + f][...], w_scr[w_at, :])
+            acc = part if acc is None else acc + part
         for i in range(len(targets)):
             outs[i][at, :] = acc[:, i * LANES : (i + 1) * LANES].astype(BF)
 
@@ -182,8 +242,11 @@
     return jnp.where(kpos <= qpos, scores, masked)
 
 
-def forward_body(pos_ref, q_ref, kv_ref, far_ref, down_ref, o_ref, lse_ref, mid_ref, vt_scr, oft_scr):
-    later = pos_ref[3]
+def forward_body(
+    wide, pos_ref, q_ref, kv_ref, far_ref, adapt_ref, o_ref, lse_ref, mid_ref, vt_scr, oft_scr
+):
+    later, own = pos_ref[3], pos_ref[4]
+    down = adapt_ref[:, pl.ds(pl.multiple_of(wide + own * LANES, LANES), LANES)]
     tokens = q_ref.shape[0]
     block = min(QUERY_BLOCK, tokens)
     vt_scr[...] = kv_ref[1].T
@@ -193,7 +256,7 @@
         out = block_out.T
         o_ref[qs, :] = out
         lse_ref[:, qs] = norm
-        mid_ref[qs, :] = nt(out.astype(BF), down_ref[...])
+        mid_ref[qs, :] = nt(out.astype(BF), down)
 
     def near(q0):
         return score_block(kv_ref[0, : q0 + block, :], q_ref[q0 : q0 + block, :], 0, q0)
@@ -327,7 +390,8 @@
 def adapters_body(half, pos_ref, o_ref, *refs):
     both, grads, out_ref, scr = refs[:half], refs[half : 2 * half], refs[-2], refs[-1]
     mine = pos_ref[0]
-    rank = out_ref.shape[0]
+    count, rank_rows = out_ref.shape[:2]
+    rank = count * rank_rows
     rows, wide = grads[0].shape
     total = both[0][...].astype(F32)
     for s in range(1, half):
@@ -339,8 +403,11 @@
         at = pl.ds(pl.multiple_of((mine ^ s) * rows, rows), rows)
         part = nn(scr[at, :].T[rank:, :], grads[s][...])
         acc = part if acc is None else acc + part
-    out_ref[:, :wide] = adapter_scale * acc
-    out_ref[:, wide:] = nn(total.T[:rank, :], o_ref[...].astype(BF))
+    acc = adapter_scale * acc
+    low = nn(total.T[:rank, :], o_ref[...].astype(BF))
+    for c in range(count):
+        out_ref[c, :, :wide] = acc[c * rank_rows : (c + 1) * rank_rows, :]
+        out_ref[c, :, wide:] = low[c * rank_rows : (c + 1) * rank_rows, :]
 
 
 def on_device(
@@ -416,7 +483,7 @@
         sds((w_rows, w_cols), BF),
         [],
         frozen_weight_codes,
-        block_scale_index,
+        block_scale_index.T,
         block_scale_table.reshape(-1, LANES),
         jnp.asarray(levels),
     )
@@ -454,17 +521,16 @@
     )
     far = to_later(key_value)
 
-    up_chunks = adapter_up_matrix.reshape(rank_rows, strips, half, w_rows).transpose(2, 0, 1, 3)
-    up_chunks = up_chunks.reshape(half, rank_rows, slot)
-    up_chunks = jnp.pad(up_chunks, ((0, 0), (0, 0), (0, wide - slot)))
-    down_chunks = jnp.broadcast_to(adapter_down_matrix, (half,) + adapter_down_matrix.shape)
-    chunks = jnp.concatenate([up_chunks, down_chunks], axis=2)
-    chunks = jnp.broadcast_to(chunks, (planes,) + chunks.shape).reshape(n_ctx * rank_rows, -1)
+    chunks = call(
+        functools.partial(adapter_chunks_body, half, strips, wide),
+        sds((n_ctx, rank_rows, wide + heads * HEAD_WIDTH), BF),
+        [],
+        adapter_up_matrix,
+        adapter_down_matrix,
+    )
     adapters = lax.all_to_all(chunks, "ctx", split_axis=0, concat_axis=0, tiled=True)
-    up = adapters[:, :wide]
-    down = adapters[:, wide:]
-    down_head = lax.dynamic_slice_in_dim(down, own * HEAD_WIDTH, HEAD_WIDTH, 1)
-    ups = [across(up, f) for f in range(fsdp)]
+    adapters = adapters.reshape(rank, -1)
+    ups = [across(adapters, f) for f in range(fsdp)]
     lora = call(
         functools.partial(lora_body, half, fsdp),
         sds((tokens, rank), F32),
@@ -484,8 +550,7 @@
                 pltpu.VMEM((rank, LANES * len(targets)), BF),
             ],
             pos,
-            lora,
-            down,
+            *ups,
             *swapped,
             *weights,
             n_scalar=1,
@@ -498,22 +563,22 @@
     partial.update({s: in_plane(x, s) for s, x in rest.items()})
 
     out, norm, mid = call(
-        forward_body,
+        functools.partial(forward_body, wide),
         [sds((tokens, LANES), F32), sds((1, tokens), F32), sds((tokens, rank), F32)],
         [pltpu.VMEM((LANES, tokens), BF), pltpu.VMEM((LANES, tokens), BF)],
         pos,
         query,
         key_value,
         far,
-        down_head,
-        n_scalar=1,
-    )
-    mid = sum(across(mid, f) for f in range(fsdp))
-    both = jnp.concatenate([lora, mid], axis=1).astype(BF)
+        adapters,
+        n_scalar=1,
+    )
+    mids = [across(mid, f) for f in range(fsdp)]
+    both = call(join_body, sds((tokens, 2 * rank), BF), [], lora, *mids)
     both = [in_plane(both, s) for s in range(half)]
     adapter_grads = call(
         functools.partial(adapters_body, half),
-        sds((rank, wide + HEAD_WIDTH), F32),
+        sds((n_ctx, rank_rows, wide + HEAD_WIDTH), F32),
         [pltpu.VMEM((tokens, 2 * rank), BF)],
         pos,
         out,
@@ -522,12 +587,14 @@
         n_scalar=1,
     )
     reduced = lax.all_to_all(adapter_grads, "ctx", split_axis=0, concat_axis=0, tiled=True)
-    reduced = jnp.sum(reduced.reshape(planes, half, rank_rows, -1), axis=0)
-    up_grad = reduced[:, :, :slot].reshape(half, rank_rows, strips, w_rows)
-    up_grad = up_grad.transpose(1, 2, 0, 3).reshape(rank_rows, grad_cols)
-    down_grad = reduced[:, :, wide:]
-    down_grad = jnp.where(core % 2 == 0, down_grad, jnp.roll(down_grad, half // 2, axis=0))
-    down_grad = down_grad.transpose(1, 0, 2).reshape(rank_rows, heads * HEAD_WIDTH)
+    up_grad, down_grad = call(
+        functools.partial(adapter_grads_body, half, strips, slot, wide),
+        [sds((rank_rows, grad_cols), F32), sds((rank_rows, heads * HEAD_WIDTH), F32)],
+        [],
+        pos,
+        reduced,
+        n_scalar=1,
+    )
 
     far_part, dq_far, grad_out, delta = call(
         functools.partial(far_body, half),

time: 135 us -> 114 us (0.84)
  Pallas kernels: 38.7 us -> 20.2 us
  local copies, waits for them, and re-layouts: 12.6 us -> 5.5 us
  waiting for transfers between devices: 31.8 us -> 36.2 us
  starting transfers between devices: 48.7 us -> 51 us
  other arithmetic: 1.85 us -> 0 us
    pallas_call x13 -> x16, Pallas kernels: 38.7 us -> 20.2 us  [call(): pl.pallas_call(body, out_shape=outs, in_specs=[SM] * n_scalar + [VM] * (l...]
    ppermute x15, waiting for transfers between devices: 16.6 us -> 23.3 us  [in_plane(): return lax.ppermute(x, 'ctx', [(i, i ^ s) for i in range(n_ctx)])]
    ppermute x3, starting transfers between devices: 3.95 us -> 8.42 us  [along(): lax.ppermute(x, 'ctx', [(i, (i + s * half) % n_ctx) for i in range(n_ctx)])]
    unnamed x69 -> x24, local copies, waits for them, and re-layouts: 7.83 us -> 4.47 us
    all_to_all x1, starting transfers between devices: 4.9 us -> 7.05 us  [on_device(): lax.all_to_all(chunks, 'ctx', split_axis=0, concat_axis=0, tiled=True)]
    all_to_all x2 -> x0, local copies, waits for them, and re-layouts: 1.72 us -> none  [the longest x1 1.68 us: on_device(): lax.all_to_all(adapter_grads, 'ctx', split_axis=0, concat_axis=0, tiled=T...]
    all_to_all x1, waiting for transfers between devices: 4.55 us -> 2.84 us  [on_device(): lax.all_to_all(chunks, 'ctx', split_axis=0, concat_axis=0, tiled=True)]
    ppermute x1, starting transfers between devices: 3.49 us -> 2.01 us  [to_later(): return lax.ppermute(x, ('ctx', 'fsdp'), pairs)]
  transfers between devices with their start and end apart: 28 -> 28, of which waited for: 8 -> 9; matrix products, arithmetic and copies ran while one was open for 3% -> 1% of each run, Pallas kernels for 27% -> 16%
where the time goes in v1:
time: 114 us
  starting transfers between devices  51 us (45%)
  waiting for transfers between devices  36.2 us (32%)
  Pallas kernels  20.2 us (18%)
  local copies, waits for them, and re-layouts  5.5 us (5%)
    ppermute x15, waiting for transfers between devices, in_plane(): return lax.ppermute(x, 'ctx', [(i, i ^ s) for i in range(n_ctx)])  23.3 us
    ppermute x15, starting transfers between devices, in_plane(): return lax.ppermute(x, 'ctx', [(i, i ^ s) for i in range(n_ctx)])  20.3 us
    pallas_call x16, Pallas kernels, call(): pl.pallas_call(body, out_shape=outs, in_specs=[SM] * n_scalar + [VM] * (l...  20.2 us
    ppermute x3, waiting for transfers between devices, along(): lax.ppermute(x, 'ctx', [(i, (i + s * half) % n_ctx) for i in range(n_ctx)])  10.1 us
    all_to_all x1, starting transfers between devices, on_device(): lax.all_to_all(adapter_grads, 'ctx', split_axis=0, concat_axis=0, tiled=T...  10.1 us
    ppermute x3, starting transfers between devices, along(): lax.ppermute(x, 'ctx', [(i, (i + s * half) % n_ctx) for i in range(n_ctx)])  8.42 us
    all_to_all x1, starting transfers between devices, on_device(): lax.all_to_all(chunks, 'ctx', split_axis=0, concat_axis=0, tiled=True)  7.05 us
    unnamed x24, local copies, waits for them, and re-layouts  4.47 us
  transfers between devices with their start and end apart: 28, of which 9 were waited for; matrix products, arithmetic and copies ran while one was open for 1% of the time, Pallas kernels for 16%

profile of v1, /device:TPU:0, one launch (start us, length us, event | category | flops | bytes accessed | tf_op | source)
XLA Modules:
  0.0 113.9 jit_solution(1473932766565802451)
XLA Ops:
  0.7 0.1 stack.23.pos_ref
  0.8 1.2 %copy-done.2 = bf16[192,2560]{1,0:T(8,128)(2,1)S(1)} copy-done((bf16[192,2560]{1,0:T(8,128)(2,1)S(1)}, bf16[192,2560]{1,0:T(8,128)(2,1)}, u32[]{:S(2)}) %copy-start.2) | copy-done | bytes 983064
  2.0 1.0 shard_map.140
  3.0 4.0 %collective-permute-start.9 = (bf16[192,640]{1,0:T(8,128)(2,1)S(1)}, bf16[192,640]{1,0:T(8,128)(2,1)S(1)}, u32[]{:S(2)}, u32[]{:S(2)}) collective-permute-start(bf16[192,640]{1,0:T(8,128)(2,1)S(1)} %get-tuple-element.46), channel_id=1, source_target_pairs={{0,6},{2,4},{4,2},{6,0},{8,14},{10,12},{12,10},{14,8},{16,22},{18,... | collective-permute-start | bytes 737288 | tf_op jit(solution)/shard_map/ppermute | solution.py:454
  7.0 0.5 collective-permute-start.5
  7.5 0.9 copy-done.5
  8.4 0.9 copy-done.6
  9.4 0.6 shard_map.137
  10.0 1.6 %collective-permute-start = (bf16[3,192,128]{2,1,0:T(8,128)(2,1)S(1)}, bf16[3,192,128]{2,1,0:T(8,128)(2,1)S(1)}, u32[]{:S(2)}, u32[]{:S(2)}) collective-permute-start(bf16[3,192,128]{2,1,0:T(8,128)(2,1)S(1)} %get-tuple-element.38), channel_id=1, source_target_pairs={{0,2},{2,0},{4,6},{6,4},{8,10},{10,8},{12,14},{14,12},{16,18},{18,... | collective-permute-start | bytes 442376 | tf_op jit(solution)/shard_map/ppermute | solution.py:454
  11.6 0.5 collective-permute-start.1
  12.1 1.5 %collective-permute-start.2 = (bf16[3,192,128]{2,1,0:T(8,128)(2,1)S(1)}, bf16[3,192,128]{2,1,0:T(8,128)(2,1)S(1)}, u32[]{:S(2)}, u32[]{:S(2)}) collective-permute-start(bf16[3,192,128]{2,1,0:T(8,128)(2,1)S(1)} %get-tuple-element.40), channel_id=1, source_target_pairs={{0,6},{2,4},{4,2},{6,0},{8,14},{10,12},{12,10},{14,8},{16,22},{18,... | collective-permute-start | bytes 442376 | tf_op jit(solution)/shard_map/ppermute | solution.py:454
  13.6 9.2 %collective-permute-done.refs_1_ = bf16[3,192,128]{2,1,0:T(8,128)(2,1)S(1)} collective-permute-done((bf16[3,192,128]{2,1,0:T(8,128)(2,1)S(1)}, bf16[3,192,128]{2,1,0:T(8,128)(2,1)S(1)}, u32[]{:S(2)}, u32[]{:S(2)}) %collective-permute-start) | collective-permute-done | bytes 147488 | tf_op jit(solution)/shard_map/ppermute | solution.py:454
  22.7 0.0 collective-permute-start.7
  22.8 0.7 copy-done.10
  23.4 1.0 shard_map.141.refs_10_
  24.5 0.0 collective-permute-done.1.refs_2_
  24.5 2.1 %collective-permute-start.11 = (bf16[320,512]{1,0:T(8,128)(2,1)S(1)}, bf16[320,512]{1,0:T(8,128)(2,1)S(1)}, u32[]{:S(2)}, u32[]{:S(2)}) collective-permute-start(bf16[320,512]{1,0:T(8,128)(2,1)S(1)} %shard_map.141.refs_10_), channel_id=1, source_target_pairs={{0,8},{2,10},{4,12},{6,14},{8,16},{10,18},{12,20},{14,22},{16,24},... | collective-permute-start | bytes 983048 | tf_op jit(solution)/shard_map/ppermute | solution.py:459
  26.6 2.6 %collective-permute-start.12 = (bf16[320,512]{1,0:T(8,128)(2,1)S(1)}, bf16[320,512]{1,0:T(8,128)(2,1)}, u32[]{:S(2)}, u32[]{:S(2)}) collective-permute-start(bf16[320,512]{1,0:T(8,128)(2,1)S(1)} %shard_map.141.refs_10_), channel_id=1, source_target_pairs={{0,16},{2,18},{4,20},{6,22},{8,24},{10,26},{12,28},{14,30},{16,0},... | collective-permute-start | bytes 983048 | tf_op jit(solution)/shard_map/ppermute | solution.py:459
  29.2 0.6 shard_map.138
  29.8 2.0 %collective-permute-start.17 = (bf16[2,768,128]{2,1,0:T(8,128)(2,1)S(1)}, bf16[2,768,128]{2,1,0:T(8,128)(2,1)S(1)}, u32[]{:S(2)}, u32[]{:S(2)}) collective-permute-start(bf16[2,768,128]{2,1,0:T(8,128)(2,1)S(1)} %get-tuple-element.42.kv_ref), channel_id=1, source_target_pairs={{0,8},{2,10},{5,13},{7,15},{9,17},{11,19},{12,20},{14,22},{16,24},... | collective-permute-start | bytes 1179656 | tf_op jit(solution)/shard_map/ppermute | solution.py:474
  31.8 0.1 collective-permute-start.4
  31.9 0.7 shard_map.139
  32.7 7.0 %all-to-all-start = ((bf16[16,4,1152]{2,1,0:T(4,128)(2,1)}), bf16[16,4,1152]{2,1,0:T(4,128)(2,1)}, u32[]{:S(2)}, u32[]{:S(2)}) async-start(bf16[16,4,1152]{2,1,0:T(4,128)(2,1)} %shard_map.139), calls=%async_computation | async-start | bytes 294912 | tf_op jit(solution)/shard_map/all_to_all | solution.py:531
  39.7 3.7 %collective-permute-start.13 = (bf16[320,512]{1,0:T(8,128)(2,1)S(1)}, bf16[320,512]{1,0:T(8,128)(2,1)}, u32[]{:S(2)}, u32[]{:S(2)}) collective-permute-start(bf16[320,512]{1,0:T(8,128)(2,1)S(1)} %shard_map.141.refs_10_), channel_id=1, source_target_pairs={{0,24},{2,26},{4,28},{6,30},{8,0},{10,2},{12,4},{14,6},{16,8},{18,... | collective-permute-start | bytes 983048 | tf_op jit(solution)/shard_map/ppermute | solution.py:459
  43.5 0.0 collective-permute-done.4.refs_3_
  43.5 0.7 copy-done
  44.2 0.5 collective-permute-start.6
  44.7 9.5 %collective-permute-done.12.refs_12_ = bf16[320,512]{1,0:T(8,128)(2,1)} collective-permute-done((bf16[320,512]{1,0:T(8,128)(2,1)S(1)}, bf16[320,512]{1,0:T(8,128)(2,1)}, u32[]{:S(2)}, u32[]{:S(2)}) %collective-permute-start.12) | collective-permute-done | bytes 327712 | tf_op jit(solution)/shard_map/ppermute | solution.py:459
  54.2 2.8 %all-to-all-done = bf16[16,4,1152]{2,1,0:T(4,128)(2,1)} async-done(((bf16[16,4,1152]{2,1,0:T(4,128)(2,1)}), bf16[16,4,1152]{2,1,0:T(4,128)(2,1)}, u32[]{:S(2)}, u32[]{:S(2)}) %all-to-all-start) | async-done | bytes 147488 | tf_op jit(solution)/shard_map/all_to_all | solution.py:531
  57.0 0.9 reshape.16.refs_0_.adapt_ref
  58.0 0.0 collective-permute-done.17.far_ref.refs_5_
  58.0 0.1 collective-permute-start.3
  58.1 2.3 %shard_map.144 = (f32[768,128]{1,0:T(8,128)S(1)}, f32[1,768]{1,0:T(1,128)S(1)}, f32[768,64]{1,0:T(8,128)S(1)}) custom-call(s32[5]{0:T(128)S(1)} %stack.23.pos_ref, bf16[768,128]{1,0:T(8,128)(2,1)S(1)} %get-tuple-element.41.q_ref.refs_4_, bf16[2,768,128]{2,1,0:T(8,128)(2,1)S(1)} %get-tuple-element.42.kv_ref, ...), custom_call_target="tpu_custom_call" | custom-call | tf_op jit(solution)/shard_map/pallas_call | solution.py:58
  60.4 0.7 collective-permute-done.13.refs_13_
  61.0 1.2 %collective-permute-start.22 = (f32[768,64]{1,0:T(8,128)S(1)}, f32[768,64]{1,0:T(8,128)S(1)}, u32[]{:S(2)}, u32[]{:S(2)}) collective-permute-start(f32[768,64]{1,0:T(8,128)S(1)} %get-tuple-element.66.refs_0_), channel_id=1, source_target_pairs={{0,1},{1,0},{2,3},{3,2},{4,5},{5,4},{6,7},{7,6},{8,9},{9,8},{10,11... | collective-permute-start | bytes 589832 | tf_op jit(solution)/shard_map/ppermute | solution.py:464
  62.2 0.0 collective-permute-done.8.refs_7_
  62.2 2.3 %shard_map.143 = (bf16[768,128]{1,0:T(8,128)(2,1)S(1)}, bf16[768,128]{1,0:T(8,128)(2,1)S(1)}) custom-call(s32[5]{0:T(128)S(1)} %stack.23.pos_ref, bf16[64,1152]{1,0:T(8,128)(2,1)S(1)} %reshape.16.refs_0_.adapt_ref, bf16[64,1152]{1,0:T(8,128)(2,1)S(1)} %collective-permute-done.3.refs_1_, bf16[192,640]{1,0:T(8,128)(2,1)S(1)} %get-tuple-element.43.refs_2_.refs_4_, ...), custom_call_target="tpu_custom_call" | custom-call | tf_op jit(solution)/shard_map/pallas_call | solution.py:58
  64.5 1.3 %collective-permute-start.15 = (bf16[768,128]{1,0:T(8,128)(2,1)S(1)}, bf16[768,128]{1,0:T(8,128)(2,1)S(1)}, u32[]{:S(2)}, u32[]{:S(2)}) collective-permute-start(bf16[768,128]{1,0:T(8,128)(2,1)S(1)} %get-tuple-element.49), channel_id=1, source_target_pairs={{0,4},{2,6},{4,0},{6,2},{8,12},{10,14},{12,8},{14,10},{16,20},{18,... | collective-permute-start | bytes 589832 | tf_op jit(solution)/shard_map/ppermute | solution.py:454
  65.8 1.0 collective-permute-start.16
  66.8 2.3 %shard_map.142 = (bf16[768,128]{1,0:T(8,128)(2,1)S(1)}, bf16[768,128]{1,0:T(8,128)(2,1)S(1)}) custom-call(s32[5]{0:T(128)S(1)} %stack.23.pos_ref, bf16[64,1152]{1,0:T(8,128)(2,1)S(1)} %reshape.16.refs_0_.adapt_ref, bf16[64,1152]{1,0:T(8,128)(2,1)S(1)} %collective-permute-done.3.refs_1_, bf16[192,640]{1,0:T(8,128)(2,1)S(1)} %get-tuple-element.43.refs_2_.refs_4_, ...), custom_call_target="tpu_custom_call" | custom-call | tf_op jit(solution)/shard_map/pallas_call | solution.py:58
  69.1 1.4 %collective-permute-start.14 = (bf16[768,128]{1,0:T(8,128)(2,1)S(1)}, bf16[768,128]{1,0:T(8,128)(2,1)S(1)}, u32[]{:S(2)}, u32[]{:S(2)}) collective-permute-start(bf16[768,128]{1,0:T(8,128)(2,1)S(1)} %get-tuple-element.48), channel_id=1, source_target_pairs={{0,2},{2,0},{4,6},{6,4},{8,10},{10,8},{12,14},{14,12},{16,18},{18,... | collective-permute-start | bytes 589832 | tf_op jit(solution)/shard_map/ppermute | solution.py:454
  70.5 1.2 %shard_map.149.lora_ref = f32[768,64]{1,0:T(8,128)S(1)} custom-call(s32[5]{0:T(128)S(1)} %stack.23.pos_ref, bf16[64,1152]{1,0:T(8,128)(2,1)S(1)} %reshape.16.refs_0_.adapt_ref, bf16[64,1152]{1,0:T(8,128)(2,1)S(1)} %collective-permute-done.3.refs_1_, bf16[192,640]{1,0:T(8,128)(2,1)S(1)} %get-tuple-element.43.refs_2_.refs_4_, ...), custom_call_target="tpu_custom_call" | custom-call | tf_op jit(solution)/shard_map/pallas_call | solution.py:58
  71.7 0.0 collective-permute-done.22.refs_1_
  71.7 0.1 shard_map.150.refs_0_
  71.8 0.8 collective-permute-start.23
  72.6 1.9 %collective-permute-start.24 = (bf16[768,128]{1,0:T(8,128)(2,1)S(1)}, bf16[768,128]{1,0:T(8,128)(2,1)S(1)}, u32[]{:S(2)}, u32[]{:S(2)}) collective-permute-start(bf16[768,128]{1,0:T(8,128)(2,1)S(1)} %shard_map.150.refs_0_), channel_id=1, source_target_pairs={{0,4},{2,6},{4,0},{6,2},{8,12},{10,14},{12,8},{14,10},{16,20},{18,... | collective-permute-start | bytes 589832 | tf_op jit(solution)/shard_map/ppermute | solution.py:454
  74.5 1.9 %collective-permute-done.15.refs_2_ = bf16[768,128]{1,0:T(8,128)(2,1)S(1)} collective-permute-done((bf16[768,128]{1,0:T(8,128)(2,1)S(1)}, bf16[768,128]{1,0:T(8,128)(2,1)S(1)}, u32[]{:S(2)}, u32[]{:S(2)}) %collective-permute-start.15) | collective-permute-done | bytes 196640 | tf_op jit(solution)/shard_map/ppermute | solution.py:454
  76.5 2.2 %collective-permute-start.25 = (bf16[768,128]{1,0:T(8,128)(2,1)S(1)}, bf16[768,128]{1,0:T(8,128)(2,1)S(1)}, u32[]{:S(2)}, u32[]{:S(2)}) collective-permute-start(bf16[768,128]{1,0:T(8,128)(2,1)S(1)} %shard_map.150.refs_0_), channel_id=1, source_target_pairs={{0,6},{2,4},{4,2},{6,0},{8,14},{10,12},{12,10},{14,8},{16,22},{18,... | collective-permute-start | bytes 589832 | tf_op jit(solution)/shard_map/ppermute | solution.py:454
  78.7 0.0 collective-permute-done.16.refs_3_
  78.7 1.0 shard_map.145
  79.7 1.3 %collective-permute-start.18 = (bf16[2,768,128]{2,1,0:T(8,128)(2,1)S(1)}, bf16[2,768,128]{2,1,0:T(8,128)(2,1)S(1)}, u32[]{:S(2)}, u32[]{:S(2)}) collective-permute-start(bf16[2,768,128]{2,1,0:T(8,128)(2,1)S(1)} %get-tuple-element.58), channel_id=1, source_target_pairs={{8,0},{10,2},{13,5},{15,7},{17,9},{19,11},{20,12},{22,14},{24,16},... | collective-permute-start | bytes 1179656 | tf_op jit(solution)/shard_map/ppermute | solution.py:477
  81.0 0.8 collective-permute-done.23.refs_1_
  81.8 4.6 %collective-permute-done.25.refs_3_ = bf16[768,128]{1,0:T(8,128)(2,1)S(1)} collective-permute-done((bf16[768,128]{1,0:T(8,128)(2,1)S(1)}, bf16[768,128]{1,0:T(8,128)(2,1)S(1)}, u32[]{:S(2)}, u32[]{:S(2)}) %collective-permute-start.25) | collective-permute-done | bytes 196640 | tf_op jit(solution)/shard_map/ppermute | solution.py:454
  86.4 1.8 %shard_map.151 = f32[16,4,768]{2,1,0:T(4,128)} custom-call(s32[5]{0:T(128)S(1)} %stack.23.pos_ref, f32[768,128]{1,0:T(8,128)S(1)} %get-tuple-element.51.refs_6_.o_ref, bf16[768,128]{1,0:T(8,128)(2,1)S(1)} %shard_map.150.refs_0_, bf16[768,128]{1,0:T(8,128)(2,1)S(1)} %collective-permute-done.23.refs_1_, bf16[768,128]{1,0:T(8,128)(2,1)S(1)} %collective-permute-done.24.refs_2_, ...), custom_call_target="tpu_custom_call" | custom-call | tf_op jit(solution)/shard_map/pallas_call | solution.py:58
  88.2 10.1 %all-to-all-start.1 = ((f32[16,4,768]{2,1,0:T(4,128)}), f32[16,4,768]{2,1,0:T(4,128)S(1)}, u32[]{:S(2)}, u32[]{:S(2)}) async-start(f32[16,4,768]{2,1,0:T(4,128)} %shard_map.151), calls=%async_computation.1 | async-start | bytes 393216 | tf_op jit(solution)/shard_map/all_to_all | solution.py:589
  98.3 1.8 %shard_map.146 = (bf16[768,128]{1,0:T(8,128)(2,1)S(1)}, f32[2,768,128]{2,1,0:T(8,128)S(1)}) custom-call(s32[5]{0:T(128)S(1)} %stack.23.pos_ref, bf16[768,128]{1,0:T(8,128)(2,1)S(1)} %get-tuple-element.41.q_ref.refs_4_, bf16[2,768,128]{2,1,0:T(8,128)(2,1)S(1)} %get-tuple-element.42.kv_ref, bf16[768,128]{1,0:T(8,128)(2,1)S(1)} %get-tuple-element.53.do_ref, ...), custom_call_target="tpu_custom_call" | custom-call | tf_op jit(solution)/shard_map/pallas_call | solution.py:58
  100.1 0.6 shard_map.147
  100.8 2.0 %collective-permute-start.19 = (bf16[3,192,128]{2,1,0:T(8,128)(2,1)S(1)}, bf16[3,192,128]{2,1,0:T(8,128)(2,1)S(1)}, u32[]{:S(2)}, u32[]{:S(2)}) collective-permute-start(bf16[3,192,128]{2,1,0:T(8,128)(2,1)S(1)} %get-tuple-element.60), channel_id=1, source_target_pairs={{0,2},{2,0},{4,6},{6,4},{8,10},{10,8},{12,14},{14,12},{16,18},{18,... | collective-permute-start | bytes 442376 | tf_op jit(solution)/shard_map/ppermute | solution.py:454
  102.8 1.5 %collective-permute-start.20 = (bf16[3,192,128]{2,1,0:T(8,128)(2,1)S(1)}, bf16[3,192,128]{2,1,0:T(8,128)(2,1)S(1)}, u32[]{:S(2)}, u32[]{:S(2)}) collective-permute-start(bf16[3,192,128]{2,1,0:T(8,128)(2,1)S(1)} %get-tuple-element.61), channel_id=1, source_target_pairs={{0,4},{2,6},{4,0},{6,2},{8,12},{10,14},{12,8},{14,10},{16,20},{18,... | collective-permute-start | bytes 442376 | tf_op jit(solution)/shard_map/ppermute | solution.py:454
  104.2 0.1 collective-permute-start.21
  104.3 3.8 %collective-permute-done.19.refs_1_ = bf16[3,192,128]{2,1,0:T(8,128)(2,1)S(1)} collective-permute-done((bf16[3,192,128]{2,1,0:T(8,128)(2,1)S(1)}, bf16[3,192,128]{2,1,0:T(8,128)(2,1)S(1)}, u32[]{:S(2)}, u32[]{:S(2)}) %collective-permute-start.19) | collective-permute-done | bytes 147488 | tf_op jit(solution)/shard_map/ppermute | solution.py:454
  108.1 3.1 %collective-permute-done.20.refs_2_ = bf16[3,192,128]{2,1,0:T(8,128)(2,1)S(1)} collective-permute-done((bf16[3,192,128]{2,1,0:T(8,128)(2,1)S(1)}, bf16[3,192,128]{2,1,0:T(8,128)(2,1)S(1)}, u32[]{:S(2)}, u32[]{:S(2)}) %collective-permute-start.20) | collective-permute-done | bytes 147488 | tf_op jit(solution)/shard_map/ppermute | solution.py:454
  111.2 1.4 %shard_map.148 = (bf16[192,512]{1,0:T(8,128)(2,1)}, bf16[192,512]{1,0:T(8,128)(2,1)}, bf16[192,512]{1,0:T(8,128)(2,1)}) custom-call(s32[5]{0:T(128)S(1)} %stack.23.pos_ref, bf16[3,192,128]{2,1,0:T(8,128)(2,1)S(1)} %get-tuple-element.59.refs_0_, bf16[3,192,128]{2,1,0:T(8,128)(2,1)S(1)} %collective-permute-done.19.refs_1_, ...), custom_call_target="tpu_custom_call" | custom-call | tf_op jit(solution)/shard_map/pallas_call | solution.py:58
  112.6 1.2 %shard_map.152 = (f32[4,2560]{1,0:T(4,128)}, f32[4,512]{1,0:T(4,128)}) custom-call(s32[5]{0:T(128)S(1)} %stack.23.pos_ref, f32[16,4,768]{2,1,0:T(4,128)S(1)} %all-to-all-done.1.in_ref), custom_call_target="tpu_custom_call" | custom-call | tf_op jit(solution)/shard_map/pallas_call | solution.py:58
  (34 shorter events, 0.1 us)
Async XLA Ops:
  0.8 1.2 %copy-start.2 = (bf16[192,2560]{1,0:T(8,128)(2,1)S(1)}, bf16[192,2560]{1,0:T(8,128)(2,1)}, u32[]{:S(2)}) copy-start(bf16[192,2560]{1,0:T(8,128)(2,1)} %g_ref.1) | copy-start | bytes 2949124
  2.0 5.6 %copy-start.4 = (bf16[192,512]{1,0:T(8,128)(2,1)S(1)}, bf16[192,512]{1,0:T(8,128)(2,1)}, u32[]{:S(2)}) copy-start(bf16[192,512]{1,0:T(8,128)(2,1)} %q_ref.1) | copy-start | bytes 589828
  2.0 20.8 %copy-start.3 = (s32[320,512]{1,0:T(8,128)S(1)}, s32[320,512]{1,0:T(8,128)}, u32[]{:S(2)}) copy-start(s32[320,512]{1,0:T(8,128)} %codes_ref.1) | copy-start | bytes 1966084
  3.0 26.8 %collective-permute-start.9 = (bf16[192,640]{1,0:T(8,128)(2,1)S(1)}, bf16[192,640]{1,0:T(8,128)(2,1)S(1)}, u32[]{:S(2)}, u32[]{:S(2)}) collective-permute-start(bf16[192,640]{1,0:T(8,128)(2,1)S(1)} %get-tuple-element.46), channel_id=1, source_target_pairs={{0,6},{2,4},{4,2},{6,0},{8,14},{10,12},{12,10},{14,8},{16,22},{18,... | collective-permute-start | bytes 737288 | tf_op jit(solution)/shard_map/ppermute | solution.py:454
  7.0 24.8 %collective-permute-start.5 = (bf16[192,640]{1,0:T(8,128)(2,1)S(1)}, bf16[192,640]{1,0:T(8,128)(2,1)S(1)}, u32[]{:S(2)}, u32[]{:S(2)}) collective-permute-start(bf16[192,640]{1,0:T(8,128)(2,1)S(1)} %get-tuple-element.44), channel_id=1, source_target_pairs={{0,2},{2,0},{4,6},{6,4},{8,10},{10,8},{12,14},{14,12},{16,18},{18,... | collective-permute-start | bytes 737288 | tf_op jit(solution)/shard_map/ppermute | solution.py:454
  7.5 0.9 copy-start.5
  8.4 0.9 copy-start.6
  9.4 13.4 %copy-start.8 = (s32[320,8]{0,1:T(8,128)S(1)}, s32[320,8]{0,1:T(8,128)}, u32[]{:S(2)}) copy-start(s32[320,8]{0,1:T(8,128)} %param.15) | copy-start | bytes 30724
  10.0 12.7 %collective-permute-start = (bf16[3,192,128]{2,1,0:T(8,128)(2,1)S(1)}, bf16[3,192,128]{2,1,0:T(8,128)(2,1)S(1)}, u32[]{:S(2)}, u32[]{:S(2)}) collective-permute-start(bf16[3,192,128]{2,1,0:T(8,128)(2,1)S(1)} %get-tuple-element.38), channel_id=1, source_target_pairs={{0,2},{2,0},{4,6},{6,4},{8,10},{10,8},{12,14},{14,12},{16,18},{18,... | collective-permute-start | bytes 442376 | tf_op jit(solution)/shard_map/ppermute | solution.py:454
  11.6 12.9 %collective-permute-start.1 = (bf16[3,192,128]{2,1,0:T(8,128)(2,1)S(1)}, bf16[3,192,128]{2,1,0:T(8,128)(2,1)S(1)}, u32[]{:S(2)}, u32[]{:S(2)}) collective-permute-start(bf16[3,192,128]{2,1,0:T(8,128)(2,1)S(1)} %get-tuple-element.39), channel_id=1, source_target_pairs={{0,4},{2,6},{4,0},{6,2},{8,12},{10,14},{12,8},{14,10},{16,20},{18,... | collective-permute-start | bytes 442376 | tf_op jit(solution)/shard_map/ppermute | solution.py:454
  12.1 14.5 %collective-permute-start.2 = (bf16[3,192,128]{2,1,0:T(8,128)(2,1)S(1)}, bf16[3,192,128]{2,1,0:T(8,128)(2,1)S(1)}, u32[]{:S(2)}, u32[]{:S(2)}) collective-permute-start(bf16[3,192,128]{2,1,0:T(8,128)(2,1)S(1)} %get-tuple-element.40), channel_id=1, source_target_pairs={{0,6},{2,4},{4,2},{6,0},{8,14},{10,12},{12,10},{14,8},{16,22},{18,... | collective-permute-start | bytes 442376 | tf_op jit(solution)/shard_map/ppermute | solution.py:454
  22.7 17.0 %collective-permute-start.7 = (bf16[192,640]{1,0:T(8,128)(2,1)S(1)}, bf16[192,640]{1,0:T(8,128)(2,1)S(1)}, u32[]{:S(2)}, u32[]{:S(2)}) collective-permute-start(bf16[192,640]{1,0:T(8,128)(2,1)S(1)} %get-tuple-element.45), channel_id=1, source_target_pairs={{0,4},{2,6},{4,0},{6,2},{8,12},{10,14},{12,8},{14,10},{16,20},{18,... | collective-permute-start | bytes 737288 | tf_op jit(solution)/shard_map/ppermute | solution.py:454
  22.8 0.7 copy-start.10
  22.8 0.7 copy-start.11
  24.5 19.0 %collective-permute-start.11 = (bf16[320,512]{1,0:T(8,128)(2,1)S(1)}, bf16[320,512]{1,0:T(8,128)(2,1)S(1)}, u32[]{:S(2)}, u32[]{:S(2)}) collective-permute-start(bf16[320,512]{1,0:T(8,128)(2,1)S(1)} %shard_map.141.refs_10_), channel_id=1, source_target_pairs={{0,8},{2,10},{4,12},{6,14},{8,16},{10,18},{12,20},{14,22},{16,24},... | collective-permute-start | bytes 983048 | tf_op jit(solution)/shard_map/ppermute | solution.py:459
  26.6 27.6 %collective-permute-start.12 = (bf16[320,512]{1,0:T(8,128)(2,1)S(1)}, bf16[320,512]{1,0:T(8,128)(2,1)}, u32[]{:S(2)}, u32[]{:S(2)}) collective-permute-start(bf16[320,512]{1,0:T(8,128)(2,1)S(1)} %shard_map.141.refs_10_), channel_id=1, source_target_pairs={{0,16},{2,18},{4,20},{6,22},{8,24},{10,26},{12,28},{14,30},{16,0},... | collective-permute-start | bytes 983048 | tf_op jit(solution)/shard_map/ppermute | solution.py:459
  29.2 2.7 %copy-start.7 = (bf16[4,2560]{1,0:T(4,128)(2,1)S(1)}, bf16[4,2560]{1,0:T(4,128)(2,1)}, u32[]{:S(2)}) copy-start(bf16[4,2560]{1,0:T(4,128)(2,1)} %up_ref.1) | copy-start | bytes 61444
  29.2 2.7 %copy-start.9 = (bf16[4,512]{1,0:T(4,128)(2,1)S(1)}, bf16[4,512]{1,0:T(4,128)(2,1)}, u32[]{:S(2)}) copy-start(bf16[4,512]{1,0:T(4,128)(2,1)} %down_ref.1) | copy-start | bytes 12292
  29.8 28.2 %collective-permute-start.17 = (bf16[2,768,128]{2,1,0:T(8,128)(2,1)S(1)}, bf16[2,768,128]{2,1,0:T(8,128)(2,1)S(1)}, u32[]{:S(2)}, u32[]{:S(2)}) collective-permute-start(bf16[2,768,128]{2,1,0:T(8,128)(2,1)S(1)} %get-tuple-element.42.kv_ref), channel_id=1, source_target_pairs={{0,8},{2,10},{5,13},{7,15},{9,17},{11,19},{12,20},{14,22},{16,24},... | collective-permute-start | bytes 1179656 | tf_op jit(solution)/shard_map/ppermute | solution.py:474
  31.8 11.6 %collective-permute-start.4 = (bf16[192,640]{1,0:T(8,128)(2,1)S(1)}, bf16[192,640]{1,0:T(8,128)(2,1)S(1)}, u32[]{:S(2)}, u32[]{:S(2)}) collective-permute-start(bf16[192,640]{1,0:T(8,128)(2,1)S(1)} %get-tuple-element.43.refs_2_.refs_4_), channel_id=1, source_target_pairs={{0,1},{1,0},{2,3},{3,2},{4,5},{5,4},{6,7},{7,6},{8,9},{9,8},{10,11... | collective-permute-start | bytes 737288 | tf_op jit(solution)/shard_map/ppermute | solution.py:464
  32.7 24.3 %all-to-all-start = ((bf16[16,4,1152]{2,1,0:T(4,128)(2,1)}), bf16[16,4,1152]{2,1,0:T(4,128)(2,1)}, u32[]{:S(2)}, u32[]{:S(2)}) async-start(bf16[16,4,1152]{2,1,0:T(4,128)(2,1)} %shard_map.139), calls=%async_computation | async-start | bytes 294912 | tf_op jit(solution)/shard_map/all_to_all | solution.py:531
  39.7 21.3 %collective-permute-start.13 = (bf16[320,512]{1,0:T(8,128)(2,1)S(1)}, bf16[320,512]{1,0:T(8,128)(2,1)}, u32[]{:S(2)}, u32[]{:S(2)}) collective-permute-start(bf16[320,512]{1,0:T(8,128)(2,1)S(1)} %shard_map.141.refs_10_), channel_id=1, source_target_pairs={{0,24},{2,26},{4,28},{6,30},{8,0},{10,2},{12,4},{14,6},{16,8},{18,... | collective-permute-start | bytes 983048 | tf_op jit(solution)/shard_map/ppermute | solution.py:459
  43.5 18.7 %collective-permute-start.10 = (bf16[192,640]{1,0:T(8,128)(2,1)S(1)}, bf16[192,640]{1,0:T(8,128)(2,1)S(1)}, u32[]{:S(2)}, u32[]{:S(2)}) collective-permute-start(bf16[192,640]{1,0:T(8,128)(2,1)S(1)} %collective-permute-done.9.refs_8_.refs_7_), channel_id=1, source_target_pairs={{0,1},{1,0},{2,3},{3,2},{4,5},{5,4},{6,7},{7,6},{8,9},{9,8},{10,11... | collective-permute-start | bytes 737288 | tf_op jit(solution)/shard_map/ppermute | solution.py:464
  43.5 0.7 copy-start
  44.2 18.0 %collective-permute-start.6 = (bf16[192,640]{1,0:T(8,128)(2,1)S(1)}, bf16[192,640]{1,0:T(8,128)(2,1)S(1)}, u32[]{:S(2)}, u32[]{:S(2)}) collective-permute-start(bf16[192,640]{1,0:T(8,128)(2,1)S(1)} %collective-permute-done.5.refs_4_.refs_5_), channel_id=1, source_target_pairs={{0,1},{1,0},{2,3},{3,2},{4,5},{5,4},{6,7},{7,6},{8,9},{9,8},{10,11... | collective-permute-start | bytes 737288 | tf_op jit(solution)/shard_map/ppermute | solution.py:464
  54.2 8.0 %collective-permute-start.8 = (bf16[192,640]{1,0:T(8,128)(2,1)S(1)}, bf16[192,640]{1,0:T(8,128)(2,1)S(1)}, u32[]{:S(2)}, u32[]{:S(2)}) collective-permute-start(bf16[192,640]{1,0:T(8,128)(2,1)S(1)} %collective-permute-done.7.refs_6_), channel_id=1, source_target_pairs={{0,1},{1,0},{2,3},{3,2},{4,5},{5,4},{6,7},{7,6},{8,9},{9,8},{10,11... | collective-permute-start | bytes 737288 | tf_op jit(solution)/shard_map/ppermute | solution.py:464
  58.0 4.2 %collective-permute-start.3 = (bf16[64,1152]{1,0:T(8,128)(2,1)S(1)}, bf16[64,1152]{1,0:T(8,128)(2,1)S(1)}, u32[]{:S(2)}, u32[]{:S(2)}) collective-permute-start(bf16[64,1152]{1,0:T(8,128)(2,1)S(1)} %reshape.16.refs_0_.adapt_ref), channel_id=1, source_target_pairs={{0,1},{1,0},{2,3},{3,2},{4,5},{5,4},{6,7},{7,6},{8,9},{9,8},{10,11... | collective-permute-start | bytes 442376 | tf_op jit(solution)/shard_map/ppermute | solution.py:464
  58.1 4.2 %copy-start.1 = (bf16[320,512]{1,0:T(8,128)(2,1)S(1)}, bf16[320,512]{1,0:T(8,128)(2,1)}, u32[]{:S(2)}) copy-start(bf16[320,512]{1,0:T(8,128)(2,1)} %copy-done) | copy-start | bytes 983044
  61.0 10.7 %collective-permute-start.22 = (f32[768,64]{1,0:T(8,128)S(1)}, f32[768,64]{1,0:T(8,128)S(1)}, u32[]{:S(2)}, u32[]{:S(2)}) collective-permute-start(f32[768,64]{1,0:T(8,128)S(1)} %get-tuple-element.66.refs_0_), channel_id=1, source_target_pairs={{0,1},{1,0},{2,3},{3,2},{4,5},{5,4},{6,7},{7,6},{8,9},{9,8},{10,11... | collective-permute-start | bytes 589832 | tf_op jit(solution)/shard_map/ppermute | solution.py:464
  64.5 11.9 %collective-permute-start.15 = (bf16[768,128]{1,0:T(8,128)(2,1)S(1)}, bf16[768,128]{1,0:T(8,128)(2,1)S(1)}, u32[]{:S(2)}, u32[]{:S(2)}) collective-permute-start(bf16[768,128]{1,0:T(8,128)(2,1)S(1)} %get-tuple-element.49), channel_id=1, source_target_pairs={{0,4},{2,6},{4,0},{6,2},{8,12},{10,14},{12,8},{14,10},{16,20},{18,... | collective-permute-start | bytes 589832 | tf_op jit(solution)/shard_map/ppermute | solution.py:454
  65.8 12.9 %collective-permute-start.16 = (bf16[768,128]{1,0:T(8,128)(2,1)S(1)}, bf16[768,128]{1,0:T(8,128)(2,1)S(1)}, u32[]{:S(2)}, u32[]{:S(2)}) collective-permute-start(bf16[768,128]{1,0:T(8,128)(2,1)S(1)} %get-tuple-element.50), channel_id=1, source_target_pairs={{0,6},{2,4},{4,2},{6,0},{8,14},{10,12},{12,10},{14,8},{16,22},{18,... | collective-permute-start | bytes 589832 | tf_op jit(solution)/shard_map/ppermute | solution.py:454
  69.1 9.6 %collective-permute-start.14 = (bf16[768,128]{1,0:T(8,128)(2,1)S(1)}, bf16[768,128]{1,0:T(8,128)(2,1)S(1)}, u32[]{:S(2)}, u32[]{:S(2)}) collective-permute-start(bf16[768,128]{1,0:T(8,128)(2,1)S(1)} %get-tuple-element.48), channel_id=1, source_target_pairs={{0,2},{2,0},{4,6},{6,4},{8,10},{10,8},{12,14},{14,12},{16,18},{18,... | collective-permute-start | bytes 589832 | tf_op jit(solution)/shard_map/ppermute | solution.py:454
  71.8 10.0 %collective-permute-start.23 = (bf16[768,128]{1,0:T(8,128)(2,1)S(1)}, bf16[768,128]{1,0:T(8,128)(2,1)S(1)}, u32[]{:S(2)}, u32[]{:S(2)}) collective-permute-start(bf16[768,128]{1,0:T(8,128)(2,1)S(1)} %shard_map.150.refs_0_), channel_id=1, source_target_pairs={{0,2},{2,0},{4,6},{6,4},{8,10},{10,8},{12,14},{14,12},{16,18},{18,... | collective-permute-start | bytes 589832 | tf_op jit(solution)/shard_map/ppermute | solution.py:454
  72.6 9.2 %collective-permute-start.24 = (bf16[768,128]{1,0:T(8,128)(2,1)S(1)}, bf16[768,128]{1,0:T(8,128)(2,1)S(1)}, u32[]{:S(2)}, u32[]{:S(2)}) collective-permute-start(bf16[768,128]{1,0:T(8,128)(2,1)S(1)} %shard_map.150.refs_0_), channel_id=1, source_target_pairs={{0,4},{2,6},{4,0},{6,2},{8,12},{10,14},{12,8},{14,10},{16,20},{18,... | collective-permute-start | bytes 589832 | tf_op jit(solution)/shard_map/ppermute | solution.py:454
  76.5 9.9 %collective-permute-start.25 = (bf16[768,128]{1,0:T(8,128)(2,1)S(1)}, bf16[768,128]{1,0:T(8,128)(2,1)S(1)}, u32[]{:S(2)}, u32[]{:S(2)}) collective-permute-start(bf16[768,128]{1,0:T(8,128)(2,1)S(1)} %shard_map.150.refs_0_), channel_id=1, source_target_pairs={{0,6},{2,4},{4,2},{6,0},{8,14},{10,12},{12,10},{14,8},{16,22},{18,... | collective-permute-start | bytes 589832 | tf_op jit(solution)/shard_map/ppermute | solution.py:454
  79.7 20.4 %collective-permute-start.18 = (bf16[2,768,128]{2,1,0:T(8,128)(2,1)S(1)}, bf16[2,768,128]{2,1,0:T(8,128)(2,1)S(1)}, u32[]{:S(2)}, u32[]{:S(2)}) collective-permute-start(bf16[2,768,128]{2,1,0:T(8,128)(2,1)S(1)} %get-tuple-element.58), channel_id=1, source_target_pairs={{8,0},{10,2},{13,5},{15,7},{17,9},{19,11},{20,12},{22,14},{24,16},... | collective-permute-start | bytes 1179656 | tf_op jit(solution)/shard_map/ppermute | solution.py:477
  88.2 24.4 %all-to-all-start.1 = ((f32[16,4,768]{2,1,0:T(4,128)}), f32[16,4,768]{2,1,0:T(4,128)S(1)}, u32[]{:S(2)}, u32[]{:S(2)}) async-start(f32[16,4,768]{2,1,0:T(4,128)} %shard_map.151), calls=%async_computation.1 | async-start | bytes 393216 | tf_op jit(solution)/shard_map/all_to_all | solution.py:589
  100.8 7.3 %collective-permute-start.19 = (bf16[3,192,128]{2,1,0:T(8,128)(2,1)S(1)}, bf16[3,192,128]{2,1,0:T(8,128)(2,1)S(1)}, u32[]{:S(2)}, u32[]{:S(2)}) collective-permute-start(bf16[3,192,128]{2,1,0:T(8,128)(2,1)S(1)} %get-tuple-element.60), channel_id=1, source_target_pairs={{0,2},{2,0},{4,6},{6,4},{8,10},{10,8},{12,14},{14,12},{16,18},{18,... | collective-permute-start | bytes 442376 | tf_op jit(solution)/shard_map/ppermute | solution.py:454
  102.8 8.4 %collective-permute-start.20 = (bf16[3,192,128]{2,1,0:T(8,128)(2,1)S(1)}, bf16[3,192,128]{2,1,0:T(8,128)(2,1)S(1)}, u32[]{:S(2)}, u32[]{:S(2)}) collective-permute-start(bf16[3,192,128]{2,1,0:T(8,128)(2,1)S(1)} %get-tuple-element.61), channel_id=1, source_target_pairs={{0,4},{2,6},{4,0},{6,2},{8,12},{10,14},{12,8},{14,10},{16,20},{18,... | collective-permute-start | bytes 442376 | tf_op jit(solution)/shard_map/ppermute | solution.py:454
  104.2 6.9 %collective-permute-start.21 = (bf16[3,192,128]{2,1,0:T(8,128)(2,1)S(1)}, bf16[3,192,128]{2,1,0:T(8,128)(2,1)S(1)}, u32[]{:S(2)}, u32[]{:S(2)}) collective-permute-start(bf16[3,192,128]{2,1,0:T(8,128)(2,1)S(1)} %get-tuple-element.62), channel_id=1, source_target_pairs={{0,6},{2,4},{4,2},{6,0},{8,14},{10,12},{12,10},{14,8},{16,22},{18,... | collective-permute-start | bytes 442376 | tf_op jit(solution)/shard_map/ppermute | solution.py:454

commit v2 on v1

--- a/solution.py
+++ b/solution.py
@@ -2,7 +2,6 @@
 
 import jax
 import jax.numpy as jnp
-import numpy as np
 from jax import lax
 from jax.experimental import pallas as pl
 from jax.experimental.pallas import tpu as pltpu
@@ -40,6 +39,7 @@
 F32 = jnp.float32
 VM = pl.BlockSpec(memory_space=pltpu.VMEM)
 SM = pl.BlockSpec(memory_space=pltpu.SMEM)
+HB = pl.BlockSpec(memory_space=pltpu.HBM)
 
 
 def sds(shape, dtype):
@@ -54,18 +54,35 @@
     return jnp.dot(a, b, preferred_element_type=F32)
 
 
-def call(body, outs, scratch, *args, n_scalar=0):
+def call(body, outs, scratch, *args, n_scalar=0, in_hbm=False):
+    if in_hbm:
+        args = args[:n_scalar] + tuple(
+            pltpu.with_memory_space_constraint(x, pltpu.HBM) for x in args[n_scalar:]
+        )
+    spec = HB if in_hbm else VM
     return pl.pallas_call(
         body,
         out_shape=outs,
-        in_specs=[SM] * n_scalar + [VM] * (len(args) - n_scalar),
+        in_specs=[SM] * n_scalar + [spec] * (len(args) - n_scalar),
         out_specs=jax.tree.map(lambda _: VM, outs),
         scratch_shapes=scratch,
         compiler_params=pltpu.CompilerParams(vmem_limit_bytes=KERNEL_VMEM),
     )(*args)
 
 
-def dequant_body(codes_ref, index_ref, table_ref, nf4_ref, out_ref):
+def fetch(sources, targets, sem):
+    copies = [
+        pltpu.make_async_copy(src, to, sem.at[i])
+        for i, (src, to) in enumerate(zip(sources, targets))
+    ]
+    for copy in copies:
+        copy.start()
+    for copy in copies:
+        copy.wait()
+
+
+def dequant_body(codes_in, index_in, table_in, out_ref, codes_ref, index_ref, table_ref, sem):
+    fetch((codes_in, index_in, table_in), (codes_ref, index_ref, table_ref), sem)
     rows, cols = codes_ref.shape
     groups = index_ref.shape[0]
     parts = table_ref.shape[0]
@@ -87,7 +104,11 @@
         scales.append(scale)
     scales = jnp.concatenate(scales, axis=1).T[:rows, :]
     lane = lax.broadcasted_iota(jnp.int32, (rows, LANES), 1)
-    levels = jnp.broadcast_to(nf4_ref[...], (rows, LANES))
+    place = lax.broadcasted_iota(jnp.int32, (8, LANES), 1)
+    levels = jnp.zeros((8, LANES), F32)
+    for i, level in enumerate(nf4_values):
+        levels = jnp.where(place == i, level, levels)
+    levels = jnp.broadcast_to(levels[:1], (rows, LANES))
     for b in range(cols // LANES):
         code = codes_ref[:, b * LANES : (b + 1) * LANES]
         value = jnp.take_along_axis(levels, code, axis=1)
@@ -152,7 +173,9 @@
                 out_refs[s][...] = jnp.concatenate(pieces, axis=1)
 
 
-def pack_heads_body(half, pos_ref, q_ref, k_ref, v_ref, *out_refs):
+def pack_heads_body(half, pos_ref, q_in, k_in, v_in, *refs):
+    out_refs, (q_ref, k_ref, v_ref, sem) = refs[:half], refs[half:]
+    fetch((q_in, k_in, v_in), (q_ref, k_ref, v_ref), sem)
     own = pos_ref[4]
     for s in range(half):
         cols = pl.ds(pl.multiple_of((own ^ s) * LANES, LANES), LANES)
@@ -185,12 +208,21 @@
         out_ref[at, :] = adapter_scale * total
 
 
-def join_body(lora_ref, *refs):
+def join_body(pos_ref, lora_ref, *refs):
     mids, out_ref = refs[:-1], refs[-1]
+    rows = out_ref.shape[0]
     mid = mids[0][...]
     for m in mids[1:]:
         mid = mid + m[...]
-    out_ref[...] = jnp.concatenate([lora_ref[...], mid], axis=1).astype(BF)
+    lora = lora_ref[pl.ds(pl.multiple_of(pos_ref[2] * rows, rows), rows), :]
+    out_ref[...] = jnp.concatenate([lora, mid], axis=1).astype(BF)
+
+
+def total_body(*refs):
+    total = refs[0][...].astype(F32)
+    for ref in refs[1:-1]:
+        total = total + ref[...].astype(F32)
+    refs[-1][...] = total.astype(BF)
 
 
 def project_body(half, planes, fsdp, slot, targets, pos_ref, *refs):
@@ -242,10 +274,9 @@
     return jnp.where(kpos <= qpos, scores, masked)
 
 
-def forward_body(
-    wide, pos_ref, q_ref, kv_ref, far_ref, adapt_ref, o_ref, lse_ref, mid_ref, vt_scr, oft_scr
-):
-    later, own = pos_ref[3], pos_ref[4]
+def forward_body(fsdp, wide, pos_ref, q_ref, kv_ref, far_ref, adapt_ref, o_ref, lse_ref, *refs):
+    mid_refs, (vt_scr, oft_scr, mid_ref) = refs[:fsdp], refs[fsdp:]
+    core, later, own = pos_ref[2], pos_ref[3], pos_ref[4]
     down = adapt_ref[:, pl.ds(pl.multiple_of(wide + own * LANES, LANES), LANES)]
     tokens = q_ref.shape[0]
     block = min(QUERY_BLOCK, tokens)
@@ -287,6 +318,11 @@
                 oft_scr[...], far_prob.astype(BF)
             )
             finish(q0, out / total, top + jnp.log(total))
+
+    rows = tokens // fsdp
+    for s in range(fsdp):
+        to = lax.rem(core + s, fsdp)
+        mid_refs[s][...] = mid_ref[pl.ds(pl.multiple_of(to * rows, rows), rows), :]
 
 
 def grad_block(key, value, query, grad, norm, delta, k0, q0):
@@ -387,24 +423,23 @@
             outs[i][:, at] = pieces[s][i]
 
 
-def adapters_body(half, pos_ref, o_ref, *refs):
-    both, grads, out_ref, scr = refs[:half], refs[half : 2 * half], refs[-2], refs[-1]
-    mine = pos_ref[0]
+def adapters_body(half, fsdp, pos_ref, o_ref, *refs):
+    both, grads, (out_ref, scr) = refs[:fsdp], refs[fsdp : fsdp + half], refs[fsdp + half :]
+    mine, core = pos_ref[0], pos_ref[2]
     count, rank_rows = out_ref.shape[:2]
     rank = count * rank_rows
     rows, wide = grads[0].shape
-    total = both[0][...].astype(F32)
-    for s in range(1, half):
-        total = total + both[s][...].astype(F32)
-    total = total.astype(BF)
-    scr[...] = total
+    part_rows = both[0].shape[0]
+    for s in range(fsdp):
+        src = lax.rem(core + (fsdp - s), fsdp)
+        scr[pl.ds(pl.multiple_of(src * part_rows, part_rows), part_rows), :] = both[s][...]
     acc = None
     for s in range(half):
         at = pl.ds(pl.multiple_of((mine ^ s) * rows, rows), rows)
         part = nn(scr[at, :].T[rank:, :], grads[s][...])
         acc = part if acc is None else acc + part
     acc = adapter_scale * acc
-    low = nn(total.T[:rank, :], o_ref[...].astype(BF))
+    low = nn(scr[...].T[:rank, :], o_ref[...].astype(BF))
     for c in range(count):
         out_ref[c, :, :wide] = acc[c * rank_rows : (c + 1) * rank_rows, :]
         out_ref[c, :, wide:] = low[c * rank_rows : (c + 1) * rank_rows, :]
@@ -476,16 +511,17 @@
     def to_earlier(x):
         return lax.ppermute(x, ("ctx", "fsdp"), [(b, a) for a, b in pairs])
 
-    levels = np.zeros((1, LANES), np.float32)
-    levels[0, : len(nf4_values)] = nf4_values
+    table = block_scale_table.reshape(-1, LANES)
+    index = block_scale_index.T
     weight = call(
         dequant_body,
         sds((w_rows, w_cols), BF),
-        [],
+        [pltpu.VMEM(x.shape, x.dtype) for x in (frozen_weight_codes, index, table)]
+        + [pltpu.SemaphoreType.DMA((3,))],
         frozen_weight_codes,
-        block_scale_index.T,
-        block_scale_table.reshape(-1, LANES),
-        jnp.asarray(levels),
+        index,
+        table,
+        in_hbm=True,
     )
     weights = [along(weight, s) for s in range(planes)]
 
@@ -503,12 +539,13 @@
     packed = call(
         functools.partial(pack_heads_body, half),
         [sds((3, rows, LANES), BF)] * half,
-        [],
+        [pltpu.VMEM(rotated_query_rows.shape, BF)] * 3 + [pltpu.SemaphoreType.DMA((3,))],
         pos,
         rotated_query_rows,
         rotated_key_rows,
         saved_value_rows,
         n_scalar=1,
+        in_hbm=True,
     )
     packed = [in_plane(x, s) for s, x in enumerate(packed)]
     query, key_value = call(
@@ -562,10 +599,16 @@
     rest = dict(zip(second, project(tuple(second))))
     partial.update({s: in_plane(x, s) for s, x in rest.items()})
 
-    out, norm, mid = call(
-        functools.partial(forward_body, wide),
-        [sds((tokens, LANES), F32), sds((1, tokens), F32), sds((tokens, rank), F32)],
-        [pltpu.VMEM((LANES, tokens), BF), pltpu.VMEM((LANES, tokens), BF)],
+    part_rows = tokens // fsdp
+    out, norm, *mids = call(
+        functools.partial(forward_body, fsdp, wide),
+        [sds((tokens, LANES), F32), sds((1, tokens), F32)]
+        + [sds((part_rows, rank), F32)] * fsdp,
+        [
+            pltpu.VMEM((LANES, tokens), BF),
+            pltpu.VMEM((LANES, tokens), BF),
+            pltpu.VMEM((tokens, rank), F32),
+        ],
         pos,
         query,
         key_value,
@@ -573,11 +616,13 @@
         adapters,
         n_scalar=1,
     )
-    mids = [across(mid, f) for f in range(fsdp)]
-    both = call(join_body, sds((tokens, 2 * rank), BF), [], lora, *mids)
+    mids = [across(x, f) for f, x in enumerate(mids)]
+    both = call(join_body, sds((part_rows, 2 * rank), BF), [], pos, lora, *mids, n_scalar=1)
     both = [in_plane(both, s) for s in range(half)]
+    both = call(total_body, sds((part_rows, 2 * rank), BF), [], *both)
+    both = [across(both, f) for f in range(fsdp)]
     adapter_grads = call(
-        functools.partial(adapters_body, half),
+        functools.partial(adapters_body, half, fsdp),
         sds((n_ctx, rank_rows, wide + HEAD_WIDTH), F32),
         [pltpu.VMEM((tokens, 2 * rank), BF)],
         pos,

time: 114 us -> 109 us (0.956)
  starting transfers between devices: 51 us -> 40.5 us
  waiting for transfers between devices: 36.2 us -> 40 us
  Pallas kernels: 20.2 us -> 22.9 us
  local copies, waits for them, and re-layouts: 5.5 us -> 3.93 us
    all_to_all x1, waiting for transfers between devices: 2.84 us -> 12.4 us  [on_device(): lax.all_to_all(chunks, 'ctx', split_axis=0, concat_axis=0, tiled=True)]
    ppermute x15, waiting for transfers between devices: 23.3 us -> 13.9 us  [in_plane(): return lax.ppermute(x, 'ctx', [(i, i ^ s) for i in range(n_ctx)])]
    all_to_all x1, starting transfers between devices: 10.1 us -> 3.52 us  [on_device(): lax.all_to_all(adapter_grads, 'ctx', split_axis=0, concat_axis=0, tiled=T...]
    all_to_all x1, starting transfers between devices: 7.05 us -> 4.16 us  [on_device(): lax.all_to_all(chunks, 'ctx', split_axis=0, concat_axis=0, tiled=True)]
    all_to_all x1, waiting for transfers between devices: 0.01 us -> 2.83 us  [on_device(): lax.all_to_all(adapter_grads, 'ctx', split_axis=0, concat_axis=0, tiled=T...]
    pallas_call x16 -> x17, Pallas kernels: 20.2 us -> 22.9 us  [call(): pl.pallas_call(body, out_shape=outs, in_specs=[SM] * n_scalar + [spec] *...]
    ppermute x6 -> x7, waiting for transfers between devices: 0.02 us -> 2.66 us  [across(): return lax.ppermute(x, 'fsdp', [(i, (i + s) % fsdp) for i in range(fsdp)])]
    ppermute x3, waiting for transfers between devices: 10.1 us -> 8.22 us  [along(): lax.ppermute(x, 'ctx', [(i, (i + s * half) % n_ctx) for i in range(n_ctx)])]
  transfers between devices with their start and end apart: 28 -> 29, of which waited for: 9 -> 10; matrix products, arithmetic and copies ran while one was open for 1% -> 1% of each run, Pallas kernels for 16% -> 19%
where the time goes in v2:
time: 109 us; the launch traced here: 108 us
  starting transfers between devices  40.5 us (37%)
  waiting for transfers between devices  40 us (37%)
  Pallas kernels  22.9 us (21%)
  local copies, waits for them, and re-layouts  3.93 us (4%)
    pallas_call x17, Pallas kernels, call(): pl.pallas_call(body, out_shape=outs, in_specs=[SM] * n_scalar + [spec] *...  22.9 us
    ppermute x15, starting transfers between devices, in_plane(): return lax.ppermute(x, 'ctx', [(i, i ^ s) for i in range(n_ctx)])  19.9 us
    ppermute x15, waiting for transfers between devices, in_plane(): return lax.ppermute(x, 'ctx', [(i, i ^ s) for i in range(n_ctx)])  13.9 us
    all_to_all x1, waiting for transfers between devices, on_device(): lax.all_to_all(chunks, 'ctx', split_axis=0, concat_axis=0, tiled=True)  12.4 us
    ppermute x3, waiting for transfers between devices, along(): lax.ppermute(x, 'ctx', [(i, (i + s * half) % n_ctx) for i in range(n_ctx)])  8.22 us
    ppermute x3, starting transfers between devices, along(): lax.ppermute(x, 'ctx', [(i, (i + s * half) % n_ctx) for i in range(n_ctx)])  6.64 us
    all_to_all x1, starting transfers between devices, on_device(): lax.all_to_all(chunks, 'ctx', split_axis=0, concat_axis=0, tiled=True)  4.16 us
    ppermute x1, starting transfers between devices, to_later(): return lax.ppermute(x, ('ctx', 'fsdp'), pairs)  3.7 us
  transfers between devices with their start and end apart: 29, of which 10 were waited for; matrix products, arithmetic and copies ran while one was open for 1% of the time, Pallas kernels for 19%

profile of v2, /device:TPU:0, one launch (start us, length us, event | category | flops | bytes accessed | tf_op | source)
XLA Modules:
  0.0 108.3 jit_solution(11080564023282533864)
XLA Ops:
  0.7 0.1 stack.23.pos_ref
  0.8 1.2 %copy-done.2 = bf16[192,2560]{1,0:T(8,128)(2,1)S(1)} copy-done((bf16[192,2560]{1,0:T(8,128)(2,1)S(1)}, bf16[192,2560]{1,0:T(8,128)(2,1)}, u32[]{:S(2)}) %copy-start.2) | copy-done | bytes 983064
  2.0 1.0 shard_map.131
  3.0 4.0 %collective-permute-start.9 = (bf16[192,640]{1,0:T(8,128)(2,1)S(1)}, bf16[192,640]{1,0:T(8,128)(2,1)S(1)}, u32[]{:S(2)}, u32[]{:S(2)}) collective-permute-start(bf16[192,640]{1,0:T(8,128)(2,1)S(1)} %get-tuple-element.47), channel_id=1, source_target_pairs={{0,6},{2,4},{4,2},{6,0},{8,14},{10,12},{12,10},{14,8},{16,22},{18,... | collective-permute-start | bytes 737288 | tf_op jit(solution)/shard_map/ppermute | solution.py:489
  7.0 0.5 collective-permute-start.5
  7.5 1.8 %shard_map.128 = (bf16[3,192,128]{2,1,0:T(8,128)(2,1)S(1)}, bf16[3,192,128]{2,1,0:T(8,128)(2,1)S(1)}, bf16[3,192,128]{2,1,0:T(8,128)(2,1)S(1)}, bf16[3,192,128]{2,1,0:T(8,128)(2,1)S(1)}) custom-call(s32[5]{0:T(128)S(1)} %stack.23.pos_ref, bf16[192,512]{1,0:T(8,128)(2,1)} %q_in.1, bf16[192,512]{1,0:T(8,128)(2,1)} %k_in.1, bf16[192,512]{1,0:T(8,128)(2,1)} %v_in.1), custom_call_target="tpu_custom_call" | custom-call | tf_op jit(solution)/shard_map/pallas_call | solution.py:63
  9.3 1.6 %collective-permute-start = (bf16[3,192,128]{2,1,0:T(8,128)(2,1)S(1)}, bf16[3,192,128]{2,1,0:T(8,128)(2,1)S(1)}, u32[]{:S(2)}, u32[]{:S(2)}) collective-permute-start(bf16[3,192,128]{2,1,0:T(8,128)(2,1)S(1)} %get-tuple-element.39), channel_id=1, source_target_pairs={{0,2},{2,0},{4,6},{6,4},{8,10},{10,8},{12,14},{14,12},{16,18},{18,... | collective-permute-start | bytes 442376 | tf_op jit(solution)/shard_map/ppermute | solution.py:489
  10.9 0.5 collective-permute-start.1
  11.4 1.5 %collective-permute-start.2 = (bf16[3,192,128]{2,1,0:T(8,128)(2,1)S(1)}, bf16[3,192,128]{2,1,0:T(8,128)(2,1)S(1)}, u32[]{:S(2)}, u32[]{:S(2)}) collective-permute-start(bf16[3,192,128]{2,1,0:T(8,128)(2,1)S(1)} %get-tuple-element.41), channel_id=1, source_target_pairs={{0,6},{2,4},{4,2},{6,0},{8,14},{10,12},{12,10},{14,8},{16,22},{18,... | collective-permute-start | bytes 442376 | tf_op jit(solution)/shard_map/ppermute | solution.py:489
  12.9 2.2 %shard_map.132.refs_10_ = bf16[320,512]{1,0:T(8,128)(2,1)S(1)} custom-call(s32[320,512]{1,0:T(8,128)} %codes_in.1, s32[8,320]{1,0:T(8,128)} %bitcast.7, f32[2,128]{1,0:T(2,128)} %bitcast.8), custom_call_target="tpu_custom_call" | custom-call | tf_op jit(solution)/shard_map/pallas_call | solution.py:63
  15.0 7.7 %collective-permute-done.refs_1_ = bf16[3,192,128]{2,1,0:T(8,128)(2,1)S(1)} collective-permute-done((bf16[3,192,128]{2,1,0:T(8,128)(2,1)S(1)}, bf16[3,192,128]{2,1,0:T(8,128)(2,1)S(1)}, u32[]{:S(2)}, u32[]{:S(2)}) %collective-permute-start) | collective-permute-done | bytes 147488 | tf_op jit(solution)/shard_map/ppermute | solution.py:489
  22.7 1.6 %collective-permute-start.11 = (bf16[320,512]{1,0:T(8,128)(2,1)S(1)}, bf16[320,512]{1,0:T(8,128)(2,1)S(1)}, u32[]{:S(2)}, u32[]{:S(2)}) collective-permute-start(bf16[320,512]{1,0:T(8,128)(2,1)S(1)} %shard_map.132.refs_10_), channel_id=1, source_target_pairs={{0,8},{2,10},{4,12},{6,14},{8,16},{10,18},{12,20},{14,22},{16,24},... | collective-permute-start | bytes 983048 | tf_op jit(solution)/shard_map/ppermute | solution.py:494
  24.3 2.6 %collective-permute-start.12 = (bf16[320,512]{1,0:T(8,128)(2,1)S(1)}, bf16[320,512]{1,0:T(8,128)(2,1)}, u32[]{:S(2)}, u32[]{:S(2)}) collective-permute-start(bf16[320,512]{1,0:T(8,128)(2,1)S(1)} %shard_map.132.refs_10_), channel_id=1, source_target_pairs={{0,16},{2,18},{4,20},{6,22},{8,24},{10,26},{12,28},{14,30},{16,0},... | collective-permute-start | bytes 983048 | tf_op jit(solution)/shard_map/ppermute | solution.py:494
  26.9 0.5 collective-permute-start.7
  27.4 2.5 %collective-permute-start.13 = (bf16[320,512]{1,0:T(8,128)(2,1)S(1)}, bf16[320,512]{1,0:T(8,128)(2,1)}, u32[]{:S(2)}, u32[]{:S(2)}) collective-permute-start(bf16[320,512]{1,0:T(8,128)(2,1)S(1)} %shard_map.132.refs_10_), channel_id=1, source_target_pairs={{0,24},{2,26},{4,28},{6,30},{8,0},{10,2},{12,4},{14,6},{16,8},{18,... | collective-permute-start | bytes 983048 | tf_op jit(solution)/shard_map/ppermute | solution.py:494
  29.9 0.7 shard_map.130
  30.6 4.2 %all-to-all-start = ((bf16[16,4,1152]{2,1,0:T(4,128)(2,1)}), bf16[16,4,1152]{2,1,0:T(4,128)(2,1)}, u32[]{:S(2)}, u32[]{:S(2)}) async-start(bf16[16,4,1152]{2,1,0:T(4,128)(2,1)} %shard_map.130), calls=%async_computation | async-start | bytes 294912 | tf_op jit(solution)/shard_map/all_to_all | solution.py:568
  34.8 0.6 shard_map.129
  35.4 0.0 collective-permute-done.7.refs_6_.refs_4_
  35.4 3.7 %collective-permute-start.17 = (bf16[2,768,128]{2,1,0:T(8,128)(2,1)S(1)}, bf16[2,768,128]{2,1,0:T(8,128)(2,1)S(1)}, u32[]{:S(2)}, u32[]{:S(2)}) collective-permute-start(bf16[2,768,128]{2,1,0:T(8,128)(2,1)S(1)} %get-tuple-element.43.kv_ref), channel_id=1, source_target_pairs={{0,8},{2,10},{5,13},{7,15},{9,17},{11,19},{12,20},{14,22},{16,24},... | collective-permute-start | bytes 1179656 | tf_op jit(solution)/shard_map/ppermute | solution.py:509
  39.1 0.1 collective-permute-start.10
  39.2 0.0 collective-permute-done.11.refs_11_
  39.2 0.7 copy-done
  40.0 0.5 collective-permute-start.6
  40.4 8.2 %collective-permute-done.12.refs_12_ = bf16[320,512]{1,0:T(8,128)(2,1)} collective-permute-done((bf16[320,512]{1,0:T(8,128)(2,1)S(1)}, bf16[320,512]{1,0:T(8,128)(2,1)}, u32[]{:S(2)}, u32[]{:S(2)}) %collective-permute-start.12) | collective-permute-done | bytes 327712 | tf_op jit(solution)/shard_map/ppermute | solution.py:494
  48.7 0.0 collective-permute-start.8
  48.7 12.4 %all-to-all-done = bf16[16,4,1152]{2,1,0:T(4,128)(2,1)} async-done(((bf16[16,4,1152]{2,1,0:T(4,128)(2,1)}), bf16[16,4,1152]{2,1,0:T(4,128)(2,1)}, u32[]{:S(2)}, u32[]{:S(2)}) %all-to-all-start) | async-done | bytes 147488 | tf_op jit(solution)/shard_map/all_to_all | solution.py:568
  61.1 0.9 reshape.16.refs_0_.adapt_ref
  62.0 0.0 collective-permute-done.13.refs_13_
  62.0 0.1 collective-permute-start.3
  62.1 1.4 %collective-permute-done.3.refs_1_ = bf16[64,1152]{1,0:T(8,128)(2,1)S(1)} collective-permute-done((bf16[64,1152]{1,0:T(8,128)(2,1)S(1)}, bf16[64,1152]{1,0:T(8,128)(2,1)S(1)}, u32[]{:S(2)}, u32[]{:S(2)}) %collective-permute-start.3) | collective-permute-done | bytes 147488 | tf_op jit(solution)/shard_map/ppermute | solution.py:499
  63.5 0.0 collective-permute-done.10.refs_9_
  63.5 1.0 copy-done.1
  64.5 2.3 %shard_map.134 = (bf16[768,128]{1,0:T(8,128)(2,1)S(1)}, bf16[768,128]{1,0:T(8,128)(2,1)S(1)}) custom-call(s32[5]{0:T(128)S(1)} %stack.23.pos_ref, bf16[64,1152]{1,0:T(8,128)(2,1)S(1)} %reshape.16.refs_0_.adapt_ref, bf16[64,1152]{1,0:T(8,128)(2,1)S(1)} %collective-permute-done.3.refs_1_, bf16[192,640]{1,0:T(8,128)(2,1)S(1)} %get-tuple-element.44.refs_2_, ...), custom_call_target="tpu_custom_call" | custom-call | tf_op jit(solution)/shard_map/pallas_call | solution.py:63
  66.8 1.7 %collective-permute-start.15 = (bf16[768,128]{1,0:T(8,128)(2,1)S(1)}, bf16[768,128]{1,0:T(8,128)(2,1)S(1)}, u32[]{:S(2)}, u32[]{:S(2)}) collective-permute-start(bf16[768,128]{1,0:T(8,128)(2,1)S(1)} %get-tuple-element.50), channel_id=1, source_target_pairs={{0,4},{2,6},{4,0},{6,2},{8,12},{10,14},{12,8},{14,10},{16,20},{18,... | collective-permute-start | bytes 589832 | tf_op jit(solution)/shard_map/ppermute | solution.py:489
  68.5 0.3 collective-permute-start.16
  68.8 2.3 %shard_map.133 = (bf16[768,128]{1,0:T(8,128)(2,1)S(1)}, bf16[768,128]{1,0:T(8,128)(2,1)S(1)}) custom-call(s32[5]{0:T(128)S(1)} %stack.23.pos_ref, bf16[64,1152]{1,0:T(8,128)(2,1)S(1)} %reshape.16.refs_0_.adapt_ref, bf16[64,1152]{1,0:T(8,128)(2,1)S(1)} %collective-permute-done.3.refs_1_, bf16[192,640]{1,0:T(8,128)(2,1)S(1)} %get-tuple-element.44.refs_2_, ...), custom_call_target="tpu_custom_call" | custom-call | tf_op jit(solution)/shard_map/pallas_call | solution.py:63
  71.1 1.6 %collective-permute-start.14 = (bf16[768,128]{1,0:T(8,128)(2,1)S(1)}, bf16[768,128]{1,0:T(8,128)(2,1)S(1)}, u32[]{:S(2)}, u32[]{:S(2)}) collective-permute-start(bf16[768,128]{1,0:T(8,128)(2,1)S(1)} %get-tuple-element.49), channel_id=1, source_target_pairs={{0,2},{2,0},{4,6},{6,4},{8,10},{10,8},{12,14},{14,12},{16,18},{18,... | collective-permute-start | bytes 589832 | tf_op jit(solution)/shard_map/ppermute | solution.py:489
  72.7 2.3 %shard_map.135 = (f32[768,128]{1,0:T(8,128)S(1)}, f32[1,768]{1,0:T(1,128)S(1)}, f32[384,64]{1,0:T(8,128)S(1)}, f32[384,64]{1,0:T(8,128)S(1)}) custom-call(s32[5]{0:T(128)S(1)} %stack.23.pos_ref, bf16[768,128]{1,0:T(8,128)(2,1)S(1)} %get-tuple-element.42.q_ref.refs_4_, bf16[2,768,128]{2,1,0:T(8,128)(2,1)S(1)} %get-tuple-element.43.kv_ref, ...), custom_call_target="tpu_custom_call" | custom-call | tf_op jit(solution)/shard_map/pallas_call | solution.py:63
  75.0 0.6 collective-permute-start.22
  75.6 1.2 %shard_map.140.lora_ref = f32[768,64]{1,0:T(8,128)S(1)} custom-call(s32[5]{0:T(128)S(1)} %stack.23.pos_ref, bf16[64,1152]{1,0:T(8,128)(2,1)S(1)} %reshape.16.refs_0_.adapt_ref, bf16[64,1152]{1,0:T(8,128)(2,1)S(1)} %collective-permute-done.3.refs_1_, bf16[192,640]{1,0:T(8,128)(2,1)S(1)} %get-tuple-element.44.refs_2_, ...), custom_call_target="tpu_custom_call" | custom-call | tf_op jit(solution)/shard_map/pallas_call | solution.py:63
  76.9 0.6 shard_map.141.refs_0_
  77.5 0.6 collective-permute-start.23
  78.1 2.6 %collective-permute-start.24 = (bf16[384,128]{1,0:T(8,128)(2,1)S(1)}, bf16[384,128]{1,0:T(8,128)(2,1)S(1)}, u32[]{:S(2)}, u32[]{:S(2)}) collective-permute-start(bf16[384,128]{1,0:T(8,128)(2,1)S(1)} %shard_map.141.refs_0_), channel_id=1, source_target_pairs={{0,4},{2,6},{4,0},{6,2},{8,12},{10,14},{12,8},{14,10},{16,20},{18,... | collective-permute-start | bytes 294920 | tf_op jit(solution)/shard_map/ppermute | solution.py:489
  80.7 0.9 collective-permute-start.25
  81.6 1.0 shard_map.136
  82.6 1.3 %collective-permute-start.18 = (bf16[2,768,128]{2,1,0:T(8,128)(2,1)S(1)}, bf16[2,768,128]{2,1,0:T(8,128)(2,1)S(1)}, u32[]{:S(2)}, u32[]{:S(2)}) collective-permute-start(bf16[2,768,128]{2,1,0:T(8,128)(2,1)S(1)} %get-tuple-element.59), channel_id=1, source_target_pairs={{8,0},{10,2},{13,5},{15,7},{17,9},{19,11},{20,12},{22,14},{24,16},... | collective-permute-start | bytes 1179656 | tf_op jit(solution)/shard_map/ppermute | solution.py:512
  84.0 1.1 collective-permute-done.24.refs_2_
  85.0 1.7 %collective-permute-done.25.refs_3_ = bf16[384,128]{1,0:T(8,128)(2,1)S(1)} collective-permute-done((bf16[384,128]{1,0:T(8,128)(2,1)S(1)}, bf16[384,128]{1,0:T(8,128)(2,1)S(1)}, u32[]{:S(2)}, u32[]{:S(2)}) %collective-permute-start.25) | collective-permute-done | bytes 98336 | tf_op jit(solution)/shard_map/ppermute | solution.py:489
  86.7 0.1 shard_map.142.refs_0_
  86.7 0.1 collective-permute-start.26
  86.8 1.3 %collective-permute-done.26.refs_1_ = bf16[384,128]{1,0:T(8,128)(2,1)S(1)} collective-permute-done((bf16[384,128]{1,0:T(8,128)(2,1)S(1)}, bf16[384,128]{1,0:T(8,128)(2,1)S(1)}, u32[]{:S(2)}, u32[]{:S(2)}) %collective-permute-start.26) | collective-permute-done | bytes 98336 | tf_op jit(solution)/shard_map/ppermute | solution.py:499
  88.1 1.7 %shard_map.143 = f32[16,4,768]{2,1,0:T(4,128)} custom-call(s32[5]{0:T(128)S(1)} %stack.23.pos_ref, f32[768,128]{1,0:T(8,128)S(1)} %get-tuple-element.52.refs_6_.o_ref, bf16[384,128]{1,0:T(8,128)(2,1)S(1)} %shard_map.142.refs_0_, bf16[384,128]{1,0:T(8,128)(2,1)S(1)} %collective-permute-done.26.refs_1_, bf16[192,640]{1,0:T(8,128)(2,1)S(1)} %get-tuple-element.44.refs_2_, ...), custom_call_target="tpu_custom_call" | custom-call | tf_op jit(solution)/shard_map/pallas_call | solution.py:63
  89.8 3.5 %all-to-all-start.1 = ((f32[16,4,768]{2,1,0:T(4,128)}), f32[16,4,768]{2,1,0:T(4,128)S(1)}, u32[]{:S(2)}, u32[]{:S(2)}) async-start(f32[16,4,768]{2,1,0:T(4,128)} %shard_map.143), calls=%async_computation.1 | async-start | bytes 393216 | tf_op jit(solution)/shard_map/all_to_all | solution.py:634
  93.3 1.8 %shard_map.137 = (bf16[768,128]{1,0:T(8,128)(2,1)S(1)}, f32[2,768,128]{2,1,0:T(8,128)S(1)}) custom-call(s32[5]{0:T(128)S(1)} %stack.23.pos_ref, bf16[768,128]{1,0:T(8,128)(2,1)S(1)} %get-tuple-element.42.q_ref.refs_4_, bf16[2,768,128]{2,1,0:T(8,128)(2,1)S(1)} %get-tuple-element.43.kv_ref, bf16[768,128]{1,0:T(8,128)(2,1)S(1)} %get-tuple-element.54.do_ref, ...), custom_call_target="tpu_custom_call" | custom-call | tf_op jit(solution)/shard_map/pallas_call | solution.py:63
  95.2 0.6 shard_map.138
  95.8 1.9 %collective-permute-start.19 = (bf16[3,192,128]{2,1,0:T(8,128)(2,1)S(1)}, bf16[3,192,128]{2,1,0:T(8,128)(2,1)S(1)}, u32[]{:S(2)}, u32[]{:S(2)}) collective-permute-start(bf16[3,192,128]{2,1,0:T(8,128)(2,1)S(1)} %get-tuple-element.61), channel_id=1, source_target_pairs={{0,2},{2,0},{4,6},{6,4},{8,10},{10,8},{12,14},{14,12},{16,18},{18,... | collective-permute-start | bytes 442376 | tf_op jit(solution)/shard_map/ppermute | solution.py:489
  97.7 1.5 %collective-permute-start.20 = (bf16[3,192,128]{2,1,0:T(8,128)(2,1)S(1)}, bf16[3,192,128]{2,1,0:T(8,128)(2,1)S(1)}, u32[]{:S(2)}, u32[]{:S(2)}) collective-permute-start(bf16[3,192,128]{2,1,0:T(8,128)(2,1)S(1)} %get-tuple-element.62), channel_id=1, source_target_pairs={{0,4},{2,6},{4,0},{6,2},{8,12},{10,14},{12,8},{14,10},{16,20},{18,... | collective-permute-start | bytes 442376 | tf_op jit(solution)/shard_map/ppermute | solution.py:489
  99.2 0.2 collective-permute-start.21
  99.4 2.8 %all-to-all-done.1.in_ref = f32[16,4,768]{2,1,0:T(4,128)S(1)} async-done(((f32[16,4,768]{2,1,0:T(4,128)}), f32[16,4,768]{2,1,0:T(4,128)S(1)}, u32[]{:S(2)}, u32[]{:S(2)}) %all-to-all-start.1) | async-done | bytes 196640 | tf_op jit(solution)/shard_map/all_to_all | solution.py:634
  102.2 1.2 %shard_map.144 = (f32[4,2560]{1,0:T(4,128)}, f32[4,512]{1,0:T(4,128)}) custom-call(s32[5]{0:T(128)S(1)} %stack.23.pos_ref, f32[16,4,768]{2,1,0:T(4,128)S(1)} %all-to-all-done.1.in_ref), custom_call_target="tpu_custom_call" | custom-call | tf_op jit(solution)/shard_map/pallas_call | solution.py:63
  103.4 2.1 %collective-permute-done.20.refs_2_ = bf16[3,192,128]{2,1,0:T(8,128)(2,1)S(1)} collective-permute-done((bf16[3,192,128]{2,1,0:T(8,128)(2,1)S(1)}, bf16[3,192,128]{2,1,0:T(8,128)(2,1)S(1)}, u32[]{:S(2)}, u32[]{:S(2)}) %collective-permute-start.20) | collective-permute-done | bytes 147488 | tf_op jit(solution)/shard_map/ppermute | solution.py:489
  105.6 1.3 %collective-permute-done.21.refs_3_ = bf16[3,192,128]{2,1,0:T(8,128)(2,1)S(1)} collective-permute-done((bf16[3,192,128]{2,1,0:T(8,128)(2,1)S(1)}, bf16[3,192,128]{2,1,0:T(8,128)(2,1)S(1)}, u32[]{:S(2)}, u32[]{:S(2)}) %collective-permute-start.21) | collective-permute-done | bytes 147488 | tf_op jit(solution)/shard_map/ppermute | solution.py:489
  106.9 1.4 %shard_map.139 = (bf16[192,512]{1,0:T(8,128)(2,1)}, bf16[192,512]{1,0:T(8,128)(2,1)}, bf16[192,512]{1,0:T(8,128)(2,1)}) custom-call(s32[5]{0:T(128)S(1)} %stack.23.pos_ref, bf16[3,192,128]{2,1,0:T(8,128)(2,1)S(1)} %get-tuple-element.60.refs_0_, bf16[3,192,128]{2,1,0:T(8,128)(2,1)S(1)} %collective-permute-done.19.refs_1_, ...), custom_call_target="tpu_custom_call" | custom-call | tf_op jit(solution)/shard_map/pallas_call | solution.py:63
  (23 shorter events, 0.1 us)
Async XLA Ops:
  0.8 1.2 %copy-start.2 = (bf16[192,2560]{1,0:T(8,128)(2,1)S(1)}, bf16[192,2560]{1,0:T(8,128)(2,1)}, u32[]{:S(2)}) copy-start(bf16[192,2560]{1,0:T(8,128)(2,1)} %g_ref.1) | copy-start | bytes 2949124
  3.0 24.4 %collective-permute-start.9 = (bf16[192,640]{1,0:T(8,128)(2,1)S(1)}, bf16[192,640]{1,0:T(8,128)(2,1)S(1)}, u32[]{:S(2)}, u32[]{:S(2)}) collective-permute-start(bf16[192,640]{1,0:T(8,128)(2,1)S(1)} %get-tuple-element.47), channel_id=1, source_target_pairs={{0,6},{2,4},{4,2},{6,0},{8,14},{10,12},{12,10},{14,8},{16,22},{18,... | collective-permute-start | bytes 737288 | tf_op jit(solution)/shard_map/ppermute | solution.py:489
  7.0 20.5 %collective-permute-start.5 = (bf16[192,640]{1,0:T(8,128)(2,1)S(1)}, bf16[192,640]{1,0:T(8,128)(2,1)S(1)}, u32[]{:S(2)}, u32[]{:S(2)}) collective-permute-start(bf16[192,640]{1,0:T(8,128)(2,1)S(1)} %get-tuple-element.45), channel_id=1, source_target_pairs={{0,2},{2,0},{4,6},{6,4},{8,10},{10,8},{12,14},{14,12},{16,18},{18,... | collective-permute-start | bytes 737288 | tf_op jit(solution)/shard_map/ppermute | solution.py:489
  9.3 13.4 %collective-permute-start = (bf16[3,192,128]{2,1,0:T(8,128)(2,1)S(1)}, bf16[3,192,128]{2,1,0:T(8,128)(2,1)S(1)}, u32[]{:S(2)}, u32[]{:S(2)}) collective-permute-start(bf16[3,192,128]{2,1,0:T(8,128)(2,1)S(1)} %get-tuple-element.39), channel_id=1, source_target_pairs={{0,2},{2,0},{4,6},{6,4},{8,10},{10,8},{12,14},{14,12},{16,18},{18,... | collective-permute-start | bytes 442376 | tf_op jit(solution)/shard_map/ppermute | solution.py:489
  10.9 13.5 %collective-permute-start.1 = (bf16[3,192,128]{2,1,0:T(8,128)(2,1)S(1)}, bf16[3,192,128]{2,1,0:T(8,128)(2,1)S(1)}, u32[]{:S(2)}, u32[]{:S(2)}) collective-permute-start(bf16[3,192,128]{2,1,0:T(8,128)(2,1)S(1)} %get-tuple-element.40), channel_id=1, source_target_pairs={{0,4},{2,6},{4,0},{6,2},{8,12},{10,14},{12,8},{14,10},{16,20},{18,... | collective-permute-start | bytes 442376 | tf_op jit(solution)/shard_map/ppermute | solution.py:489
  11.4 15.5 %collective-permute-start.2 = (bf16[3,192,128]{2,1,0:T(8,128)(2,1)S(1)}, bf16[3,192,128]{2,1,0:T(8,128)(2,1)S(1)}, u32[]{:S(2)}, u32[]{:S(2)}) collective-permute-start(bf16[3,192,128]{2,1,0:T(8,128)(2,1)S(1)} %get-tuple-element.41), channel_id=1, source_target_pairs={{0,6},{2,4},{4,2},{6,0},{8,14},{10,12},{12,10},{14,8},{16,22},{18,... | collective-permute-start | bytes 442376 | tf_op jit(solution)/shard_map/ppermute | solution.py:489
  12.9 17.0 %copy-start.3 = (bf16[4,2560]{1,0:T(4,128)(2,1)S(1)}, bf16[4,2560]{1,0:T(4,128)(2,1)}, u32[]{:S(2)}) copy-start(bf16[4,2560]{1,0:T(4,128)(2,1)} %up_ref.1) | copy-start | bytes 61444
  12.9 17.0 %copy-start.4 = (bf16[4,512]{1,0:T(4,128)(2,1)S(1)}, bf16[4,512]{1,0:T(4,128)(2,1)}, u32[]{:S(2)}) copy-start(bf16[4,512]{1,0:T(4,128)(2,1)} %down_ref.1) | copy-start | bytes 12292
  22.7 16.5 %collective-permute-start.11 = (bf16[320,512]{1,0:T(8,128)(2,1)S(1)}, bf16[320,512]{1,0:T(8,128)(2,1)S(1)}, u32[]{:S(2)}, u32[]{:S(2)}) collective-permute-start(bf16[320,512]{1,0:T(8,128)(2,1)S(1)} %shard_map.132.refs_10_), channel_id=1, source_target_pairs={{0,8},{2,10},{4,12},{6,14},{8,16},{10,18},{12,20},{14,22},{16,24},... | collective-permute-start | bytes 983048 | tf_op jit(solution)/shard_map/ppermute | solution.py:494
  24.3 24.3 %collective-permute-start.12 = (bf16[320,512]{1,0:T(8,128)(2,1)S(1)}, bf16[320,512]{1,0:T(8,128)(2,1)}, u32[]{:S(2)}, u32[]{:S(2)}) collective-permute-start(bf16[320,512]{1,0:T(8,128)(2,1)S(1)} %shard_map.132.refs_10_), channel_id=1, source_target_pairs={{0,16},{2,18},{4,20},{6,22},{8,24},{10,26},{12,28},{14,30},{16,0},... | collective-permute-start | bytes 983048 | tf_op jit(solution)/shard_map/ppermute | solution.py:494
  26.9 8.5 %collective-permute-start.7 = (bf16[192,640]{1,0:T(8,128)(2,1)S(1)}, bf16[192,640]{1,0:T(8,128)(2,1)S(1)}, u32[]{:S(2)}, u32[]{:S(2)}) collective-permute-start(bf16[192,640]{1,0:T(8,128)(2,1)S(1)} %get-tuple-element.46), channel_id=1, source_target_pairs={{0,4},{2,6},{4,0},{6,2},{8,12},{10,14},{12,8},{14,10},{16,20},{18,... | collective-permute-start | bytes 737288 | tf_op jit(solution)/shard_map/ppermute | solution.py:489
  27.4 11.7 %collective-permute-start.4 = (bf16[192,640]{1,0:T(8,128)(2,1)S(1)}, bf16[192,640]{1,0:T(8,128)(2,1)S(1)}, u32[]{:S(2)}, u32[]{:S(2)}) collective-permute-start(bf16[192,640]{1,0:T(8,128)(2,1)S(1)} %get-tuple-element.44.refs_2_), channel_id=1, source_target_pairs={{0,1},{1,0},{2,3},{3,2},{4,5},{5,4},{6,7},{7,6},{8,9},{9,8},{10,11... | collective-permute-start | bytes 737288 | tf_op jit(solution)/shard_map/ppermute | solution.py:499
  27.4 34.6 %collective-permute-start.13 = (bf16[320,512]{1,0:T(8,128)(2,1)S(1)}, bf16[320,512]{1,0:T(8,128)(2,1)}, u32[]{:S(2)}, u32[]{:S(2)}) collective-permute-start(bf16[320,512]{1,0:T(8,128)(2,1)S(1)} %shard_map.132.refs_10_), channel_id=1, source_target_pairs={{0,24},{2,26},{4,28},{6,30},{8,0},{10,2},{12,4},{14,6},{16,8},{18,... | collective-permute-start | bytes 983048 | tf_op jit(solution)/shard_map/ppermute | solution.py:494
  30.6 30.4 %all-to-all-start = ((bf16[16,4,1152]{2,1,0:T(4,128)(2,1)}), bf16[16,4,1152]{2,1,0:T(4,128)(2,1)}, u32[]{:S(2)}, u32[]{:S(2)}) async-start(bf16[16,4,1152]{2,1,0:T(4,128)(2,1)} %shard_map.130), calls=%async_computation | async-start | bytes 294912 | tf_op jit(solution)/shard_map/all_to_all | solution.py:568
  35.4 37.3 %collective-permute-start.17 = (bf16[2,768,128]{2,1,0:T(8,128)(2,1)S(1)}, bf16[2,768,128]{2,1,0:T(8,128)(2,1)S(1)}, u32[]{:S(2)}, u32[]{:S(2)}) collective-permute-start(bf16[2,768,128]{2,1,0:T(8,128)(2,1)S(1)} %get-tuple-element.43.kv_ref), channel_id=1, source_target_pairs={{0,8},{2,10},{5,13},{7,15},{9,17},{11,19},{12,20},{14,22},{16,24},... | collective-permute-start | bytes 1179656 | tf_op jit(solution)/shard_map/ppermute | solution.py:509
  39.1 24.3 %collective-permute-start.10 = (bf16[192,640]{1,0:T(8,128)(2,1)S(1)}, bf16[192,640]{1,0:T(8,128)(2,1)S(1)}, u32[]{:S(2)}, u32[]{:S(2)}) collective-permute-start(bf16[192,640]{1,0:T(8,128)(2,1)S(1)} %collective-permute-done.9.refs_8_.refs_5_), channel_id=1, source_target_pairs={{0,1},{1,0},{2,3},{3,2},{4,5},{5,4},{6,7},{7,6},{8,9},{9,8},{10,11... | collective-permute-start | bytes 737288 | tf_op jit(solution)/shard_map/ppermute | solution.py:499
  39.2 0.7 copy-start
  40.0 23.5 %collective-permute-start.6 = (bf16[192,640]{1,0:T(8,128)(2,1)S(1)}, bf16[192,640]{1,0:T(8,128)(2,1)S(1)}, u32[]{:S(2)}, u32[]{:S(2)}) collective-permute-start(bf16[192,640]{1,0:T(8,128)(2,1)S(1)} %collective-permute-done.5.refs_4_.refs_3_), channel_id=1, source_target_pairs={{0,1},{1,0},{2,3},{3,2},{4,5},{5,4},{6,7},{7,6},{8,9},{9,8},{10,11... | collective-permute-start | bytes 737288 | tf_op jit(solution)/shard_map/ppermute | solution.py:499
  48.7 14.8 %collective-permute-start.8 = (bf16[192,640]{1,0:T(8,128)(2,1)S(1)}, bf16[192,640]{1,0:T(8,128)(2,1)S(1)}, u32[]{:S(2)}, u32[]{:S(2)}) collective-permute-start(bf16[192,640]{1,0:T(8,128)(2,1)S(1)} %collective-permute-done.7.refs_6_.refs_4_), channel_id=1, source_target_pairs={{0,1},{1,0},{2,3},{3,2},{4,5},{5,4},{6,7},{7,6},{8,9},{9,8},{10,11... | collective-permute-start | bytes 737288 | tf_op jit(solution)/shard_map/ppermute | solution.py:499
  62.0 1.4 %collective-permute-start.3 = (bf16[64,1152]{1,0:T(8,128)(2,1)S(1)}, bf16[64,1152]{1,0:T(8,128)(2,1)S(1)}, u32[]{:S(2)}, u32[]{:S(2)}) collective-permute-start(bf16[64,1152]{1,0:T(8,128)(2,1)S(1)} %reshape.16.refs_0_.adapt_ref), channel_id=1, source_target_pairs={{0,1},{1,0},{2,3},{3,2},{4,5},{5,4},{6,7},{7,6},{8,9},{9,8},{10,11... | collective-permute-start | bytes 442376 | tf_op jit(solution)/shard_map/ppermute | solution.py:499
  63.5 1.0 copy-start.1
  66.8 13.9 %collective-permute-start.15 = (bf16[768,128]{1,0:T(8,128)(2,1)S(1)}, bf16[768,128]{1,0:T(8,128)(2,1)S(1)}, u32[]{:S(2)}, u32[]{:S(2)}) collective-permute-start(bf16[768,128]{1,0:T(8,128)(2,1)S(1)} %get-tuple-element.50), channel_id=1, source_target_pairs={{0,4},{2,6},{4,0},{6,2},{8,12},{10,14},{12,8},{14,10},{16,20},{18,... | collective-permute-start | bytes 589832 | tf_op jit(solution)/shard_map/ppermute | solution.py:489
  68.5 13.1 %collective-permute-start.16 = (bf16[768,128]{1,0:T(8,128)(2,1)S(1)}, bf16[768,128]{1,0:T(8,128)(2,1)S(1)}, u32[]{:S(2)}, u32[]{:S(2)}) collective-permute-start(bf16[768,128]{1,0:T(8,128)(2,1)S(1)} %get-tuple-element.51), channel_id=1, source_target_pairs={{0,6},{2,4},{4,2},{6,0},{8,14},{10,12},{12,10},{14,8},{16,22},{18,... | collective-permute-start | bytes 589832 | tf_op jit(solution)/shard_map/ppermute | solution.py:489
  71.1 10.5 %collective-permute-start.14 = (bf16[768,128]{1,0:T(8,128)(2,1)S(1)}, bf16[768,128]{1,0:T(8,128)(2,1)S(1)}, u32[]{:S(2)}, u32[]{:S(2)}) collective-permute-start(bf16[768,128]{1,0:T(8,128)(2,1)S(1)} %get-tuple-element.49), channel_id=1, source_target_pairs={{0,2},{2,0},{4,6},{6,4},{8,10},{10,8},{12,14},{14,12},{16,18},{18,... | collective-permute-start | bytes 589832 | tf_op jit(solution)/shard_map/ppermute | solution.py:489
  75.0 1.9 %collective-permute-start.22 = (f32[384,64]{1,0:T(8,128)S(1)}, f32[384,64]{1,0:T(8,128)S(1)}, u32[]{:S(2)}, u32[]{:S(2)}) collective-permute-start(f32[384,64]{1,0:T(8,128)S(1)} %get-tuple-element.68), channel_id=1, source_target_pairs={{0,1},{1,0},{2,3},{3,2},{4,5},{5,4},{6,7},{7,6},{8,9},{9,8},{10,11... | collective-permute-start | bytes 294920 | tf_op jit(solution)/shard_map/ppermute | solution.py:499
  77.5 6.4 %collective-permute-start.23 = (bf16[384,128]{1,0:T(8,128)(2,1)S(1)}, bf16[384,128]{1,0:T(8,128)(2,1)S(1)}, u32[]{:S(2)}, u32[]{:S(2)}) collective-permute-start(bf16[384,128]{1,0:T(8,128)(2,1)S(1)} %shard_map.141.refs_0_), channel_id=1, source_target_pairs={{0,2},{2,0},{4,6},{6,4},{8,10},{10,8},{12,14},{14,12},{16,18},{18,... | collective-permute-start | bytes 294920 | tf_op jit(solution)/shard_map/ppermute | solution.py:489
  78.1 6.9 %collective-permute-start.24 = (bf16[384,128]{1,0:T(8,128)(2,1)S(1)}, bf16[384,128]{1,0:T(8,128)(2,1)S(1)}, u32[]{:S(2)}, u32[]{:S(2)}) collective-permute-start(bf16[384,128]{1,0:T(8,128)(2,1)S(1)} %shard_map.141.refs_0_), channel_id=1, source_target_pairs={{0,4},{2,6},{4,0},{6,2},{8,12},{10,14},{12,8},{14,10},{16,20},{18,... | collective-permute-start | bytes 294920 | tf_op jit(solution)/shard_map/ppermute | solution.py:489
  80.7 6.0 %collective-permute-start.25 = (bf16[384,128]{1,0:T(8,128)(2,1)S(1)}, bf16[384,128]{1,0:T(8,128)(2,1)S(1)}, u32[]{:S(2)}, u32[]{:S(2)}) collective-permute-start(bf16[384,128]{1,0:T(8,128)(2,1)S(1)} %shard_map.141.refs_0_), channel_id=1, source_target_pairs={{0,6},{2,4},{4,2},{6,0},{8,14},{10,12},{12,10},{14,8},{16,22},{18,... | collective-permute-start | bytes 294920 | tf_op jit(solution)/shard_map/ppermute | solution.py:489
  82.6 12.5 %collective-permute-start.18 = (bf16[2,768,128]{2,1,0:T(8,128)(2,1)S(1)}, bf16[2,768,128]{2,1,0:T(8,128)(2,1)S(1)}, u32[]{:S(2)}, u32[]{:S(2)}) collective-permute-start(bf16[2,768,128]{2,1,0:T(8,128)(2,1)S(1)} %get-tuple-element.59), channel_id=1, source_target_pairs={{8,0},{10,2},{13,5},{15,7},{17,9},{19,11},{20,12},{22,14},{24,16},... | collective-permute-start | bytes 1179656 | tf_op jit(solution)/shard_map/ppermute | solution.py:512
  86.7 1.4 %collective-permute-start.26 = (bf16[384,128]{1,0:T(8,128)(2,1)S(1)}, bf16[384,128]{1,0:T(8,128)(2,1)S(1)}, u32[]{:S(2)}, u32[]{:S(2)}) collective-permute-start(bf16[384,128]{1,0:T(8,128)(2,1)S(1)} %shard_map.142.refs_0_), channel_id=1, source_target_pairs={{0,1},{1,0},{2,3},{3,2},{4,5},{5,4},{6,7},{7,6},{8,9},{9,8},{10,11... | collective-permute-start | bytes 294920 | tf_op jit(solution)/shard_map/ppermute | solution.py:499
  89.8 12.4 %all-to-all-start.1 = ((f32[16,4,768]{2,1,0:T(4,128)}), f32[16,4,768]{2,1,0:T(4,128)S(1)}, u32[]{:S(2)}, u32[]{:S(2)}) async-start(f32[16,4,768]{2,1,0:T(4,128)} %shard_map.143), calls=%async_computation.1 | async-start | bytes 393216 | tf_op jit(solution)/shard_map/all_to_all | solution.py:634
  95.8 7.6 %collective-permute-start.19 = (bf16[3,192,128]{2,1,0:T(8,128)(2,1)S(1)}, bf16[3,192,128]{2,1,0:T(8,128)(2,1)S(1)}, u32[]{:S(2)}, u32[]{:S(2)}) collective-permute-start(bf16[3,192,128]{2,1,0:T(8,128)(2,1)S(1)} %get-tuple-element.61), channel_id=1, source_target_pairs={{0,2},{2,0},{4,6},{6,4},{8,10},{10,8},{12,14},{14,12},{16,18},{18,... | collective-permute-start | bytes 442376 | tf_op jit(solution)/shard_map/ppermute | solution.py:489
  97.7 7.9 %collective-permute-start.20 = (bf16[3,192,128]{2,1,0:T(8,128)(2,1)S(1)}, bf16[3,192,128]{2,1,0:T(8,128)(2,1)S(1)}, u32[]{:S(2)}, u32[]{:S(2)}) collective-permute-start(bf16[3,192,128]{2,1,0:T(8,128)(2,1)S(1)} %get-tuple-element.62), channel_id=1, source_target_pairs={{0,4},{2,6},{4,0},{6,2},{8,12},{10,14},{12,8},{14,10},{16,20},{18,... | collective-permute-start | bytes 442376 | tf_op jit(solution)/shard_map/ppermute | solution.py:489
  99.2 7.7 %collective-permute-start.21 = (bf16[3,192,128]{2,1,0:T(8,128)(2,1)S(1)}, bf16[3,192,128]{2,1,0:T(8,128)(2,1)S(1)}, u32[]{:S(2)}, u32[]{:S(2)}) collective-permute-start(bf16[3,192,128]{2,1,0:T(8,128)(2,1)S(1)} %get-tuple-element.63), channel_id=1, source_target_pairs={{0,6},{2,4},{4,2},{6,0},{8,14},{10,12},{12,10},{14,8},{16,22},{18,... | collective-permute-start | bytes 442376 | tf_op jit(solution)/shard_map/ppermute | solution.py:489

commit v3 on v2

--- a/solution.py
+++ b/solution.py
@@ -119,37 +119,59 @@
         out_ref[:, b * LANES : (b + 1) * LANES] = (value * scale).astype(BF)
 
 
-def adapter_chunks_body(half, strips, wide, up_ref, down_ref, out_ref):
-    count, rank_rows = out_ref.shape[:2]
-    step = up_ref.shape[1] // strips
+def raw_body(n_ups, *refs):
+    ins, out_refs, sem = refs[: n_ups + 1], refs[n_ups + 1 : -1], refs[-1]
+    out_ref = out_refs[0]
+    at = 0
+    copies = []
+    for i, ref in enumerate(ins):
+        width = ref.shape[1]
+        copies.append(pltpu.make_async_copy(ref, out_ref.at[:, at : at + width], sem.at[i]))
+        at += width
+    for copy in copies:
+        copy.start()
+    for copy in copies:
+        copy.wait()
+
+
+def chunks_body(half, fsdp, strips, wide, pos_ref, *refs):
+    ins, out_refs = refs[:-half], refs[-half:]
+    mine = pos_ref[0]
+    rank_rows, cols = ins[0].shape
+    grad_cols = (cols - half * LANES) // fsdp
+    step = grad_cols // strips
     width = step // half
     short = wide - strips * width
-    for j in range(half):
-        pieces = [
-            up_ref[:, i * step + j * width : i * step + (j + 1) * width] for i in range(strips)
-        ]
-        if short:
-            pieces.append(jnp.zeros((rank_rows, short), BF))
-        chunk = jnp.concatenate(pieces, axis=1)
-        for p in range(count // half):
-            out_ref[p * half + j, :, :wide] = chunk
-            out_ref[p * half + j, :, wide:] = down_ref[...]
-
-
-def adapter_grads_body(half, strips, slot, wide, pos_ref, in_ref, up_ref, down_ref):
-    core = pos_ref[2]
-    planes = in_ref.shape[0] // half
-    width = slot // strips
-    step = half * width
-    for j in range(half):
-        total = in_ref[j]
-        for p in range(1, planes):
-            total = total + in_ref[p * half + j]
-        for i in range(strips):
-            to = i * step + j * width
-            up_ref[:, to : to + width] = total[:, i * width : (i + 1) * width]
-        head = j ^ ((core & 1) * (half // 2))
-        down_ref[:, pl.ds(pl.multiple_of(head * LANES, LANES), LANES)] = total[:, wide:]
+    for s in range(half):
+        for jv in range(half):
+
+            @pl.when((mine ^ s) == jv)
+            def _(s=s, jv=jv):
+                for p, ref in enumerate(ins):
+                    for f in range(fsdp):
+                        base = f * grad_cols + jv * width
+                        pieces = [
+                            ref[:, base + i * step : base + i * step + width]
+                            for i in range(strips)
+                        ]
+                        if short:
+                            pieces.append(jnp.zeros((rank_rows, short), BF))
+                        out_refs[s][p, :, f * wide : (f + 1) * wide] = jnp.concatenate(
+                            pieces, axis=1
+                        )
+                    out_refs[s][p, :, fsdp * wide :] = ref[:, fsdp * grad_cols :]
+
+
+def relay_body(pos_ref, above_ref, below_ref, inner_ref, outer_ref):
+    @pl.when(pos_ref[1] == 1)
+    def _():
+        inner_ref[...] = above_ref[...]
+        outer_ref[...] = below_ref[...]
+
+    @pl.when(pos_ref[1] != 1)
+    def _():
+        inner_ref[...] = below_ref[...]
+        outer_ref[...] = above_ref[...]
 
 
 def pack_grad_body(half, strips, pos_ref, g_ref, *out_refs):
@@ -195,14 +217,24 @@
         kv_out[1, at, :] = pieces[s][2]
 
 
-def lora_body(half, fsdp, pos_ref, *refs):
-    ups, grads, out_ref = refs[:fsdp], refs[fsdp:-1], refs[-1]
+def ranks_body(half, pos_ref, *refs):
+    pieces, (out_ref, scr) = refs[:half], refs[half:]
+    mine = pos_ref[0]
+    planes = scr.shape[1]
+    for s in range(half):
+        scr[mine ^ s] = pieces[s][...].astype(F32)
+    parts = [scr[j, p] for p in range(planes) for j in range(half)]
+    out_ref[...] = jnp.concatenate(parts, axis=0).astype(BF)
+
+
+def lora_body(half, fsdp, pos_ref, adapt_ref, *refs):
+    grads, out_ref = refs[:-1], refs[-1]
     mine = pos_ref[0]
     rows, wide = grads[0].shape
     for s in range(half):
         total = None
         for f in range(fsdp):
-            part = nt(grads[s * fsdp + f][...], ups[f][:, :wide])
+            part = nt(grads[s * fsdp + f][...], adapt_ref[:, f * wide : (f + 1) * wide])
             total = part if total is None else total + part
         at = pl.ds(pl.multiple_of((mine ^ s) * rows, rows), rows)
         out_ref[at, :] = adapter_scale * total
@@ -225,11 +257,11 @@
     refs[-1][...] = total.astype(BF)
 
 
-def project_body(half, planes, fsdp, slot, targets, pos_ref, *refs):
-    ups = refs[:fsdp]
-    grads = refs[fsdp : fsdp + half * fsdp]
-    weights = refs[fsdp + half * fsdp : fsdp + half * fsdp + planes]
-    outs = refs[fsdp + half * fsdp + planes : -2]
+def project_body(half, planes, fsdp, slot, targets, pos_ref, adapt_ref, *refs):
+    grads = refs[: half * fsdp]
+    weights = refs[half * fsdp : -2 - len(targets)]
+    n_weights = len(weights)
+    outs = refs[-2 - len(targets) : -2]
     w_scr, d_scr = refs[-2:]
     mine, plane, core, own = pos_ref[0], pos_ref[1], pos_ref[2], pos_ref[4]
     rows_each = weights[0].shape[0]
@@ -239,18 +271,29 @@
         w_scr[planes * rows_each :, :] = jnp.zeros((tail, w_scr.shape[1]), BF)
     for i, t in enumerate(targets):
         cols = pl.ds(pl.multiple_of((own ^ t) * LANES, LANES), LANES)
-        d_cols = pl.ds(pl.multiple_of(wide + (own ^ t) * LANES, LANES), LANES)
+        d_cols = pl.ds(pl.multiple_of(fsdp * wide + (own ^ t) * LANES, LANES), LANES)
         to = slice(i * LANES, (i + 1) * LANES)
-        d_scr[:, to] = ups[0][:, d_cols]
-        for s in range(planes):
-            src = lax.rem(plane + (planes - s), planes)
-            at = pl.ds(pl.multiple_of(src * rows_each, rows_each), rows_each)
-            w_scr[at, to] = weights[s][:, cols]
+        d_scr[:, to] = adapt_ref[:, d_cols]
+        if n_weights == planes:
+            sources = [lax.rem(plane + (planes - s), planes) for s in range(planes)]
+        else:
+            away = lax.rem(plane + 2, planes)
+            inside = (plane == 1) | (plane == 2)
+            sources = [plane, lax.rem(plane + planes - 1, planes), lax.rem(plane + 1, planes)]
+            sources += [jnp.where(inside, away, -1), jnp.where(inside, -1, away)]
+        for piece, src in zip(weights, sources):
+
+            @pl.when(src >= 0)
+            def _(piece=piece, src=src, to=to, cols=cols):
+                at = pl.ds(pl.multiple_of(src * rows_each, rows_each), rows_each)
+                w_scr[at, to] = piece[:, cols]
+
     for f in range(fsdp):
         src = lax.rem(core + (fsdp - f), fsdp)
         at = pl.ds(pl.multiple_of(src * slot, 16), slot)
+        up = adapt_ref[:, f * wide : (f + 1) * wide]
         low = lax.dot_general(
-            ups[f][:, :wide], d_scr[...], (((0,), (0,)), ((), ())), preferred_element_type=F32
+            up, d_scr[...], (((0,), (0,)), ((), ())), preferred_element_type=F32
         )
         w_scr[at, :] = (w_scr[at, :].astype(F32) + adapter_scale * low[:slot]).astype(BF)
     for s in range(half):
@@ -274,10 +317,18 @@
     return jnp.where(kpos <= qpos, scores, masked)
 
 
-def forward_body(fsdp, wide, pos_ref, q_ref, kv_ref, far_ref, adapt_ref, o_ref, lse_ref, *refs):
-    mid_refs, (vt_scr, oft_scr, mid_ref) = refs[:fsdp], refs[fsdp:]
-    core, later, own = pos_ref[2], pos_ref[3], pos_ref[4]
-    down = adapt_ref[:, pl.ds(pl.multiple_of(wide + own * LANES, LANES), LANES)]
+def middle_body(fsdp, wide, pos_ref, o_ref, adapt_ref, *refs):
+    core, own = pos_ref[2], pos_ref[4]
+    down = adapt_ref[:, pl.ds(pl.multiple_of(fsdp * wide + own * LANES, LANES), LANES)]
+    rows = o_ref.shape[0] // fsdp
+    for s in range(fsdp):
+        to = lax.rem(core + s, fsdp)
+        part = o_ref[pl.ds(pl.multiple_of(to * rows, rows), rows), :]
+        refs[s][...] = nt(part.astype(BF), down)
+
+
+def forward_body(pos_ref, q_ref, kv_ref, far_ref, o_ref, lse_ref, vt_scr, oft_scr):
+    later = pos_ref[3]
     tokens = q_ref.shape[0]
     block = min(QUERY_BLOCK, tokens)
     vt_scr[...] = kv_ref[1].T
@@ -287,7 +338,6 @@
         out = block_out.T
         o_ref[qs, :] = out
         lse_ref[:, qs] = norm
-        mid_ref[qs, :] = nt(out.astype(BF), down)
 
     def near(q0):
         return score_block(kv_ref[0, : q0 + block, :], q_ref[q0 : q0 + block, :], 0, q0)
@@ -318,11 +368,6 @@
                 oft_scr[...], far_prob.astype(BF)
             )
             finish(q0, out / total, top + jnp.log(total))
-
-    rows = tokens // fsdp
-    for s in range(fsdp):
-        to = lax.rem(core + s, fsdp)
-        mid_refs[s][...] = mid_ref[pl.ds(pl.multiple_of(to * rows, rows), rows), :]
 
 
 def grad_block(key, value, query, grad, norm, delta, k0, q0):
@@ -423,11 +468,28 @@
             outs[i][:, at] = pieces[s][i]
 
 
-def adapters_body(half, fsdp, pos_ref, o_ref, *refs):
-    both, grads, (out_ref, scr) = refs[:fsdp], refs[fsdp : fsdp + half], refs[fsdp + half :]
-    mine, core = pos_ref[0], pos_ref[2]
-    count, rank_rows = out_ref.shape[:2]
-    rank = count * rank_rows
+def adapter_grads_body(half, strips, slot, wide, pos_ref, in_ref, up_ref, down_ref):
+    core = pos_ref[2]
+    planes = in_ref.shape[0] // half
+    width = slot // strips
+    step = half * width
+    for j in range(half):
+        total = in_ref[j]
+        for p in range(1, planes):
+            total = total + in_ref[p * half + j]
+        for i in range(strips):
+            to = i * step + j * width
+            up_ref[:, to : to + width] = total[:, i * width : (i + 1) * width]
+        head = j ^ ((core & 1) * (half // 2))
+        down_ref[:, pl.ds(pl.multiple_of(head * LANES, LANES), LANES)] = total[:, wide:]
+
+
+def adapters_body(half, fsdp, planes, pos_ref, o_ref, *refs):
+    both, grads = refs[:fsdp], refs[fsdp : fsdp + half]
+    out_ref, scr = refs[fsdp + half :]
+    mine, plane, core = pos_ref[0], pos_ref[1], pos_ref[2]
+    rank_rows = out_ref.shape[1]
+    rank = planes * half * rank_rows
     rows, wide = grads[0].shape
     part_rows = both[0].shape[0]
     for s in range(fsdp):
@@ -440,9 +502,12 @@
         acc = part if acc is None else acc + part
     acc = adapter_scale * acc
     low = nn(scr[...].T[:rank, :], o_ref[...].astype(BF))
-    for c in range(count):
-        out_ref[c, :, :wide] = acc[c * rank_rows : (c + 1) * rank_rows, :]
-        out_ref[c, :, wide:] = low[c * rank_rows : (c + 1) * rank_rows, :]
+    for p in range(planes):
+        for j in range(half):
+            at = (p * half + j) * rank_rows
+            to = lax.rem(plane + (planes - p), planes) * half + j
+            out_ref[to, :, :wide] = acc[at : at + rank_rows, :]
+            out_ref[to, :, wide:] = low[at : at + rank_rows, :]
 
 
 def on_device(
@@ -493,6 +558,13 @@
             return x
         return lax.ppermute(x, "ctx", [(i, (i + s * half) % n_ctx) for i in range(n_ctx)])
 
+    def from_plane(x, *moves):
+        route = []
+        for group, step in zip(moves[::2], moves[1::2]):
+            for p in group:
+                route += [(p * half + j, (p + step) * half + j) for j in range(half)]
+        return lax.ppermute(x, "ctx", route)
+
     def across(x, s):
         if s == 0:
             return x
@@ -523,7 +595,16 @@
         table,
         in_hbm=True,
     )
-    weights = [along(weight, s) for s in range(planes)]
+    if planes == 4:
+        weights = [weight, along(weight, 1), along(weight, planes - 1)]
+    else:
+        weights = [along(weight, s) for s in range(planes)]
+    if planes == 4:
+        inner, outer = call(
+            relay_body, [sds(weight.shape, BF)] * 2, [], pos, *weights[1:], n_scalar=1
+        )
+        weights.append(from_plane(inner, (1,), 1, (2,), -1))
+        weights.append(from_plane(outer, (1,), -1, (2,), 1))
 
     grads = call(
         functools.partial(pack_grad_body, half, strips),
@@ -535,6 +616,35 @@
     )
     grads = [in_plane(x, s) for s, x in enumerate(grads)]
     swapped = [across(g, f) for g in grads for f in range(fsdp)]
+
+    raw_ups = [across(adapter_up_matrix, f) for f in range(fsdp)]
+    raw = call(
+        functools.partial(raw_body, fsdp),
+        [sds((rank_rows, fsdp * grad_cols + heads * HEAD_WIDTH), BF)],
+        [pltpu.SemaphoreType.DMA((fsdp + 1,))],
+        *raw_ups,
+        adapter_down_matrix,
+        in_hbm=True,
+    )[0]
+    raws = [along(raw, s) for s in range(planes)]
+    adapter_cols = fsdp * wide + heads * HEAD_WIDTH
+    chunks = call(
+        functools.partial(chunks_body, half, fsdp, strips, wide),
+        [sds((planes, rank_rows, adapter_cols), BF)] * half,
+        [],
+        pos,
+        *raws,
+        n_scalar=1,
+    )
+    chunks = [in_plane(x, s) for s, x in enumerate(chunks)]
+    adapters = call(
+        functools.partial(ranks_body, half),
+        sds((rank, adapter_cols), BF),
+        [pltpu.VMEM((half, planes, rank_rows, adapter_cols), F32)],
+        pos,
+        *chunks,
+        n_scalar=1,
+    )
 
     packed = call(
         functools.partial(pack_heads_body, half),
@@ -557,23 +667,12 @@
         n_scalar=1,
     )
     far = to_later(key_value)
-
-    chunks = call(
-        functools.partial(adapter_chunks_body, half, strips, wide),
-        sds((n_ctx, rank_rows, wide + heads * HEAD_WIDTH), BF),
-        [],
-        adapter_up_matrix,
-        adapter_down_matrix,
-    )
-    adapters = lax.all_to_all(chunks, "ctx", split_axis=0, concat_axis=0, tiled=True)
-    adapters = adapters.reshape(rank, -1)
-    ups = [across(adapters, f) for f in range(fsdp)]
     lora = call(
         functools.partial(lora_body, half, fsdp),
         sds((tokens, rank), F32),
         [],
         pos,
-        *ups,
+        adapters,
         *swapped,
         n_scalar=1,
     )
@@ -587,7 +686,7 @@
                 pltpu.VMEM((rank, LANES * len(targets)), BF),
             ],
             pos,
-            *ups,
+            adapters,
             *swapped,
             *weights,
             n_scalar=1,
@@ -600,19 +699,22 @@
     partial.update({s: in_plane(x, s) for s, x in rest.items()})
 
     part_rows = tokens // fsdp
-    out, norm, *mids = call(
-        functools.partial(forward_body, fsdp, wide),
-        [sds((tokens, LANES), F32), sds((1, tokens), F32)]
-        + [sds((part_rows, rank), F32)] * fsdp,
-        [
-            pltpu.VMEM((LANES, tokens), BF),
-            pltpu.VMEM((LANES, tokens), BF),
-            pltpu.VMEM((tokens, rank), F32),
-        ],
+    out, norm = call(
+        forward_body,
+        [sds((tokens, LANES), F32), sds((1, tokens), F32)],
+        [pltpu.VMEM((LANES, tokens), BF), pltpu.VMEM((LANES, tokens), BF)],
         pos,
         query,
         key_value,
         far,
+        n_scalar=1,
+    )
+    mids = call(
+        functools.partial(middle_body, fsdp, wide),
+        [sds((part_rows, rank), F32)] * fsdp,
+        [],
+        pos,
+        out,
         adapters,
         n_scalar=1,
     )
@@ -622,7 +724,7 @@
     both = call(total_body, sds((part_rows, 2 * rank), BF), [], *both)
     both = [across(both, f) for f in range(fsdp)]
     adapter_grads = call(
-        functools.partial(adapters_body, half, fsdp),
+        functools.partial(adapters_body, half, fsdp, planes),
         sds((n_ctx, rank_rows, wide + HEAD_WIDTH), F32),
         [pltpu.VMEM((tokens, 2 * rank), BF)],
         pos,

time: 109 us -> 104 us (0.954)
  waiting for transfers between devices: 40 us -> 32.1 us
  starting transfers between devices: 40.5 us -> 45.2 us
  local copies, waits for them, and re-layouts: 3.93 us -> 0.69 us
  Pallas kernels: 22.9 us -> 24.8 us
    all_to_all x1 -> x0, waiting for transfers between devices: 12.4 us -> none  [on_device(): lax.all_to_all(chunks, 'ctx', split_axis=0, concat_axis=0, tiled=True)]
    ppermute x3 -> x5, waiting for transfers between devices: 8.22 us -> 0.01 us  [along(): lax.ppermute(x, 'ctx', [(i, (i + s * half) % n_ctx) for i in range(n_ctx)])]
    ppermute x0 -> x2, waiting for transfers between devices: none -> 6.6 us  [from_plane(): return lax.ppermute(x, 'ctx', route)]
    ppermute x15 -> x18, waiting for transfers between devices: 13.9 us -> 19.4 us  [in_plane(): return lax.ppermute(x, 'ctx', [(i, i ^ s) for i in range(n_ctx)])]
    all_to_all x1 -> x0, starting transfers between devices: 4.16 us -> none  [on_device(): lax.all_to_all(chunks, 'ctx', split_axis=0, concat_axis=0, tiled=True)]
    ppermute x3 -> x5, starting transfers between devices: 6.64 us -> 10.8 us  [along(): lax.ppermute(x, 'ctx', [(i, (i + s * half) % n_ctx) for i in range(n_ctx)])]
    ppermute x15 -> x18, starting transfers between devices: 19.9 us -> 22.2 us  [in_plane(): return lax.ppermute(x, 'ctx', [(i, i ^ s) for i in range(n_ctx)])]
    unnamed x10 -> x4, local copies, waits for them, and re-layouts: 2.9 us -> 0.61 us
  transfers between devices with their start and end apart: 29 -> 35, of which waited for: 10 -> 16; matrix products, arithmetic and copies ran while one was open for 1% -> 0% of each run, Pallas kernels for 19% -> 22%
where the time goes in v3:
time: 104 us
  starting transfers between devices  45.2 us (43%)
  waiting for transfers between devices  32.1 us (31%)
  Pallas kernels  24.8 us (24%)
    pallas_call x21, Pallas kernels, call(): pl.pallas_call(body, out_shape=outs, in_specs=[SM] * n_scalar + [spec] *...  24.8 us
    ppermute x18, starting transfers between devices, in_plane(): return lax.ppermute(x, 'ctx', [(i, i ^ s) for i in range(n_ctx)])  22.2 us
    ppermute x18, waiting for transfers between devices, in_plane(): return lax.ppermute(x, 'ctx', [(i, i ^ s) for i in range(n_ctx)])  19.4 us
    ppermute x5, starting transfers between devices, along(): lax.ppermute(x, 'ctx', [(i, (i + s * half) % n_ctx) for i in range(n_ctx)])  10.8 us
    ppermute x2, waiting for transfers between devices, from_plane(): return lax.ppermute(x, 'ctx', route)  6.6 us
    ppermute x1, starting transfers between devices, to_later(): return lax.ppermute(x, ('ctx', 'fsdp'), pairs)  4.17 us
    all_to_all x1, starting transfers between devices, on_device(): lax.all_to_all(adapter_grads, 'ctx', split_axis=0, concat_axis=0, tiled=T...  3.52 us
    ppermute x7, waiting for transfers between devices, across(): return lax.ppermute(x, 'fsdp', [(i, (i + s) % fsdp) for i in range(fsdp)])  3.27 us
  transfers between devices with their start and end apart: 35, of which 16 were waited for; matrix products, arithmetic and copies ran while one was open for 0% of the time, Pallas kernels for 22%

profile of v3, /device:TPU:0, one launch (start us, length us, event | category | flops | bytes accessed | tf_op | source)
XLA Modules:
  0.0 103.7 jit_solution(10567072920483510937)
XLA Ops:
  0.6 0.6 collective-permute-start.3
  1.2 1.1 %collective-permute-done.3.refs_1_ = bf16[4,2560]{1,0:T(4,128)(2,1)S(1)} collective-permute-done((bf16[4,2560]{1,0:T(4,128)(2,1)}, bf16[4,2560]{1,0:T(4,128)(2,1)S(1)}, u32[]{:S(2)}, u32[]{:S(2)}) %collective-permute-start.3) | collective-permute-done | bytes 20512 | tf_op jit(solution)/shard_map/ppermute | solution.py:571
  2.3 0.6 copy-done.1
  2.9 0.8 shard_map.130.refs_0_
  3.6 3.0 %collective-permute-start.4 = (bf16[4,5632]{1,0:T(4,128)(2,1)S(1)}, bf16[4,5632]{1,0:T(4,128)(2,1)S(1)}, u32[]{:S(2)}, u32[]{:S(2)}) collective-permute-start(bf16[4,5632]{1,0:T(4,128)(2,1)S(1)} %shard_map.130.refs_0_), channel_id=1, source_target_pairs={{0,8},{2,10},{4,12},{6,14},{8,16},{10,18},{12,20},{14,22},{16,24},... | collective-permute-start | bytes 135176 | tf_op jit(solution)/shard_map/ppermute | solution.py:559
  6.6 2.6 %collective-permute-start.5 = (bf16[4,5632]{1,0:T(4,128)(2,1)S(1)}, bf16[4,5632]{1,0:T(4,128)(2,1)S(1)}, u32[]{:S(2)}, u32[]{:S(2)}) collective-permute-start(bf16[4,5632]{1,0:T(4,128)(2,1)S(1)} %shard_map.130.refs_0_), channel_id=1, source_target_pairs={{0,16},{2,18},{4,20},{6,22},{8,24},{10,26},{12,28},{14,30},{16,0},... | collective-permute-start | bytes 135176 | tf_op jit(solution)/shard_map/ppermute | solution.py:559
  9.2 1.3 %collective-permute-start.6 = (bf16[4,5632]{1,0:T(4,128)(2,1)S(1)}, bf16[4,5632]{1,0:T(4,128)(2,1)S(1)}, u32[]{:S(2)}, u32[]{:S(2)}) collective-permute-start(bf16[4,5632]{1,0:T(4,128)(2,1)S(1)} %shard_map.130.refs_0_), channel_id=1, source_target_pairs={{0,24},{2,26},{4,28},{6,30},{8,0},{10,2},{12,4},{14,6},{16,8},{18,... | collective-permute-start | bytes 135176 | tf_op jit(solution)/shard_map/ppermute | solution.py:559
  10.5 2.1 %shard_map.134.refs_8_ = bf16[320,512]{1,0:T(8,128)(2,1)S(1)} custom-call(s32[320,512]{1,0:T(8,128)} %codes_in.1, s32[8,320]{1,0:T(8,128)} %bitcast.7, f32[2,128]{1,0:T(2,128)} %bitcast.8), custom_call_target="tpu_custom_call" | custom-call | tf_op jit(solution)/shard_map/pallas_call | solution.py:63
  12.7 0.7 collective-permute-start.17
  13.4 3.1 %collective-permute-start.18 = (bf16[320,512]{1,0:T(8,128)(2,1)S(1)}, bf16[320,512]{1,0:T(8,128)(2,1)S(1)}, u32[]{:S(2)}, u32[]{:S(2)}) collective-permute-start(bf16[320,512]{1,0:T(8,128)(2,1)S(1)} %shard_map.134.refs_8_), channel_id=1, source_target_pairs={{0,24},{2,26},{4,28},{6,30},{8,0},{10,2},{12,4},{14,6},{16,8},{18,... | collective-permute-start | bytes 983048 | tf_op jit(solution)/shard_map/ppermute | solution.py:559
  16.7 1.0 shard_map.131
  17.7 1.6 %collective-permute-start.7 = (bf16[4,4,1792]{2,1,0:T(4,128)(2,1)S(1)}, bf16[4,4,1792]{2,1,0:T(4,128)(2,1)S(1)}, u32[]{:S(2)}, u32[]{:S(2)}) collective-permute-start(bf16[4,4,1792]{2,1,0:T(4,128)(2,1)S(1)} %get-tuple-element.51), channel_id=1, source_target_pairs={{0,2},{2,0},{4,6},{6,4},{8,10},{10,8},{12,14},{14,12},{16,18},{18,... | collective-permute-start | bytes 172040 | tf_op jit(solution)/shard_map/ppermute | solution.py:554
  19.2 1.5 %collective-permute-start.8 = (bf16[4,4,1792]{2,1,0:T(4,128)(2,1)S(1)}, bf16[4,4,1792]{2,1,0:T(4,128)(2,1)S(1)}, u32[]{:S(2)}, u32[]{:S(2)}) collective-permute-start(bf16[4,4,1792]{2,1,0:T(4,128)(2,1)S(1)} %get-tuple-element.52), channel_id=1, source_target_pairs={{0,4},{2,6},{4,0},{6,2},{8,12},{10,14},{12,8},{14,10},{16,20},{18,... | collective-permute-start | bytes 172040 | tf_op jit(solution)/shard_map/ppermute | solution.py:554
  20.7 0.5 collective-permute-start.9
  21.2 1.0 shard_map.133
  22.3 1.5 %collective-permute-start.11 = (bf16[192,640]{1,0:T(8,128)(2,1)S(1)}, bf16[192,640]{1,0:T(8,128)(2,1)S(1)}, u32[]{:S(2)}, u32[]{:S(2)}) collective-permute-start(bf16[192,640]{1,0:T(8,128)(2,1)S(1)} %get-tuple-element.55), channel_id=1, source_target_pairs={{0,2},{2,0},{4,6},{6,4},{8,10},{10,8},{12,14},{14,12},{16,18},{18,... | collective-permute-start | bytes 737288 | tf_op jit(solution)/shard_map/ppermute | solution.py:554
  23.8 1.8 %shard_map.128 = (bf16[3,192,128]{2,1,0:T(8,128)(2,1)S(1)}, bf16[3,192,128]{2,1,0:T(8,128)(2,1)S(1)}, bf16[3,192,128]{2,1,0:T(8,128)(2,1)S(1)}, bf16[3,192,128]{2,1,0:T(8,128)(2,1)S(1)}) custom-call(s32[5]{0:T(128)S(1)} %stack.23.pos_ref, bf16[192,512]{1,0:T(8,128)(2,1)} %q_in.1, bf16[192,512]{1,0:T(8,128)(2,1)} %k_in.1, bf16[192,512]{1,0:T(8,128)(2,1)} %v_in.1), custom_call_target="tpu_custom_call" | custom-call | tf_op jit(solution)/shard_map/pallas_call | solution.py:63
  25.6 0.6 collective-permute-start
  26.4 1.3 %collective-permute-start.1 = (bf16[3,192,128]{2,1,0:T(8,128)(2,1)S(1)}, bf16[3,192,128]{2,1,0:T(8,128)(2,1)S(1)}, u32[]{:S(2)}, u32[]{:S(2)}) collective-permute-start(bf16[3,192,128]{2,1,0:T(8,128)(2,1)S(1)} %get-tuple-element.46), channel_id=1, source_target_pairs={{0,4},{2,6},{4,0},{6,2},{8,12},{10,14},{12,8},{14,10},{16,20},{18,... | collective-permute-start | bytes 442376 | tf_op jit(solution)/shard_map/ppermute | solution.py:554
  27.8 4.1 %collective-permute-done.refs_1_ = bf16[3,192,128]{2,1,0:T(8,128)(2,1)S(1)} collective-permute-done((bf16[3,192,128]{2,1,0:T(8,128)(2,1)S(1)}, bf16[3,192,128]{2,1,0:T(8,128)(2,1)S(1)}, u32[]{:S(2)}, u32[]{:S(2)}) %collective-permute-start) | collective-permute-done | bytes 147488 | tf_op jit(solution)/shard_map/ppermute | solution.py:554
  31.9 1.5 %collective-permute-start.13 = (bf16[192,640]{1,0:T(8,128)(2,1)S(1)}, bf16[192,640]{1,0:T(8,128)(2,1)S(1)}, u32[]{:S(2)}, u32[]{:S(2)}) collective-permute-start(bf16[192,640]{1,0:T(8,128)(2,1)S(1)} %get-tuple-element.56), channel_id=1, source_target_pairs={{0,4},{2,6},{4,0},{6,2},{8,12},{10,14},{12,8},{14,10},{16,20},{18,... | collective-permute-start | bytes 737288 | tf_op jit(solution)/shard_map/ppermute | solution.py:554
  33.4 1.4 %collective-permute-start.15 = (bf16[192,640]{1,0:T(8,128)(2,1)S(1)}, bf16[192,640]{1,0:T(8,128)(2,1)S(1)}, u32[]{:S(2)}, u32[]{:S(2)}) collective-permute-start(bf16[192,640]{1,0:T(8,128)(2,1)S(1)} %get-tuple-element.57), channel_id=1, source_target_pairs={{0,6},{2,4},{4,2},{6,0},{8,14},{10,12},{12,10},{14,8},{16,22},{18,... | collective-permute-start | bytes 737288 | tf_op jit(solution)/shard_map/ppermute | solution.py:554
  34.8 1.6 %collective-permute-start.2 = (bf16[3,192,128]{2,1,0:T(8,128)(2,1)S(1)}, bf16[3,192,128]{2,1,0:T(8,128)(2,1)S(1)}, u32[]{:S(2)}, u32[]{:S(2)}) collective-permute-start(bf16[3,192,128]{2,1,0:T(8,128)(2,1)S(1)} %get-tuple-element.47), channel_id=1, source_target_pairs={{0,6},{2,4},{4,2},{6,0},{8,14},{10,12},{12,10},{14,8},{16,22},{18,... | collective-permute-start | bytes 442376 | tf_op jit(solution)/shard_map/ppermute | solution.py:554
  36.4 0.6 shard_map.135
  37.0 8.6 %collective-permute-done.2.refs_3_ = bf16[3,192,128]{2,1,0:T(8,128)(2,1)S(1)} collective-permute-done((bf16[3,192,128]{2,1,0:T(8,128)(2,1)S(1)}, bf16[3,192,128]{2,1,0:T(8,128)(2,1)S(1)}, u32[]{:S(2)}, u32[]{:S(2)}) %collective-permute-start.2) | collective-permute-done | bytes 147488 | tf_op jit(solution)/shard_map/ppermute | solution.py:554
  45.7 0.7 collective-permute-start.19
  46.3 1.3 %collective-permute-start.20 = (bf16[320,512]{1,0:T(8,128)(2,1)S(1)}, bf16[320,512]{1,0:T(8,128)(2,1)S(1)}, u32[]{:S(2)}, u32[]{:S(2)}) collective-permute-start(bf16[320,512]{1,0:T(8,128)(2,1)S(1)} %get-tuple-element.59), channel_id=1, source_target_pairs={{8,0},{10,2},{12,4},{14,6},{16,24},{18,26},{20,28},{22,30},{9,1},{... | collective-permute-start | bytes 983048 | tf_op jit(solution)/shard_map/ppermute | solution.py:566
  47.6 0.6 shard_map.129
  48.2 0.4 collective-permute-done.13.refs_4_
  48.7 4.2 %collective-permute-start.24 = (bf16[2,768,128]{2,1,0:T(8,128)(2,1)S(1)}, bf16[2,768,128]{2,1,0:T(8,128)(2,1)S(1)}, u32[]{:S(2)}, u32[]{:S(2)}) collective-permute-start(bf16[2,768,128]{2,1,0:T(8,128)(2,1)S(1)} %get-tuple-element.49.kv_ref), channel_id=1, source_target_pairs={{0,8},{2,10},{5,13},{7,15},{9,17},{11,19},{12,20},{14,22},{16,24},... | collective-permute-start | bytes 1179656 | tf_op jit(solution)/shard_map/ppermute | solution.py:581
  52.9 0.5 collective-permute-start.16
  53.4 0.6 shard_map.132.adapt_ref
  54.1 0.3 collective-permute-done.14.refs_5_
  54.4 0.4 collective-permute-done.16.refs_7_
  54.8 6.6 %collective-permute-done.20.refs_12_ = bf16[320,512]{1,0:T(8,128)(2,1)S(1)} collective-permute-done((bf16[320,512]{1,0:T(8,128)(2,1)S(1)}, bf16[320,512]{1,0:T(8,128)(2,1)S(1)}, u32[]{:S(2)}, u32[]{:S(2)}) %collective-permute-start.20) | collective-permute-done | bytes 327712 | tf_op jit(solution)/shard_map/ppermute | solution.py:566
  61.4 1.9 %shard_map.136 = (bf16[768,128]{1,0:T(8,128)(2,1)S(1)}, bf16[768,128]{1,0:T(8,128)(2,1)S(1)}) custom-call(s32[5]{0:T(128)S(1)} %stack.23.pos_ref, bf16[64,1792]{1,0:T(8,128)(2,1)S(1)} %shard_map.132.adapt_ref, bf16[192,640]{1,0:T(8,128)(2,1)S(1)} %get-tuple-element.54.refs_0_.refs_2_, bf16[192,640]{1,0:T(8,128)(2,1)S(1)} %collective-permute-done.10.refs_1_, ...), custom_call_target="tpu_custom_call" | custom-call | tf_op jit(solution)/shard_map/pallas_call | solution.py:63
  63.3 1.5 %collective-permute-start.21 = (bf16[768,128]{1,0:T(8,128)(2,1)S(1)}, bf16[768,128]{1,0:T(8,128)(2,1)S(1)}, u32[]{:S(2)}, u32[]{:S(2)}) collective-permute-start(bf16[768,128]{1,0:T(8,128)(2,1)S(1)} %get-tuple-element.61), channel_id=1, source_target_pairs={{0,2},{2,0},{4,6},{6,4},{8,10},{10,8},{12,14},{14,12},{16,18},{18,... | collective-permute-start | bytes 589832 | tf_op jit(solution)/shard_map/ppermute | solution.py:554
  64.8 1.9 %shard_map.137 = (bf16[768,128]{1,0:T(8,128)(2,1)S(1)}, bf16[768,128]{1,0:T(8,128)(2,1)S(1)}) custom-call(s32[5]{0:T(128)S(1)} %stack.23.pos_ref, bf16[64,1792]{1,0:T(8,128)(2,1)S(1)} %shard_map.132.adapt_ref, bf16[192,640]{1,0:T(8,128)(2,1)S(1)} %get-tuple-element.54.refs_0_.refs_2_, bf16[192,640]{1,0:T(8,128)(2,1)S(1)} %collective-permute-done.10.refs_1_, ...), custom_call_target="tpu_custom_call" | custom-call | tf_op jit(solution)/shard_map/pallas_call | solution.py:63
  66.7 0.6 collective-permute-start.22
  67.3 1.5 %collective-permute-start.23 = (bf16[768,128]{1,0:T(8,128)(2,1)S(1)}, bf16[768,128]{1,0:T(8,128)(2,1)S(1)}, u32[]{:S(2)}, u32[]{:S(2)}) collective-permute-start(bf16[768,128]{1,0:T(8,128)(2,1)S(1)} %get-tuple-element.63), channel_id=1, source_target_pairs={{0,6},{2,4},{4,2},{6,0},{8,14},{10,12},{12,10},{14,8},{16,22},{18,... | collective-permute-start | bytes 589832 | tf_op jit(solution)/shard_map/ppermute | solution.py:554
  68.8 2.0 %shard_map.138 = (f32[768,128]{1,0:T(8,128)S(1)}, f32[1,768]{1,0:T(1,128)S(1)}) custom-call(s32[5]{0:T(128)S(1)} %stack.23.pos_ref, bf16[768,128]{1,0:T(8,128)(2,1)S(1)} %get-tuple-element.48.q_ref.refs_4_, bf16[2,768,128]{2,1,0:T(8,128)(2,1)S(1)} %get-tuple-element.49.kv_ref, bf16[2,768,128]{2,1,0:T(8,128)(2,1)S(1)} %collective-permute-done.24.far_ref.refs_5_), custom_call_target="tpu_custom_call" | custom-call | tf_op jit(solution)/shard_map/pallas_call | solution.py:63
  70.8 0.7 shard_map.144
  71.7 1.2 %shard_map.143.lora_ref = f32[768,64]{1,0:T(8,128)S(1)} custom-call(s32[5]{0:T(128)S(1)} %stack.23.pos_ref, bf16[64,1792]{1,0:T(8,128)(2,1)S(1)} %shard_map.132.adapt_ref, bf16[192,640]{1,0:T(8,128)(2,1)S(1)} %get-tuple-element.54.refs_0_.refs_2_, bf16[192,640]{1,0:T(8,128)(2,1)S(1)} %collective-permute-done.10.refs_1_, ...), custom_call_target="tpu_custom_call" | custom-call | tf_op jit(solution)/shard_map/pallas_call | solution.py:63
  72.9 0.2 collective-permute-done.29.refs_1_
  73.1 0.6 shard_map.145.refs_0_
  73.7 1.5 %collective-permute-start.30 = (bf16[384,128]{1,0:T(8,128)(2,1)S(1)}, bf16[384,128]{1,0:T(8,128)(2,1)S(1)}, u32[]{:S(2)}, u32[]{:S(2)}) collective-permute-start(bf16[384,128]{1,0:T(8,128)(2,1)S(1)} %shard_map.145.refs_0_), channel_id=1, source_target_pairs={{0,2},{2,0},{4,6},{6,4},{8,10},{10,8},{12,14},{14,12},{16,18},{18,... | collective-permute-start | bytes 294920 | tf_op jit(solution)/shard_map/ppermute | solution.py:554
  75.3 1.3 %collective-permute-start.31 = (bf16[384,128]{1,0:T(8,128)(2,1)S(1)}, bf16[384,128]{1,0:T(8,128)(2,1)S(1)}, u32[]{:S(2)}, u32[]{:S(2)}) collective-permute-start(bf16[384,128]{1,0:T(8,128)(2,1)S(1)} %shard_map.145.refs_0_), channel_id=1, source_target_pairs={{0,4},{2,6},{4,0},{6,2},{8,12},{10,14},{12,8},{14,10},{16,20},{18,... | collective-permute-start | bytes 294920 | tf_op jit(solution)/shard_map/ppermute | solution.py:554
  76.6 0.7 collective-permute-start.32
  77.3 1.0 shard_map.139
  78.3 1.3 %collective-permute-start.25 = (bf16[2,768,128]{2,1,0:T(8,128)(2,1)S(1)}, bf16[2,768,128]{2,1,0:T(8,128)(2,1)S(1)}, u32[]{:S(2)}, u32[]{:S(2)}) collective-permute-start(bf16[2,768,128]{2,1,0:T(8,128)(2,1)S(1)} %get-tuple-element.71), channel_id=1, source_target_pairs={{8,0},{10,2},{13,5},{15,7},{17,9},{19,11},{20,12},{22,14},{24,16},... | collective-permute-start | bytes 1179656 | tf_op jit(solution)/shard_map/ppermute | solution.py:584
  79.6 1.4 %collective-permute-done.31.refs_2_ = bf16[384,128]{1,0:T(8,128)(2,1)S(1)} collective-permute-done((bf16[384,128]{1,0:T(8,128)(2,1)S(1)}, bf16[384,128]{1,0:T(8,128)(2,1)S(1)}, u32[]{:S(2)}, u32[]{:S(2)}) %collective-permute-start.31) | collective-permute-done | bytes 98336 | tf_op jit(solution)/shard_map/ppermute | solution.py:554
  81.0 1.1 %collective-permute-done.32.refs_3_ = bf16[384,128]{1,0:T(8,128)(2,1)S(1)} collective-permute-done((bf16[384,128]{1,0:T(8,128)(2,1)S(1)}, bf16[384,128]{1,0:T(8,128)(2,1)S(1)}, u32[]{:S(2)}, u32[]{:S(2)}) %collective-permute-start.32) | collective-permute-done | bytes 98336 | tf_op jit(solution)/shard_map/ppermute | solution.py:554
  82.2 1.3 %collective-permute-done.33.refs_1_ = bf16[384,128]{1,0:T(8,128)(2,1)S(1)} collective-permute-done((bf16[384,128]{1,0:T(8,128)(2,1)S(1)}, bf16[384,128]{1,0:T(8,128)(2,1)S(1)}, u32[]{:S(2)}, u32[]{:S(2)}) %collective-permute-start.33) | collective-permute-done | bytes 98336 | tf_op jit(solution)/shard_map/ppermute | solution.py:571
  83.5 1.7 %shard_map.147 = f32[16,4,768]{2,1,0:T(4,128)} custom-call(s32[5]{0:T(128)S(1)} %stack.23.pos_ref, f32[768,128]{1,0:T(8,128)S(1)} %get-tuple-element.64.refs_6_.o_ref, bf16[384,128]{1,0:T(8,128)(2,1)S(1)} %shard_map.146.refs_0_, bf16[384,128]{1,0:T(8,128)(2,1)S(1)} %collective-permute-done.33.refs_1_, ...), custom_call_target="tpu_custom_call" | custom-call | tf_op jit(solution)/shard_map/pallas_call | solution.py:63
  85.2 3.5 %all-to-all-start = ((f32[16,4,768]{2,1,0:T(4,128)}), f32[16,4,768]{2,1,0:T(4,128)S(1)}, u32[]{:S(2)}, u32[]{:S(2)}) async-start(f32[16,4,768]{2,1,0:T(4,128)} %shard_map.147), calls=%async_computation | async-start | bytes 393216 | tf_op jit(solution)/shard_map/all_to_all | solution.py:736
  88.7 1.8 %shard_map.140 = (bf16[768,128]{1,0:T(8,128)(2,1)S(1)}, f32[2,768,128]{2,1,0:T(8,128)S(1)}) custom-call(s32[5]{0:T(128)S(1)} %stack.23.pos_ref, bf16[768,128]{1,0:T(8,128)(2,1)S(1)} %get-tuple-element.48.q_ref.refs_4_, bf16[2,768,128]{2,1,0:T(8,128)(2,1)S(1)} %get-tuple-element.49.kv_ref, bf16[768,128]{1,0:T(8,128)(2,1)S(1)} %get-tuple-element.66.do_ref, ...), custom_call_target="tpu_custom_call" | custom-call | tf_op jit(solution)/shard_map/pallas_call | solution.py:63
  90.6 0.6 shard_map.141
  91.2 1.9 %collective-permute-start.26 = (bf16[3,192,128]{2,1,0:T(8,128)(2,1)S(1)}, bf16[3,192,128]{2,1,0:T(8,128)(2,1)S(1)}, u32[]{:S(2)}, u32[]{:S(2)}) collective-permute-start(bf16[3,192,128]{2,1,0:T(8,128)(2,1)S(1)} %get-tuple-element.73), channel_id=1, source_target_pairs={{0,2},{2,0},{4,6},{6,4},{8,10},{10,8},{12,14},{14,12},{16,18},{18,... | collective-permute-start | bytes 442376 | tf_op jit(solution)/shard_map/ppermute | solution.py:554
  93.1 1.5 %collective-permute-start.27 = (bf16[3,192,128]{2,1,0:T(8,128)(2,1)S(1)}, bf16[3,192,128]{2,1,0:T(8,128)(2,1)S(1)}, u32[]{:S(2)}, u32[]{:S(2)}) collective-permute-start(bf16[3,192,128]{2,1,0:T(8,128)(2,1)S(1)} %get-tuple-element.74), channel_id=1, source_target_pairs={{0,4},{2,6},{4,0},{6,2},{8,12},{10,14},{12,8},{14,10},{16,20},{18,... | collective-permute-start | bytes 442376 | tf_op jit(solution)/shard_map/ppermute | solution.py:554
  94.8 2.8 %all-to-all-done.in_ref = f32[16,4,768]{2,1,0:T(4,128)S(1)} async-done(((f32[16,4,768]{2,1,0:T(4,128)}), f32[16,4,768]{2,1,0:T(4,128)S(1)}, u32[]{:S(2)}, u32[]{:S(2)}) %all-to-all-start) | async-done | bytes 196640 | tf_op jit(solution)/shard_map/all_to_all | solution.py:736
  97.6 1.2 %shard_map.148 = (f32[4,2560]{1,0:T(4,128)}, f32[4,512]{1,0:T(4,128)}) custom-call(s32[5]{0:T(128)S(1)} %stack.23.pos_ref, f32[16,4,768]{2,1,0:T(4,128)S(1)} %all-to-all-done.in_ref), custom_call_target="tpu_custom_call" | custom-call | tf_op jit(solution)/shard_map/pallas_call | solution.py:63
  98.9 2.1 %collective-permute-done.27.refs_2_ = bf16[3,192,128]{2,1,0:T(8,128)(2,1)S(1)} collective-permute-done((bf16[3,192,128]{2,1,0:T(8,128)(2,1)S(1)}, bf16[3,192,128]{2,1,0:T(8,128)(2,1)S(1)}, u32[]{:S(2)}, u32[]{:S(2)}) %collective-permute-start.27) | collective-permute-done | bytes 147488 | tf_op jit(solution)/shard_map/ppermute | solution.py:554
  101.0 1.3 %collective-permute-done.28.refs_3_ = bf16[3,192,128]{2,1,0:T(8,128)(2,1)S(1)} collective-permute-done((bf16[3,192,128]{2,1,0:T(8,128)(2,1)S(1)}, bf16[3,192,128]{2,1,0:T(8,128)(2,1)S(1)}, u32[]{:S(2)}, u32[]{:S(2)}) %collective-permute-start.28) | collective-permute-done | bytes 147488 | tf_op jit(solution)/shard_map/ppermute | solution.py:554
  102.3 1.4 %shard_map.142 = (bf16[192,512]{1,0:T(8,128)(2,1)}, bf16[192,512]{1,0:T(8,128)(2,1)}, bf16[192,512]{1,0:T(8,128)(2,1)}) custom-call(s32[5]{0:T(128)S(1)} %stack.23.pos_ref, bf16[3,192,128]{2,1,0:T(8,128)(2,1)S(1)} %get-tuple-element.72.refs_0_, bf16[3,192,128]{2,1,0:T(8,128)(2,1)S(1)} %collective-permute-done.26.refs_1_, ...), custom_call_target="tpu_custom_call" | custom-call | tf_op jit(solution)/shard_map/pallas_call | solution.py:63
  (32 shorter events, 0.9 us)
Async XLA Ops:
  0.6 20.6 %copy-start = (bf16[192,2560]{1,0:T(8,128)(2,1)S(1)}, bf16[192,2560]{1,0:T(8,128)(2,1)}, u32[]{:S(2)}) copy-start(bf16[192,2560]{1,0:T(8,128)(2,1)} %g_ref.1) | copy-start | bytes 2949124
  0.6 1.6 %collective-permute-start.3 = (bf16[4,2560]{1,0:T(4,128)(2,1)}, bf16[4,2560]{1,0:T(4,128)(2,1)S(1)}, u32[]{:S(2)}, u32[]{:S(2)}) collective-permute-start(bf16[4,2560]{1,0:T(4,128)(2,1)} %refs_0_.1), channel_id=1, source_target_pairs={{0,1},{1,0},{2,3},{3,2},{4,5},{5,4},{6,7},{7,6},{8,9},{9,8},{10,11... | collective-permute-start | bytes 61448 | tf_op jit(solution)/shard_map/ppermute | solution.py:571
  2.3 0.6 copy-start.1
  3.6 13.0 %collective-permute-start.4 = (bf16[4,5632]{1,0:T(4,128)(2,1)S(1)}, bf16[4,5632]{1,0:T(4,128)(2,1)S(1)}, u32[]{:S(2)}, u32[]{:S(2)}) collective-permute-start(bf16[4,5632]{1,0:T(4,128)(2,1)S(1)} %shard_map.130.refs_0_), channel_id=1, source_target_pairs={{0,8},{2,10},{4,12},{6,14},{8,16},{10,18},{12,20},{14,22},{16,24},... | collective-permute-start | bytes 135176 | tf_op jit(solution)/shard_map/ppermute | solution.py:559
  6.6 10.1 %collective-permute-start.5 = (bf16[4,5632]{1,0:T(4,128)(2,1)S(1)}, bf16[4,5632]{1,0:T(4,128)(2,1)S(1)}, u32[]{:S(2)}, u32[]{:S(2)}) collective-permute-start(bf16[4,5632]{1,0:T(4,128)(2,1)S(1)} %shard_map.130.refs_0_), channel_id=1, source_target_pairs={{0,16},{2,18},{4,20},{6,22},{8,24},{10,26},{12,28},{14,30},{16,0},... | collective-permute-start | bytes 135176 | tf_op jit(solution)/shard_map/ppermute | solution.py:559
  9.2 7.5 %collective-permute-start.6 = (bf16[4,5632]{1,0:T(4,128)(2,1)S(1)}, bf16[4,5632]{1,0:T(4,128)(2,1)S(1)}, u32[]{:S(2)}, u32[]{:S(2)}) collective-permute-start(bf16[4,5632]{1,0:T(4,128)(2,1)S(1)} %shard_map.130.refs_0_), channel_id=1, source_target_pairs={{0,24},{2,26},{4,28},{6,30},{8,0},{10,2},{12,4},{14,6},{16,8},{18,... | collective-permute-start | bytes 135176 | tf_op jit(solution)/shard_map/ppermute | solution.py:559
  12.7 22.1 %collective-permute-start.17 = (bf16[320,512]{1,0:T(8,128)(2,1)S(1)}, bf16[320,512]{1,0:T(8,128)(2,1)S(1)}, u32[]{:S(2)}, u32[]{:S(2)}) collective-permute-start(bf16[320,512]{1,0:T(8,128)(2,1)S(1)} %shard_map.134.refs_8_), channel_id=1, source_target_pairs={{0,8},{2,10},{4,12},{6,14},{8,16},{10,18},{12,20},{14,22},{16,24},... | collective-permute-start | bytes 983048 | tf_op jit(solution)/shard_map/ppermute | solution.py:559
  13.4 21.4 %collective-permute-start.18 = (bf16[320,512]{1,0:T(8,128)(2,1)S(1)}, bf16[320,512]{1,0:T(8,128)(2,1)S(1)}, u32[]{:S(2)}, u32[]{:S(2)}) collective-permute-start(bf16[320,512]{1,0:T(8,128)(2,1)S(1)} %shard_map.134.refs_8_), channel_id=1, source_target_pairs={{0,24},{2,26},{4,28},{6,30},{8,0},{10,2},{12,4},{14,6},{16,8},{18,... | collective-permute-start | bytes 983048 | tf_op jit(solution)/shard_map/ppermute | solution.py:559
  17.7 4.7 %collective-permute-start.7 = (bf16[4,4,1792]{2,1,0:T(4,128)(2,1)S(1)}, bf16[4,4,1792]{2,1,0:T(4,128)(2,1)S(1)}, u32[]{:S(2)}, u32[]{:S(2)}) collective-permute-start(bf16[4,4,1792]{2,1,0:T(4,128)(2,1)S(1)} %get-tuple-element.51), channel_id=1, source_target_pairs={{0,2},{2,0},{4,6},{6,4},{8,10},{10,8},{12,14},{14,12},{16,18},{18,... | collective-permute-start | bytes 172040 | tf_op jit(solution)/shard_map/ppermute | solution.py:554
  19.2 6.4 %collective-permute-start.8 = (bf16[4,4,1792]{2,1,0:T(4,128)(2,1)S(1)}, bf16[4,4,1792]{2,1,0:T(4,128)(2,1)S(1)}, u32[]{:S(2)}, u32[]{:S(2)}) collective-permute-start(bf16[4,4,1792]{2,1,0:T(4,128)(2,1)S(1)} %get-tuple-element.52), channel_id=1, source_target_pairs={{0,4},{2,6},{4,0},{6,2},{8,12},{10,14},{12,8},{14,10},{16,20},{18,... | collective-permute-start | bytes 172040 | tf_op jit(solution)/shard_map/ppermute | solution.py:554
  20.7 5.7 %collective-permute-start.9 = (bf16[4,4,1792]{2,1,0:T(4,128)(2,1)S(1)}, bf16[4,4,1792]{2,1,0:T(4,128)(2,1)S(1)}, u32[]{:S(2)}, u32[]{:S(2)}) collective-permute-start(bf16[4,4,1792]{2,1,0:T(4,128)(2,1)S(1)} %get-tuple-element.53), channel_id=1, source_target_pairs={{0,6},{2,4},{4,2},{6,0},{8,14},{10,12},{12,10},{14,8},{16,22},{18,... | collective-permute-start | bytes 172040 | tf_op jit(solution)/shard_map/ppermute | solution.py:554
  22.3 11.1 %collective-permute-start.11 = (bf16[192,640]{1,0:T(8,128)(2,1)S(1)}, bf16[192,640]{1,0:T(8,128)(2,1)S(1)}, u32[]{:S(2)}, u32[]{:S(2)}) collective-permute-start(bf16[192,640]{1,0:T(8,128)(2,1)S(1)} %get-tuple-element.55), channel_id=1, source_target_pairs={{0,2},{2,0},{4,6},{6,4},{8,10},{10,8},{12,14},{14,12},{16,18},{18,... | collective-permute-start | bytes 737288 | tf_op jit(solution)/shard_map/ppermute | solution.py:554
  25.6 6.3 %collective-permute-start = (bf16[3,192,128]{2,1,0:T(8,128)(2,1)S(1)}, bf16[3,192,128]{2,1,0:T(8,128)(2,1)S(1)}, u32[]{:S(2)}, u32[]{:S(2)}) collective-permute-start(bf16[3,192,128]{2,1,0:T(8,128)(2,1)S(1)} %get-tuple-element.45), channel_id=1, source_target_pairs={{0,2},{2,0},{4,6},{6,4},{8,10},{10,8},{12,14},{14,12},{16,18},{18,... | collective-permute-start | bytes 442376 | tf_op jit(solution)/shard_map/ppermute | solution.py:554
  26.4 5.5 %collective-permute-start.1 = (bf16[3,192,128]{2,1,0:T(8,128)(2,1)S(1)}, bf16[3,192,128]{2,1,0:T(8,128)(2,1)S(1)}, u32[]{:S(2)}, u32[]{:S(2)}) collective-permute-start(bf16[3,192,128]{2,1,0:T(8,128)(2,1)S(1)} %get-tuple-element.46), channel_id=1, source_target_pairs={{0,4},{2,6},{4,0},{6,2},{8,12},{10,14},{12,8},{14,10},{16,20},{18,... | collective-permute-start | bytes 442376 | tf_op jit(solution)/shard_map/ppermute | solution.py:554
  31.9 14.5 %collective-permute-start.10 = (bf16[192,640]{1,0:T(8,128)(2,1)S(1)}, bf16[192,640]{1,0:T(8,128)(2,1)S(1)}, u32[]{:S(2)}, u32[]{:S(2)}) collective-permute-start(bf16[192,640]{1,0:T(8,128)(2,1)S(1)} %get-tuple-element.54.refs_0_.refs_2_), channel_id=1, source_target_pairs={{0,1},{1,0},{2,3},{3,2},{4,5},{5,4},{6,7},{7,6},{8,9},{9,8},{10,11... | collective-permute-start | bytes 737288 | tf_op jit(solution)/shard_map/ppermute | solution.py:571
  31.9 16.8 %collective-permute-start.13 = (bf16[192,640]{1,0:T(8,128)(2,1)S(1)}, bf16[192,640]{1,0:T(8,128)(2,1)S(1)}, u32[]{:S(2)}, u32[]{:S(2)}) collective-permute-start(bf16[192,640]{1,0:T(8,128)(2,1)S(1)} %get-tuple-element.56), channel_id=1, source_target_pairs={{0,4},{2,6},{4,0},{6,2},{8,12},{10,14},{12,8},{14,10},{16,20},{18,... | collective-permute-start | bytes 737288 | tf_op jit(solution)/shard_map/ppermute | solution.py:554
  33.4 19.4 %collective-permute-start.15 = (bf16[192,640]{1,0:T(8,128)(2,1)S(1)}, bf16[192,640]{1,0:T(8,128)(2,1)S(1)}, u32[]{:S(2)}, u32[]{:S(2)}) collective-permute-start(bf16[192,640]{1,0:T(8,128)(2,1)S(1)} %get-tuple-element.57), channel_id=1, source_target_pairs={{0,6},{2,4},{4,2},{6,0},{8,14},{10,12},{12,10},{14,8},{16,22},{18,... | collective-permute-start | bytes 737288 | tf_op jit(solution)/shard_map/ppermute | solution.py:554
  34.8 18.1 %collective-permute-start.12 = (bf16[192,640]{1,0:T(8,128)(2,1)S(1)}, bf16[192,640]{1,0:T(8,128)(2,1)S(1)}, u32[]{:S(2)}, u32[]{:S(2)}) collective-permute-start(bf16[192,640]{1,0:T(8,128)(2,1)S(1)} %collective-permute-done.11.refs_2_.refs_3_), channel_id=1, source_target_pairs={{0,1},{1,0},{2,3},{3,2},{4,5},{5,4},{6,7},{7,6},{8,9},{9,8},{10,11... | collective-permute-start | bytes 737288 | tf_op jit(solution)/shard_map/ppermute | solution.py:571
  34.8 10.8 %collective-permute-start.2 = (bf16[3,192,128]{2,1,0:T(8,128)(2,1)S(1)}, bf16[3,192,128]{2,1,0:T(8,128)(2,1)S(1)}, u32[]{:S(2)}, u32[]{:S(2)}) collective-permute-start(bf16[3,192,128]{2,1,0:T(8,128)(2,1)S(1)} %get-tuple-element.47), channel_id=1, source_target_pairs={{0,6},{2,4},{4,2},{6,0},{8,14},{10,12},{12,10},{14,8},{16,22},{18,... | collective-permute-start | bytes 442376 | tf_op jit(solution)/shard_map/ppermute | solution.py:554
  45.7 9.1 %collective-permute-start.19 = (bf16[320,512]{1,0:T(8,128)(2,1)S(1)}, bf16[320,512]{1,0:T(8,128)(2,1)S(1)}, u32[]{:S(2)}, u32[]{:S(2)}) collective-permute-start(bf16[320,512]{1,0:T(8,128)(2,1)S(1)} %get-tuple-element.58), channel_id=1, source_target_pairs={{8,16},{10,18},{12,20},{14,22},{16,8},{18,10},{20,12},{22,14},{9,1... | collective-permute-start | bytes 983048 | tf_op jit(solution)/shard_map/ppermute | solution.py:566
  46.3 15.0 %collective-permute-start.20 = (bf16[320,512]{1,0:T(8,128)(2,1)S(1)}, bf16[320,512]{1,0:T(8,128)(2,1)S(1)}, u32[]{:S(2)}, u32[]{:S(2)}) collective-permute-start(bf16[320,512]{1,0:T(8,128)(2,1)S(1)} %get-tuple-element.59), channel_id=1, source_target_pairs={{8,0},{10,2},{12,4},{14,6},{16,24},{18,26},{20,28},{22,30},{9,1},{... | collective-permute-start | bytes 983048 | tf_op jit(solution)/shard_map/ppermute | solution.py:566
  48.7 20.1 %collective-permute-start.24 = (bf16[2,768,128]{2,1,0:T(8,128)(2,1)S(1)}, bf16[2,768,128]{2,1,0:T(8,128)(2,1)S(1)}, u32[]{:S(2)}, u32[]{:S(2)}) collective-permute-start(bf16[2,768,128]{2,1,0:T(8,128)(2,1)S(1)} %get-tuple-element.49.kv_ref), channel_id=1, source_target_pairs={{0,8},{2,10},{5,13},{7,15},{9,17},{11,19},{12,20},{14,22},{16,24},... | collective-permute-start | bytes 1179656 | tf_op jit(solution)/shard_map/ppermute | solution.py:581
  52.9 1.6 %collective-permute-start.14 = (bf16[192,640]{1,0:T(8,128)(2,1)S(1)}, bf16[192,640]{1,0:T(8,128)(2,1)S(1)}, u32[]{:S(2)}, u32[]{:S(2)}) collective-permute-start(bf16[192,640]{1,0:T(8,128)(2,1)S(1)} %collective-permute-done.13.refs_4_), channel_id=1, source_target_pairs={{0,1},{1,0},{2,3},{3,2},{4,5},{5,4},{6,7},{7,6},{8,9},{9,8},{10,11... | collective-permute-start | bytes 737288 | tf_op jit(solution)/shard_map/ppermute | solution.py:571
  52.9 1.8 %collective-permute-start.16 = (bf16[192,640]{1,0:T(8,128)(2,1)S(1)}, bf16[192,640]{1,0:T(8,128)(2,1)S(1)}, u32[]{:S(2)}, u32[]{:S(2)}) collective-permute-start(bf16[192,640]{1,0:T(8,128)(2,1)S(1)} %collective-permute-done.15.refs_6_.refs_5_), channel_id=1, source_target_pairs={{0,1},{1,0},{2,3},{3,2},{4,5},{5,4},{6,7},{7,6},{8,9},{9,8},{10,11... | collective-permute-start | bytes 737288 | tf_op jit(solution)/shard_map/ppermute | solution.py:571
  63.3 13.3 %collective-permute-start.21 = (bf16[768,128]{1,0:T(8,128)(2,1)S(1)}, bf16[768,128]{1,0:T(8,128)(2,1)S(1)}, u32[]{:S(2)}, u32[]{:S(2)}) collective-permute-start(bf16[768,128]{1,0:T(8,128)(2,1)S(1)} %get-tuple-element.61), channel_id=1, source_target_pairs={{0,2},{2,0},{4,6},{6,4},{8,10},{10,8},{12,14},{14,12},{16,18},{18,... | collective-permute-start | bytes 589832 | tf_op jit(solution)/shard_map/ppermute | solution.py:554
  66.7 10.6 %collective-permute-start.22 = (bf16[768,128]{1,0:T(8,128)(2,1)S(1)}, bf16[768,128]{1,0:T(8,128)(2,1)S(1)}, u32[]{:S(2)}, u32[]{:S(2)}) collective-permute-start(bf16[768,128]{1,0:T(8,128)(2,1)S(1)} %get-tuple-element.62), channel_id=1, source_target_pairs={{0,4},{2,6},{4,0},{6,2},{8,12},{10,14},{12,8},{14,10},{16,20},{18,... | collective-permute-start | bytes 589832 | tf_op jit(solution)/shard_map/ppermute | solution.py:554
  67.3 10.0 %collective-permute-start.23 = (bf16[768,128]{1,0:T(8,128)(2,1)S(1)}, bf16[768,128]{1,0:T(8,128)(2,1)S(1)}, u32[]{:S(2)}, u32[]{:S(2)}) collective-permute-start(bf16[768,128]{1,0:T(8,128)(2,1)S(1)} %get-tuple-element.63), channel_id=1, source_target_pairs={{0,6},{2,4},{4,2},{6,0},{8,14},{10,12},{12,10},{14,8},{16,22},{18,... | collective-permute-start | bytes 589832 | tf_op jit(solution)/shard_map/ppermute | solution.py:554
  71.6 1.5 %collective-permute-start.29 = (f32[384,64]{1,0:T(8,128)S(1)}, f32[384,64]{1,0:T(8,128)S(1)}, u32[]{:S(2)}, u32[]{:S(2)}) collective-permute-start(f32[384,64]{1,0:T(8,128)S(1)} %get-tuple-element.80), channel_id=1, source_target_pairs={{0,1},{1,0},{2,3},{3,2},{4,5},{5,4},{6,7},{7,6},{8,9},{9,8},{10,11... | collective-permute-start | bytes 294920 | tf_op jit(solution)/shard_map/ppermute | solution.py:571
  73.7 5.9 %collective-permute-start.30 = (bf16[384,128]{1,0:T(8,128)(2,1)S(1)}, bf16[384,128]{1,0:T(8,128)(2,1)S(1)}, u32[]{:S(2)}, u32[]{:S(2)}) collective-permute-start(bf16[384,128]{1,0:T(8,128)(2,1)S(1)} %shard_map.145.refs_0_), channel_id=1, source_target_pairs={{0,2},{2,0},{4,6},{6,4},{8,10},{10,8},{12,14},{14,12},{16,18},{18,... | collective-permute-start | bytes 294920 | tf_op jit(solution)/shard_map/ppermute | solution.py:554
  75.3 5.8 %collective-permute-start.31 = (bf16[384,128]{1,0:T(8,128)(2,1)S(1)}, bf16[384,128]{1,0:T(8,128)(2,1)S(1)}, u32[]{:S(2)}, u32[]{:S(2)}) collective-permute-start(bf16[384,128]{1,0:T(8,128)(2,1)S(1)} %shard_map.145.refs_0_), channel_id=1, source_target_pairs={{0,4},{2,6},{4,0},{6,2},{8,12},{10,14},{12,8},{14,10},{16,20},{18,... | collective-permute-start | bytes 294920 | tf_op jit(solution)/shard_map/ppermute | solution.py:554
  76.6 5.5 %collective-permute-start.32 = (bf16[384,128]{1,0:T(8,128)(2,1)S(1)}, bf16[384,128]{1,0:T(8,128)(2,1)S(1)}, u32[]{:S(2)}, u32[]{:S(2)}) collective-permute-start(bf16[384,128]{1,0:T(8,128)(2,1)S(1)} %shard_map.145.refs_0_), channel_id=1, source_target_pairs={{0,6},{2,4},{4,2},{6,0},{8,14},{10,12},{12,10},{14,8},{16,22},{18,... | collective-permute-start | bytes 294920 | tf_op jit(solution)/shard_map/ppermute | solution.py:554
  78.3 12.3 %collective-permute-start.25 = (bf16[2,768,128]{2,1,0:T(8,128)(2,1)S(1)}, bf16[2,768,128]{2,1,0:T(8,128)(2,1)S(1)}, u32[]{:S(2)}, u32[]{:S(2)}) collective-permute-start(bf16[2,768,128]{2,1,0:T(8,128)(2,1)S(1)} %get-tuple-element.71), channel_id=1, source_target_pairs={{8,0},{10,2},{13,5},{15,7},{17,9},{19,11},{20,12},{22,14},{24,16},... | collective-permute-start | bytes 1179656 | tf_op jit(solution)/shard_map/ppermute | solution.py:584
  82.1 1.4 %collective-permute-start.33 = (bf16[384,128]{1,0:T(8,128)(2,1)S(1)}, bf16[384,128]{1,0:T(8,128)(2,1)S(1)}, u32[]{:S(2)}, u32[]{:S(2)}) collective-permute-start(bf16[384,128]{1,0:T(8,128)(2,1)S(1)} %shard_map.146.refs_0_), channel_id=1, source_target_pairs={{0,1},{1,0},{2,3},{3,2},{4,5},{5,4},{6,7},{7,6},{8,9},{9,8},{10,11... | collective-permute-start | bytes 294920 | tf_op jit(solution)/shard_map/ppermute | solution.py:571
  85.2 12.4 %all-to-all-start = ((f32[16,4,768]{2,1,0:T(4,128)}), f32[16,4,768]{2,1,0:T(4,128)S(1)}, u32[]{:S(2)}, u32[]{:S(2)}) async-start(f32[16,4,768]{2,1,0:T(4,128)} %shard_map.147), calls=%async_computation | async-start | bytes 393216 | tf_op jit(solution)/shard_map/all_to_all | solution.py:736
  91.2 7.6 %collective-permute-start.26 = (bf16[3,192,128]{2,1,0:T(8,128)(2,1)S(1)}, bf16[3,192,128]{2,1,0:T(8,128)(2,1)S(1)}, u32[]{:S(2)}, u32[]{:S(2)}) collective-permute-start(bf16[3,192,128]{2,1,0:T(8,128)(2,1)S(1)} %get-tuple-element.73), channel_id=1, source_target_pairs={{0,2},{2,0},{4,6},{6,4},{8,10},{10,8},{12,14},{14,12},{16,18},{18,... | collective-permute-start | bytes 442376 | tf_op jit(solution)/shard_map/ppermute | solution.py:554
  93.1 7.9 %collective-permute-start.27 = (bf16[3,192,128]{2,1,0:T(8,128)(2,1)S(1)}, bf16[3,192,128]{2,1,0:T(8,128)(2,1)S(1)}, u32[]{:S(2)}, u32[]{:S(2)}) collective-permute-start(bf16[3,192,128]{2,1,0:T(8,128)(2,1)S(1)} %get-tuple-element.74), channel_id=1, source_target_pairs={{0,4},{2,6},{4,0},{6,2},{8,12},{10,14},{12,8},{14,10},{16,20},{18,... | collective-permute-start | bytes 442376 | tf_op jit(solution)/shard_map/ppermute | solution.py:554
  94.6 7.7 %collective-permute-start.28 = (bf16[3,192,128]{2,1,0:T(8,128)(2,1)S(1)}, bf16[3,192,128]{2,1,0:T(8,128)(2,1)S(1)}, u32[]{:S(2)}, u32[]{:S(2)}) collective-permute-start(bf16[3,192,128]{2,1,0:T(8,128)(2,1)S(1)} %get-tuple-element.75), channel_id=1, source_target_pairs={{0,6},{2,4},{4,2},{6,0},{8,14},{10,12},{12,10},{14,8},{16,22},{18,... | collective-permute-start | bytes 442376 | tf_op jit(solution)/shard_map/ppermute | solution.py:554

commit v4 on v3

--- a/solution.py
+++ b/solution.py
@@ -119,49 +119,6 @@
         out_ref[:, b * LANES : (b + 1) * LANES] = (value * scale).astype(BF)
 
 
-def raw_body(n_ups, *refs):
-    ins, out_refs, sem = refs[: n_ups + 1], refs[n_ups + 1 : -1], refs[-1]
-    out_ref = out_refs[0]
-    at = 0
-    copies = []
-    for i, ref in enumerate(ins):
-        width = ref.shape[1]
-        copies.append(pltpu.make_async_copy(ref, out_ref.at[:, at : at + width], sem.at[i]))
-        at += width
-    for copy in copies:
-        copy.start()
-    for copy in copies:
-        copy.wait()
-
-
-def chunks_body(half, fsdp, strips, wide, pos_ref, *refs):
-    ins, out_refs = refs[:-half], refs[-half:]
-    mine = pos_ref[0]
-    rank_rows, cols = ins[0].shape
-    grad_cols = (cols - half * LANES) // fsdp
-    step = grad_cols // strips
-    width = step // half
-    short = wide - strips * width
-    for s in range(half):
-        for jv in range(half):
-
-            @pl.when((mine ^ s) == jv)
-            def _(s=s, jv=jv):
-                for p, ref in enumerate(ins):
-                    for f in range(fsdp):
-                        base = f * grad_cols + jv * width
-                        pieces = [
-                            ref[:, base + i * step : base + i * step + width]
-                            for i in range(strips)
-                        ]
-                        if short:
-                            pieces.append(jnp.zeros((rank_rows, short), BF))
-                        out_refs[s][p, :, f * wide : (f + 1) * wide] = jnp.concatenate(
-                            pieces, axis=1
-                        )
-                    out_refs[s][p, :, fsdp * wide :] = ref[:, fsdp * grad_cols :]
-
-
 def relay_body(pos_ref, above_ref, below_ref, inner_ref, outer_ref):
     @pl.when(pos_ref[1] == 1)
     def _():
@@ -174,70 +131,82 @@
         outer_ref[...] = above_ref[...]
 
 
-def pack_grad_body(half, strips, pos_ref, g_ref, *out_refs):
-    mine = pos_ref[0]
-    rows = g_ref.shape[0]
-    step = g_ref.shape[1] // strips
+def pack_body(half, strips, wide, pos_ref, *refs):
+    ins, outs, chunks = refs[:6], refs[6 : 6 + half], refs[6 + half : 6 + 2 * half]
+    scr, sem = refs[6 + 2 * half : -1], refs[-1]
+    fetch(ins, scr, sem)
+    mine, own = pos_ref[0], pos_ref[4]
+    up_ref, down_ref = scr[4], scr[5]
+    step = up_ref.shape[1] // strips
     width = step // half
+    short = wide - strips * width
+
+    def strip(ref, jv):
+        pieces = [ref[:, i * step + jv * width : i * step + (jv + 1) * width] for i in range(strips)]
+        if short:
+            pieces.append(jnp.zeros((ref.shape[0], short), BF))
+        return jnp.concatenate(pieces, axis=1)
+
     for s in range(half):
-        to = mine ^ s
+        out, chunk = outs[s], chunks[s]
+        cols = pl.ds(pl.multiple_of((own ^ s) * LANES, LANES), LANES)
+        for i in range(3):
+            out[:, wide + i * LANES : wide + (i + 1) * LANES] = scr[i][:, cols]
+        chunk[:, wide:] = down_ref[...]
         for jv in range(half):
 
-            @pl.when(to == jv)
-            def _(s=s, jv=jv):
-                pieces = [
-                    g_ref[:, i * step + jv * width : i * step + (jv + 1) * width]
-                    for i in range(strips)
-                ]
-                short = out_refs[s].shape[1] - strips * width
-                if short:
-                    pieces.append(jnp.zeros((rows, short), BF))
-                out_refs[s][...] = jnp.concatenate(pieces, axis=1)
-
-
-def pack_heads_body(half, pos_ref, q_in, k_in, v_in, *refs):
-    out_refs, (q_ref, k_ref, v_ref, sem) = refs[:half], refs[half:]
-    fetch((q_in, k_in, v_in), (q_ref, k_ref, v_ref), sem)
-    own = pos_ref[4]
+            @pl.when((mine ^ s) == jv)
+            def _(out=out, chunk=chunk, jv=jv):
+                out[:, :wide] = strip(scr[3], jv)
+                chunk[:, :wide] = strip(up_ref, jv)
+
+
+def stack_body(half, pos_ref, *refs):
     for s in range(half):
-        cols = pl.ds(pl.multiple_of((own ^ s) * LANES, LANES), LANES)
-        out_refs[s][0] = q_ref[:, cols]
-        out_refs[s][1] = k_ref[:, cols]
-        out_refs[s][2] = v_ref[:, cols]
-
-
-def assemble_body(half, pos_ref, *refs):
+        refs[half][pos_ref[0] ^ s] = refs[s][...]
+
+
+def assemble_body(half, wide, pos_ref, *refs):
     pieces, (q_out, kv_out) = refs[:half], refs[half:]
     mine = pos_ref[0]
-    rows = pieces[0].shape[1]
+    rows = pieces[0].shape[0]
     for s in range(half):
         at = pl.ds(pl.multiple_of((mine ^ s) * rows, rows), rows)
-        q_out[at, :] = pieces[s][0]
-        kv_out[0, at, :] = pieces[s][1]
-        kv_out[1, at, :] = pieces[s][2]
-
-
-def ranks_body(half, pos_ref, *refs):
-    pieces, (out_ref, scr) = refs[:half], refs[half:]
-    mine = pos_ref[0]
-    planes = scr.shape[1]
-    for s in range(half):
-        scr[mine ^ s] = pieces[s][...].astype(F32)
-    parts = [scr[j, p] for p in range(planes) for j in range(half)]
-    out_ref[...] = jnp.concatenate(parts, axis=0).astype(BF)
-
-
-def lora_body(half, fsdp, pos_ref, adapt_ref, *refs):
-    grads, out_ref = refs[:-1], refs[-1]
-    mine = pos_ref[0]
-    rows, wide = grads[0].shape
-    for s in range(half):
+        q_out[at, :] = pieces[s][:, wide : wide + LANES]
+        kv_out[0, at, :] = pieces[s][:, wide + LANES : wide + 2 * LANES]
+        kv_out[1, at, :] = pieces[s][:, wide + 2 * LANES :]
+
+
+def ranks_body(*refs):
+    parts = [ref[j].astype(F32) for ref in refs[:-1] for j in range(ref.shape[0])]
+    refs[-1][...] = jnp.concatenate(parts, axis=0).astype(BF)
+
+
+def lora_body(half, fsdp, wide, pos_ref, *refs):
+    adapts, grads, out_ref = refs[:fsdp], refs[fsdp:-1], refs[-1]
+    mine, core = pos_ref[0], pos_ref[2]
+    rows = grads[0].shape[0]
+
+    def write(pieces):
         total = None
         for f in range(fsdp):
-            part = nt(grads[s * fsdp + f][...], adapt_ref[:, f * wide : (f + 1) * wide])
+            left = jnp.concatenate([grads[s * fsdp + f][:, :wide] for s in pieces], axis=0)
+            part = nt(left, adapts[f][:, :wide])
             total = part if total is None else total + part
-        at = pl.ds(pl.multiple_of((mine ^ s) * rows, rows), rows)
-        out_ref[at, :] = adapter_scale * total
+        total = adapter_scale * total
+        for i, s in enumerate(pieces):
+            at = pl.ds(pl.multiple_of((mine ^ s) * rows, rows), rows)
+            out_ref[at, :] = total[i * rows : (i + 1) * rows, :]
+
+    if fsdp == 2:
+        for first in range(0, half, 2):
+
+            @pl.when((mine ^ first) // 2 == core)
+            def _(first=first):
+                write((first, first + 1))
+
+    else:
+        write(tuple(range(half)))
 
 
 def join_body(pos_ref, lora_ref, *refs):
@@ -257,7 +226,8 @@
     refs[-1][...] = total.astype(BF)
 
 
-def project_body(half, planes, fsdp, slot, targets, pos_ref, adapt_ref, *refs):
+def project_body(half, planes, fsdp, slot, wide, targets, pos_ref, *refs):
+    adapts, refs = refs[:fsdp], refs[fsdp:]
     grads = refs[: half * fsdp]
     weights = refs[half * fsdp : -2 - len(targets)]
     n_weights = len(weights)
@@ -265,15 +235,15 @@
     w_scr, d_scr = refs[-2:]
     mine, plane, core, own = pos_ref[0], pos_ref[1], pos_ref[2], pos_ref[4]
     rows_each = weights[0].shape[0]
-    rows, wide = grads[0].shape
+    rows = grads[0].shape[0]
     tail = w_scr.shape[0] - planes * rows_each
     if tail:
         w_scr[planes * rows_each :, :] = jnp.zeros((tail, w_scr.shape[1]), BF)
     for i, t in enumerate(targets):
         cols = pl.ds(pl.multiple_of((own ^ t) * LANES, LANES), LANES)
-        d_cols = pl.ds(pl.multiple_of(fsdp * wide + (own ^ t) * LANES, LANES), LANES)
+        d_cols = pl.ds(pl.multiple_of(wide + (own ^ t) * LANES, LANES), LANES)
         to = slice(i * LANES, (i + 1) * LANES)
-        d_scr[:, to] = adapt_ref[:, d_cols]
+        d_scr[:, to] = adapts[0][:, d_cols]
         if n_weights == planes:
             sources = [lax.rem(plane + (planes - s), planes) for s in range(planes)]
         else:
@@ -291,21 +261,23 @@
     for f in range(fsdp):
         src = lax.rem(core + (fsdp - f), fsdp)
         at = pl.ds(pl.multiple_of(src * slot, 16), slot)
-        up = adapt_ref[:, f * wide : (f + 1) * wide]
+        up = adapts[f][:, :wide]
         low = lax.dot_general(
             up, d_scr[...], (((0,), (0,)), ((), ())), preferred_element_type=F32
         )
         w_scr[at, :] = (w_scr[at, :].astype(F32) + adapter_scale * low[:slot]).astype(BF)
+    acc = None
+    for f in range(fsdp):
+        src = lax.rem(core + (fsdp - f), fsdp)
+        w_at = pl.ds(pl.multiple_of(src * slot, 16), wide)
+        left = jnp.concatenate([grads[s * fsdp + f][:, :wide] for s in range(half)], axis=0)
+        part = nn(left, w_scr[w_at, :])
+        acc = part if acc is None else acc + part
     for s in range(half):
         at = pl.ds(pl.multiple_of((mine ^ s) * rows, rows), rows)
-        acc = None
-        for f in range(fsdp):
-            src = lax.rem(core + (fsdp - f), fsdp)
-            w_at = pl.ds(pl.multiple_of(src * slot, 16), wide)
-            part = nn(grads[s * fsdp + f][...], w_scr[w_at, :])
-            acc = part if acc is None else acc + part
         for i in range(len(targets)):
-            outs[i][at, :] = acc[:, i * LANES : (i + 1) * LANES].astype(BF)
+            block = acc[s * rows : (s + 1) * rows, i * LANES : (i + 1) * LANES]
+            outs[i][at, :] = block.astype(BF)
 
 
 def score_block(key, query, k0, q0):
@@ -317,26 +289,16 @@
     return jnp.where(kpos <= qpos, scores, masked)
 
 
-def middle_body(fsdp, wide, pos_ref, o_ref, adapt_ref, *refs):
-    core, own = pos_ref[2], pos_ref[4]
-    down = adapt_ref[:, pl.ds(pl.multiple_of(fsdp * wide + own * LANES, LANES), LANES)]
-    rows = o_ref.shape[0] // fsdp
-    for s in range(fsdp):
-        to = lax.rem(core + s, fsdp)
-        part = o_ref[pl.ds(pl.multiple_of(to * rows, rows), rows), :]
-        refs[s][...] = nt(part.astype(BF), down)
-
-
-def forward_body(pos_ref, q_ref, kv_ref, far_ref, o_ref, lse_ref, vt_scr, oft_scr):
-    later = pos_ref[3]
+def forward_body(fsdp, wide, pos_ref, q_ref, kv_ref, far_ref, adapt_ref, o_ref, lse_ref, *refs):
+    mid_refs, (vt_scr, oft_scr) = refs[:fsdp], refs[fsdp:]
+    core, later, own = pos_ref[2], pos_ref[3], pos_ref[4]
     tokens = q_ref.shape[0]
     block = min(QUERY_BLOCK, tokens)
     vt_scr[...] = kv_ref[1].T
 
     def finish(q0, block_out, norm):
         qs = slice(q0, q0 + block)
-        out = block_out.T
-        o_ref[qs, :] = out
+        o_ref[qs, :] = block_out.T
         lse_ref[:, qs] = norm
 
     def near(q0):
@@ -368,6 +330,13 @@
                 oft_scr[...], far_prob.astype(BF)
             )
             finish(q0, out / total, top + jnp.log(total))
+
+    down = adapt_ref[:, pl.ds(pl.multiple_of(wide + own * LANES, LANES), LANES)]
+    rows = tokens // fsdp
+    for s in range(fsdp):
+        to = lax.rem(core + s, fsdp)
+        part = o_ref[pl.ds(pl.multiple_of(to * rows, rows), rows), :]
+        mid_refs[s][...] = nt(part.astype(BF), down)
 
 
 def grad_block(key, value, query, grad, norm, delta, k0, q0):
@@ -484,13 +453,13 @@
         down_ref[:, pl.ds(pl.multiple_of(head * LANES, LANES), LANES)] = total[:, wide:]
 
 
-def adapters_body(half, fsdp, planes, pos_ref, o_ref, *refs):
+def adapters_body(half, fsdp, planes, wide, pos_ref, o_ref, *refs):
     both, grads = refs[:fsdp], refs[fsdp : fsdp + half]
     out_ref, scr = refs[fsdp + half :]
     mine, plane, core = pos_ref[0], pos_ref[1], pos_ref[2]
     rank_rows = out_ref.shape[1]
     rank = planes * half * rank_rows
-    rows, wide = grads[0].shape
+    rows = grads[0].shape[0]
     part_rows = both[0].shape[0]
     for s in range(fsdp):
         src = lax.rem(core + (fsdp - s), fsdp)
@@ -498,7 +467,7 @@
     acc = None
     for s in range(half):
         at = pl.ds(pl.multiple_of((mine ^ s) * rows, rows), rows)
-        part = nn(scr[at, :].T[rank:, :], grads[s][...])
+        part = nn(scr[at, :].T[rank:, :], grads[s][:, :wide])
         acc = part if acc is None else acc + part
     acc = adapter_scale * acc
     low = nn(scr[...].T[:rank, :], o_ref[...].astype(BF))
@@ -596,7 +565,9 @@
         in_hbm=True,
     )
     if planes == 4:
-        weights = [weight, along(weight, 1), along(weight, planes - 1)]
+        weights = [weight]
+        for s in (1, planes - 1):
+            weights.append(along(weight, s))
     else:
         weights = [along(weight, s) for s in range(planes)]
     if planes == 4:
@@ -606,60 +577,41 @@
         weights.append(from_plane(inner, (1,), 1, (2,), -1))
         weights.append(from_plane(outer, (1,), -1, (2,), 1))
 
-    grads = call(
-        functools.partial(pack_grad_body, half, strips),
-        [sds((rows, wide), BF)] * half,
-        [],
-        pos,
-        projection_output_gradient,
-        n_scalar=1,
-    )
-    grads = [in_plane(x, s) for s, x in enumerate(grads)]
-    swapped = [across(g, f) for g in grads for f in range(fsdp)]
-
-    raw_ups = [across(adapter_up_matrix, f) for f in range(fsdp)]
-    raw = call(
-        functools.partial(raw_body, fsdp),
-        [sds((rank_rows, fsdp * grad_cols + heads * HEAD_WIDTH), BF)],
-        [pltpu.SemaphoreType.DMA((fsdp + 1,))],
-        *raw_ups,
-        adapter_down_matrix,
-        in_hbm=True,
-    )[0]
-    raws = [along(raw, s) for s in range(planes)]
-    adapter_cols = fsdp * wide + heads * HEAD_WIDTH
-    chunks = call(
-        functools.partial(chunks_body, half, fsdp, strips, wide),
-        [sds((planes, rank_rows, adapter_cols), BF)] * half,
-        [],
-        pos,
-        *raws,
-        n_scalar=1,
-    )
-    chunks = [in_plane(x, s) for s, x in enumerate(chunks)]
-    adapters = call(
-        functools.partial(ranks_body, half),
-        sds((rank, adapter_cols), BF),
-        [pltpu.VMEM((half, planes, rank_rows, adapter_cols), F32)],
-        pos,
-        *chunks,
-        n_scalar=1,
-    )
-
-    packed = call(
-        functools.partial(pack_heads_body, half),
-        [sds((3, rows, LANES), BF)] * half,
-        [pltpu.VMEM(rotated_query_rows.shape, BF)] * 3 + [pltpu.SemaphoreType.DMA((3,))],
-        pos,
+    adapter_cols = wide + heads * HEAD_WIDTH
+    sources = (
         rotated_query_rows,
         rotated_key_rows,
         saved_value_rows,
+        projection_output_gradient,
+        adapter_up_matrix,
+        adapter_down_matrix,
+    )
+    packed = call(
+        functools.partial(pack_body, half, strips, wide),
+        [sds((rows, wide + 3 * LANES), BF)] * half + [sds((rank_rows, adapter_cols), BF)] * half,
+        [pltpu.VMEM(x.shape, BF) for x in sources] + [pltpu.SemaphoreType.DMA((6,))],
+        pos,
+        *sources,
         n_scalar=1,
         in_hbm=True,
     )
-    packed = [in_plane(x, s) for s, x in enumerate(packed)]
+    chunks = [in_plane(x, s) for s, x in enumerate(packed[half:])]
+    packed = [in_plane(x, s) for s, x in enumerate(packed[:half])]
+    swapped = [across(g, f) for g in packed for f in range(fsdp)]
+    adapters = call(
+        functools.partial(stack_body, half),
+        sds((half, rank_rows, adapter_cols), BF),
+        [],
+        pos,
+        *chunks,
+        n_scalar=1,
+    )
+    adapters = [along(adapters, s) for s in range(planes)]
+    adapters = call(ranks_body, sds((rank, adapter_cols), BF), [], *adapters)
+    adapts = [across(adapters, f) for f in range(fsdp)]
+
     query, key_value = call(
-        functools.partial(assemble_body, half),
+        functools.partial(assemble_body, half, wide),
         [sds((tokens, LANES), BF), sds((2, tokens, LANES), BF)],
         [],
         pos,
@@ -668,25 +620,25 @@
     )
     far = to_later(key_value)
     lora = call(
-        functools.partial(lora_body, half, fsdp),
+        functools.partial(lora_body, half, fsdp, wide),
         sds((tokens, rank), F32),
         [],
         pos,
-        adapters,
+        *adapts,
         *swapped,
         n_scalar=1,
     )
 
     def project(targets):
         return call(
-            functools.partial(project_body, half, planes, fsdp, slot, targets),
+            functools.partial(project_body, half, planes, fsdp, slot, wide, targets),
             [sds((tokens, LANES), BF)] * len(targets),
             [
                 pltpu.VMEM((planes * w_rows + wide - slot, LANES * len(targets)), BF),
                 pltpu.VMEM((rank, LANES * len(targets)), BF),
             ],
             pos,
-            adapters,
+            *adapts,
             *swapped,
             *weights,
             n_scalar=1,
@@ -699,22 +651,15 @@
     partial.update({s: in_plane(x, s) for s, x in rest.items()})
 
     part_rows = tokens // fsdp
-    out, norm = call(
-        forward_body,
-        [sds((tokens, LANES), F32), sds((1, tokens), F32)],
+    out, norm, *mids = call(
+        functools.partial(forward_body, fsdp, wide),
+        [sds((tokens, LANES), F32), sds((1, tokens), F32)]
+        + [sds((part_rows, rank), F32)] * fsdp,
         [pltpu.VMEM((LANES, tokens), BF), pltpu.VMEM((LANES, tokens), BF)],
         pos,
         query,
         key_value,
         far,
-        n_scalar=1,
-    )
-    mids = call(
-        functools.partial(middle_body, fsdp, wide),
-        [sds((part_rows, rank), F32)] * fsdp,
-        [],
-        pos,
-        out,
         adapters,
         n_scalar=1,
     )
@@ -724,13 +669,13 @@
     both = call(total_body, sds((part_rows, 2 * rank), BF), [], *both)
     both = [across(both, f) for f in range(fsdp)]
     adapter_grads = call(
-        functools.partial(adapters_body, half, fsdp, planes),
+        functools.partial(adapters_body, half, fsdp, planes, wide),
         sds((n_ctx, rank_rows, wide + HEAD_WIDTH), F32),
         [pltpu.VMEM((tokens, 2 * rank), BF)],
         pos,
         out,
         *both,
-        *grads,
+        *packed,
         n_scalar=1,
     )
     reduced = lax.all_to_all(adapter_grads, "ctx", split_axis=0, concat_axis=0, tiled=True)

time: 104 us -> 103 us (level)
  waiting for transfers between devices: 32.1 us -> 40.4 us
  starting transfers between devices: 45.2 us -> 39.3 us
  Pallas kernels: 24.8 us -> 22.2 us
    ppermute x18 -> x15, starting transfers between devices: 22.2 us -> 17.1 us  [in_plane(): return lax.ppermute(x, 'ctx', [(i, i ^ s) for i in range(n_ctx)])]
    ppermute x5, waiting for transfers between devices: 0.01 us -> 3.9 us  [along(): lax.ppermute(x, 'ctx', [(i, (i + s * half) % n_ctx) for i in range(n_ctx)])]
    ppermute x18 -> x15, waiting for transfers between devices: 19.4 us -> 22.5 us  [in_plane(): return lax.ppermute(x, 'ctx', [(i, i ^ s) for i in range(n_ctx)])]
    pallas_call x21 -> x18, Pallas kernels: 24.8 us -> 22.2 us  [call(): pl.pallas_call(body, out_shape=outs, in_specs=[SM] * n_scalar + [spec] *...]
    ppermute x2, waiting for transfers between devices: 6.6 us -> 9.18 us  [from_plane(): return lax.ppermute(x, 'ctx', route)]
    ppermute x7, waiting for transfers between devices: 3.27 us -> 2 us  [across(): return lax.ppermute(x, 'fsdp', [(i, (i + s) % fsdp) for i in range(fsdp)])]
    ppermute x5, starting transfers between devices: 10.8 us -> 9.65 us  [along(): lax.ppermute(x, 'ctx', [(i, (i + s * half) % n_ctx) for i in range(n_ctx)])]
  transfers between devices with their start and end apart: 35 -> 32, of which waited for: 16 -> 18; matrix products, arithmetic and copies ran while one was open for 0% -> 0% of each run, Pallas kernels for 22% -> 18%
where the time goes in v4:
time: 103 us
  waiting for transfers between devices  40.4 us (39%)
  starting transfers between devices  39.3 us (38%)
  Pallas kernels  22.2 us (22%)
    ppermute x15, waiting for transfers between devices, in_plane(): return lax.ppermute(x, 'ctx', [(i, i ^ s) for i in range(n_ctx)])  22.5 us
    pallas_call x18, Pallas kernels, call(): pl.pallas_call(body, out_shape=outs, in_specs=[SM] * n_scalar + [spec] *...  22.2 us
    ppermute x15, starting transfers between devices, in_plane(): return lax.ppermute(x, 'ctx', [(i, i ^ s) for i in range(n_ctx)])  17.1 us
    ppermute x5, starting transfers between devices, along(): lax.ppermute(x, 'ctx', [(i, (i + s * half) % n_ctx) for i in range(n_ctx)])  9.65 us
    ppermute x2, waiting for transfers between devices, from_plane(): return lax.ppermute(x, 'ctx', route)  9.18 us
    ppermute x1, starting transfers between devices, to_later(): return lax.ppermute(x, ('ctx', 'fsdp'), pairs)  4.59 us
    ppermute x5, waiting for transfers between devices, along(): lax.ppermute(x, 'ctx', [(i, (i + s * half) % n_ctx) for i in range(n_ctx)])  3.9 us
    all_to_all x1, starting transfers between devices, on_device(): lax.all_to_all(adapter_grads, 'ctx', split_axis=0, concat_axis=0, tiled=T...  3.52 us
  transfers between devices with their start and end apart: 32, of which 18 were waited for; matrix products, arithmetic and copies ran while one was open for 0% of the time, Pallas kernels for 18%

profile of v4, /device:TPU:0, one launch (start us, length us, event | category | flops | bytes accessed | tf_op | source)
XLA Modules:
  0.0 102.9 jit_solution(5495153145049062062)
XLA Ops:
  0.6 2.1 %shard_map.132.refs_10_ = bf16[320,512]{1,0:T(8,128)(2,1)S(1)} custom-call(s32[320,512]{1,0:T(8,128)} %codes_in.1, s32[8,320]{1,0:T(8,128)} %bitcast.7, f32[2,128]{1,0:T(2,128)} %bitcast.8), custom_call_target="tpu_custom_call" | custom-call | tf_op jit(solution)/shard_map/pallas_call | solution.py:63
  2.8 5.1 %collective-permute-start.15 = (bf16[320,512]{1,0:T(8,128)(2,1)S(1)}, bf16[320,512]{1,0:T(8,128)(2,1)S(1)}, u32[]{:S(2)}, u32[]{:S(2)}) collective-permute-start(bf16[320,512]{1,0:T(8,128)(2,1)S(1)} %shard_map.132.refs_10_), channel_id=1, source_target_pairs={{0,24},{2,26},{4,28},{6,30},{8,0},{10,2},{12,4},{14,6},{16,8},{18,... | collective-permute-start | bytes 983048 | tf_op jit(solution)/shard_map/ppermute | solution.py:528
  7.9 0.0 collective-permute-start.14
  7.9 0.1 stack.23.pos_ref
  8.0 2.8 %shard_map.128 = (bf16[192,1024]{1,0:T(8,128)(2,1)S(1)}, bf16[192,1024]{1,0:T(8,128)(2,1)S(1)}, bf16[192,1024]{1,0:T(8,128)(2,1)S(1)}, bf16[192,1024]{1,0:T(8,12...) custom-call(s32[5]{0:T(128)S(1)} %stack.23.pos_ref, ...), custom_call_target="tpu_custom_call" | custom-call | tf_op jit(solution)/shard_map/pallas_call | solution.py:63
  10.8 1.6 %collective-permute-start.3 = (bf16[4,1152]{1,0:T(4,128)(2,1)S(1)}, bf16[4,1152]{1,0:T(4,128)(2,1)S(1)}, u32[]{:S(2)}, u32[]{:S(2)}) collective-permute-start(bf16[4,1152]{1,0:T(4,128)(2,1)S(1)} %get-tuple-element.47), channel_id=1, source_target_pairs={{0,2},{2,0},{4,6},{6,4},{8,10},{10,8},{12,14},{14,12},{16,18},{18,... | collective-permute-start | bytes 27656 | tf_op jit(solution)/shard_map/ppermute | solution.py:523
  12.3 1.5 %collective-permute-start.4 = (bf16[4,1152]{1,0:T(4,128)(2,1)S(1)}, bf16[4,1152]{1,0:T(4,128)(2,1)S(1)}, u32[]{:S(2)}, u32[]{:S(2)}) collective-permute-start(bf16[4,1152]{1,0:T(4,128)(2,1)S(1)} %get-tuple-element.48), channel_id=1, source_target_pairs={{0,4},{2,6},{4,0},{6,2},{8,12},{10,14},{12,8},{14,10},{16,20},{18,... | collective-permute-start | bytes 27656 | tf_op jit(solution)/shard_map/ppermute | solution.py:523
  13.8 0.5 collective-permute-start.5
  14.3 0.2 collective-permute-done.3.refs_1_
  14.5 1.5 %collective-permute-done.4.refs_2_ = bf16[4,1152]{1,0:T(4,128)(2,1)S(1)} collective-permute-done((bf16[4,1152]{1,0:T(4,128)(2,1)S(1)}, bf16[4,1152]{1,0:T(4,128)(2,1)S(1)}, u32[]{:S(2)}, u32[]{:S(2)}) %collective-permute-start.4) | collective-permute-done | bytes 9248 | tf_op jit(solution)/shard_map/ppermute | solution.py:523
  16.0 2.4 %collective-permute-done.5.refs_3_ = bf16[4,1152]{1,0:T(4,128)(2,1)S(1)} collective-permute-done((bf16[4,1152]{1,0:T(4,128)(2,1)S(1)}, bf16[4,1152]{1,0:T(4,128)(2,1)S(1)}, u32[]{:S(2)}, u32[]{:S(2)}) %collective-permute-start.5) | collective-permute-done | bytes 9248 | tf_op jit(solution)/shard_map/ppermute | solution.py:523
  18.4 0.5 shard_map.130.refs_0_
  19.0 3.9 %collective-permute-start.8 = (bf16[4,4,1152]{2,1,0:T(4,128)(2,1)S(1)}, bf16[4,4,1152]{2,1,0:T(4,128)(2,1)S(1)}, u32[]{:S(2)}, u32[]{:S(2)}) collective-permute-start(bf16[4,4,1152]{2,1,0:T(4,128)(2,1)S(1)} %shard_map.130.refs_0_), channel_id=1, source_target_pairs={{0,24},{2,26},{4,28},{6,30},{8,0},{10,2},{12,4},{14,6},{16,8},{18,... | collective-permute-start | bytes 110600 | tf_op jit(solution)/shard_map/ppermute | solution.py:528
  22.8 0.6 collective-permute-start.6
  23.5 1.0 collective-permute-done.8.refs_3_
  24.5 0.7 collective-permute-start
  25.2 2.5 %collective-permute-done.7.refs_2_ = bf16[4,4,1152]{2,1,0:T(4,128)(2,1)S(1)} collective-permute-done((bf16[4,4,1152]{2,1,0:T(4,128)(2,1)S(1)}, bf16[4,4,1152]{2,1,0:T(4,128)(2,1)S(1)}, u32[]{:S(2)}, u32[]{:S(2)}) %collective-permute-start.7) | collective-permute-done | bytes 36896 | tf_op jit(solution)/shard_map/ppermute | solution.py:528
  27.7 0.5 collective-permute-start.1
  28.2 0.4 collective-permute-done.6.refs_1_
  28.6 1.1 %collective-permute-start.2 = (bf16[192,1024]{1,0:T(8,128)(2,1)S(1)}, bf16[192,1024]{1,0:T(8,128)(2,1)S(1)}, u32[]{:S(2)}, u32[]{:S(2)}) collective-permute-start(bf16[192,1024]{1,0:T(8,128)(2,1)S(1)} %get-tuple-element.43), channel_id=1, source_target_pairs={{0,6},{2,4},{4,2},{6,0},{8,14},{10,12},{12,10},{14,8},{16,22},{18,... | collective-permute-start | bytes 1179656 | tf_op jit(solution)/shard_map/ppermute | solution.py:523
  29.7 0.1 collective-permute-start.9
  29.8 0.5 collective-permute-start.10
  30.3 0.6 shard_map.133
  30.9 0.3 collective-permute-done.9.refs_1_
  31.2 0.7 collective-permute-start.16
  31.9 4.6 %collective-permute-done.refs_1_.refs_4_.refs_3_ = bf16[192,1024]{1,0:T(8,128)(2,1)S(1)} collective-permute-done((bf16[192,1024]{1,0:T(8,128)(2,1)S(1)}, bf16[192,1024]{1,0:T(8,128)(2,1)S(1)}, u32[]{:S(2)}, u32[]{:S(2)}) %collective-permute-start) | collective-permute-done | bytes 393248 | tf_op jit(solution)/shard_map/ppermute | solution.py:523
  36.5 7.8 %collective-permute-done.1.refs_2_.refs_6_.refs_4_ = bf16[192,1024]{1,0:T(8,128)(2,1)S(1)} collective-permute-done((bf16[192,1024]{1,0:T(8,128)(2,1)S(1)}, bf16[192,1024]{1,0:T(8,128)(2,1)S(1)}, u32[]{:S(2)}, u32[]{:S(2)}) %collective-permute-start.1) | collective-permute-done | bytes 393248 | tf_op jit(solution)/shard_map/ppermute | solution.py:523
  44.2 0.5 collective-permute-start.13
  44.7 1.3 %collective-permute-start.17 = (bf16[320,512]{1,0:T(8,128)(2,1)S(1)}, bf16[320,512]{1,0:T(8,128)(2,1)S(1)}, u32[]{:S(2)}, u32[]{:S(2)}) collective-permute-start(bf16[320,512]{1,0:T(8,128)(2,1)S(1)} %get-tuple-element.51), channel_id=1, source_target_pairs={{8,0},{10,2},{12,4},{14,6},{16,24},{18,26},{20,28},{22,30},{9,1},{... | collective-permute-start | bytes 983048 | tf_op jit(solution)/shard_map/ppermute | solution.py:535
  46.0 0.6 shard_map.129
  46.7 4.6 %collective-permute-start.21 = (bf16[2,768,128]{2,1,0:T(8,128)(2,1)S(1)}, bf16[2,768,128]{2,1,0:T(8,128)(2,1)S(1)}, u32[]{:S(2)}, u32[]{:S(2)}) collective-permute-start(bf16[2,768,128]{2,1,0:T(8,128)(2,1)S(1)} %get-tuple-element.45.kv_ref), channel_id=1, source_target_pairs={{0,8},{2,10},{5,13},{7,15},{9,17},{11,19},{12,20},{14,22},{16,24},... | collective-permute-start | bytes 1179656 | tf_op jit(solution)/shard_map/ppermute | solution.py:550
  51.3 9.2 %collective-permute-done.17.refs_14_ = bf16[320,512]{1,0:T(8,128)(2,1)S(1)} collective-permute-done((bf16[320,512]{1,0:T(8,128)(2,1)S(1)}, bf16[320,512]{1,0:T(8,128)(2,1)S(1)}, u32[]{:S(2)}, u32[]{:S(2)}) %collective-permute-start.17) | collective-permute-done | bytes 327712 | tf_op jit(solution)/shard_map/ppermute | solution.py:535
  60.5 1.9 %shard_map.135 = (bf16[768,128]{1,0:T(8,128)(2,1)S(1)}, bf16[768,128]{1,0:T(8,128)(2,1)S(1)}) custom-call(s32[5]{0:T(128)S(1)} %stack.23.pos_ref, bf16[64,1152]{1,0:T(8,128)(2,1)S(1)} %shard_map.131.refs_0_.adapt_ref, bf16[64,1152]{1,0:T(8,128)(2,1)S(1)} %collective-permute-done.9.refs_1_, bf16[192,1024]{1,0:T(8,128)(2,1)S(1)} %get-tuple-element.40.refs_0_.refs_2_, ...), custom_call_target="tpu_custom_call" | custom-call | tf_op jit(solution)/shard_map/pallas_call | solution.py:63
  62.4 1.8 %collective-permute-start.19 = (bf16[768,128]{1,0:T(8,128)(2,1)S(1)}, bf16[768,128]{1,0:T(8,128)(2,1)S(1)}, u32[]{:S(2)}, u32[]{:S(2)}) collective-permute-start(bf16[768,128]{1,0:T(8,128)(2,1)S(1)} %get-tuple-element.54), channel_id=1, source_target_pairs={{0,4},{2,6},{4,0},{6,2},{8,12},{10,14},{12,8},{14,10},{16,20},{18,... | collective-permute-start | bytes 589832 | tf_op jit(solution)/shard_map/ppermute | solution.py:523
  64.2 1.4 %collective-permute-start.20 = (bf16[768,128]{1,0:T(8,128)(2,1)S(1)}, bf16[768,128]{1,0:T(8,128)(2,1)S(1)}, u32[]{:S(2)}, u32[]{:S(2)}) collective-permute-start(bf16[768,128]{1,0:T(8,128)(2,1)S(1)} %get-tuple-element.55), channel_id=1, source_target_pairs={{0,6},{2,4},{4,2},{6,0},{8,14},{10,12},{12,10},{14,8},{16,22},{18,... | collective-permute-start | bytes 589832 | tf_op jit(solution)/shard_map/ppermute | solution.py:523
  65.6 1.8 %shard_map.134 = (bf16[768,128]{1,0:T(8,128)(2,1)S(1)}, bf16[768,128]{1,0:T(8,128)(2,1)S(1)}) custom-call(s32[5]{0:T(128)S(1)} %stack.23.pos_ref, bf16[64,1152]{1,0:T(8,128)(2,1)S(1)} %shard_map.131.refs_0_.adapt_ref, bf16[64,1152]{1,0:T(8,128)(2,1)S(1)} %collective-permute-done.9.refs_1_, bf16[192,1024]{1,0:T(8,128)(2,1)S(1)} %get-tuple-element.40.refs_0_.refs_2_, ...), custom_call_target="tpu_custom_call" | custom-call | tf_op jit(solution)/shard_map/pallas_call | solution.py:63
  67.5 0.4 collective-permute-start.18
  67.8 2.2 %shard_map.136 = (f32[768,128]{1,0:T(8,128)S(1)}, f32[1,768]{1,0:T(1,128)S(1)}, f32[384,64]{1,0:T(8,128)S(1)}, f32[384,64]{1,0:T(8,128)S(1)}) custom-call(s32[5]{0:T(128)S(1)} %stack.23.pos_ref, bf16[768,128]{1,0:T(8,128)(2,1)S(1)} %get-tuple-element.44.q_ref.refs_4_, bf16[2,768,128]{2,1,0:T(8,128)(2,1)S(1)} %get-tuple-element.45.kv_ref, ...), custom_call_target="tpu_custom_call" | custom-call | tf_op jit(solution)/shard_map/pallas_call | solution.py:63
  70.1 0.1 collective-permute-start.26
  70.1 1.0 shard_map.141.lora_ref
  71.1 0.5 collective-permute-done.26.refs_1_
  71.6 0.6 shard_map.142.refs_0_
  72.2 3.4 %collective-permute-start.29 = (bf16[384,128]{1,0:T(8,128)(2,1)S(1)}, bf16[384,128]{1,0:T(8,128)(2,1)S(1)}, u32[]{:S(2)}, u32[]{:S(2)}) collective-permute-start(bf16[384,128]{1,0:T(8,128)(2,1)S(1)} %shard_map.142.refs_0_), channel_id=1, source_target_pairs={{0,6},{2,4},{4,2},{6,0},{8,14},{10,12},{12,10},{14,8},{16,22},{18,... | collective-permute-start | bytes 294920 | tf_op jit(solution)/shard_map/ppermute | solution.py:523
  75.6 0.7 collective-permute-start.27
  76.3 1.0 shard_map.137
  77.3 1.3 %collective-permute-start.22 = (bf16[2,768,128]{2,1,0:T(8,128)(2,1)S(1)}, bf16[2,768,128]{2,1,0:T(8,128)(2,1)S(1)}, u32[]{:S(2)}, u32[]{:S(2)}) collective-permute-start(bf16[2,768,128]{2,1,0:T(8,128)(2,1)S(1)} %get-tuple-element.63), channel_id=1, source_target_pairs={{8,0},{10,2},{13,5},{15,7},{17,9},{19,11},{20,12},{22,14},{24,16},... | collective-permute-start | bytes 1179656 | tf_op jit(solution)/shard_map/ppermute | solution.py:553
  78.6 0.2 collective-permute-done.29.refs_3_
  78.8 2.0 %collective-permute-done.28.refs_2_ = bf16[384,128]{1,0:T(8,128)(2,1)S(1)} collective-permute-done((bf16[384,128]{1,0:T(8,128)(2,1)S(1)}, bf16[384,128]{1,0:T(8,128)(2,1)S(1)}, u32[]{:S(2)}, u32[]{:S(2)}) %collective-permute-start.28) | collective-permute-done | bytes 98336 | tf_op jit(solution)/shard_map/ppermute | solution.py:523
  80.8 0.4 collective-permute-done.27.refs_1_
  81.3 0.1 shard_map.143.refs_0_
  81.3 0.1 collective-permute-start.30
  81.4 1.3 %collective-permute-done.30.refs_1_ = bf16[384,128]{1,0:T(8,128)(2,1)S(1)} collective-permute-done((bf16[384,128]{1,0:T(8,128)(2,1)S(1)}, bf16[384,128]{1,0:T(8,128)(2,1)S(1)}, u32[]{:S(2)}, u32[]{:S(2)}) %collective-permute-start.30) | collective-permute-done | bytes 98336 | tf_op jit(solution)/shard_map/ppermute | solution.py:540
  82.7 1.7 %shard_map.144 = f32[16,4,768]{2,1,0:T(4,128)} custom-call(s32[5]{0:T(128)S(1)} %stack.23.pos_ref, f32[768,128]{1,0:T(8,128)S(1)} %get-tuple-element.56.refs_6_.o_ref, bf16[384,128]{1,0:T(8,128)(2,1)S(1)} %shard_map.143.refs_0_, bf16[384,128]{1,0:T(8,128)(2,1)S(1)} %collective-permute-done.30.refs_1_, ...), custom_call_target="tpu_custom_call" | custom-call | tf_op jit(solution)/shard_map/pallas_call | solution.py:63
  84.4 3.5 %all-to-all-start = ((f32[16,4,768]{2,1,0:T(4,128)}), f32[16,4,768]{2,1,0:T(4,128)S(1)}, u32[]{:S(2)}, u32[]{:S(2)}) async-start(f32[16,4,768]{2,1,0:T(4,128)} %shard_map.144), calls=%async_computation | async-start | bytes 393216 | tf_op jit(solution)/shard_map/all_to_all | solution.py:681
  87.9 1.9 %shard_map.138 = (bf16[768,128]{1,0:T(8,128)(2,1)S(1)}, f32[2,768,128]{2,1,0:T(8,128)S(1)}) custom-call(s32[5]{0:T(128)S(1)} %stack.23.pos_ref, bf16[768,128]{1,0:T(8,128)(2,1)S(1)} %get-tuple-element.44.q_ref.refs_4_, bf16[2,768,128]{2,1,0:T(8,128)(2,1)S(1)} %get-tuple-element.45.kv_ref, bf16[768,128]{1,0:T(8,128)(2,1)S(1)} %get-tuple-element.58.do_ref, ...), custom_call_target="tpu_custom_call" | custom-call | tf_op jit(solution)/shard_map/pallas_call | solution.py:63
  89.8 0.6 shard_map.139
  90.4 1.9 %collective-permute-start.23 = (bf16[3,192,128]{2,1,0:T(8,128)(2,1)S(1)}, bf16[3,192,128]{2,1,0:T(8,128)(2,1)S(1)}, u32[]{:S(2)}, u32[]{:S(2)}) collective-permute-start(bf16[3,192,128]{2,1,0:T(8,128)(2,1)S(1)} %get-tuple-element.65), channel_id=1, source_target_pairs={{0,2},{2,0},{4,6},{6,4},{8,10},{10,8},{12,14},{14,12},{16,18},{18,... | collective-permute-start | bytes 442376 | tf_op jit(solution)/shard_map/ppermute | solution.py:523
  92.3 1.5 %collective-permute-start.24 = (bf16[3,192,128]{2,1,0:T(8,128)(2,1)S(1)}, bf16[3,192,128]{2,1,0:T(8,128)(2,1)S(1)}, u32[]{:S(2)}, u32[]{:S(2)}) collective-permute-start(bf16[3,192,128]{2,1,0:T(8,128)(2,1)S(1)} %get-tuple-element.66), channel_id=1, source_target_pairs={{0,4},{2,6},{4,0},{6,2},{8,12},{10,14},{12,8},{14,10},{16,20},{18,... | collective-permute-start | bytes 442376 | tf_op jit(solution)/shard_map/ppermute | solution.py:523
  93.7 0.2 collective-permute-start.25
  94.0 2.8 %all-to-all-done.in_ref = f32[16,4,768]{2,1,0:T(4,128)S(1)} async-done(((f32[16,4,768]{2,1,0:T(4,128)}), f32[16,4,768]{2,1,0:T(4,128)S(1)}, u32[]{:S(2)}, u32[]{:S(2)}) %all-to-all-start) | async-done | bytes 196640 | tf_op jit(solution)/shard_map/all_to_all | solution.py:681
  96.8 1.2 %shard_map.145 = (f32[4,2560]{1,0:T(4,128)}, f32[4,512]{1,0:T(4,128)}) custom-call(s32[5]{0:T(128)S(1)} %stack.23.pos_ref, f32[16,4,768]{2,1,0:T(4,128)S(1)} %all-to-all-done.in_ref), custom_call_target="tpu_custom_call" | custom-call | tf_op jit(solution)/shard_map/pallas_call | solution.py:63
  98.0 2.1 %collective-permute-done.24.refs_2_ = bf16[3,192,128]{2,1,0:T(8,128)(2,1)S(1)} collective-permute-done((bf16[3,192,128]{2,1,0:T(8,128)(2,1)S(1)}, bf16[3,192,128]{2,1,0:T(8,128)(2,1)S(1)}, u32[]{:S(2)}, u32[]{:S(2)}) %collective-permute-start.24) | collective-permute-done | bytes 147488 | tf_op jit(solution)/shard_map/ppermute | solution.py:523
  100.2 1.3 %collective-permute-done.25.refs_3_ = bf16[3,192,128]{2,1,0:T(8,128)(2,1)S(1)} collective-permute-done((bf16[3,192,128]{2,1,0:T(8,128)(2,1)S(1)}, bf16[3,192,128]{2,1,0:T(8,128)(2,1)S(1)}, u32[]{:S(2)}, u32[]{:S(2)}) %collective-permute-start.25) | collective-permute-done | bytes 147488 | tf_op jit(solution)/shard_map/ppermute | solution.py:523
  101.4 1.4 %shard_map.140 = (bf16[192,512]{1,0:T(8,128)(2,1)}, bf16[192,512]{1,0:T(8,128)(2,1)}, bf16[192,512]{1,0:T(8,128)(2,1)}) custom-call(s32[5]{0:T(128)S(1)} %stack.23.pos_ref, bf16[3,192,128]{2,1,0:T(8,128)(2,1)S(1)} %get-tuple-element.64.refs_0_, bf16[3,192,128]{2,1,0:T(8,128)(2,1)S(1)} %collective-permute-done.23.refs_1_, ...), custom_call_target="tpu_custom_call" | custom-call | tf_op jit(solution)/shard_map/pallas_call | solution.py:63
  (19 shorter events, 0.1 us)
Async XLA Ops:
  2.8 27.0 %collective-permute-start.15 = (bf16[320,512]{1,0:T(8,128)(2,1)S(1)}, bf16[320,512]{1,0:T(8,128)(2,1)S(1)}, u32[]{:S(2)}, u32[]{:S(2)}) collective-permute-start(bf16[320,512]{1,0:T(8,128)(2,1)S(1)} %shard_map.132.refs_10_), channel_id=1, source_target_pairs={{0,24},{2,26},{4,28},{6,30},{8,0},{10,2},{12,4},{14,6},{16,8},{18,... | collective-permute-start | bytes 983048 | tf_op jit(solution)/shard_map/ppermute | solution.py:528
  7.9 21.9 %collective-permute-start.14 = (bf16[320,512]{1,0:T(8,128)(2,1)S(1)}, bf16[320,512]{1,0:T(8,128)(2,1)S(1)}, u32[]{:S(2)}, u32[]{:S(2)}) collective-permute-start(bf16[320,512]{1,0:T(8,128)(2,1)S(1)} %shard_map.132.refs_10_), channel_id=1, source_target_pairs={{0,8},{2,10},{4,12},{6,14},{8,16},{10,18},{12,20},{14,22},{16,24},... | collective-permute-start | bytes 983048 | tf_op jit(solution)/shard_map/ppermute | solution.py:528
  10.8 3.7 %collective-permute-start.3 = (bf16[4,1152]{1,0:T(4,128)(2,1)S(1)}, bf16[4,1152]{1,0:T(4,128)(2,1)S(1)}, u32[]{:S(2)}, u32[]{:S(2)}) collective-permute-start(bf16[4,1152]{1,0:T(4,128)(2,1)S(1)} %get-tuple-element.47), channel_id=1, source_target_pairs={{0,2},{2,0},{4,6},{6,4},{8,10},{10,8},{12,14},{14,12},{16,18},{18,... | collective-permute-start | bytes 27656 | tf_op jit(solution)/shard_map/ppermute | solution.py:523
  12.3 3.7 %collective-permute-start.4 = (bf16[4,1152]{1,0:T(4,128)(2,1)S(1)}, bf16[4,1152]{1,0:T(4,128)(2,1)S(1)}, u32[]{:S(2)}, u32[]{:S(2)}) collective-permute-start(bf16[4,1152]{1,0:T(4,128)(2,1)S(1)} %get-tuple-element.48), channel_id=1, source_target_pairs={{0,4},{2,6},{4,0},{6,2},{8,12},{10,14},{12,8},{14,10},{16,20},{18,... | collective-permute-start | bytes 27656 | tf_op jit(solution)/shard_map/ppermute | solution.py:523
  13.8 4.6 %collective-permute-start.5 = (bf16[4,1152]{1,0:T(4,128)(2,1)S(1)}, bf16[4,1152]{1,0:T(4,128)(2,1)S(1)}, u32[]{:S(2)}, u32[]{:S(2)}) collective-permute-start(bf16[4,1152]{1,0:T(4,128)(2,1)S(1)} %get-tuple-element.49), channel_id=1, source_target_pairs={{0,6},{2,4},{4,2},{6,0},{8,14},{10,12},{12,10},{14,8},{16,22},{18,... | collective-permute-start | bytes 27656 | tf_op jit(solution)/shard_map/ppermute | solution.py:523
  19.0 5.5 %collective-permute-start.8 = (bf16[4,4,1152]{2,1,0:T(4,128)(2,1)S(1)}, bf16[4,4,1152]{2,1,0:T(4,128)(2,1)S(1)}, u32[]{:S(2)}, u32[]{:S(2)}) collective-permute-start(bf16[4,4,1152]{2,1,0:T(4,128)(2,1)S(1)} %shard_map.130.refs_0_), channel_id=1, source_target_pairs={{0,24},{2,26},{4,28},{6,30},{8,0},{10,2},{12,4},{14,6},{16,8},{18,... | collective-permute-start | bytes 110600 | tf_op jit(solution)/shard_map/ppermute | solution.py:528
  22.8 4.9 %collective-permute-start.7 = (bf16[4,4,1152]{2,1,0:T(4,128)(2,1)S(1)}, bf16[4,4,1152]{2,1,0:T(4,128)(2,1)S(1)}, u32[]{:S(2)}, u32[]{:S(2)}) collective-permute-start(bf16[4,4,1152]{2,1,0:T(4,128)(2,1)S(1)} %shard_map.130.refs_0_), channel_id=1, source_target_pairs={{0,16},{2,18},{4,20},{6,22},{8,24},{10,26},{12,28},{14,30},{16,0},... | collective-permute-start | bytes 110600 | tf_op jit(solution)/shard_map/ppermute | solution.py:528
  22.8 5.8 %collective-permute-start.6 = (bf16[4,4,1152]{2,1,0:T(4,128)(2,1)S(1)}, bf16[4,4,1152]{2,1,0:T(4,128)(2,1)S(1)}, u32[]{:S(2)}, u32[]{:S(2)}) collective-permute-start(bf16[4,4,1152]{2,1,0:T(4,128)(2,1)S(1)} %shard_map.130.refs_0_), channel_id=1, source_target_pairs={{0,8},{2,10},{4,12},{6,14},{8,16},{10,18},{12,20},{14,22},{16,24},... | collective-permute-start | bytes 110600 | tf_op jit(solution)/shard_map/ppermute | solution.py:528
  24.5 12.0 %collective-permute-start = (bf16[192,1024]{1,0:T(8,128)(2,1)S(1)}, bf16[192,1024]{1,0:T(8,128)(2,1)S(1)}, u32[]{:S(2)}, u32[]{:S(2)}) collective-permute-start(bf16[192,1024]{1,0:T(8,128)(2,1)S(1)} %get-tuple-element.41), channel_id=1, source_target_pairs={{0,2},{2,0},{4,6},{6,4},{8,10},{10,8},{12,14},{14,12},{16,18},{18,... | collective-permute-start | bytes 1179656 | tf_op jit(solution)/shard_map/ppermute | solution.py:523
  27.7 16.5 %collective-permute-start.1 = (bf16[192,1024]{1,0:T(8,128)(2,1)S(1)}, bf16[192,1024]{1,0:T(8,128)(2,1)S(1)}, u32[]{:S(2)}, u32[]{:S(2)}) collective-permute-start(bf16[192,1024]{1,0:T(8,128)(2,1)S(1)} %get-tuple-element.42), channel_id=1, source_target_pairs={{0,4},{2,6},{4,0},{6,2},{8,12},{10,14},{12,8},{14,10},{16,20},{18,... | collective-permute-start | bytes 1179656 | tf_op jit(solution)/shard_map/ppermute | solution.py:523
  28.6 15.6 %collective-permute-start.2 = (bf16[192,1024]{1,0:T(8,128)(2,1)S(1)}, bf16[192,1024]{1,0:T(8,128)(2,1)S(1)}, u32[]{:S(2)}, u32[]{:S(2)}) collective-permute-start(bf16[192,1024]{1,0:T(8,128)(2,1)S(1)} %get-tuple-element.43), channel_id=1, source_target_pairs={{0,6},{2,4},{4,2},{6,0},{8,14},{10,12},{12,10},{14,8},{16,22},{18,... | collective-permute-start | bytes 1179656 | tf_op jit(solution)/shard_map/ppermute | solution.py:523
  29.7 1.4 %collective-permute-start.9 = (bf16[64,1152]{1,0:T(8,128)(2,1)S(1)}, bf16[64,1152]{1,0:T(8,128)(2,1)S(1)}, u32[]{:S(2)}, u32[]{:S(2)}) collective-permute-start(bf16[64,1152]{1,0:T(8,128)(2,1)S(1)} %shard_map.131.refs_0_.adapt_ref), channel_id=1, source_target_pairs={{0,1},{1,0},{2,3},{3,2},{4,5},{5,4},{6,7},{7,6},{8,9},{9,8},{10,11... | collective-permute-start | bytes 442376 | tf_op jit(solution)/shard_map/ppermute | solution.py:540
  29.8 14.9 %collective-permute-start.10 = (bf16[192,1024]{1,0:T(8,128)(2,1)S(1)}, bf16[192,1024]{1,0:T(8,128)(2,1)S(1)}, u32[]{:S(2)}, u32[]{:S(2)}) collective-permute-start(bf16[192,1024]{1,0:T(8,128)(2,1)S(1)} %get-tuple-element.40.refs_0_.refs_2_), channel_id=1, source_target_pairs={{0,1},{1,0},{2,3},{3,2},{4,5},{5,4},{6,7},{7,6},{8,9},{9,8},{10,11... | collective-permute-start | bytes 1179656 | tf_op jit(solution)/shard_map/ppermute | solution.py:540
  31.2 15.5 %collective-permute-start.16 = (bf16[320,512]{1,0:T(8,128)(2,1)S(1)}, bf16[320,512]{1,0:T(8,128)(2,1)S(1)}, u32[]{:S(2)}, u32[]{:S(2)}) collective-permute-start(bf16[320,512]{1,0:T(8,128)(2,1)S(1)} %get-tuple-element.50), channel_id=1, source_target_pairs={{8,16},{10,18},{12,20},{14,22},{16,8},{18,10},{20,12},{22,14},{9,1... | collective-permute-start | bytes 983048 | tf_op jit(solution)/shard_map/ppermute | solution.py:535
  36.5 24.0 %collective-permute-start.11 = (bf16[192,1024]{1,0:T(8,128)(2,1)S(1)}, bf16[192,1024]{1,0:T(8,128)(2,1)S(1)}, u32[]{:S(2)}, u32[]{:S(2)}) collective-permute-start(bf16[192,1024]{1,0:T(8,128)(2,1)S(1)} %collective-permute-done.refs_1_.refs_4_.refs_3_), channel_id=1, source_target_pairs={{0,1},{1,0},{2,3},{3,2},{4,5},{5,4},{6,7},{7,6},{8,9},{9,8},{10,11... | collective-permute-start | bytes 1179656 | tf_op jit(solution)/shard_map/ppermute | solution.py:540
  44.2 16.3 %collective-permute-start.12 = (bf16[192,1024]{1,0:T(8,128)(2,1)S(1)}, bf16[192,1024]{1,0:T(8,128)(2,1)S(1)}, u32[]{:S(2)}, u32[]{:S(2)}) collective-permute-start(bf16[192,1024]{1,0:T(8,128)(2,1)S(1)} %collective-permute-done.1.refs_2_.refs_6_.refs_4_), channel_id=1, source_target_pairs={{0,1},{1,0},{2,3},{3,2},{4,5},{5,4},{6,7},{7,6},{8,9},{9,8},{10,11... | collective-permute-start | bytes 1179656 | tf_op jit(solution)/shard_map/ppermute | solution.py:540
  44.2 16.2 %collective-permute-start.13 = (bf16[192,1024]{1,0:T(8,128)(2,1)S(1)}, bf16[192,1024]{1,0:T(8,128)(2,1)S(1)}, u32[]{:S(2)}, u32[]{:S(2)}) collective-permute-start(bf16[192,1024]{1,0:T(8,128)(2,1)S(1)} %collective-permute-done.2.refs_3_.refs_8_.refs_5_), channel_id=1, source_target_pairs={{0,1},{1,0},{2,3},{3,2},{4,5},{5,4},{6,7},{7,6},{8,9},{9,8},{10,11... | collective-permute-start | bytes 1179656 | tf_op jit(solution)/shard_map/ppermute | solution.py:540
  44.7 15.7 %collective-permute-start.17 = (bf16[320,512]{1,0:T(8,128)(2,1)S(1)}, bf16[320,512]{1,0:T(8,128)(2,1)S(1)}, u32[]{:S(2)}, u32[]{:S(2)}) collective-permute-start(bf16[320,512]{1,0:T(8,128)(2,1)S(1)} %get-tuple-element.51), channel_id=1, source_target_pairs={{8,0},{10,2},{12,4},{14,6},{16,24},{18,26},{20,28},{22,30},{9,1},{... | collective-permute-start | bytes 983048 | tf_op jit(solution)/shard_map/ppermute | solution.py:535
  46.7 21.1 %collective-permute-start.21 = (bf16[2,768,128]{2,1,0:T(8,128)(2,1)S(1)}, bf16[2,768,128]{2,1,0:T(8,128)(2,1)S(1)}, u32[]{:S(2)}, u32[]{:S(2)}) collective-permute-start(bf16[2,768,128]{2,1,0:T(8,128)(2,1)S(1)} %get-tuple-element.45.kv_ref), channel_id=1, source_target_pairs={{0,8},{2,10},{5,13},{7,15},{9,17},{11,19},{12,20},{14,22},{16,24},... | collective-permute-start | bytes 1179656 | tf_op jit(solution)/shard_map/ppermute | solution.py:550
  62.4 13.3 %collective-permute-start.19 = (bf16[768,128]{1,0:T(8,128)(2,1)S(1)}, bf16[768,128]{1,0:T(8,128)(2,1)S(1)}, u32[]{:S(2)}, u32[]{:S(2)}) collective-permute-start(bf16[768,128]{1,0:T(8,128)(2,1)S(1)} %get-tuple-element.54), channel_id=1, source_target_pairs={{0,4},{2,6},{4,0},{6,2},{8,12},{10,14},{12,8},{14,10},{16,20},{18,... | collective-permute-start | bytes 589832 | tf_op jit(solution)/shard_map/ppermute | solution.py:523
  64.2 12.1 %collective-permute-start.20 = (bf16[768,128]{1,0:T(8,128)(2,1)S(1)}, bf16[768,128]{1,0:T(8,128)(2,1)S(1)}, u32[]{:S(2)}, u32[]{:S(2)}) collective-permute-start(bf16[768,128]{1,0:T(8,128)(2,1)S(1)} %get-tuple-element.55), channel_id=1, source_target_pairs={{0,6},{2,4},{4,2},{6,0},{8,14},{10,12},{12,10},{14,8},{16,22},{18,... | collective-permute-start | bytes 589832 | tf_op jit(solution)/shard_map/ppermute | solution.py:523
  67.5 8.9 %collective-permute-start.18 = (bf16[768,128]{1,0:T(8,128)(2,1)S(1)}, bf16[768,128]{1,0:T(8,128)(2,1)S(1)}, u32[]{:S(2)}, u32[]{:S(2)}) collective-permute-start(bf16[768,128]{1,0:T(8,128)(2,1)S(1)} %get-tuple-element.53), channel_id=1, source_target_pairs={{0,2},{2,0},{4,6},{6,4},{8,10},{10,8},{12,14},{14,12},{16,18},{18,... | collective-permute-start | bytes 589832 | tf_op jit(solution)/shard_map/ppermute | solution.py:523
  70.1 1.5 %collective-permute-start.26 = (f32[384,64]{1,0:T(8,128)S(1)}, f32[384,64]{1,0:T(8,128)S(1)}, u32[]{:S(2)}, u32[]{:S(2)}) collective-permute-start(f32[384,64]{1,0:T(8,128)S(1)} %get-tuple-element.72), channel_id=1, source_target_pairs={{0,1},{1,0},{2,3},{3,2},{4,5},{5,4},{6,7},{7,6},{8,9},{9,8},{10,11... | collective-permute-start | bytes 294920 | tf_op jit(solution)/shard_map/ppermute | solution.py:540
  72.2 6.6 %collective-permute-start.29 = (bf16[384,128]{1,0:T(8,128)(2,1)S(1)}, bf16[384,128]{1,0:T(8,128)(2,1)S(1)}, u32[]{:S(2)}, u32[]{:S(2)}) collective-permute-start(bf16[384,128]{1,0:T(8,128)(2,1)S(1)} %shard_map.142.refs_0_), channel_id=1, source_target_pairs={{0,6},{2,4},{4,2},{6,0},{8,14},{10,12},{12,10},{14,8},{16,22},{18,... | collective-permute-start | bytes 294920 | tf_op jit(solution)/shard_map/ppermute | solution.py:523
  75.6 5.2 %collective-permute-start.28 = (bf16[384,128]{1,0:T(8,128)(2,1)S(1)}, bf16[384,128]{1,0:T(8,128)(2,1)S(1)}, u32[]{:S(2)}, u32[]{:S(2)}) collective-permute-start(bf16[384,128]{1,0:T(8,128)(2,1)S(1)} %shard_map.142.refs_0_), channel_id=1, source_target_pairs={{0,4},{2,6},{4,0},{6,2},{8,12},{10,14},{12,8},{14,10},{16,20},{18,... | collective-permute-start | bytes 294920 | tf_op jit(solution)/shard_map/ppermute | solution.py:523
  75.6 5.6 %collective-permute-start.27 = (bf16[384,128]{1,0:T(8,128)(2,1)S(1)}, bf16[384,128]{1,0:T(8,128)(2,1)S(1)}, u32[]{:S(2)}, u32[]{:S(2)}) collective-permute-start(bf16[384,128]{1,0:T(8,128)(2,1)S(1)} %shard_map.142.refs_0_), channel_id=1, source_target_pairs={{0,2},{2,0},{4,6},{6,4},{8,10},{10,8},{12,14},{14,12},{16,18},{18,... | collective-permute-start | bytes 294920 | tf_op jit(solution)/shard_map/ppermute | solution.py:523
  77.3 12.4 %collective-permute-start.22 = (bf16[2,768,128]{2,1,0:T(8,128)(2,1)S(1)}, bf16[2,768,128]{2,1,0:T(8,128)(2,1)S(1)}, u32[]{:S(2)}, u32[]{:S(2)}) collective-permute-start(bf16[2,768,128]{2,1,0:T(8,128)(2,1)S(1)} %get-tuple-element.63), channel_id=1, source_target_pairs={{8,0},{10,2},{13,5},{15,7},{17,9},{19,11},{20,12},{22,14},{24,16},... | collective-permute-start | bytes 1179656 | tf_op jit(solution)/shard_map/ppermute | solution.py:553
  81.3 1.4 %collective-permute-start.30 = (bf16[384,128]{1,0:T(8,128)(2,1)S(1)}, bf16[384,128]{1,0:T(8,128)(2,1)S(1)}, u32[]{:S(2)}, u32[]{:S(2)}) collective-permute-start(bf16[384,128]{1,0:T(8,128)(2,1)S(1)} %shard_map.143.refs_0_), channel_id=1, source_target_pairs={{0,1},{1,0},{2,3},{3,2},{4,5},{5,4},{6,7},{7,6},{8,9},{9,8},{10,11... | collective-permute-start | bytes 294920 | tf_op jit(solution)/shard_map/ppermute | solution.py:540
  84.4 12.4 %all-to-all-start = ((f32[16,4,768]{2,1,0:T(4,128)}), f32[16,4,768]{2,1,0:T(4,128)S(1)}, u32[]{:S(2)}, u32[]{:S(2)}) async-start(f32[16,4,768]{2,1,0:T(4,128)} %shard_map.144), calls=%async_computation | async-start | bytes 393216 | tf_op jit(solution)/shard_map/all_to_all | solution.py:681
  90.4 7.6 %collective-permute-start.23 = (bf16[3,192,128]{2,1,0:T(8,128)(2,1)S(1)}, bf16[3,192,128]{2,1,0:T(8,128)(2,1)S(1)}, u32[]{:S(2)}, u32[]{:S(2)}) collective-permute-start(bf16[3,192,128]{2,1,0:T(8,128)(2,1)S(1)} %get-tuple-element.65), channel_id=1, source_target_pairs={{0,2},{2,0},{4,6},{6,4},{8,10},{10,8},{12,14},{14,12},{16,18},{18,... | collective-permute-start | bytes 442376 | tf_op jit(solution)/shard_map/ppermute | solution.py:523
  92.3 7.9 %collective-permute-start.24 = (bf16[3,192,128]{2,1,0:T(8,128)(2,1)S(1)}, bf16[3,192,128]{2,1,0:T(8,128)(2,1)S(1)}, u32[]{:S(2)}, u32[]{:S(2)}) collective-permute-start(bf16[3,192,128]{2,1,0:T(8,128)(2,1)S(1)} %get-tuple-element.66), channel_id=1, source_target_pairs={{0,4},{2,6},{4,0},{6,2},{8,12},{10,14},{12,8},{14,10},{16,20},{18,... | collective-permute-start | bytes 442376 | tf_op jit(solution)/shard_map/ppermute | solution.py:523
  93.7 7.7 %collective-permute-start.25 = (bf16[3,192,128]{2,1,0:T(8,128)(2,1)S(1)}, bf16[3,192,128]{2,1,0:T(8,128)(2,1)S(1)}, u32[]{:S(2)}, u32[]{:S(2)}) collective-permute-start(bf16[3,192,128]{2,1,0:T(8,128)(2,1)S(1)} %get-tuple-element.67), channel_id=1, source_target_pairs={{0,6},{2,4},{4,2},{6,0},{8,14},{10,12},{12,10},{14,8},{16,22},{18,... | collective-permute-start | bytes 442376 | tf_op jit(solution)/shard_map/ppermute | solution.py:523

commit v5 on v4

--- a/solution.py
+++ b/solution.py
@@ -11,6 +11,8 @@
 HALF_GROUP_DEV = 4
 LANES = 128
 QUERY_BLOCK = 256
+FORWARD_BLOCK = 384
+SCORE_SCALE = HEAD_WIDTH**-0.5
 KERNEL_VMEM = 16 << 20
 
 nf4_values = (
@@ -54,7 +56,7 @@
     return jnp.dot(a, b, preferred_element_type=F32)
 
 
-def call(body, outs, scratch, *args, n_scalar=0, in_hbm=False):
+def call(body, outs, scratch, *args, n_scalar=0, in_hbm=False, out_hbm=False):
     if in_hbm:
         args = args[:n_scalar] + tuple(
             pltpu.with_memory_space_constraint(x, pltpu.HBM) for x in args[n_scalar:]
@@ -64,7 +66,7 @@
         body,
         out_shape=outs,
         in_specs=[SM] * n_scalar + [spec] * (len(args) - n_scalar),
-        out_specs=jax.tree.map(lambda _: VM, outs),
+        out_specs=jax.tree.map(lambda _: HB if out_hbm else VM, outs),
         scratch_shapes=scratch,
         compiler_params=pltpu.CompilerParams(vmem_limit_bytes=KERNEL_VMEM),
     )(*args)
@@ -281,7 +283,7 @@
 
 
 def score_block(key, query, k0, q0):
-    scores = nt(key, query) * (HEAD_WIDTH**-0.5)
+    scores = nt(key, query) * SCORE_SCALE
     if k0 is None or k0 + key.shape[0] - 1 <= q0:
         return scores
     kpos = k0 + lax.broadcasted_iota(jnp.int32, scores.shape, 0)
@@ -289,47 +291,52 @@
     return jnp.where(kpos <= qpos, scores, masked)
 
 
-def forward_body(fsdp, wide, pos_ref, q_ref, kv_ref, far_ref, adapt_ref, o_ref, lse_ref, *refs):
-    mid_refs, (vt_scr, oft_scr) = refs[:fsdp], refs[fsdp:]
+def near_forward_body(q_ref, kv_ref, acc_ref, top_ref, total_ref, vt_scr):
+    tokens = q_ref.shape[0]
+    block = min(FORWARD_BLOCK, tokens)
+    vt_scr[...] = kv_ref[1].T
+    for q0 in range(0, tokens, block):
+        qs = slice(q0, q0 + block)
+        depth = q0 + block
+        scores = score_block(kv_ref[0, :depth, :], q_ref[qs, :], 0, q0)
+        top = jnp.max(scores, axis=0, keepdims=True)
+        prob = jnp.exp(scores - top)
+        top_ref[:, qs] = top
+        total_ref[:, qs] = jnp.sum(prob, axis=0, keepdims=True)
+        acc_ref[:, qs] = nn(vt_scr[:, :depth], prob.astype(BF))
+
+
+def forward_body(fsdp, wide, pos_ref, q_ref, far_ref, acc_ref, top_ref, total_ref, adapt_ref, *refs):
+    o_ref, lse_ref, inverse_ref, prob_ref = refs[:4]
+    mid_refs, oft_scr = refs[4 : 4 + fsdp], refs[4 + fsdp]
     core, later, own = pos_ref[2], pos_ref[3], pos_ref[4]
     tokens = q_ref.shape[0]
-    block = min(QUERY_BLOCK, tokens)
-    vt_scr[...] = kv_ref[1].T
-
-    def finish(q0, block_out, norm):
-        qs = slice(q0, q0 + block)
-        o_ref[qs, :] = block_out.T
-        lse_ref[:, qs] = norm
-
-    def near(q0):
-        return score_block(kv_ref[0, : q0 + block, :], q_ref[q0 : q0 + block, :], 0, q0)
+    block = min(FORWARD_BLOCK, tokens)
 
     @pl.when(later == 0)
     def _():
-        for q0 in range(0, tokens, block):
-            scores = near(q0)
-            top = jnp.max(scores, axis=0, keepdims=True)
-            prob = jnp.exp(scores - top)
-            total = jnp.sum(prob, axis=0, keepdims=True)
-            out = nn(vt_scr[:, : q0 + block], prob.astype(BF)) / total
-            finish(q0, out, top + jnp.log(total))
+        inverse = 1.0 / total_ref[...]
+        inverse_ref[...] = inverse
+        lse_ref[...] = top_ref[...] + jnp.log(total_ref[...])
+        o_ref[...] = (acc_ref[...] * inverse).T
 
     @pl.when(later != 0)
     def _():
         oft_scr[...] = far_ref[1].T
         for q0 in range(0, tokens, block):
-            scores = near(q0)
-            far = score_block(far_ref[0], q_ref[q0 : q0 + block, :], None, q0)
-            top = jnp.maximum(
-                jnp.max(scores, axis=0, keepdims=True), jnp.max(far, axis=0, keepdims=True)
-            )
-            prob = jnp.exp(scores - top)
-            far_prob = jnp.exp(far - top)
-            total = jnp.sum(prob, axis=0, keepdims=True) + jnp.sum(far_prob, axis=0, keepdims=True)
-            out = nn(vt_scr[:, : q0 + block], prob.astype(BF)) + nn(
-                oft_scr[...], far_prob.astype(BF)
-            )
-            finish(q0, out / total, top + jnp.log(total))
+            qs = slice(q0, q0 + block)
+            far = score_block(far_ref[0], q_ref[qs, :], None, q0)
+            top = jnp.maximum(top_ref[:, qs], jnp.max(far, axis=0, keepdims=True))
+            prob = jnp.exp(far - top)
+            shrink = jnp.exp(top_ref[:, qs] - top)
+            total = total_ref[:, qs] * shrink + jnp.sum(prob, axis=0, keepdims=True)
+            half_prob = prob.astype(BF)
+            prob_ref[:, qs] = half_prob
+            inverse = 1.0 / total
+            inverse_ref[:, qs] = inverse
+            lse_ref[:, qs] = top + jnp.log(total)
+            out = (acc_ref[:, qs] * shrink + nn(oft_scr[...], half_prob)) * inverse
+            o_ref[qs, :] = out.T
 
     down = adapt_ref[:, pl.ds(pl.multiple_of(wide + own * LANES, LANES), LANES)]
     rows = tokens // fsdp
@@ -342,14 +349,13 @@
 def grad_block(key, value, query, grad, norm, delta, k0, q0):
     prob = jnp.exp(score_block(key, query, k0, q0) - norm)
     prob_grad = nt(value, grad)
-    score_grad = prob * (prob_grad - delta) * (HEAD_WIDTH**-0.5)
-    return prob.astype(BF), score_grad.astype(BF)
+    return prob.astype(BF), (prob * (prob_grad - delta)).astype(BF)
 
 
 def far_body(half, pos_ref, *refs):
     parts = refs[:half]
-    q_ref, far_ref, o_ref, norm_ref = refs[half : half + 4]
-    far_out, dq_ref, do_ref, delta_ref, kt_scr = refs[half + 4 :]
+    q_ref, far_ref, o_ref, inverse_ref, prob_ref = refs[half : half + 5]
+    far_out, dq_ref, do_ref, delta_ref, kt_scr = refs[half + 5 :]
     later = pos_ref[3]
     tokens = q_ref.shape[0]
     block = min(QUERY_BLOCK, tokens)
@@ -365,17 +371,11 @@
         kt_scr[...] = far_ref[0].T
         for k0 in range(0, tokens, block):
             ks = slice(k0, k0 + block)
-            prob, score_grad = grad_block(
-                far_ref[0, ks, :],
-                far_ref[1, ks, :],
-                q_ref[...],
-                do_ref[...],
-                norm_ref[...],
-                delta_ref[...],
-                None,
-                0,
-            )
-            far_out[0, ks, :] = nn(score_grad, q_ref[...]).astype(BF)
+            full = prob_ref[ks, :].astype(F32) * inverse_ref[...]
+            prob_grad = nt(far_ref[1, ks, :], do_ref[...])
+            score_grad = (full * (prob_grad - delta_ref[...])).astype(BF)
+            prob = full.astype(BF)
+            far_out[0, ks, :] = (SCORE_SCALE * nn(score_grad, q_ref[...])).astype(BF)
             far_out[1, ks, :] = nn(prob, do_ref[...]).astype(BF)
             part = nn(kt_scr[:, ks], score_grad)
             if k0:
@@ -406,7 +406,7 @@
             0,
             q0,
         )
-        dk = nn(score_grad, q_ref[qs, :])
+        dk = SCORE_SCALE * nn(score_grad, q_ref[qs, :])
         dv = nn(prob, do_ref[qs, :])
         if q0:
             near_ref[0, :q0, :] += dk[:q0]
@@ -414,7 +414,7 @@
         near_ref[0, qs, :] = dk[q0:]
         near_ref[1, qs, :] = dv[q0:]
         dq = dq_in[:, qs] + nn(kt_scr[:, :depth], score_grad)
-        dq_ref[qs, :] = dq.T.astype(BF)
+        dq_ref[qs, :] = (SCORE_SCALE * dq).T.astype(BF)
 
 
 def merge_body(half, pos_ref, dq_ref, near_ref, back_ref, *out_refs):
@@ -429,12 +429,19 @@
 
 
 def unpack_body(half, pos_ref, *refs):
-    pieces, outs = refs[:half], refs[half:]
+    pieces, outs, sem = refs[:half], refs[half:-1], refs[-1]
     own = pos_ref[4]
+    copies = []
     for s in range(half):
-        at = pl.ds(pl.multiple_of((own ^ s) * LANES, LANES), LANES)
+        cols = pl.ds(pl.multiple_of((own ^ s) * LANES, LANES), LANES)
         for i in range(3):
-            outs[i][:, at] = pieces[s][i]
+            copies.append(
+                pltpu.make_async_copy(pieces[s].at[i], outs[i].at[:, cols], sem.at[s * 3 + i])
+            )
+    for copy in copies:
+        copy.start()
+    for copy in copies:
+        copy.wait()
 
 
 def adapter_grads_body(half, strips, slot, wide, pos_ref, in_ref, up_ref, down_ref):
@@ -651,15 +658,25 @@
     partial.update({s: in_plane(x, s) for s, x in rest.items()})
 
     part_rows = tokens // fsdp
-    out, norm, *mids = call(
-        functools.partial(forward_body, fsdp, wide),
-        [sds((tokens, LANES), F32), sds((1, tokens), F32)]
-        + [sds((part_rows, rank), F32)] * fsdp,
-        [pltpu.VMEM((LANES, tokens), BF), pltpu.VMEM((LANES, tokens), BF)],
-        pos,
+    row = sds((1, tokens), F32)
+    near_acc, near_top, near_total = call(
+        near_forward_body,
+        [sds((LANES, tokens), F32), row, row],
+        [pltpu.VMEM((LANES, tokens), BF)],
         query,
         key_value,
+    )
+    out, norm, inverse, far_prob, *mids = call(
+        functools.partial(forward_body, fsdp, wide),
+        [sds((tokens, LANES), F32), row, row, sds((tokens, tokens), BF)]
+        + [sds((part_rows, rank), F32)] * fsdp,
+        [pltpu.VMEM((LANES, tokens), BF)],
+        pos,
+        query,
         far,
+        near_acc,
+        near_top,
+        near_total,
         adapters,
         n_scalar=1,
     )
@@ -702,7 +719,8 @@
         query,
         far,
         out,
-        norm,
+        inverse,
+        far_prob,
         n_scalar=1,
     )
     back = to_earlier(far_part)
@@ -733,10 +751,11 @@
     query_grad, key_grad, value_grad = call(
         functools.partial(unpack_body, half),
         [sds((rows, heads * HEAD_WIDTH), BF)] * 3,
-        [],
+        [pltpu.SemaphoreType.DMA((3 * half,))],
         pos,
         *merged,
         n_scalar=1,
+        out_hbm=True,
     )
     return query_grad, key_grad, value_grad, down_grad, up_grad
 

time: 103 us -> 104 us (level)
    pallas_call x18 -> x19, Pallas kernels: 22.2 us -> 21.8 us  [call(): pl.pallas_call(body, out_shape=outs, in_specs=[SM] * n_scalar + [spec] *...]
where the time goes in v5:
time: 104 us; the launch traced here: 103 us
  waiting for transfers between devices  40.6 us (39%)
  starting transfers between devices  40.2 us (39%)
  Pallas kernels  21.8 us (21%)
    ppermute x15, waiting for transfers between devices, in_plane(): return lax.ppermute(x, 'ctx', [(i, i ^ s) for i in range(n_ctx)])  22.7 us
    pallas_call x19, Pallas kernels, call(): pl.pallas_call(body, out_shape=outs, in_specs=[SM] * n_scalar + [spec] *...  21.8 us
    ppermute x15, starting transfers between devices, in_plane(): return lax.ppermute(x, 'ctx', [(i, i ^ s) for i in range(n_ctx)])  17.9 us
    ppermute x5, starting transfers between devices, along(): lax.ppermute(x, 'ctx', [(i, (i + s * half) % n_ctx) for i in range(n_ctx)])  9.65 us
    ppermute x2, waiting for transfers between devices, from_plane(): return lax.ppermute(x, 'ctx', route)  9.18 us
    ppermute x1, starting transfers between devices, to_later(): return lax.ppermute(x, ('ctx', 'fsdp'), pairs)  4.59 us
    ppermute x5, waiting for transfers between devices, along(): lax.ppermute(x, 'ctx', [(i, (i + s * half) % n_ctx) for i in range(n_ctx)])  3.9 us
    all_to_all x1, starting transfers between devices, on_device(): lax.all_to_all(adapter_grads, 'ctx', split_axis=0, concat_axis=0, tiled=T...  3.52 us
  transfers between devices with their start and end apart: 32, of which 18 were waited for; matrix products, arithmetic and copies ran while one was open for 0% of the time, Pallas kernels for 18%

profile of v5, /device:TPU:0, one launch (start us, length us, event | category | flops | bytes accessed | tf_op | source)
XLA Modules:
  0.0 103.5 jit_solution(14702392288731202889)
XLA Ops:
  0.6 2.1 %shard_map.132.refs_10_ = bf16[320,512]{1,0:T(8,128)(2,1)S(1)} custom-call(s32[320,512]{1,0:T(8,128)} %codes_in.1, s32[8,320]{1,0:T(8,128)} %bitcast.7, f32[2,128]{1,0:T(2,128)} %bitcast.8), custom_call_target="tpu_custom_call" | custom-call | tf_op jit(solution)/shard_map/pallas_call | solution.py:65
  2.8 5.1 %collective-permute-start.15 = (bf16[320,512]{1,0:T(8,128)(2,1)S(1)}, bf16[320,512]{1,0:T(8,128)(2,1)S(1)}, u32[]{:S(2)}, u32[]{:S(2)}) collective-permute-start(bf16[320,512]{1,0:T(8,128)(2,1)S(1)} %shard_map.132.refs_10_), channel_id=1, source_target_pairs={{0,24},{2,26},{4,28},{6,30},{8,0},{10,2},{12,4},{14,6},{16,8},{18,... | collective-permute-start | bytes 983048 | tf_op jit(solution)/shard_map/ppermute | solution.py:535
  7.9 0.1 stack.23.pos_ref
  8.0 2.8 %shard_map.128 = (bf16[192,1024]{1,0:T(8,128)(2,1)S(1)}, bf16[192,1024]{1,0:T(8,128)(2,1)S(1)}, bf16[192,1024]{1,0:T(8,128)(2,1)S(1)}, bf16[192,1024]{1,0:T(8,12...) custom-call(s32[5]{0:T(128)S(1)} %stack.23.pos_ref, ...), custom_call_target="tpu_custom_call" | custom-call | tf_op jit(solution)/shard_map/pallas_call | solution.py:65
  10.8 1.6 %collective-permute-start.3 = (bf16[4,1152]{1,0:T(4,128)(2,1)S(1)}, bf16[4,1152]{1,0:T(4,128)(2,1)S(1)}, u32[]{:S(2)}, u32[]{:S(2)}) collective-permute-start(bf16[4,1152]{1,0:T(4,128)(2,1)S(1)} %get-tuple-element.52), channel_id=1, source_target_pairs={{0,2},{2,0},{4,6},{6,4},{8,10},{10,8},{12,14},{14,12},{16,18},{18,... | collective-permute-start | bytes 27656 | tf_op jit(solution)/shard_map/ppermute | solution.py:530
  12.3 1.5 %collective-permute-start.4 = (bf16[4,1152]{1,0:T(4,128)(2,1)S(1)}, bf16[4,1152]{1,0:T(4,128)(2,1)S(1)}, u32[]{:S(2)}, u32[]{:S(2)}) collective-permute-start(bf16[4,1152]{1,0:T(4,128)(2,1)S(1)} %get-tuple-element.53), channel_id=1, source_target_pairs={{0,4},{2,6},{4,0},{6,2},{8,12},{10,14},{12,8},{14,10},{16,20},{18,... | collective-permute-start | bytes 27656 | tf_op jit(solution)/shard_map/ppermute | solution.py:530
  13.8 0.5 collective-permute-start.5
  14.3 0.2 collective-permute-done.3.refs_1_
  14.5 1.5 %collective-permute-done.4.refs_2_ = bf16[4,1152]{1,0:T(4,128)(2,1)S(1)} collective-permute-done((bf16[4,1152]{1,0:T(4,128)(2,1)S(1)}, bf16[4,1152]{1,0:T(4,128)(2,1)S(1)}, u32[]{:S(2)}, u32[]{:S(2)}) %collective-permute-start.4) | collective-permute-done | bytes 9248 | tf_op jit(solution)/shard_map/ppermute | solution.py:530
  16.0 2.4 %collective-permute-done.5.refs_3_ = bf16[4,1152]{1,0:T(4,128)(2,1)S(1)} collective-permute-done((bf16[4,1152]{1,0:T(4,128)(2,1)S(1)}, bf16[4,1152]{1,0:T(4,128)(2,1)S(1)}, u32[]{:S(2)}, u32[]{:S(2)}) %collective-permute-start.5) | collective-permute-done | bytes 9248 | tf_op jit(solution)/shard_map/ppermute | solution.py:530
  18.4 0.5 shard_map.130.refs_0_
  19.0 3.9 %collective-permute-start.8 = (bf16[4,4,1152]{2,1,0:T(4,128)(2,1)S(1)}, bf16[4,4,1152]{2,1,0:T(4,128)(2,1)S(1)}, u32[]{:S(2)}, u32[]{:S(2)}) collective-permute-start(bf16[4,4,1152]{2,1,0:T(4,128)(2,1)S(1)} %shard_map.130.refs_0_), channel_id=1, source_target_pairs={{0,24},{2,26},{4,28},{6,30},{8,0},{10,2},{12,4},{14,6},{16,8},{18,... | collective-permute-start | bytes 110600 | tf_op jit(solution)/shard_map/ppermute | solution.py:535
  22.8 0.6 collective-permute-start.6
  23.5 1.0 collective-permute-done.8.refs_3_
  24.5 0.7 collective-permute-start
  25.2 2.5 %collective-permute-done.7.refs_2_ = bf16[4,4,1152]{2,1,0:T(4,128)(2,1)S(1)} collective-permute-done((bf16[4,4,1152]{2,1,0:T(4,128)(2,1)S(1)}, bf16[4,4,1152]{2,1,0:T(4,128)(2,1)S(1)}, u32[]{:S(2)}, u32[]{:S(2)}) %collective-permute-start.7) | collective-permute-done | bytes 36896 | tf_op jit(solution)/shard_map/ppermute | solution.py:535
  27.7 0.5 collective-permute-start.1
  28.2 0.4 collective-permute-done.6.refs_1_
  28.6 1.1 %collective-permute-start.2 = (bf16[192,1024]{1,0:T(8,128)(2,1)S(1)}, bf16[192,1024]{1,0:T(8,128)(2,1)S(1)}, u32[]{:S(2)}, u32[]{:S(2)}) collective-permute-start(bf16[192,1024]{1,0:T(8,128)(2,1)S(1)} %get-tuple-element.48), channel_id=1, source_target_pairs={{0,6},{2,4},{4,2},{6,0},{8,14},{10,12},{12,10},{14,8},{16,22},{18,... | collective-permute-start | bytes 1179656 | tf_op jit(solution)/shard_map/ppermute | solution.py:530
  29.7 0.1 collective-permute-start.9
  29.8 0.5 collective-permute-start.10
  30.3 0.6 shard_map.133
  30.9 0.3 collective-permute-done.9.refs_1_
  31.2 0.7 collective-permute-start.16
  31.9 4.6 %collective-permute-done.refs_1_.refs_4_.refs_3_ = bf16[192,1024]{1,0:T(8,128)(2,1)S(1)} collective-permute-done((bf16[192,1024]{1,0:T(8,128)(2,1)S(1)}, bf16[192,1024]{1,0:T(8,128)(2,1)S(1)}, u32[]{:S(2)}, u32[]{:S(2)}) %collective-permute-start) | collective-permute-done | bytes 393248 | tf_op jit(solution)/shard_map/ppermute | solution.py:530
  36.5 7.8 %collective-permute-done.1.refs_2_.refs_6_.refs_4_ = bf16[192,1024]{1,0:T(8,128)(2,1)S(1)} collective-permute-done((bf16[192,1024]{1,0:T(8,128)(2,1)S(1)}, bf16[192,1024]{1,0:T(8,128)(2,1)S(1)}, u32[]{:S(2)}, u32[]{:S(2)}) %collective-permute-start.1) | collective-permute-done | bytes 393248 | tf_op jit(solution)/shard_map/ppermute | solution.py:530
  44.2 0.5 collective-permute-start.13
  44.7 1.3 %collective-permute-start.17 = (bf16[320,512]{1,0:T(8,128)(2,1)S(1)}, bf16[320,512]{1,0:T(8,128)(2,1)S(1)}, u32[]{:S(2)}, u32[]{:S(2)}) collective-permute-start(bf16[320,512]{1,0:T(8,128)(2,1)S(1)} %get-tuple-element.56), channel_id=1, source_target_pairs={{8,0},{10,2},{12,4},{14,6},{16,24},{18,26},{20,28},{22,30},{9,1},{... | collective-permute-start | bytes 983048 | tf_op jit(solution)/shard_map/ppermute | solution.py:542
  46.0 0.6 shard_map.129
  46.7 4.6 %collective-permute-start.21 = (bf16[2,768,128]{2,1,0:T(8,128)(2,1)S(1)}, bf16[2,768,128]{2,1,0:T(8,128)(2,1)S(1)}, u32[]{:S(2)}, u32[]{:S(2)}) collective-permute-start(bf16[2,768,128]{2,1,0:T(8,128)(2,1)S(1)} %get-tuple-element.50.kv_ref), channel_id=1, source_target_pairs={{0,8},{2,10},{5,13},{7,15},{9,17},{11,19},{12,20},{14,22},{16,24},... | collective-permute-start | bytes 1179656 | tf_op jit(solution)/shard_map/ppermute | solution.py:557
  51.3 9.2 %collective-permute-done.17.refs_14_ = bf16[320,512]{1,0:T(8,128)(2,1)S(1)} collective-permute-done((bf16[320,512]{1,0:T(8,128)(2,1)S(1)}, bf16[320,512]{1,0:T(8,128)(2,1)S(1)}, u32[]{:S(2)}, u32[]{:S(2)}) %collective-permute-start.17) | collective-permute-done | bytes 327712 | tf_op jit(solution)/shard_map/ppermute | solution.py:542
  60.5 1.9 %shard_map.135 = (bf16[768,128]{1,0:T(8,128)(2,1)S(1)}, bf16[768,128]{1,0:T(8,128)(2,1)S(1)}) custom-call(s32[5]{0:T(128)S(1)} %stack.23.pos_ref, bf16[64,1152]{1,0:T(8,128)(2,1)S(1)} %shard_map.131.refs_0_.adapt_ref, bf16[64,1152]{1,0:T(8,128)(2,1)S(1)} %collective-permute-done.9.refs_1_, bf16[192,1024]{1,0:T(8,128)(2,1)S(1)} %get-tuple-element.45.refs_0_.refs_2_, ...), custom_call_target="tpu_custom_call" | custom-call | tf_op jit(solution)/shard_map/pallas_call | solution.py:65
  62.4 1.8 %collective-permute-start.19 = (bf16[768,128]{1,0:T(8,128)(2,1)S(1)}, bf16[768,128]{1,0:T(8,128)(2,1)S(1)}, u32[]{:S(2)}, u32[]{:S(2)}) collective-permute-start(bf16[768,128]{1,0:T(8,128)(2,1)S(1)} %get-tuple-element.59), channel_id=1, source_target_pairs={{0,4},{2,6},{4,0},{6,2},{8,12},{10,14},{12,8},{14,10},{16,20},{18,... | collective-permute-start | bytes 589832 | tf_op jit(solution)/shard_map/ppermute | solution.py:530
  64.2 1.4 %collective-permute-start.20 = (bf16[768,128]{1,0:T(8,128)(2,1)S(1)}, bf16[768,128]{1,0:T(8,128)(2,1)S(1)}, u32[]{:S(2)}, u32[]{:S(2)}) collective-permute-start(bf16[768,128]{1,0:T(8,128)(2,1)S(1)} %get-tuple-element.60), channel_id=1, source_target_pairs={{0,6},{2,4},{4,2},{6,0},{8,14},{10,12},{12,10},{14,8},{16,22},{18,... | collective-permute-start | bytes 589832 | tf_op jit(solution)/shard_map/ppermute | solution.py:530
  65.6 1.9 %shard_map.134 = (bf16[768,128]{1,0:T(8,128)(2,1)S(1)}, bf16[768,128]{1,0:T(8,128)(2,1)S(1)}) custom-call(s32[5]{0:T(128)S(1)} %stack.23.pos_ref, bf16[64,1152]{1,0:T(8,128)(2,1)S(1)} %shard_map.131.refs_0_.adapt_ref, bf16[64,1152]{1,0:T(8,128)(2,1)S(1)} %collective-permute-done.9.refs_1_, bf16[192,1024]{1,0:T(8,128)(2,1)S(1)} %get-tuple-element.45.refs_0_.refs_2_, ...), custom_call_target="tpu_custom_call" | custom-call | tf_op jit(solution)/shard_map/pallas_call | solution.py:65
  67.5 0.4 collective-permute-start.18
  67.8 1.0 shard_map.136
  68.9 0.9 shard_map.137
  69.8 0.1 collective-permute-start.26
  69.9 1.0 shard_map.142.lora_ref
  70.8 0.5 collective-permute-done.26.refs_1_
  71.3 0.6 shard_map.143.refs_0_
  71.9 4.2 %collective-permute-start.29 = (bf16[384,128]{1,0:T(8,128)(2,1)S(1)}, bf16[384,128]{1,0:T(8,128)(2,1)S(1)}, u32[]{:S(2)}, u32[]{:S(2)}) collective-permute-start(bf16[384,128]{1,0:T(8,128)(2,1)S(1)} %shard_map.143.refs_0_), channel_id=1, source_target_pairs={{0,6},{2,4},{4,2},{6,0},{8,14},{10,12},{12,10},{14,8},{16,22},{18,... | collective-permute-start | bytes 294920 | tf_op jit(solution)/shard_map/ppermute | solution.py:530
  76.2 0.7 collective-permute-start.27
  76.8 0.8 shard_map.138
  77.7 1.3 %collective-permute-start.22 = (bf16[2,768,128]{2,1,0:T(8,128)(2,1)S(1)}, bf16[2,768,128]{2,1,0:T(8,128)(2,1)S(1)}, u32[]{:S(2)}, u32[]{:S(2)}) collective-permute-start(bf16[2,768,128]{2,1,0:T(8,128)(2,1)S(1)} %get-tuple-element.73), channel_id=1, source_target_pairs={{8,0},{10,2},{13,5},{15,7},{17,9},{19,11},{20,12},{22,14},{24,16},... | collective-permute-start | bytes 1179656 | tf_op jit(solution)/shard_map/ppermute | solution.py:560
  79.0 0.4 collective-permute-done.29.refs_3_
  79.4 2.0 %collective-permute-done.28.refs_2_ = bf16[384,128]{1,0:T(8,128)(2,1)S(1)} collective-permute-done((bf16[384,128]{1,0:T(8,128)(2,1)S(1)}, bf16[384,128]{1,0:T(8,128)(2,1)S(1)}, u32[]{:S(2)}, u32[]{:S(2)}) %collective-permute-start.28) | collective-permute-done | bytes 98336 | tf_op jit(solution)/shard_map/ppermute | solution.py:530
  81.4 0.4 collective-permute-done.27.refs_1_
  81.8 0.1 shard_map.144.refs_0_
  81.9 0.1 collective-permute-start.30
  81.9 1.3 %collective-permute-done.30.refs_1_ = bf16[384,128]{1,0:T(8,128)(2,1)S(1)} collective-permute-done((bf16[384,128]{1,0:T(8,128)(2,1)S(1)}, bf16[384,128]{1,0:T(8,128)(2,1)S(1)}, u32[]{:S(2)}, u32[]{:S(2)}) %collective-permute-start.30) | collective-permute-done | bytes 98336 | tf_op jit(solution)/shard_map/ppermute | solution.py:547
  83.2 1.7 %shard_map.145 = f32[16,4,768]{2,1,0:T(4,128)} custom-call(s32[5]{0:T(128)S(1)} %stack.23.pos_ref, f32[768,128]{1,0:T(8,128)S(1)} %get-tuple-element.64.refs_6_.o_ref, bf16[384,128]{1,0:T(8,128)(2,1)S(1)} %shard_map.144.refs_0_, bf16[384,128]{1,0:T(8,128)(2,1)S(1)} %collective-permute-done.30.refs_1_, ...), custom_call_target="tpu_custom_call" | custom-call | tf_op jit(solution)/shard_map/pallas_call | solution.py:65
  84.9 3.5 %all-to-all-start = ((f32[16,4,768]{2,1,0:T(4,128)}), f32[16,4,768]{2,1,0:T(4,128)S(1)}, u32[]{:S(2)}, u32[]{:S(2)}) async-start(f32[16,4,768]{2,1,0:T(4,128)} %shard_map.145), calls=%async_computation | async-start | bytes 393216 | tf_op jit(solution)/shard_map/all_to_all | solution.py:698
  88.4 1.9 %shard_map.139 = (bf16[768,128]{1,0:T(8,128)(2,1)S(1)}, f32[2,768,128]{2,1,0:T(8,128)S(1)}) custom-call(s32[5]{0:T(128)S(1)} %stack.23.pos_ref, bf16[768,128]{1,0:T(8,128)(2,1)S(1)} %get-tuple-element.49.q_ref.refs_4_, bf16[2,768,128]{2,1,0:T(8,128)(2,1)S(1)} %get-tuple-element.50.kv_ref, bf16[768,128]{1,0:T(8,128)(2,1)S(1)} %get-tuple-element.67.do_ref, ...), custom_call_target="tpu_custom_call" | custom-call | tf_op jit(solution)/shard_map/pallas_call | solution.py:65
  90.4 0.6 shard_map.140
  91.0 1.9 %collective-permute-start.23 = (bf16[3,192,128]{2,1,0:T(8,128)(2,1)S(1)}, bf16[3,192,128]{2,1,0:T(8,128)(2,1)S(1)}, u32[]{:S(2)}, u32[]{:S(2)}) collective-permute-start(bf16[3,192,128]{2,1,0:T(8,128)(2,1)S(1)} %get-tuple-element.75), channel_id=1, source_target_pairs={{0,2},{2,0},{4,6},{6,4},{8,10},{10,8},{12,14},{14,12},{16,18},{18,... | collective-permute-start | bytes 442376 | tf_op jit(solution)/shard_map/ppermute | solution.py:530
  92.9 1.5 %collective-permute-start.24 = (bf16[3,192,128]{2,1,0:T(8,128)(2,1)S(1)}, bf16[3,192,128]{2,1,0:T(8,128)(2,1)S(1)}, u32[]{:S(2)}, u32[]{:S(2)}) collective-permute-start(bf16[3,192,128]{2,1,0:T(8,128)(2,1)S(1)} %get-tuple-element.76), channel_id=1, source_target_pairs={{0,4},{2,6},{4,0},{6,2},{8,12},{10,14},{12,8},{14,10},{16,20},{18,... | collective-permute-start | bytes 442376 | tf_op jit(solution)/shard_map/ppermute | solution.py:530
  94.3 0.2 collective-permute-start.25
  94.6 2.8 %all-to-all-done.in_ref = f32[16,4,768]{2,1,0:T(4,128)S(1)} async-done(((f32[16,4,768]{2,1,0:T(4,128)}), f32[16,4,768]{2,1,0:T(4,128)S(1)}, u32[]{:S(2)}, u32[]{:S(2)}) %all-to-all-start) | async-done | bytes 196640 | tf_op jit(solution)/shard_map/all_to_all | solution.py:698
  97.3 1.2 %shard_map.146 = (f32[4,2560]{1,0:T(4,128)}, f32[4,512]{1,0:T(4,128)}) custom-call(s32[5]{0:T(128)S(1)} %stack.23.pos_ref, f32[16,4,768]{2,1,0:T(4,128)S(1)} %all-to-all-done.in_ref), custom_call_target="tpu_custom_call" | custom-call | tf_op jit(solution)/shard_map/pallas_call | solution.py:65
  98.6 2.1 %collective-permute-done.24.refs_2_ = bf16[3,192,128]{2,1,0:T(8,128)(2,1)S(1)} collective-permute-done((bf16[3,192,128]{2,1,0:T(8,128)(2,1)S(1)}, bf16[3,192,128]{2,1,0:T(8,128)(2,1)S(1)}, u32[]{:S(2)}, u32[]{:S(2)}) %collective-permute-start.24) | collective-permute-done | bytes 147488 | tf_op jit(solution)/shard_map/ppermute | solution.py:530
  100.7 1.3 %collective-permute-done.25.refs_3_ = bf16[3,192,128]{2,1,0:T(8,128)(2,1)S(1)} collective-permute-done((bf16[3,192,128]{2,1,0:T(8,128)(2,1)S(1)}, bf16[3,192,128]{2,1,0:T(8,128)(2,1)S(1)}, u32[]{:S(2)}, u32[]{:S(2)}) %collective-permute-start.25) | collective-permute-done | bytes 147488 | tf_op jit(solution)/shard_map/ppermute | solution.py:530
  102.0 1.4 %shard_map.141 = (bf16[192,512]{1,0:T(8,128)(2,1)}, bf16[192,512]{1,0:T(8,128)(2,1)}, bf16[192,512]{1,0:T(8,128)(2,1)}) custom-call(s32[5]{0:T(128)S(1)} %stack.23.pos_ref, bf16[3,192,128]{2,1,0:T(8,128)(2,1)S(1)} %get-tuple-element.74.refs_0_, bf16[3,192,128]{2,1,0:T(8,128)(2,1)S(1)} %collective-permute-done.23.refs_1_, ...), custom_call_target="tpu_custom_call" | custom-call | tf_op jit(solution)/shard_map/pallas_call | solution.py:65
  (20 shorter events, 0.1 us)
Async XLA Ops:
  2.8 27.0 %collective-permute-start.15 = (bf16[320,512]{1,0:T(8,128)(2,1)S(1)}, bf16[320,512]{1,0:T(8,128)(2,1)S(1)}, u32[]{:S(2)}, u32[]{:S(2)}) collective-permute-start(bf16[320,512]{1,0:T(8,128)(2,1)S(1)} %shard_map.132.refs_10_), channel_id=1, source_target_pairs={{0,24},{2,26},{4,28},{6,30},{8,0},{10,2},{12,4},{14,6},{16,8},{18,... | collective-permute-start | bytes 983048 | tf_op jit(solution)/shard_map/ppermute | solution.py:535
  7.9 21.9 %collective-permute-start.14 = (bf16[320,512]{1,0:T(8,128)(2,1)S(1)}, bf16[320,512]{1,0:T(8,128)(2,1)S(1)}, u32[]{:S(2)}, u32[]{:S(2)}) collective-permute-start(bf16[320,512]{1,0:T(8,128)(2,1)S(1)} %shard_map.132.refs_10_), channel_id=1, source_target_pairs={{0,8},{2,10},{4,12},{6,14},{8,16},{10,18},{12,20},{14,22},{16,24},... | collective-permute-start | bytes 983048 | tf_op jit(solution)/shard_map/ppermute | solution.py:535
  10.8 3.7 %collective-permute-start.3 = (bf16[4,1152]{1,0:T(4,128)(2,1)S(1)}, bf16[4,1152]{1,0:T(4,128)(2,1)S(1)}, u32[]{:S(2)}, u32[]{:S(2)}) collective-permute-start(bf16[4,1152]{1,0:T(4,128)(2,1)S(1)} %get-tuple-element.52), channel_id=1, source_target_pairs={{0,2},{2,0},{4,6},{6,4},{8,10},{10,8},{12,14},{14,12},{16,18},{18,... | collective-permute-start | bytes 27656 | tf_op jit(solution)/shard_map/ppermute | solution.py:530
  12.3 3.7 %collective-permute-start.4 = (bf16[4,1152]{1,0:T(4,128)(2,1)S(1)}, bf16[4,1152]{1,0:T(4,128)(2,1)S(1)}, u32[]{:S(2)}, u32[]{:S(2)}) collective-permute-start(bf16[4,1152]{1,0:T(4,128)(2,1)S(1)} %get-tuple-element.53), channel_id=1, source_target_pairs={{0,4},{2,6},{4,0},{6,2},{8,12},{10,14},{12,8},{14,10},{16,20},{18,... | collective-permute-start | bytes 27656 | tf_op jit(solution)/shard_map/ppermute | solution.py:530
  13.8 4.6 %collective-permute-start.5 = (bf16[4,1152]{1,0:T(4,128)(2,1)S(1)}, bf16[4,1152]{1,0:T(4,128)(2,1)S(1)}, u32[]{:S(2)}, u32[]{:S(2)}) collective-permute-start(bf16[4,1152]{1,0:T(4,128)(2,1)S(1)} %get-tuple-element.54), channel_id=1, source_target_pairs={{0,6},{2,4},{4,2},{6,0},{8,14},{10,12},{12,10},{14,8},{16,22},{18,... | collective-permute-start | bytes 27656 | tf_op jit(solution)/shard_map/ppermute | solution.py:530
  19.0 5.5 %collective-permute-start.8 = (bf16[4,4,1152]{2,1,0:T(4,128)(2,1)S(1)}, bf16[4,4,1152]{2,1,0:T(4,128)(2,1)S(1)}, u32[]{:S(2)}, u32[]{:S(2)}) collective-permute-start(bf16[4,4,1152]{2,1,0:T(4,128)(2,1)S(1)} %shard_map.130.refs_0_), channel_id=1, source_target_pairs={{0,24},{2,26},{4,28},{6,30},{8,0},{10,2},{12,4},{14,6},{16,8},{18,... | collective-permute-start | bytes 110600 | tf_op jit(solution)/shard_map/ppermute | solution.py:535
  22.8 4.9 %collective-permute-start.7 = (bf16[4,4,1152]{2,1,0:T(4,128)(2,1)S(1)}, bf16[4,4,1152]{2,1,0:T(4,128)(2,1)S(1)}, u32[]{:S(2)}, u32[]{:S(2)}) collective-permute-start(bf16[4,4,1152]{2,1,0:T(4,128)(2,1)S(1)} %shard_map.130.refs_0_), channel_id=1, source_target_pairs={{0,16},{2,18},{4,20},{6,22},{8,24},{10,26},{12,28},{14,30},{16,0},... | collective-permute-start | bytes 110600 | tf_op jit(solution)/shard_map/ppermute | solution.py:535
  22.8 5.8 %collective-permute-start.6 = (bf16[4,4,1152]{2,1,0:T(4,128)(2,1)S(1)}, bf16[4,4,1152]{2,1,0:T(4,128)(2,1)S(1)}, u32[]{:S(2)}, u32[]{:S(2)}) collective-permute-start(bf16[4,4,1152]{2,1,0:T(4,128)(2,1)S(1)} %shard_map.130.refs_0_), channel_id=1, source_target_pairs={{0,8},{2,10},{4,12},{6,14},{8,16},{10,18},{12,20},{14,22},{16,24},... | collective-permute-start | bytes 110600 | tf_op jit(solution)/shard_map/ppermute | solution.py:535
  24.5 12.0 %collective-permute-start = (bf16[192,1024]{1,0:T(8,128)(2,1)S(1)}, bf16[192,1024]{1,0:T(8,128)(2,1)S(1)}, u32[]{:S(2)}, u32[]{:S(2)}) collective-permute-start(bf16[192,1024]{1,0:T(8,128)(2,1)S(1)} %get-tuple-element.46), channel_id=1, source_target_pairs={{0,2},{2,0},{4,6},{6,4},{8,10},{10,8},{12,14},{14,12},{16,18},{18,... | collective-permute-start | bytes 1179656 | tf_op jit(solution)/shard_map/ppermute | solution.py:530
  27.7 16.5 %collective-permute-start.1 = (bf16[192,1024]{1,0:T(8,128)(2,1)S(1)}, bf16[192,1024]{1,0:T(8,128)(2,1)S(1)}, u32[]{:S(2)}, u32[]{:S(2)}) collective-permute-start(bf16[192,1024]{1,0:T(8,128)(2,1)S(1)} %get-tuple-element.47), channel_id=1, source_target_pairs={{0,4},{2,6},{4,0},{6,2},{8,12},{10,14},{12,8},{14,10},{16,20},{18,... | collective-permute-start | bytes 1179656 | tf_op jit(solution)/shard_map/ppermute | solution.py:530
  28.6 15.6 %collective-permute-start.2 = (bf16[192,1024]{1,0:T(8,128)(2,1)S(1)}, bf16[192,1024]{1,0:T(8,128)(2,1)S(1)}, u32[]{:S(2)}, u32[]{:S(2)}) collective-permute-start(bf16[192,1024]{1,0:T(8,128)(2,1)S(1)} %get-tuple-element.48), channel_id=1, source_target_pairs={{0,6},{2,4},{4,2},{6,0},{8,14},{10,12},{12,10},{14,8},{16,22},{18,... | collective-permute-start | bytes 1179656 | tf_op jit(solution)/shard_map/ppermute | solution.py:530
  29.7 1.4 %collective-permute-start.9 = (bf16[64,1152]{1,0:T(8,128)(2,1)S(1)}, bf16[64,1152]{1,0:T(8,128)(2,1)S(1)}, u32[]{:S(2)}, u32[]{:S(2)}) collective-permute-start(bf16[64,1152]{1,0:T(8,128)(2,1)S(1)} %shard_map.131.refs_0_.adapt_ref), channel_id=1, source_target_pairs={{0,1},{1,0},{2,3},{3,2},{4,5},{5,4},{6,7},{7,6},{8,9},{9,8},{10,11... | collective-permute-start | bytes 442376 | tf_op jit(solution)/shard_map/ppermute | solution.py:547
  29.8 14.9 %collective-permute-start.10 = (bf16[192,1024]{1,0:T(8,128)(2,1)S(1)}, bf16[192,1024]{1,0:T(8,128)(2,1)S(1)}, u32[]{:S(2)}, u32[]{:S(2)}) collective-permute-start(bf16[192,1024]{1,0:T(8,128)(2,1)S(1)} %get-tuple-element.45.refs_0_.refs_2_), channel_id=1, source_target_pairs={{0,1},{1,0},{2,3},{3,2},{4,5},{5,4},{6,7},{7,6},{8,9},{9,8},{10,11... | collective-permute-start | bytes 1179656 | tf_op jit(solution)/shard_map/ppermute | solution.py:547
  31.2 15.5 %collective-permute-start.16 = (bf16[320,512]{1,0:T(8,128)(2,1)S(1)}, bf16[320,512]{1,0:T(8,128)(2,1)S(1)}, u32[]{:S(2)}, u32[]{:S(2)}) collective-permute-start(bf16[320,512]{1,0:T(8,128)(2,1)S(1)} %get-tuple-element.55), channel_id=1, source_target_pairs={{8,16},{10,18},{12,20},{14,22},{16,8},{18,10},{20,12},{22,14},{9,1... | collective-permute-start | bytes 983048 | tf_op jit(solution)/shard_map/ppermute | solution.py:542
  36.5 24.0 %collective-permute-start.11 = (bf16[192,1024]{1,0:T(8,128)(2,1)S(1)}, bf16[192,1024]{1,0:T(8,128)(2,1)S(1)}, u32[]{:S(2)}, u32[]{:S(2)}) collective-permute-start(bf16[192,1024]{1,0:T(8,128)(2,1)S(1)} %collective-permute-done.refs_1_.refs_4_.refs_3_), channel_id=1, source_target_pairs={{0,1},{1,0},{2,3},{3,2},{4,5},{5,4},{6,7},{7,6},{8,9},{9,8},{10,11... | collective-permute-start | bytes 1179656 | tf_op jit(solution)/shard_map/ppermute | solution.py:547
  44.2 16.3 %collective-permute-start.12 = (bf16[192,1024]{1,0:T(8,128)(2,1)S(1)}, bf16[192,1024]{1,0:T(8,128)(2,1)S(1)}, u32[]{:S(2)}, u32[]{:S(2)}) collective-permute-start(bf16[192,1024]{1,0:T(8,128)(2,1)S(1)} %collective-permute-done.1.refs_2_.refs_6_.refs_4_), channel_id=1, source_target_pairs={{0,1},{1,0},{2,3},{3,2},{4,5},{5,4},{6,7},{7,6},{8,9},{9,8},{10,11... | collective-permute-start | bytes 1179656 | tf_op jit(solution)/shard_map/ppermute | solution.py:547
  44.2 16.2 %collective-permute-start.13 = (bf16[192,1024]{1,0:T(8,128)(2,1)S(1)}, bf16[192,1024]{1,0:T(8,128)(2,1)S(1)}, u32[]{:S(2)}, u32[]{:S(2)}) collective-permute-start(bf16[192,1024]{1,0:T(8,128)(2,1)S(1)} %collective-permute-done.2.refs_3_.refs_8_.refs_5_), channel_id=1, source_target_pairs={{0,1},{1,0},{2,3},{3,2},{4,5},{5,4},{6,7},{7,6},{8,9},{9,8},{10,11... | collective-permute-start | bytes 1179656 | tf_op jit(solution)/shard_map/ppermute | solution.py:547
  44.7 15.7 %collective-permute-start.17 = (bf16[320,512]{1,0:T(8,128)(2,1)S(1)}, bf16[320,512]{1,0:T(8,128)(2,1)S(1)}, u32[]{:S(2)}, u32[]{:S(2)}) collective-permute-start(bf16[320,512]{1,0:T(8,128)(2,1)S(1)} %get-tuple-element.56), channel_id=1, source_target_pairs={{8,0},{10,2},{12,4},{14,6},{16,24},{18,26},{20,28},{22,30},{9,1},{... | collective-permute-start | bytes 983048 | tf_op jit(solution)/shard_map/ppermute | solution.py:542
  46.7 22.2 %collective-permute-start.21 = (bf16[2,768,128]{2,1,0:T(8,128)(2,1)S(1)}, bf16[2,768,128]{2,1,0:T(8,128)(2,1)S(1)}, u32[]{:S(2)}, u32[]{:S(2)}) collective-permute-start(bf16[2,768,128]{2,1,0:T(8,128)(2,1)S(1)} %get-tuple-element.50.kv_ref), channel_id=1, source_target_pairs={{0,8},{2,10},{5,13},{7,15},{9,17},{11,19},{12,20},{14,22},{16,24},... | collective-permute-start | bytes 1179656 | tf_op jit(solution)/shard_map/ppermute | solution.py:557
  62.4 13.8 %collective-permute-start.19 = (bf16[768,128]{1,0:T(8,128)(2,1)S(1)}, bf16[768,128]{1,0:T(8,128)(2,1)S(1)}, u32[]{:S(2)}, u32[]{:S(2)}) collective-permute-start(bf16[768,128]{1,0:T(8,128)(2,1)S(1)} %get-tuple-element.59), channel_id=1, source_target_pairs={{0,4},{2,6},{4,0},{6,2},{8,12},{10,14},{12,8},{14,10},{16,20},{18,... | collective-permute-start | bytes 589832 | tf_op jit(solution)/shard_map/ppermute | solution.py:530
  64.2 12.7 %collective-permute-start.20 = (bf16[768,128]{1,0:T(8,128)(2,1)S(1)}, bf16[768,128]{1,0:T(8,128)(2,1)S(1)}, u32[]{:S(2)}, u32[]{:S(2)}) collective-permute-start(bf16[768,128]{1,0:T(8,128)(2,1)S(1)} %get-tuple-element.60), channel_id=1, source_target_pairs={{0,6},{2,4},{4,2},{6,0},{8,14},{10,12},{12,10},{14,8},{16,22},{18,... | collective-permute-start | bytes 589832 | tf_op jit(solution)/shard_map/ppermute | solution.py:530
  67.5 9.4 %collective-permute-start.18 = (bf16[768,128]{1,0:T(8,128)(2,1)S(1)}, bf16[768,128]{1,0:T(8,128)(2,1)S(1)}, u32[]{:S(2)}, u32[]{:S(2)}) collective-permute-start(bf16[768,128]{1,0:T(8,128)(2,1)S(1)} %get-tuple-element.58), channel_id=1, source_target_pairs={{0,2},{2,0},{4,6},{6,4},{8,10},{10,8},{12,14},{14,12},{16,18},{18,... | collective-permute-start | bytes 589832 | tf_op jit(solution)/shard_map/ppermute | solution.py:530
  69.8 1.5 %collective-permute-start.26 = (f32[384,64]{1,0:T(8,128)S(1)}, f32[384,64]{1,0:T(8,128)S(1)}, u32[]{:S(2)}, u32[]{:S(2)}) collective-permute-start(f32[384,64]{1,0:T(8,128)S(1)} %get-tuple-element.82), channel_id=1, source_target_pairs={{0,1},{1,0},{2,3},{3,2},{4,5},{5,4},{6,7},{7,6},{8,9},{9,8},{10,11... | collective-permute-start | bytes 294920 | tf_op jit(solution)/shard_map/ppermute | solution.py:547
  71.9 7.4 %collective-permute-start.29 = (bf16[384,128]{1,0:T(8,128)(2,1)S(1)}, bf16[384,128]{1,0:T(8,128)(2,1)S(1)}, u32[]{:S(2)}, u32[]{:S(2)}) collective-permute-start(bf16[384,128]{1,0:T(8,128)(2,1)S(1)} %shard_map.143.refs_0_), channel_id=1, source_target_pairs={{0,6},{2,4},{4,2},{6,0},{8,14},{10,12},{12,10},{14,8},{16,22},{18,... | collective-permute-start | bytes 294920 | tf_op jit(solution)/shard_map/ppermute | solution.py:530
  76.1 5.2 %collective-permute-start.28 = (bf16[384,128]{1,0:T(8,128)(2,1)S(1)}, bf16[384,128]{1,0:T(8,128)(2,1)S(1)}, u32[]{:S(2)}, u32[]{:S(2)}) collective-permute-start(bf16[384,128]{1,0:T(8,128)(2,1)S(1)} %shard_map.143.refs_0_), channel_id=1, source_target_pairs={{0,4},{2,6},{4,0},{6,2},{8,12},{10,14},{12,8},{14,10},{16,20},{18,... | collective-permute-start | bytes 294920 | tf_op jit(solution)/shard_map/ppermute | solution.py:530
  76.2 5.6 %collective-permute-start.27 = (bf16[384,128]{1,0:T(8,128)(2,1)S(1)}, bf16[384,128]{1,0:T(8,128)(2,1)S(1)}, u32[]{:S(2)}, u32[]{:S(2)}) collective-permute-start(bf16[384,128]{1,0:T(8,128)(2,1)S(1)} %shard_map.143.refs_0_), channel_id=1, source_target_pairs={{0,2},{2,0},{4,6},{6,4},{8,10},{10,8},{12,14},{14,12},{16,18},{18,... | collective-permute-start | bytes 294920 | tf_op jit(solution)/shard_map/ppermute | solution.py:530
  77.7 12.7 %collective-permute-start.22 = (bf16[2,768,128]{2,1,0:T(8,128)(2,1)S(1)}, bf16[2,768,128]{2,1,0:T(8,128)(2,1)S(1)}, u32[]{:S(2)}, u32[]{:S(2)}) collective-permute-start(bf16[2,768,128]{2,1,0:T(8,128)(2,1)S(1)} %get-tuple-element.73), channel_id=1, source_target_pairs={{8,0},{10,2},{13,5},{15,7},{17,9},{19,11},{20,12},{22,14},{24,16},... | collective-permute-start | bytes 1179656 | tf_op jit(solution)/shard_map/ppermute | solution.py:560
  81.9 1.4 %collective-permute-start.30 = (bf16[384,128]{1,0:T(8,128)(2,1)S(1)}, bf16[384,128]{1,0:T(8,128)(2,1)S(1)}, u32[]{:S(2)}, u32[]{:S(2)}) collective-permute-start(bf16[384,128]{1,0:T(8,128)(2,1)S(1)} %shard_map.144.refs_0_), channel_id=1, source_target_pairs={{0,1},{1,0},{2,3},{3,2},{4,5},{5,4},{6,7},{7,6},{8,9},{9,8},{10,11... | collective-permute-start | bytes 294920 | tf_op jit(solution)/shard_map/ppermute | solution.py:547
  84.9 12.4 %all-to-all-start = ((f32[16,4,768]{2,1,0:T(4,128)}), f32[16,4,768]{2,1,0:T(4,128)S(1)}, u32[]{:S(2)}, u32[]{:S(2)}) async-start(f32[16,4,768]{2,1,0:T(4,128)} %shard_map.145), calls=%async_computation | async-start | bytes 393216 | tf_op jit(solution)/shard_map/all_to_all | solution.py:698
  91.0 7.6 %collective-permute-start.23 = (bf16[3,192,128]{2,1,0:T(8,128)(2,1)S(1)}, bf16[3,192,128]{2,1,0:T(8,128)(2,1)S(1)}, u32[]{:S(2)}, u32[]{:S(2)}) collective-permute-start(bf16[3,192,128]{2,1,0:T(8,128)(2,1)S(1)} %get-tuple-element.75), channel_id=1, source_target_pairs={{0,2},{2,0},{4,6},{6,4},{8,10},{10,8},{12,14},{14,12},{16,18},{18,... | collective-permute-start | bytes 442376 | tf_op jit(solution)/shard_map/ppermute | solution.py:530
  92.9 7.9 %collective-permute-start.24 = (bf16[3,192,128]{2,1,0:T(8,128)(2,1)S(1)}, bf16[3,192,128]{2,1,0:T(8,128)(2,1)S(1)}, u32[]{:S(2)}, u32[]{:S(2)}) collective-permute-start(bf16[3,192,128]{2,1,0:T(8,128)(2,1)S(1)} %get-tuple-element.76), channel_id=1, source_target_pairs={{0,4},{2,6},{4,0},{6,2},{8,12},{10,14},{12,8},{14,10},{16,20},{18,... | collective-permute-start | bytes 442376 | tf_op jit(solution)/shard_map/ppermute | solution.py:530
  94.3 7.7 %collective-permute-start.25 = (bf16[3,192,128]{2,1,0:T(8,128)(2,1)S(1)}, bf16[3,192,128]{2,1,0:T(8,128)(2,1)S(1)}, u32[]{:S(2)}, u32[]{:S(2)}) collective-permute-start(bf16[3,192,128]{2,1,0:T(8,128)(2,1)S(1)} %get-tuple-element.77), channel_id=1, source_target_pairs={{0,6},{2,4},{4,2},{6,0},{8,14},{10,12},{12,10},{14,8},{16,22},{18,... | collective-permute-start | bytes 442376 | tf_op jit(solution)/shard_map/ppermute | solution.py:530

commit v6 on v5

--- a/solution.py
+++ b/solution.py
@@ -11,7 +11,7 @@
 HALF_GROUP_DEV = 4
 LANES = 128
 QUERY_BLOCK = 256
-FORWARD_BLOCK = 384
+FORWARD_BLOCK = 768
 SCORE_SCALE = HEAD_WIDTH**-0.5
 KERNEL_VMEM = 16 << 20
 
@@ -291,7 +291,7 @@
     return jnp.where(kpos <= qpos, scores, masked)
 
 
-def near_forward_body(q_ref, kv_ref, acc_ref, top_ref, total_ref, vt_scr):
+def near_forward_body(q_ref, kv_ref, acc_ref, top_ref, total_ref, prob_ref, vt_scr):
     tokens = q_ref.shape[0]
     block = min(FORWARD_BLOCK, tokens)
     vt_scr[...] = kv_ref[1].T
@@ -303,11 +303,13 @@
         prob = jnp.exp(scores - top)
         top_ref[:, qs] = top
         total_ref[:, qs] = jnp.sum(prob, axis=0, keepdims=True)
-        acc_ref[:, qs] = nn(vt_scr[:, :depth], prob.astype(BF))
+        half_prob = prob.astype(BF)
+        prob_ref[:depth, qs] = half_prob
+        acc_ref[:, qs] = nn(vt_scr[:, :depth], half_prob)
 
 
 def forward_body(fsdp, wide, pos_ref, q_ref, far_ref, acc_ref, top_ref, total_ref, adapt_ref, *refs):
-    o_ref, lse_ref, inverse_ref, prob_ref = refs[:4]
+    o_ref, scale_ref, inverse_ref, prob_ref = refs[:4]
     mid_refs, oft_scr = refs[4 : 4 + fsdp], refs[4 + fsdp]
     core, later, own = pos_ref[2], pos_ref[3], pos_ref[4]
     tokens = q_ref.shape[0]
@@ -317,7 +319,7 @@
     def _():
         inverse = 1.0 / total_ref[...]
         inverse_ref[...] = inverse
-        lse_ref[...] = top_ref[...] + jnp.log(total_ref[...])
+        scale_ref[...] = inverse
         o_ref[...] = (acc_ref[...] * inverse).T
 
     @pl.when(later != 0)
@@ -334,7 +336,7 @@
             prob_ref[:, qs] = half_prob
             inverse = 1.0 / total
             inverse_ref[:, qs] = inverse
-            lse_ref[:, qs] = top + jnp.log(total)
+            scale_ref[:, qs] = shrink * inverse
             out = (acc_ref[:, qs] * shrink + nn(oft_scr[...], half_prob)) * inverse
             o_ref[qs, :] = out.T
 
@@ -344,12 +346,6 @@
         to = lax.rem(core + s, fsdp)
         part = o_ref[pl.ds(pl.multiple_of(to * rows, rows), rows), :]
         mid_refs[s][...] = nt(part.astype(BF), down)
-
-
-def grad_block(key, value, query, grad, norm, delta, k0, q0):
-    prob = jnp.exp(score_block(key, query, k0, q0) - norm)
-    prob_grad = nt(value, grad)
-    return prob.astype(BF), (prob * (prob_grad - delta)).astype(BF)
 
 
 def far_body(half, pos_ref, *refs):
@@ -389,25 +385,20 @@
         dq_ref[...] = jnp.zeros(dq_ref.shape, F32)
 
 
-def near_body(pos_ref, q_ref, kv_ref, do_ref, norm_ref, delta_ref, dq_in, dq_ref, near_ref, kt_scr):
+def near_body(
+    q_ref, kv_ref, do_ref, prob_ref, scale_ref, delta_ref, dq_in, dq_ref, near_ref, kt_scr
+):
     tokens = q_ref.shape[0]
     block = min(QUERY_BLOCK, tokens)
     kt_scr[...] = kv_ref[0].T
     for q0 in range(0, tokens, block):
         qs = slice(q0, q0 + block)
         depth = q0 + block
-        prob, score_grad = grad_block(
-            kv_ref[0, :depth, :],
-            kv_ref[1, :depth, :],
-            q_ref[qs, :],
-            do_ref[qs, :],
-            norm_ref[:, qs],
-            delta_ref[:, qs],
-            0,
-            q0,
-        )
+        full = prob_ref[:depth, qs].astype(F32) * scale_ref[:, qs]
+        prob_grad = nt(kv_ref[1, :depth, :], do_ref[qs, :])
+        score_grad = (full * (prob_grad - delta_ref[:, qs])).astype(BF)
         dk = SCORE_SCALE * nn(score_grad, q_ref[qs, :])
-        dv = nn(prob, do_ref[qs, :])
+        dv = nn(full.astype(BF), do_ref[qs, :])
         if q0:
             near_ref[0, :q0, :] += dk[:q0]
             near_ref[1, :q0, :] += dv[:q0]
@@ -659,14 +650,14 @@
 
     part_rows = tokens // fsdp
     row = sds((1, tokens), F32)
-    near_acc, near_top, near_total = call(
+    near_acc, near_top, near_total, near_prob = call(
         near_forward_body,
-        [sds((LANES, tokens), F32), row, row],
+        [sds((LANES, tokens), F32), row, row, sds((tokens, tokens), BF)],
         [pltpu.VMEM((LANES, tokens), BF)],
         query,
         key_value,
     )
-    out, norm, inverse, far_prob, *mids = call(
+    out, near_scale, inverse, far_prob, *mids = call(
         functools.partial(forward_body, fsdp, wide),
         [sds((tokens, LANES), F32), row, row, sds((tokens, tokens), BF)]
         + [sds((part_rows, rank), F32)] * fsdp,
@@ -728,14 +719,13 @@
         near_body,
         [sds((tokens, LANES), BF), sds((2, tokens, LANES), F32)],
         [pltpu.VMEM((LANES, tokens), BF)],
-        pos,
         query,
         key_value,
         grad_out,
-        norm,
+        near_prob,
+        near_scale,
         delta,
         dq_far,
-        n_scalar=1,
     )
     merged = call(
         functools.partial(merge_body, half),

time: 104 us -> 103 us (level)
  transfers between devices with their start and end apart: 32 -> 32, of which waited for: 18 -> 18; matrix products, arithmetic and copies ran while one was open for 0% -> 0% of each run, Pallas kernels for 18% -> 17%
where the time goes in v6:
time: 103 us
  waiting for transfers between devices  41 us (40%)
  starting transfers between devices  40 us (39%)
  Pallas kernels  21.1 us (20%)
    ppermute x15, waiting for transfers between devices, in_plane(): return lax.ppermute(x, 'ctx', [(i, i ^ s) for i in range(n_ctx)])  22.4 us
    pallas_call x19, Pallas kernels, call(): pl.pallas_call(body, out_shape=outs, in_specs=[SM] * n_scalar + [spec] *...  21.1 us
    ppermute x15, starting transfers between devices, in_plane(): return lax.ppermute(x, 'ctx', [(i, i ^ s) for i in range(n_ctx)])  17.8 us
    ppermute x5, starting transfers between devices, along(): lax.ppermute(x, 'ctx', [(i, (i + s * half) % n_ctx) for i in range(n_ctx)])  9.65 us
    ppermute x2, waiting for transfers between devices, from_plane(): return lax.ppermute(x, 'ctx', route)  9.18 us
    ppermute x1, starting transfers between devices, to_later(): return lax.ppermute(x, ('ctx', 'fsdp'), pairs)  4.59 us
    ppermute x5, waiting for transfers between devices, along(): lax.ppermute(x, 'ctx', [(i, (i + s * half) % n_ctx) for i in range(n_ctx)])  3.9 us
    all_to_all x1, starting transfers between devices, on_device(): lax.all_to_all(adapter_grads, 'ctx', split_axis=0, concat_axis=0, tiled=T...  3.52 us
  transfers between devices with their start and end apart: 32, of which 18 were waited for; matrix products, arithmetic and copies ran while one was open for 0% of the time, Pallas kernels for 17%

profile of v6, /device:TPU:0, one launch (start us, length us, event | category | flops | bytes accessed | tf_op | source)
XLA Modules:
  0.0 103.0 jit_solution(18065509854997658319)
XLA Ops:
  0.6 2.1 %shard_map.132.refs_10_ = bf16[320,512]{1,0:T(8,128)(2,1)S(1)} custom-call(s32[320,512]{1,0:T(8,128)} %codes_in.1, s32[8,320]{1,0:T(8,128)} %bitcast.7, f32[2,128]{1,0:T(2,128)} %bitcast.8), custom_call_target="tpu_custom_call" | custom-call | tf_op jit(solution)/shard_map/pallas_call | solution.py:65
  2.8 5.1 %collective-permute-start.15 = (bf16[320,512]{1,0:T(8,128)(2,1)S(1)}, bf16[320,512]{1,0:T(8,128)(2,1)S(1)}, u32[]{:S(2)}, u32[]{:S(2)}) collective-permute-start(bf16[320,512]{1,0:T(8,128)(2,1)S(1)} %shard_map.132.refs_10_), channel_id=1, source_target_pairs={{0,24},{2,26},{4,28},{6,30},{8,0},{10,2},{12,4},{14,6},{16,8},{18,... | collective-permute-start | bytes 983048 | tf_op jit(solution)/shard_map/ppermute | solution.py:526
  7.9 0.1 stack.23.pos_ref
  8.0 2.8 %shard_map.128 = (bf16[192,1024]{1,0:T(8,128)(2,1)S(1)}, bf16[192,1024]{1,0:T(8,128)(2,1)S(1)}, bf16[192,1024]{1,0:T(8,128)(2,1)S(1)}, bf16[192,1024]{1,0:T(8,12...) custom-call(s32[5]{0:T(128)S(1)} %stack.23.pos_ref, ...), custom_call_target="tpu_custom_call" | custom-call | tf_op jit(solution)/shard_map/pallas_call | solution.py:65
  10.8 1.6 %collective-permute-start.3 = (bf16[4,1152]{1,0:T(4,128)(2,1)S(1)}, bf16[4,1152]{1,0:T(4,128)(2,1)S(1)}, u32[]{:S(2)}, u32[]{:S(2)}) collective-permute-start(bf16[4,1152]{1,0:T(4,128)(2,1)S(1)} %get-tuple-element.53), channel_id=1, source_target_pairs={{0,2},{2,0},{4,6},{6,4},{8,10},{10,8},{12,14},{14,12},{16,18},{18,... | collective-permute-start | bytes 27656 | tf_op jit(solution)/shard_map/ppermute | solution.py:521
  12.3 1.5 %collective-permute-start.4 = (bf16[4,1152]{1,0:T(4,128)(2,1)S(1)}, bf16[4,1152]{1,0:T(4,128)(2,1)S(1)}, u32[]{:S(2)}, u32[]{:S(2)}) collective-permute-start(bf16[4,1152]{1,0:T(4,128)(2,1)S(1)} %get-tuple-element.54), channel_id=1, source_target_pairs={{0,4},{2,6},{4,0},{6,2},{8,12},{10,14},{12,8},{14,10},{16,20},{18,... | collective-permute-start | bytes 27656 | tf_op jit(solution)/shard_map/ppermute | solution.py:521
  13.8 0.5 collective-permute-start.5
  14.3 0.2 collective-permute-done.3.refs_1_
  14.5 1.5 %collective-permute-done.4.refs_2_ = bf16[4,1152]{1,0:T(4,128)(2,1)S(1)} collective-permute-done((bf16[4,1152]{1,0:T(4,128)(2,1)S(1)}, bf16[4,1152]{1,0:T(4,128)(2,1)S(1)}, u32[]{:S(2)}, u32[]{:S(2)}) %collective-permute-start.4) | collective-permute-done | bytes 9248 | tf_op jit(solution)/shard_map/ppermute | solution.py:521
  16.0 2.4 %collective-permute-done.5.refs_3_ = bf16[4,1152]{1,0:T(4,128)(2,1)S(1)} collective-permute-done((bf16[4,1152]{1,0:T(4,128)(2,1)S(1)}, bf16[4,1152]{1,0:T(4,128)(2,1)S(1)}, u32[]{:S(2)}, u32[]{:S(2)}) %collective-permute-start.5) | collective-permute-done | bytes 9248 | tf_op jit(solution)/shard_map/ppermute | solution.py:521
  18.4 0.5 shard_map.130.refs_0_
  19.0 3.9 %collective-permute-start.8 = (bf16[4,4,1152]{2,1,0:T(4,128)(2,1)S(1)}, bf16[4,4,1152]{2,1,0:T(4,128)(2,1)S(1)}, u32[]{:S(2)}, u32[]{:S(2)}) collective-permute-start(bf16[4,4,1152]{2,1,0:T(4,128)(2,1)S(1)} %shard_map.130.refs_0_), channel_id=1, source_target_pairs={{0,24},{2,26},{4,28},{6,30},{8,0},{10,2},{12,4},{14,6},{16,8},{18,... | collective-permute-start | bytes 110600 | tf_op jit(solution)/shard_map/ppermute | solution.py:526
  22.8 0.6 collective-permute-start.6
  23.5 1.0 collective-permute-done.8.refs_3_
  24.5 0.7 collective-permute-start
  25.2 2.5 %collective-permute-done.7.refs_2_ = bf16[4,4,1152]{2,1,0:T(4,128)(2,1)S(1)} collective-permute-done((bf16[4,4,1152]{2,1,0:T(4,128)(2,1)S(1)}, bf16[4,4,1152]{2,1,0:T(4,128)(2,1)S(1)}, u32[]{:S(2)}, u32[]{:S(2)}) %collective-permute-start.7) | collective-permute-done | bytes 36896 | tf_op jit(solution)/shard_map/ppermute | solution.py:526
  27.7 0.5 collective-permute-start.1
  28.2 0.4 collective-permute-done.6.refs_1_
  28.6 1.1 %collective-permute-start.2 = (bf16[192,1024]{1,0:T(8,128)(2,1)S(1)}, bf16[192,1024]{1,0:T(8,128)(2,1)S(1)}, u32[]{:S(2)}, u32[]{:S(2)}) collective-permute-start(bf16[192,1024]{1,0:T(8,128)(2,1)S(1)} %get-tuple-element.49), channel_id=1, source_target_pairs={{0,6},{2,4},{4,2},{6,0},{8,14},{10,12},{12,10},{14,8},{16,22},{18,... | collective-permute-start | bytes 1179656 | tf_op jit(solution)/shard_map/ppermute | solution.py:521
  29.7 0.1 collective-permute-start.9
  29.8 0.5 collective-permute-start.10
  30.3 0.6 shard_map.133
  30.9 0.3 collective-permute-done.9.refs_1_
  31.2 0.7 collective-permute-start.16
  31.9 4.6 %collective-permute-done.refs_1_.refs_4_.refs_3_ = bf16[192,1024]{1,0:T(8,128)(2,1)S(1)} collective-permute-done((bf16[192,1024]{1,0:T(8,128)(2,1)S(1)}, bf16[192,1024]{1,0:T(8,128)(2,1)S(1)}, u32[]{:S(2)}, u32[]{:S(2)}) %collective-permute-start) | collective-permute-done | bytes 393248 | tf_op jit(solution)/shard_map/ppermute | solution.py:521
  36.5 7.8 %collective-permute-done.1.refs_2_.refs_6_.refs_4_ = bf16[192,1024]{1,0:T(8,128)(2,1)S(1)} collective-permute-done((bf16[192,1024]{1,0:T(8,128)(2,1)S(1)}, bf16[192,1024]{1,0:T(8,128)(2,1)S(1)}, u32[]{:S(2)}, u32[]{:S(2)}) %collective-permute-start.1) | collective-permute-done | bytes 393248 | tf_op jit(solution)/shard_map/ppermute | solution.py:521
  44.2 0.5 collective-permute-start.13
  44.7 1.3 %collective-permute-start.17 = (bf16[320,512]{1,0:T(8,128)(2,1)S(1)}, bf16[320,512]{1,0:T(8,128)(2,1)S(1)}, u32[]{:S(2)}, u32[]{:S(2)}) collective-permute-start(bf16[320,512]{1,0:T(8,128)(2,1)S(1)} %get-tuple-element.57), channel_id=1, source_target_pairs={{8,0},{10,2},{12,4},{14,6},{16,24},{18,26},{20,28},{22,30},{9,1},{... | collective-permute-start | bytes 983048 | tf_op jit(solution)/shard_map/ppermute | solution.py:533
  46.0 0.6 shard_map.129
  46.7 4.6 %collective-permute-start.21 = (bf16[2,768,128]{2,1,0:T(8,128)(2,1)S(1)}, bf16[2,768,128]{2,1,0:T(8,128)(2,1)S(1)}, u32[]{:S(2)}, u32[]{:S(2)}) collective-permute-start(bf16[2,768,128]{2,1,0:T(8,128)(2,1)S(1)} %get-tuple-element.51.kv_ref), channel_id=1, source_target_pairs={{0,8},{2,10},{5,13},{7,15},{9,17},{11,19},{12,20},{14,22},{16,24},... | collective-permute-start | bytes 1179656 | tf_op jit(solution)/shard_map/ppermute | solution.py:548
  51.3 9.2 %collective-permute-done.17.refs_14_ = bf16[320,512]{1,0:T(8,128)(2,1)S(1)} collective-permute-done((bf16[320,512]{1,0:T(8,128)(2,1)S(1)}, bf16[320,512]{1,0:T(8,128)(2,1)S(1)}, u32[]{:S(2)}, u32[]{:S(2)}) %collective-permute-start.17) | collective-permute-done | bytes 327712 | tf_op jit(solution)/shard_map/ppermute | solution.py:533
  60.5 1.9 %shard_map.135 = (bf16[768,128]{1,0:T(8,128)(2,1)S(1)}, bf16[768,128]{1,0:T(8,128)(2,1)S(1)}) custom-call(s32[5]{0:T(128)S(1)} %stack.23.pos_ref, bf16[64,1152]{1,0:T(8,128)(2,1)S(1)} %shard_map.131.refs_0_.adapt_ref, bf16[64,1152]{1,0:T(8,128)(2,1)S(1)} %collective-permute-done.9.refs_1_, bf16[192,1024]{1,0:T(8,128)(2,1)S(1)} %get-tuple-element.46.refs_0_.refs_2_, ...), custom_call_target="tpu_custom_call" | custom-call | tf_op jit(solution)/shard_map/pallas_call | solution.py:65
  62.4 1.8 %collective-permute-start.19 = (bf16[768,128]{1,0:T(8,128)(2,1)S(1)}, bf16[768,128]{1,0:T(8,128)(2,1)S(1)}, u32[]{:S(2)}, u32[]{:S(2)}) collective-permute-start(bf16[768,128]{1,0:T(8,128)(2,1)S(1)} %get-tuple-element.60), channel_id=1, source_target_pairs={{0,4},{2,6},{4,0},{6,2},{8,12},{10,14},{12,8},{14,10},{16,20},{18,... | collective-permute-start | bytes 589832 | tf_op jit(solution)/shard_map/ppermute | solution.py:521
  64.2 1.4 %collective-permute-start.20 = (bf16[768,128]{1,0:T(8,128)(2,1)S(1)}, bf16[768,128]{1,0:T(8,128)(2,1)S(1)}, u32[]{:S(2)}, u32[]{:S(2)}) collective-permute-start(bf16[768,128]{1,0:T(8,128)(2,1)S(1)} %get-tuple-element.61), channel_id=1, source_target_pairs={{0,6},{2,4},{4,2},{6,0},{8,14},{10,12},{12,10},{14,8},{16,22},{18,... | collective-permute-start | bytes 589832 | tf_op jit(solution)/shard_map/ppermute | solution.py:521
  65.6 1.9 %shard_map.134 = (bf16[768,128]{1,0:T(8,128)(2,1)S(1)}, bf16[768,128]{1,0:T(8,128)(2,1)S(1)}) custom-call(s32[5]{0:T(128)S(1)} %stack.23.pos_ref, bf16[64,1152]{1,0:T(8,128)(2,1)S(1)} %shard_map.131.refs_0_.adapt_ref, bf16[64,1152]{1,0:T(8,128)(2,1)S(1)} %collective-permute-done.9.refs_1_, bf16[192,1024]{1,0:T(8,128)(2,1)S(1)} %get-tuple-element.46.refs_0_.refs_2_, ...), custom_call_target="tpu_custom_call" | custom-call | tf_op jit(solution)/shard_map/pallas_call | solution.py:65
  67.5 0.4 collective-permute-start.18
  67.8 1.0 shard_map.136
  68.8 0.9 shard_map.137
  69.8 0.1 collective-permute-start.26
  69.8 1.0 shard_map.142.lora_ref
  70.8 0.5 collective-permute-done.26.refs_1_
  71.3 0.6 shard_map.143.refs_0_
  71.9 4.1 %collective-permute-start.29 = (bf16[384,128]{1,0:T(8,128)(2,1)S(1)}, bf16[384,128]{1,0:T(8,128)(2,1)S(1)}, u32[]{:S(2)}, u32[]{:S(2)}) collective-permute-start(bf16[384,128]{1,0:T(8,128)(2,1)S(1)} %shard_map.143.refs_0_), channel_id=1, source_target_pairs={{0,6},{2,4},{4,2},{6,0},{8,14},{10,12},{12,10},{14,8},{16,22},{18,... | collective-permute-start | bytes 294920 | tf_op jit(solution)/shard_map/ppermute | solution.py:521
  76.0 0.7 collective-permute-start.27
  76.7 0.8 shard_map.138
  77.5 1.3 %collective-permute-start.22 = (bf16[2,768,128]{2,1,0:T(8,128)(2,1)S(1)}, bf16[2,768,128]{2,1,0:T(8,128)(2,1)S(1)}, u32[]{:S(2)}, u32[]{:S(2)}) collective-permute-start(bf16[2,768,128]{2,1,0:T(8,128)(2,1)S(1)} %get-tuple-element.75), channel_id=1, source_target_pairs={{8,0},{10,2},{13,5},{15,7},{17,9},{19,11},{20,12},{22,14},{24,16},... | collective-permute-start | bytes 1179656 | tf_op jit(solution)/shard_map/ppermute | solution.py:551
  78.8 0.4 collective-permute-done.29.refs_3_
  79.2 2.0 %collective-permute-done.28.refs_2_ = bf16[384,128]{1,0:T(8,128)(2,1)S(1)} collective-permute-done((bf16[384,128]{1,0:T(8,128)(2,1)S(1)}, bf16[384,128]{1,0:T(8,128)(2,1)S(1)}, u32[]{:S(2)}, u32[]{:S(2)}) %collective-permute-start.28) | collective-permute-done | bytes 98336 | tf_op jit(solution)/shard_map/ppermute | solution.py:521
  81.2 0.4 collective-permute-done.27.refs_1_
  81.6 0.1 shard_map.144.refs_0_
  81.7 0.1 collective-permute-start.30
  81.8 1.3 %collective-permute-done.30.refs_1_ = bf16[384,128]{1,0:T(8,128)(2,1)S(1)} collective-permute-done((bf16[384,128]{1,0:T(8,128)(2,1)S(1)}, bf16[384,128]{1,0:T(8,128)(2,1)S(1)}, u32[]{:S(2)}, u32[]{:S(2)}) %collective-permute-start.30) | collective-permute-done | bytes 98336 | tf_op jit(solution)/shard_map/ppermute | solution.py:538
  83.1 1.7 %shard_map.145 = f32[16,4,768]{2,1,0:T(4,128)} custom-call(s32[5]{0:T(128)S(1)} %stack.23.pos_ref, f32[768,128]{1,0:T(8,128)S(1)} %get-tuple-element.65.refs_6_.o_ref, bf16[384,128]{1,0:T(8,128)(2,1)S(1)} %shard_map.144.refs_0_, bf16[384,128]{1,0:T(8,128)(2,1)S(1)} %collective-permute-done.30.refs_1_, ...), custom_call_target="tpu_custom_call" | custom-call | tf_op jit(solution)/shard_map/pallas_call | solution.py:65
  84.7 3.5 %all-to-all-start = ((f32[16,4,768]{2,1,0:T(4,128)}), f32[16,4,768]{2,1,0:T(4,128)S(1)}, u32[]{:S(2)}, u32[]{:S(2)}) async-start(f32[16,4,768]{2,1,0:T(4,128)} %shard_map.145), calls=%async_computation | async-start | bytes 393216 | tf_op jit(solution)/shard_map/all_to_all | solution.py:689
  88.3 1.2 %shard_map.139 = (bf16[768,128]{1,0:T(8,128)(2,1)S(1)}, f32[2,768,128]{2,1,0:T(8,128)S(1)}) custom-call(bf16[768,128]{1,0:T(8,128)(2,1)S(1)} %get-tuple-element.50.q_ref.refs_4_, bf16[2,768,128]{2,1,0:T(8,128)(2,1)S(1)} %get-tuple-element.51.kv_ref, bf16[768,128]{1,0:T(8,128)(2,1)S(1)} %get-tuple-element.68.do_ref, ...), custom_call_target="tpu_custom_call" | custom-call | tf_op jit(solution)/shard_map/pallas_call | solution.py:65
  89.5 0.6 shard_map.140
  90.2 1.9 %collective-permute-start.23 = (bf16[3,192,128]{2,1,0:T(8,128)(2,1)S(1)}, bf16[3,192,128]{2,1,0:T(8,128)(2,1)S(1)}, u32[]{:S(2)}, u32[]{:S(2)}) collective-permute-start(bf16[3,192,128]{2,1,0:T(8,128)(2,1)S(1)} %get-tuple-element.77), channel_id=1, source_target_pairs={{0,2},{2,0},{4,6},{6,4},{8,10},{10,8},{12,14},{14,12},{16,18},{18,... | collective-permute-start | bytes 442376 | tf_op jit(solution)/shard_map/ppermute | solution.py:521
  92.0 1.5 %collective-permute-start.24 = (bf16[3,192,128]{2,1,0:T(8,128)(2,1)S(1)}, bf16[3,192,128]{2,1,0:T(8,128)(2,1)S(1)}, u32[]{:S(2)}, u32[]{:S(2)}) collective-permute-start(bf16[3,192,128]{2,1,0:T(8,128)(2,1)S(1)} %get-tuple-element.78), channel_id=1, source_target_pairs={{0,4},{2,6},{4,0},{6,2},{8,12},{10,14},{12,8},{14,10},{16,20},{18,... | collective-permute-start | bytes 442376 | tf_op jit(solution)/shard_map/ppermute | solution.py:521
  93.5 0.2 collective-permute-start.25
  93.7 3.4 %all-to-all-done.in_ref = f32[16,4,768]{2,1,0:T(4,128)S(1)} async-done(((f32[16,4,768]{2,1,0:T(4,128)}), f32[16,4,768]{2,1,0:T(4,128)S(1)}, u32[]{:S(2)}, u32[]{:S(2)}) %all-to-all-start) | async-done | bytes 196640 | tf_op jit(solution)/shard_map/all_to_all | solution.py:689
  97.2 1.2 %shard_map.146 = (f32[4,2560]{1,0:T(4,128)}, f32[4,512]{1,0:T(4,128)}) custom-call(s32[5]{0:T(128)S(1)} %stack.23.pos_ref, f32[16,4,768]{2,1,0:T(4,128)S(1)} %all-to-all-done.in_ref), custom_call_target="tpu_custom_call" | custom-call | tf_op jit(solution)/shard_map/pallas_call | solution.py:65
  98.4 1.6 %collective-permute-done.24.refs_2_ = bf16[3,192,128]{2,1,0:T(8,128)(2,1)S(1)} collective-permute-done((bf16[3,192,128]{2,1,0:T(8,128)(2,1)S(1)}, bf16[3,192,128]{2,1,0:T(8,128)(2,1)S(1)}, u32[]{:S(2)}, u32[]{:S(2)}) %collective-permute-start.24) | collective-permute-done | bytes 147488 | tf_op jit(solution)/shard_map/ppermute | solution.py:521
  100.0 1.5 %collective-permute-done.25.refs_3_ = bf16[3,192,128]{2,1,0:T(8,128)(2,1)S(1)} collective-permute-done((bf16[3,192,128]{2,1,0:T(8,128)(2,1)S(1)}, bf16[3,192,128]{2,1,0:T(8,128)(2,1)S(1)}, u32[]{:S(2)}, u32[]{:S(2)}) %collective-permute-start.25) | collective-permute-done | bytes 147488 | tf_op jit(solution)/shard_map/ppermute | solution.py:521
  101.6 1.4 %shard_map.141 = (bf16[192,512]{1,0:T(8,128)(2,1)}, bf16[192,512]{1,0:T(8,128)(2,1)}, bf16[192,512]{1,0:T(8,128)(2,1)}) custom-call(s32[5]{0:T(128)S(1)} %stack.23.pos_ref, bf16[3,192,128]{2,1,0:T(8,128)(2,1)S(1)} %get-tuple-element.76.refs_0_, bf16[3,192,128]{2,1,0:T(8,128)(2,1)S(1)} %collective-permute-done.23.refs_1_, ...), custom_call_target="tpu_custom_call" | custom-call | tf_op jit(solution)/shard_map/pallas_call | solution.py:65
  (20 shorter events, 0.1 us)
Async XLA Ops:
  2.8 27.0 %collective-permute-start.15 = (bf16[320,512]{1,0:T(8,128)(2,1)S(1)}, bf16[320,512]{1,0:T(8,128)(2,1)S(1)}, u32[]{:S(2)}, u32[]{:S(2)}) collective-permute-start(bf16[320,512]{1,0:T(8,128)(2,1)S(1)} %shard_map.132.refs_10_), channel_id=1, source_target_pairs={{0,24},{2,26},{4,28},{6,30},{8,0},{10,2},{12,4},{14,6},{16,8},{18,... | collective-permute-start | bytes 983048 | tf_op jit(solution)/shard_map/ppermute | solution.py:526
  7.9 21.9 %collective-permute-start.14 = (bf16[320,512]{1,0:T(8,128)(2,1)S(1)}, bf16[320,512]{1,0:T(8,128)(2,1)S(1)}, u32[]{:S(2)}, u32[]{:S(2)}) collective-permute-start(bf16[320,512]{1,0:T(8,128)(2,1)S(1)} %shard_map.132.refs_10_), channel_id=1, source_target_pairs={{0,8},{2,10},{4,12},{6,14},{8,16},{10,18},{12,20},{14,22},{16,24},... | collective-permute-start | bytes 983048 | tf_op jit(solution)/shard_map/ppermute | solution.py:526
  10.8 3.7 %collective-permute-start.3 = (bf16[4,1152]{1,0:T(4,128)(2,1)S(1)}, bf16[4,1152]{1,0:T(4,128)(2,1)S(1)}, u32[]{:S(2)}, u32[]{:S(2)}) collective-permute-start(bf16[4,1152]{1,0:T(4,128)(2,1)S(1)} %get-tuple-element.53), channel_id=1, source_target_pairs={{0,2},{2,0},{4,6},{6,4},{8,10},{10,8},{12,14},{14,12},{16,18},{18,... | collective-permute-start | bytes 27656 | tf_op jit(solution)/shard_map/ppermute | solution.py:521
  12.3 3.7 %collective-permute-start.4 = (bf16[4,1152]{1,0:T(4,128)(2,1)S(1)}, bf16[4,1152]{1,0:T(4,128)(2,1)S(1)}, u32[]{:S(2)}, u32[]{:S(2)}) collective-permute-start(bf16[4,1152]{1,0:T(4,128)(2,1)S(1)} %get-tuple-element.54), channel_id=1, source_target_pairs={{0,4},{2,6},{4,0},{6,2},{8,12},{10,14},{12,8},{14,10},{16,20},{18,... | collective-permute-start | bytes 27656 | tf_op jit(solution)/shard_map/ppermute | solution.py:521
  13.8 4.6 %collective-permute-start.5 = (bf16[4,1152]{1,0:T(4,128)(2,1)S(1)}, bf16[4,1152]{1,0:T(4,128)(2,1)S(1)}, u32[]{:S(2)}, u32[]{:S(2)}) collective-permute-start(bf16[4,1152]{1,0:T(4,128)(2,1)S(1)} %get-tuple-element.55), channel_id=1, source_target_pairs={{0,6},{2,4},{4,2},{6,0},{8,14},{10,12},{12,10},{14,8},{16,22},{18,... | collective-permute-start | bytes 27656 | tf_op jit(solution)/shard_map/ppermute | solution.py:521
  19.0 5.5 %collective-permute-start.8 = (bf16[4,4,1152]{2,1,0:T(4,128)(2,1)S(1)}, bf16[4,4,1152]{2,1,0:T(4,128)(2,1)S(1)}, u32[]{:S(2)}, u32[]{:S(2)}) collective-permute-start(bf16[4,4,1152]{2,1,0:T(4,128)(2,1)S(1)} %shard_map.130.refs_0_), channel_id=1, source_target_pairs={{0,24},{2,26},{4,28},{6,30},{8,0},{10,2},{12,4},{14,6},{16,8},{18,... | collective-permute-start | bytes 110600 | tf_op jit(solution)/shard_map/ppermute | solution.py:526
  22.8 4.9 %collective-permute-start.7 = (bf16[4,4,1152]{2,1,0:T(4,128)(2,1)S(1)}, bf16[4,4,1152]{2,1,0:T(4,128)(2,1)S(1)}, u32[]{:S(2)}, u32[]{:S(2)}) collective-permute-start(bf16[4,4,1152]{2,1,0:T(4,128)(2,1)S(1)} %shard_map.130.refs_0_), channel_id=1, source_target_pairs={{0,16},{2,18},{4,20},{6,22},{8,24},{10,26},{12,28},{14,30},{16,0},... | collective-permute-start | bytes 110600 | tf_op jit(solution)/shard_map/ppermute | solution.py:526
  22.8 5.8 %collective-permute-start.6 = (bf16[4,4,1152]{2,1,0:T(4,128)(2,1)S(1)}, bf16[4,4,1152]{2,1,0:T(4,128)(2,1)S(1)}, u32[]{:S(2)}, u32[]{:S(2)}) collective-permute-start(bf16[4,4,1152]{2,1,0:T(4,128)(2,1)S(1)} %shard_map.130.refs_0_), channel_id=1, source_target_pairs={{0,8},{2,10},{4,12},{6,14},{8,16},{10,18},{12,20},{14,22},{16,24},... | collective-permute-start | bytes 110600 | tf_op jit(solution)/shard_map/ppermute | solution.py:526
  24.5 12.0 %collective-permute-start = (bf16[192,1024]{1,0:T(8,128)(2,1)S(1)}, bf16[192,1024]{1,0:T(8,128)(2,1)S(1)}, u32[]{:S(2)}, u32[]{:S(2)}) collective-permute-start(bf16[192,1024]{1,0:T(8,128)(2,1)S(1)} %get-tuple-element.47), channel_id=1, source_target_pairs={{0,2},{2,0},{4,6},{6,4},{8,10},{10,8},{12,14},{14,12},{16,18},{18,... | collective-permute-start | bytes 1179656 | tf_op jit(solution)/shard_map/ppermute | solution.py:521
  27.7 16.5 %collective-permute-start.1 = (bf16[192,1024]{1,0:T(8,128)(2,1)S(1)}, bf16[192,1024]{1,0:T(8,128)(2,1)S(1)}, u32[]{:S(2)}, u32[]{:S(2)}) collective-permute-start(bf16[192,1024]{1,0:T(8,128)(2,1)S(1)} %get-tuple-element.48), channel_id=1, source_target_pairs={{0,4},{2,6},{4,0},{6,2},{8,12},{10,14},{12,8},{14,10},{16,20},{18,... | collective-permute-start | bytes 1179656 | tf_op jit(solution)/shard_map/ppermute | solution.py:521
  28.6 15.6 %collective-permute-start.2 = (bf16[192,1024]{1,0:T(8,128)(2,1)S(1)}, bf16[192,1024]{1,0:T(8,128)(2,1)S(1)}, u32[]{:S(2)}, u32[]{:S(2)}) collective-permute-start(bf16[192,1024]{1,0:T(8,128)(2,1)S(1)} %get-tuple-element.49), channel_id=1, source_target_pairs={{0,6},{2,4},{4,2},{6,0},{8,14},{10,12},{12,10},{14,8},{16,22},{18,... | collective-permute-start | bytes 1179656 | tf_op jit(solution)/shard_map/ppermute | solution.py:521
  29.7 1.4 %collective-permute-start.9 = (bf16[64,1152]{1,0:T(8,128)(2,1)S(1)}, bf16[64,1152]{1,0:T(8,128)(2,1)S(1)}, u32[]{:S(2)}, u32[]{:S(2)}) collective-permute-start(bf16[64,1152]{1,0:T(8,128)(2,1)S(1)} %shard_map.131.refs_0_.adapt_ref), channel_id=1, source_target_pairs={{0,1},{1,0},{2,3},{3,2},{4,5},{5,4},{6,7},{7,6},{8,9},{9,8},{10,11... | collective-permute-start | bytes 442376 | tf_op jit(solution)/shard_map/ppermute | solution.py:538
  29.8 14.9 %collective-permute-start.10 = (bf16[192,1024]{1,0:T(8,128)(2,1)S(1)}, bf16[192,1024]{1,0:T(8,128)(2,1)S(1)}, u32[]{:S(2)}, u32[]{:S(2)}) collective-permute-start(bf16[192,1024]{1,0:T(8,128)(2,1)S(1)} %get-tuple-element.46.refs_0_.refs_2_), channel_id=1, source_target_pairs={{0,1},{1,0},{2,3},{3,2},{4,5},{5,4},{6,7},{7,6},{8,9},{9,8},{10,11... | collective-permute-start | bytes 1179656 | tf_op jit(solution)/shard_map/ppermute | solution.py:538
  31.2 15.5 %collective-permute-start.16 = (bf16[320,512]{1,0:T(8,128)(2,1)S(1)}, bf16[320,512]{1,0:T(8,128)(2,1)S(1)}, u32[]{:S(2)}, u32[]{:S(2)}) collective-permute-start(bf16[320,512]{1,0:T(8,128)(2,1)S(1)} %get-tuple-element.56), channel_id=1, source_target_pairs={{8,16},{10,18},{12,20},{14,22},{16,8},{18,10},{20,12},{22,14},{9,1... | collective-permute-start | bytes 983048 | tf_op jit(solution)/shard_map/ppermute | solution.py:533
  36.5 24.0 %collective-permute-start.11 = (bf16[192,1024]{1,0:T(8,128)(2,1)S(1)}, bf16[192,1024]{1,0:T(8,128)(2,1)S(1)}, u32[]{:S(2)}, u32[]{:S(2)}) collective-permute-start(bf16[192,1024]{1,0:T(8,128)(2,1)S(1)} %collective-permute-done.refs_1_.refs_4_.refs_3_), channel_id=1, source_target_pairs={{0,1},{1,0},{2,3},{3,2},{4,5},{5,4},{6,7},{7,6},{8,9},{9,8},{10,11... | collective-permute-start | bytes 1179656 | tf_op jit(solution)/shard_map/ppermute | solution.py:538
  44.2 16.3 %collective-permute-start.12 = (bf16[192,1024]{1,0:T(8,128)(2,1)S(1)}, bf16[192,1024]{1,0:T(8,128)(2,1)S(1)}, u32[]{:S(2)}, u32[]{:S(2)}) collective-permute-start(bf16[192,1024]{1,0:T(8,128)(2,1)S(1)} %collective-permute-done.1.refs_2_.refs_6_.refs_4_), channel_id=1, source_target_pairs={{0,1},{1,0},{2,3},{3,2},{4,5},{5,4},{6,7},{7,6},{8,9},{9,8},{10,11... | collective-permute-start | bytes 1179656 | tf_op jit(solution)/shard_map/ppermute | solution.py:538
  44.2 16.2 %collective-permute-start.13 = (bf16[192,1024]{1,0:T(8,128)(2,1)S(1)}, bf16[192,1024]{1,0:T(8,128)(2,1)S(1)}, u32[]{:S(2)}, u32[]{:S(2)}) collective-permute-start(bf16[192,1024]{1,0:T(8,128)(2,1)S(1)} %collective-permute-done.2.refs_3_.refs_8_.refs_5_), channel_id=1, source_target_pairs={{0,1},{1,0},{2,3},{3,2},{4,5},{5,4},{6,7},{7,6},{8,9},{9,8},{10,11... | collective-permute-start | bytes 1179656 | tf_op jit(solution)/shard_map/ppermute | solution.py:538
  44.7 15.7 %collective-permute-start.17 = (bf16[320,512]{1,0:T(8,128)(2,1)S(1)}, bf16[320,512]{1,0:T(8,128)(2,1)S(1)}, u32[]{:S(2)}, u32[]{:S(2)}) collective-permute-start(bf16[320,512]{1,0:T(8,128)(2,1)S(1)} %get-tuple-element.57), channel_id=1, source_target_pairs={{8,0},{10,2},{12,4},{14,6},{16,24},{18,26},{20,28},{22,30},{9,1},{... | collective-permute-start | bytes 983048 | tf_op jit(solution)/shard_map/ppermute | solution.py:533
  46.7 22.1 %collective-permute-start.21 = (bf16[2,768,128]{2,1,0:T(8,128)(2,1)S(1)}, bf16[2,768,128]{2,1,0:T(8,128)(2,1)S(1)}, u32[]{:S(2)}, u32[]{:S(2)}) collective-permute-start(bf16[2,768,128]{2,1,0:T(8,128)(2,1)S(1)} %get-tuple-element.51.kv_ref), channel_id=1, source_target_pairs={{0,8},{2,10},{5,13},{7,15},{9,17},{11,19},{12,20},{14,22},{16,24},... | collective-permute-start | bytes 1179656 | tf_op jit(solution)/shard_map/ppermute | solution.py:548
  62.4 13.6 %collective-permute-start.19 = (bf16[768,128]{1,0:T(8,128)(2,1)S(1)}, bf16[768,128]{1,0:T(8,128)(2,1)S(1)}, u32[]{:S(2)}, u32[]{:S(2)}) collective-permute-start(bf16[768,128]{1,0:T(8,128)(2,1)S(1)} %get-tuple-element.60), channel_id=1, source_target_pairs={{0,4},{2,6},{4,0},{6,2},{8,12},{10,14},{12,8},{14,10},{16,20},{18,... | collective-permute-start | bytes 589832 | tf_op jit(solution)/shard_map/ppermute | solution.py:521
  64.2 12.5 %collective-permute-start.20 = (bf16[768,128]{1,0:T(8,128)(2,1)S(1)}, bf16[768,128]{1,0:T(8,128)(2,1)S(1)}, u32[]{:S(2)}, u32[]{:S(2)}) collective-permute-start(bf16[768,128]{1,0:T(8,128)(2,1)S(1)} %get-tuple-element.61), channel_id=1, source_target_pairs={{0,6},{2,4},{4,2},{6,0},{8,14},{10,12},{12,10},{14,8},{16,22},{18,... | collective-permute-start | bytes 589832 | tf_op jit(solution)/shard_map/ppermute | solution.py:521
  67.5 9.2 %collective-permute-start.18 = (bf16[768,128]{1,0:T(8,128)(2,1)S(1)}, bf16[768,128]{1,0:T(8,128)(2,1)S(1)}, u32[]{:S(2)}, u32[]{:S(2)}) collective-permute-start(bf16[768,128]{1,0:T(8,128)(2,1)S(1)} %get-tuple-element.59), channel_id=1, source_target_pairs={{0,2},{2,0},{4,6},{6,4},{8,10},{10,8},{12,14},{14,12},{16,18},{18,... | collective-permute-start | bytes 589832 | tf_op jit(solution)/shard_map/ppermute | solution.py:521
  69.8 1.5 %collective-permute-start.26 = (f32[384,64]{1,0:T(8,128)S(1)}, f32[384,64]{1,0:T(8,128)S(1)}, u32[]{:S(2)}, u32[]{:S(2)}) collective-permute-start(f32[384,64]{1,0:T(8,128)S(1)} %get-tuple-element.84), channel_id=1, source_target_pairs={{0,1},{1,0},{2,3},{3,2},{4,5},{5,4},{6,7},{7,6},{8,9},{9,8},{10,11... | collective-permute-start | bytes 294920 | tf_op jit(solution)/shard_map/ppermute | solution.py:538
  71.9 7.3 %collective-permute-start.29 = (bf16[384,128]{1,0:T(8,128)(2,1)S(1)}, bf16[384,128]{1,0:T(8,128)(2,1)S(1)}, u32[]{:S(2)}, u32[]{:S(2)}) collective-permute-start(bf16[384,128]{1,0:T(8,128)(2,1)S(1)} %shard_map.143.refs_0_), channel_id=1, source_target_pairs={{0,6},{2,4},{4,2},{6,0},{8,14},{10,12},{12,10},{14,8},{16,22},{18,... | collective-permute-start | bytes 294920 | tf_op jit(solution)/shard_map/ppermute | solution.py:521
  76.0 5.2 %collective-permute-start.28 = (bf16[384,128]{1,0:T(8,128)(2,1)S(1)}, bf16[384,128]{1,0:T(8,128)(2,1)S(1)}, u32[]{:S(2)}, u32[]{:S(2)}) collective-permute-start(bf16[384,128]{1,0:T(8,128)(2,1)S(1)} %shard_map.143.refs_0_), channel_id=1, source_target_pairs={{0,4},{2,6},{4,0},{6,2},{8,12},{10,14},{12,8},{14,10},{16,20},{18,... | collective-permute-start | bytes 294920 | tf_op jit(solution)/shard_map/ppermute | solution.py:521
  76.0 5.6 %collective-permute-start.27 = (bf16[384,128]{1,0:T(8,128)(2,1)S(1)}, bf16[384,128]{1,0:T(8,128)(2,1)S(1)}, u32[]{:S(2)}, u32[]{:S(2)}) collective-permute-start(bf16[384,128]{1,0:T(8,128)(2,1)S(1)} %shard_map.143.refs_0_), channel_id=1, source_target_pairs={{0,2},{2,0},{4,6},{6,4},{8,10},{10,8},{12,14},{14,12},{16,18},{18,... | collective-permute-start | bytes 294920 | tf_op jit(solution)/shard_map/ppermute | solution.py:521
  77.5 12.0 %collective-permute-start.22 = (bf16[2,768,128]{2,1,0:T(8,128)(2,1)S(1)}, bf16[2,768,128]{2,1,0:T(8,128)(2,1)S(1)}, u32[]{:S(2)}, u32[]{:S(2)}) collective-permute-start(bf16[2,768,128]{2,1,0:T(8,128)(2,1)S(1)} %get-tuple-element.75), channel_id=1, source_target_pairs={{8,0},{10,2},{13,5},{15,7},{17,9},{19,11},{20,12},{22,14},{24,16},... | collective-permute-start | bytes 1179656 | tf_op jit(solution)/shard_map/ppermute | solution.py:551
  81.7 1.4 %collective-permute-start.30 = (bf16[384,128]{1,0:T(8,128)(2,1)S(1)}, bf16[384,128]{1,0:T(8,128)(2,1)S(1)}, u32[]{:S(2)}, u32[]{:S(2)}) collective-permute-start(bf16[384,128]{1,0:T(8,128)(2,1)S(1)} %shard_map.144.refs_0_), channel_id=1, source_target_pairs={{0,1},{1,0},{2,3},{3,2},{4,5},{5,4},{6,7},{7,6},{8,9},{9,8},{10,11... | collective-permute-start | bytes 294920 | tf_op jit(solution)/shard_map/ppermute | solution.py:538
  84.7 12.4 %all-to-all-start = ((f32[16,4,768]{2,1,0:T(4,128)}), f32[16,4,768]{2,1,0:T(4,128)S(1)}, u32[]{:S(2)}, u32[]{:S(2)}) async-start(f32[16,4,768]{2,1,0:T(4,128)} %shard_map.145), calls=%async_computation | async-start | bytes 393216 | tf_op jit(solution)/shard_map/all_to_all | solution.py:689
  90.2 8.2 %collective-permute-start.23 = (bf16[3,192,128]{2,1,0:T(8,128)(2,1)S(1)}, bf16[3,192,128]{2,1,0:T(8,128)(2,1)S(1)}, u32[]{:S(2)}, u32[]{:S(2)}) collective-permute-start(bf16[3,192,128]{2,1,0:T(8,128)(2,1)S(1)} %get-tuple-element.77), channel_id=1, source_target_pairs={{0,2},{2,0},{4,6},{6,4},{8,10},{10,8},{12,14},{14,12},{16,18},{18,... | collective-permute-start | bytes 442376 | tf_op jit(solution)/shard_map/ppermute | solution.py:521
  92.0 8.0 %collective-permute-start.24 = (bf16[3,192,128]{2,1,0:T(8,128)(2,1)S(1)}, bf16[3,192,128]{2,1,0:T(8,128)(2,1)S(1)}, u32[]{:S(2)}, u32[]{:S(2)}) collective-permute-start(bf16[3,192,128]{2,1,0:T(8,128)(2,1)S(1)} %get-tuple-element.78), channel_id=1, source_target_pairs={{0,4},{2,6},{4,0},{6,2},{8,12},{10,14},{12,8},{14,10},{16,20},{18,... | collective-permute-start | bytes 442376 | tf_op jit(solution)/shard_map/ppermute | solution.py:521
  93.5 8.1 %collective-permute-start.25 = (bf16[3,192,128]{2,1,0:T(8,128)(2,1)S(1)}, bf16[3,192,128]{2,1,0:T(8,128)(2,1)S(1)}, u32[]{:S(2)}, u32[]{:S(2)}) collective-permute-start(bf16[3,192,128]{2,1,0:T(8,128)(2,1)S(1)} %get-tuple-element.79), channel_id=1, source_target_pairs={{0,6},{2,4},{4,2},{6,0},{8,14},{10,12},{12,10},{14,8},{16,22},{18,... | collective-permute-start | bytes 442376 | tf_op jit(solution)/shard_map/ppermute | solution.py:521

commit v7 on v6

--- a/solution.py
+++ b/solution.py
@@ -462,12 +462,10 @@
     for s in range(fsdp):
         src = lax.rem(core + (fsdp - s), fsdp)
         scr[pl.ds(pl.multiple_of(src * part_rows, part_rows), part_rows), :] = both[s][...]
-    acc = None
-    for s in range(half):
-        at = pl.ds(pl.multiple_of((mine ^ s) * rows, rows), rows)
-        part = nn(scr[at, :].T[rank:, :], grads[s][:, :wide])
-        acc = part if acc is None else acc + part
-    acc = adapter_scale * acc
+    order = [pl.ds(pl.multiple_of((mine ^ s) * rows, rows), rows) for s in range(half)]
+    left = jnp.concatenate([scr[at, rank:] for at in order], axis=0)
+    right = jnp.concatenate([ref[:, :wide] for ref in grads], axis=0)
+    acc = adapter_scale * nn(left.T, right)
     low = nn(scr[...].T[:rank, :], o_ref[...].astype(BF))
     for p in range(planes):
         for j in range(half):

time: 103 us -> 103 us (level)
  no operation moved by 1% of the time
where the time goes in v7:
time: 103 us
  waiting for transfers between devices  41 us (40%)
  starting transfers between devices  40 us (39%)
  Pallas kernels  21.1 us (20%)
    ppermute x15, waiting for transfers between devices, in_plane(): return lax.ppermute(x, 'ctx', [(i, i ^ s) for i in range(n_ctx)])  22.4 us
    pallas_call x19, Pallas kernels, call(): pl.pallas_call(body, out_shape=outs, in_specs=[SM] * n_scalar + [spec] *...  21.1 us
    ppermute x15, starting transfers between devices, in_plane(): return lax.ppermute(x, 'ctx', [(i, i ^ s) for i in range(n_ctx)])  17.8 us
    ppermute x5, starting transfers between devices, along(): lax.ppermute(x, 'ctx', [(i, (i + s * half) % n_ctx) for i in range(n_ctx)])  9.65 us
    ppermute x2, waiting for transfers between devices, from_plane(): return lax.ppermute(x, 'ctx', route)  9.18 us
    ppermute x1, starting transfers between devices, to_later(): return lax.ppermute(x, ('ctx', 'fsdp'), pairs)  4.59 us
    ppermute x5, waiting for transfers between devices, along(): lax.ppermute(x, 'ctx', [(i, (i + s * half) % n_ctx) for i in range(n_ctx)])  3.9 us
    all_to_all x1, starting transfers between devices, on_device(): lax.all_to_all(adapter_grads, 'ctx', split_axis=0, concat_axis=0, tiled=T...  3.52 us
  transfers between devices with their start and end apart: 32, of which 18 were waited for; matrix products, arithmetic and copies ran while one was open for 0% of the time, Pallas kernels for 17%

profile of v7, /device:TPU:0, one launch (start us, length us, event | category | flops | bytes accessed | tf_op | source)
XLA Modules:
  0.0 103.0 jit_solution(13779648598345466063)
XLA Ops:
  0.6 2.1 %shard_map.132.refs_10_ = bf16[320,512]{1,0:T(8,128)(2,1)S(1)} custom-call(s32[320,512]{1,0:T(8,128)} %codes_in.1, s32[8,320]{1,0:T(8,128)} %bitcast.7, f32[2,128]{1,0:T(2,128)} %bitcast.8), custom_call_target="tpu_custom_call" | custom-call | tf_op jit(solution)/shard_map/pallas_call | solution.py:65
  2.8 5.1 %collective-permute-start.15 = (bf16[320,512]{1,0:T(8,128)(2,1)S(1)}, bf16[320,512]{1,0:T(8,128)(2,1)S(1)}, u32[]{:S(2)}, u32[]{:S(2)}) collective-permute-start(bf16[320,512]{1,0:T(8,128)(2,1)S(1)} %shard_map.132.refs_10_), channel_id=1, source_target_pairs={{0,24},{2,26},{4,28},{6,30},{8,0},{10,2},{12,4},{14,6},{16,8},{18,... | collective-permute-start | bytes 983048 | tf_op jit(solution)/shard_map/ppermute | solution.py:524
  7.9 0.1 stack.23.pos_ref
  8.0 2.8 %shard_map.128 = (bf16[192,1024]{1,0:T(8,128)(2,1)S(1)}, bf16[192,1024]{1,0:T(8,128)(2,1)S(1)}, bf16[192,1024]{1,0:T(8,128)(2,1)S(1)}, bf16[192,1024]{1,0:T(8,12...) custom-call(s32[5]{0:T(128)S(1)} %stack.23.pos_ref, ...), custom_call_target="tpu_custom_call" | custom-call | tf_op jit(solution)/shard_map/pallas_call | solution.py:65
  10.8 1.6 %collective-permute-start.3 = (bf16[4,1152]{1,0:T(4,128)(2,1)S(1)}, bf16[4,1152]{1,0:T(4,128)(2,1)S(1)}, u32[]{:S(2)}, u32[]{:S(2)}) collective-permute-start(bf16[4,1152]{1,0:T(4,128)(2,1)S(1)} %get-tuple-element.53), channel_id=1, source_target_pairs={{0,2},{2,0},{4,6},{6,4},{8,10},{10,8},{12,14},{14,12},{16,18},{18,... | collective-permute-start | bytes 27656 | tf_op jit(solution)/shard_map/ppermute | solution.py:519
  12.3 1.5 %collective-permute-start.4 = (bf16[4,1152]{1,0:T(4,128)(2,1)S(1)}, bf16[4,1152]{1,0:T(4,128)(2,1)S(1)}, u32[]{:S(2)}, u32[]{:S(2)}) collective-permute-start(bf16[4,1152]{1,0:T(4,128)(2,1)S(1)} %get-tuple-element.54), channel_id=1, source_target_pairs={{0,4},{2,6},{4,0},{6,2},{8,12},{10,14},{12,8},{14,10},{16,20},{18,... | collective-permute-start | bytes 27656 | tf_op jit(solution)/shard_map/ppermute | solution.py:519
  13.8 0.5 collective-permute-start.5
  14.3 0.2 collective-permute-done.3.refs_1_
  14.5 1.5 %collective-permute-done.4.refs_2_ = bf16[4,1152]{1,0:T(4,128)(2,1)S(1)} collective-permute-done((bf16[4,1152]{1,0:T(4,128)(2,1)S(1)}, bf16[4,1152]{1,0:T(4,128)(2,1)S(1)}, u32[]{:S(2)}, u32[]{:S(2)}) %collective-permute-start.4) | collective-permute-done | bytes 9248 | tf_op jit(solution)/shard_map/ppermute | solution.py:519
  16.0 2.4 %collective-permute-done.5.refs_3_ = bf16[4,1152]{1,0:T(4,128)(2,1)S(1)} collective-permute-done((bf16[4,1152]{1,0:T(4,128)(2,1)S(1)}, bf16[4,1152]{1,0:T(4,128)(2,1)S(1)}, u32[]{:S(2)}, u32[]{:S(2)}) %collective-permute-start.5) | collective-permute-done | bytes 9248 | tf_op jit(solution)/shard_map/ppermute | solution.py:519
  18.4 0.5 shard_map.130.refs_0_
  19.0 3.9 %collective-permute-start.8 = (bf16[4,4,1152]{2,1,0:T(4,128)(2,1)S(1)}, bf16[4,4,1152]{2,1,0:T(4,128)(2,1)S(1)}, u32[]{:S(2)}, u32[]{:S(2)}) collective-permute-start(bf16[4,4,1152]{2,1,0:T(4,128)(2,1)S(1)} %shard_map.130.refs_0_), channel_id=1, source_target_pairs={{0,24},{2,26},{4,28},{6,30},{8,0},{10,2},{12,4},{14,6},{16,8},{18,... | collective-permute-start | bytes 110600 | tf_op jit(solution)/shard_map/ppermute | solution.py:524
  22.8 0.6 collective-permute-start.6
  23.5 1.0 collective-permute-done.8.refs_3_
  24.5 0.7 collective-permute-start
  25.2 2.5 %collective-permute-done.7.refs_2_ = bf16[4,4,1152]{2,1,0:T(4,128)(2,1)S(1)} collective-permute-done((bf16[4,4,1152]{2,1,0:T(4,128)(2,1)S(1)}, bf16[4,4,1152]{2,1,0:T(4,128)(2,1)S(1)}, u32[]{:S(2)}, u32[]{:S(2)}) %collective-permute-start.7) | collective-permute-done | bytes 36896 | tf_op jit(solution)/shard_map/ppermute | solution.py:524
  27.7 0.5 collective-permute-start.1
  28.2 0.4 collective-permute-done.6.refs_1_
  28.6 1.1 %collective-permute-start.2 = (bf16[192,1024]{1,0:T(8,128)(2,1)S(1)}, bf16[192,1024]{1,0:T(8,128)(2,1)S(1)}, u32[]{:S(2)}, u32[]{:S(2)}) collective-permute-start(bf16[192,1024]{1,0:T(8,128)(2,1)S(1)} %get-tuple-element.49), channel_id=1, source_target_pairs={{0,6},{2,4},{4,2},{6,0},{8,14},{10,12},{12,10},{14,8},{16,22},{18,... | collective-permute-start | bytes 1179656 | tf_op jit(solution)/shard_map/ppermute | solution.py:519
  29.7 0.1 collective-permute-start.9
  29.8 0.5 collective-permute-start.10
  30.3 0.6 shard_map.133
  30.9 0.3 collective-permute-done.9.refs_1_
  31.2 0.7 collective-permute-start.16
  31.9 4.6 %collective-permute-done.refs_1_.refs_4_.refs_3_ = bf16[192,1024]{1,0:T(8,128)(2,1)S(1)} collective-permute-done((bf16[192,1024]{1,0:T(8,128)(2,1)S(1)}, bf16[192,1024]{1,0:T(8,128)(2,1)S(1)}, u32[]{:S(2)}, u32[]{:S(2)}) %collective-permute-start) | collective-permute-done | bytes 393248 | tf_op jit(solution)/shard_map/ppermute | solution.py:519
  36.5 7.8 %collective-permute-done.1.refs_2_.refs_6_.refs_4_ = bf16[192,1024]{1,0:T(8,128)(2,1)S(1)} collective-permute-done((bf16[192,1024]{1,0:T(8,128)(2,1)S(1)}, bf16[192,1024]{1,0:T(8,128)(2,1)S(1)}, u32[]{:S(2)}, u32[]{:S(2)}) %collective-permute-start.1) | collective-permute-done | bytes 393248 | tf_op jit(solution)/shard_map/ppermute | solution.py:519
  44.2 0.5 collective-permute-start.13
  44.7 1.3 %collective-permute-start.17 = (bf16[320,512]{1,0:T(8,128)(2,1)S(1)}, bf16[320,512]{1,0:T(8,128)(2,1)S(1)}, u32[]{:S(2)}, u32[]{:S(2)}) collective-permute-start(bf16[320,512]{1,0:T(8,128)(2,1)S(1)} %get-tuple-element.57), channel_id=1, source_target_pairs={{8,0},{10,2},{12,4},{14,6},{16,24},{18,26},{20,28},{22,30},{9,1},{... | collective-permute-start | bytes 983048 | tf_op jit(solution)/shard_map/ppermute | solution.py:531
  46.0 0.6 shard_map.129
  46.7 4.6 %collective-permute-start.21 = (bf16[2,768,128]{2,1,0:T(8,128)(2,1)S(1)}, bf16[2,768,128]{2,1,0:T(8,128)(2,1)S(1)}, u32[]{:S(2)}, u32[]{:S(2)}) collective-permute-start(bf16[2,768,128]{2,1,0:T(8,128)(2,1)S(1)} %get-tuple-element.51.kv_ref), channel_id=1, source_target_pairs={{0,8},{2,10},{5,13},{7,15},{9,17},{11,19},{12,20},{14,22},{16,24},... | collective-permute-start | bytes 1179656 | tf_op jit(solution)/shard_map/ppermute | solution.py:546
  51.3 9.2 %collective-permute-done.17.refs_14_ = bf16[320,512]{1,0:T(8,128)(2,1)S(1)} collective-permute-done((bf16[320,512]{1,0:T(8,128)(2,1)S(1)}, bf16[320,512]{1,0:T(8,128)(2,1)S(1)}, u32[]{:S(2)}, u32[]{:S(2)}) %collective-permute-start.17) | collective-permute-done | bytes 327712 | tf_op jit(solution)/shard_map/ppermute | solution.py:531
  60.5 1.9 %shard_map.135 = (bf16[768,128]{1,0:T(8,128)(2,1)S(1)}, bf16[768,128]{1,0:T(8,128)(2,1)S(1)}) custom-call(s32[5]{0:T(128)S(1)} %stack.23.pos_ref, bf16[64,1152]{1,0:T(8,128)(2,1)S(1)} %shard_map.131.refs_0_.adapt_ref, bf16[64,1152]{1,0:T(8,128)(2,1)S(1)} %collective-permute-done.9.refs_1_, bf16[192,1024]{1,0:T(8,128)(2,1)S(1)} %get-tuple-element.46.refs_0_.refs_2_, ...), custom_call_target="tpu_custom_call" | custom-call | tf_op jit(solution)/shard_map/pallas_call | solution.py:65
  62.4 1.8 %collective-permute-start.19 = (bf16[768,128]{1,0:T(8,128)(2,1)S(1)}, bf16[768,128]{1,0:T(8,128)(2,1)S(1)}, u32[]{:S(2)}, u32[]{:S(2)}) collective-permute-start(bf16[768,128]{1,0:T(8,128)(2,1)S(1)} %get-tuple-element.60), channel_id=1, source_target_pairs={{0,4},{2,6},{4,0},{6,2},{8,12},{10,14},{12,8},{14,10},{16,20},{18,... | collective-permute-start | bytes 589832 | tf_op jit(solution)/shard_map/ppermute | solution.py:519
  64.2 1.4 %collective-permute-start.20 = (bf16[768,128]{1,0:T(8,128)(2,1)S(1)}, bf16[768,128]{1,0:T(8,128)(2,1)S(1)}, u32[]{:S(2)}, u32[]{:S(2)}) collective-permute-start(bf16[768,128]{1,0:T(8,128)(2,1)S(1)} %get-tuple-element.61), channel_id=1, source_target_pairs={{0,6},{2,4},{4,2},{6,0},{8,14},{10,12},{12,10},{14,8},{16,22},{18,... | collective-permute-start | bytes 589832 | tf_op jit(solution)/shard_map/ppermute | solution.py:519
  65.6 1.9 %shard_map.134 = (bf16[768,128]{1,0:T(8,128)(2,1)S(1)}, bf16[768,128]{1,0:T(8,128)(2,1)S(1)}) custom-call(s32[5]{0:T(128)S(1)} %stack.23.pos_ref, bf16[64,1152]{1,0:T(8,128)(2,1)S(1)} %shard_map.131.refs_0_.adapt_ref, bf16[64,1152]{1,0:T(8,128)(2,1)S(1)} %collective-permute-done.9.refs_1_, bf16[192,1024]{1,0:T(8,128)(2,1)S(1)} %get-tuple-element.46.refs_0_.refs_2_, ...), custom_call_target="tpu_custom_call" | custom-call | tf_op jit(solution)/shard_map/pallas_call | solution.py:65
  67.5 0.4 collective-permute-start.18
  67.8 1.0 shard_map.136
  68.8 0.9 shard_map.137
  69.8 0.1 collective-permute-start.26
  69.8 1.0 shard_map.142.lora_ref
  70.8 0.5 collective-permute-done.26.refs_1_
  71.3 0.6 shard_map.143.refs_0_
  71.9 4.1 %collective-permute-start.29 = (bf16[384,128]{1,0:T(8,128)(2,1)S(1)}, bf16[384,128]{1,0:T(8,128)(2,1)S(1)}, u32[]{:S(2)}, u32[]{:S(2)}) collective-permute-start(bf16[384,128]{1,0:T(8,128)(2,1)S(1)} %shard_map.143.refs_0_), channel_id=1, source_target_pairs={{0,6},{2,4},{4,2},{6,0},{8,14},{10,12},{12,10},{14,8},{16,22},{18,... | collective-permute-start | bytes 294920 | tf_op jit(solution)/shard_map/ppermute | solution.py:519
  76.0 0.7 collective-permute-start.27
  76.7 0.8 shard_map.138
  77.5 1.3 %collective-permute-start.22 = (bf16[2,768,128]{2,1,0:T(8,128)(2,1)S(1)}, bf16[2,768,128]{2,1,0:T(8,128)(2,1)S(1)}, u32[]{:S(2)}, u32[]{:S(2)}) collective-permute-start(bf16[2,768,128]{2,1,0:T(8,128)(2,1)S(1)} %get-tuple-element.75), channel_id=1, source_target_pairs={{8,0},{10,2},{13,5},{15,7},{17,9},{19,11},{20,12},{22,14},{24,16},... | collective-permute-start | bytes 1179656 | tf_op jit(solution)/shard_map/ppermute | solution.py:549
  78.8 0.4 collective-permute-done.29.refs_3_
  79.2 2.0 %collective-permute-done.28.refs_2_ = bf16[384,128]{1,0:T(8,128)(2,1)S(1)} collective-permute-done((bf16[384,128]{1,0:T(8,128)(2,1)S(1)}, bf16[384,128]{1,0:T(8,128)(2,1)S(1)}, u32[]{:S(2)}, u32[]{:S(2)}) %collective-permute-start.28) | collective-permute-done | bytes 98336 | tf_op jit(solution)/shard_map/ppermute | solution.py:519
  81.2 0.4 collective-permute-done.27.refs_1_
  81.6 0.1 shard_map.144.refs_0_
  81.7 0.1 collective-permute-start.30
  81.8 1.3 %collective-permute-done.30.refs_1_ = bf16[384,128]{1,0:T(8,128)(2,1)S(1)} collective-permute-done((bf16[384,128]{1,0:T(8,128)(2,1)S(1)}, bf16[384,128]{1,0:T(8,128)(2,1)S(1)}, u32[]{:S(2)}, u32[]{:S(2)}) %collective-permute-start.30) | collective-permute-done | bytes 98336 | tf_op jit(solution)/shard_map/ppermute | solution.py:536
  83.1 1.7 %shard_map.145 = f32[16,4,768]{2,1,0:T(4,128)} custom-call(s32[5]{0:T(128)S(1)} %stack.23.pos_ref, f32[768,128]{1,0:T(8,128)S(1)} %get-tuple-element.65.refs_6_.o_ref, bf16[384,128]{1,0:T(8,128)(2,1)S(1)} %shard_map.144.refs_0_, bf16[384,128]{1,0:T(8,128)(2,1)S(1)} %collective-permute-done.30.refs_1_, ...), custom_call_target="tpu_custom_call" | custom-call | tf_op jit(solution)/shard_map/pallas_call | solution.py:65
  84.7 3.5 %all-to-all-start = ((f32[16,4,768]{2,1,0:T(4,128)}), f32[16,4,768]{2,1,0:T(4,128)S(1)}, u32[]{:S(2)}, u32[]{:S(2)}) async-start(f32[16,4,768]{2,1,0:T(4,128)} %shard_map.145), calls=%async_computation | async-start | bytes 393216 | tf_op jit(solution)/shard_map/all_to_all | solution.py:687
  88.3 1.2 %shard_map.139 = (bf16[768,128]{1,0:T(8,128)(2,1)S(1)}, f32[2,768,128]{2,1,0:T(8,128)S(1)}) custom-call(bf16[768,128]{1,0:T(8,128)(2,1)S(1)} %get-tuple-element.50.q_ref.refs_4_, bf16[2,768,128]{2,1,0:T(8,128)(2,1)S(1)} %get-tuple-element.51.kv_ref, bf16[768,128]{1,0:T(8,128)(2,1)S(1)} %get-tuple-element.68.do_ref, ...), custom_call_target="tpu_custom_call" | custom-call | tf_op jit(solution)/shard_map/pallas_call | solution.py:65
  89.5 0.6 shard_map.140
  90.2 1.9 %collective-permute-start.23 = (bf16[3,192,128]{2,1,0:T(8,128)(2,1)S(1)}, bf16[3,192,128]{2,1,0:T(8,128)(2,1)S(1)}, u32[]{:S(2)}, u32[]{:S(2)}) collective-permute-start(bf16[3,192,128]{2,1,0:T(8,128)(2,1)S(1)} %get-tuple-element.77), channel_id=1, source_target_pairs={{0,2},{2,0},{4,6},{6,4},{8,10},{10,8},{12,14},{14,12},{16,18},{18,... | collective-permute-start | bytes 442376 | tf_op jit(solution)/shard_map/ppermute | solution.py:519
  92.0 1.5 %collective-permute-start.24 = (bf16[3,192,128]{2,1,0:T(8,128)(2,1)S(1)}, bf16[3,192,128]{2,1,0:T(8,128)(2,1)S(1)}, u32[]{:S(2)}, u32[]{:S(2)}) collective-permute-start(bf16[3,192,128]{2,1,0:T(8,128)(2,1)S(1)} %get-tuple-element.78), channel_id=1, source_target_pairs={{0,4},{2,6},{4,0},{6,2},{8,12},{10,14},{12,8},{14,10},{16,20},{18,... | collective-permute-start | bytes 442376 | tf_op jit(solution)/shard_map/ppermute | solution.py:519
  93.5 0.2 collective-permute-start.25
  93.7 3.4 %all-to-all-done.in_ref = f32[16,4,768]{2,1,0:T(4,128)S(1)} async-done(((f32[16,4,768]{2,1,0:T(4,128)}), f32[16,4,768]{2,1,0:T(4,128)S(1)}, u32[]{:S(2)}, u32[]{:S(2)}) %all-to-all-start) | async-done | bytes 196640 | tf_op jit(solution)/shard_map/all_to_all | solution.py:687
  97.2 1.2 %shard_map.146 = (f32[4,2560]{1,0:T(4,128)}, f32[4,512]{1,0:T(4,128)}) custom-call(s32[5]{0:T(128)S(1)} %stack.23.pos_ref, f32[16,4,768]{2,1,0:T(4,128)S(1)} %all-to-all-done.in_ref), custom_call_target="tpu_custom_call" | custom-call | tf_op jit(solution)/shard_map/pallas_call | solution.py:65
  98.4 1.6 %collective-permute-done.24.refs_2_ = bf16[3,192,128]{2,1,0:T(8,128)(2,1)S(1)} collective-permute-done((bf16[3,192,128]{2,1,0:T(8,128)(2,1)S(1)}, bf16[3,192,128]{2,1,0:T(8,128)(2,1)S(1)}, u32[]{:S(2)}, u32[]{:S(2)}) %collective-permute-start.24) | collective-permute-done | bytes 147488 | tf_op jit(solution)/shard_map/ppermute | solution.py:519
  100.0 1.5 %collective-permute-done.25.refs_3_ = bf16[3,192,128]{2,1,0:T(8,128)(2,1)S(1)} collective-permute-done((bf16[3,192,128]{2,1,0:T(8,128)(2,1)S(1)}, bf16[3,192,128]{2,1,0:T(8,128)(2,1)S(1)}, u32[]{:S(2)}, u32[]{:S(2)}) %collective-permute-start.25) | collective-permute-done | bytes 147488 | tf_op jit(solution)/shard_map/ppermute | solution.py:519
  101.6 1.4 %shard_map.141 = (bf16[192,512]{1,0:T(8,128)(2,1)}, bf16[192,512]{1,0:T(8,128)(2,1)}, bf16[192,512]{1,0:T(8,128)(2,1)}) custom-call(s32[5]{0:T(128)S(1)} %stack.23.pos_ref, bf16[3,192,128]{2,1,0:T(8,128)(2,1)S(1)} %get-tuple-element.76.refs_0_, bf16[3,192,128]{2,1,0:T(8,128)(2,1)S(1)} %collective-permute-done.23.refs_1_, ...), custom_call_target="tpu_custom_call" | custom-call | tf_op jit(solution)/shard_map/pallas_call | solution.py:65
  (20 shorter events, 0.1 us)
Async XLA Ops:
  2.8 27.0 %collective-permute-start.15 = (bf16[320,512]{1,0:T(8,128)(2,1)S(1)}, bf16[320,512]{1,0:T(8,128)(2,1)S(1)}, u32[]{:S(2)}, u32[]{:S(2)}) collective-permute-start(bf16[320,512]{1,0:T(8,128)(2,1)S(1)} %shard_map.132.refs_10_), channel_id=1, source_target_pairs={{0,24},{2,26},{4,28},{6,30},{8,0},{10,2},{12,4},{14,6},{16,8},{18,... | collective-permute-start | bytes 983048 | tf_op jit(solution)/shard_map/ppermute | solution.py:524
  7.9 21.9 %collective-permute-start.14 = (bf16[320,512]{1,0:T(8,128)(2,1)S(1)}, bf16[320,512]{1,0:T(8,128)(2,1)S(1)}, u32[]{:S(2)}, u32[]{:S(2)}) collective-permute-start(bf16[320,512]{1,0:T(8,128)(2,1)S(1)} %shard_map.132.refs_10_), channel_id=1, source_target_pairs={{0,8},{2,10},{4,12},{6,14},{8,16},{10,18},{12,20},{14,22},{16,24},... | collective-permute-start | bytes 983048 | tf_op jit(solution)/shard_map/ppermute | solution.py:524
  10.8 3.7 %collective-permute-start.3 = (bf16[4,1152]{1,0:T(4,128)(2,1)S(1)}, bf16[4,1152]{1,0:T(4,128)(2,1)S(1)}, u32[]{:S(2)}, u32[]{:S(2)}) collective-permute-start(bf16[4,1152]{1,0:T(4,128)(2,1)S(1)} %get-tuple-element.53), channel_id=1, source_target_pairs={{0,2},{2,0},{4,6},{6,4},{8,10},{10,8},{12,14},{14,12},{16,18},{18,... | collective-permute-start | bytes 27656 | tf_op jit(solution)/shard_map/ppermute | solution.py:519
  12.3 3.7 %collective-permute-start.4 = (bf16[4,1152]{1,0:T(4,128)(2,1)S(1)}, bf16[4,1152]{1,0:T(4,128)(2,1)S(1)}, u32[]{:S(2)}, u32[]{:S(2)}) collective-permute-start(bf16[4,1152]{1,0:T(4,128)(2,1)S(1)} %get-tuple-element.54), channel_id=1, source_target_pairs={{0,4},{2,6},{4,0},{6,2},{8,12},{10,14},{12,8},{14,10},{16,20},{18,... | collective-permute-start | bytes 27656 | tf_op jit(solution)/shard_map/ppermute | solution.py:519
  13.8 4.6 %collective-permute-start.5 = (bf16[4,1152]{1,0:T(4,128)(2,1)S(1)}, bf16[4,1152]{1,0:T(4,128)(2,1)S(1)}, u32[]{:S(2)}, u32[]{:S(2)}) collective-permute-start(bf16[4,1152]{1,0:T(4,128)(2,1)S(1)} %get-tuple-element.55), channel_id=1, source_target_pairs={{0,6},{2,4},{4,2},{6,0},{8,14},{10,12},{12,10},{14,8},{16,22},{18,... | collective-permute-start | bytes 27656 | tf_op jit(solution)/shard_map/ppermute | solution.py:519
  19.0 5.5 %collective-permute-start.8 = (bf16[4,4,1152]{2,1,0:T(4,128)(2,1)S(1)}, bf16[4,4,1152]{2,1,0:T(4,128)(2,1)S(1)}, u32[]{:S(2)}, u32[]{:S(2)}) collective-permute-start(bf16[4,4,1152]{2,1,0:T(4,128)(2,1)S(1)} %shard_map.130.refs_0_), channel_id=1, source_target_pairs={{0,24},{2,26},{4,28},{6,30},{8,0},{10,2},{12,4},{14,6},{16,8},{18,... | collective-permute-start | bytes 110600 | tf_op jit(solution)/shard_map/ppermute | solution.py:524
  22.8 4.9 %collective-permute-start.7 = (bf16[4,4,1152]{2,1,0:T(4,128)(2,1)S(1)}, bf16[4,4,1152]{2,1,0:T(4,128)(2,1)S(1)}, u32[]{:S(2)}, u32[]{:S(2)}) collective-permute-start(bf16[4,4,1152]{2,1,0:T(4,128)(2,1)S(1)} %shard_map.130.refs_0_), channel_id=1, source_target_pairs={{0,16},{2,18},{4,20},{6,22},{8,24},{10,26},{12,28},{14,30},{16,0},... | collective-permute-start | bytes 110600 | tf_op jit(solution)/shard_map/ppermute | solution.py:524
  22.8 5.8 %collective-permute-start.6 = (bf16[4,4,1152]{2,1,0:T(4,128)(2,1)S(1)}, bf16[4,4,1152]{2,1,0:T(4,128)(2,1)S(1)}, u32[]{:S(2)}, u32[]{:S(2)}) collective-permute-start(bf16[4,4,1152]{2,1,0:T(4,128)(2,1)S(1)} %shard_map.130.refs_0_), channel_id=1, source_target_pairs={{0,8},{2,10},{4,12},{6,14},{8,16},{10,18},{12,20},{14,22},{16,24},... | collective-permute-start | bytes 110600 | tf_op jit(solution)/shard_map/ppermute | solution.py:524
  24.5 12.0 %collective-permute-start = (bf16[192,1024]{1,0:T(8,128)(2,1)S(1)}, bf16[192,1024]{1,0:T(8,128)(2,1)S(1)}, u32[]{:S(2)}, u32[]{:S(2)}) collective-permute-start(bf16[192,1024]{1,0:T(8,128)(2,1)S(1)} %get-tuple-element.47), channel_id=1, source_target_pairs={{0,2},{2,0},{4,6},{6,4},{8,10},{10,8},{12,14},{14,12},{16,18},{18,... | collective-permute-start | bytes 1179656 | tf_op jit(solution)/shard_map/ppermute | solution.py:519
  27.7 16.5 %collective-permute-start.1 = (bf16[192,1024]{1,0:T(8,128)(2,1)S(1)}, bf16[192,1024]{1,0:T(8,128)(2,1)S(1)}, u32[]{:S(2)}, u32[]{:S(2)}) collective-permute-start(bf16[192,1024]{1,0:T(8,128)(2,1)S(1)} %get-tuple-element.48), channel_id=1, source_target_pairs={{0,4},{2,6},{4,0},{6,2},{8,12},{10,14},{12,8},{14,10},{16,20},{18,... | collective-permute-start | bytes 1179656 | tf_op jit(solution)/shard_map/ppermute | solution.py:519
  28.6 15.6 %collective-permute-start.2 = (bf16[192,1024]{1,0:T(8,128)(2,1)S(1)}, bf16[192,1024]{1,0:T(8,128)(2,1)S(1)}, u32[]{:S(2)}, u32[]{:S(2)}) collective-permute-start(bf16[192,1024]{1,0:T(8,128)(2,1)S(1)} %get-tuple-element.49), channel_id=1, source_target_pairs={{0,6},{2,4},{4,2},{6,0},{8,14},{10,12},{12,10},{14,8},{16,22},{18,... | collective-permute-start | bytes 1179656 | tf_op jit(solution)/shard_map/ppermute | solution.py:519
  29.7 1.4 %collective-permute-start.9 = (bf16[64,1152]{1,0:T(8,128)(2,1)S(1)}, bf16[64,1152]{1,0:T(8,128)(2,1)S(1)}, u32[]{:S(2)}, u32[]{:S(2)}) collective-permute-start(bf16[64,1152]{1,0:T(8,128)(2,1)S(1)} %shard_map.131.refs_0_.adapt_ref), channel_id=1, source_target_pairs={{0,1},{1,0},{2,3},{3,2},{4,5},{5,4},{6,7},{7,6},{8,9},{9,8},{10,11... | collective-permute-start | bytes 442376 | tf_op jit(solution)/shard_map/ppermute | solution.py:536
  29.8 14.9 %collective-permute-start.10 = (bf16[192,1024]{1,0:T(8,128)(2,1)S(1)}, bf16[192,1024]{1,0:T(8,128)(2,1)S(1)}, u32[]{:S(2)}, u32[]{:S(2)}) collective-permute-start(bf16[192,1024]{1,0:T(8,128)(2,1)S(1)} %get-tuple-element.46.refs_0_.refs_2_), channel_id=1, source_target_pairs={{0,1},{1,0},{2,3},{3,2},{4,5},{5,4},{6,7},{7,6},{8,9},{9,8},{10,11... | collective-permute-start | bytes 1179656 | tf_op jit(solution)/shard_map/ppermute | solution.py:536
  31.2 15.5 %collective-permute-start.16 = (bf16[320,512]{1,0:T(8,128)(2,1)S(1)}, bf16[320,512]{1,0:T(8,128)(2,1)S(1)}, u32[]{:S(2)}, u32[]{:S(2)}) collective-permute-start(bf16[320,512]{1,0:T(8,128)(2,1)S(1)} %get-tuple-element.56), channel_id=1, source_target_pairs={{8,16},{10,18},{12,20},{14,22},{16,8},{18,10},{20,12},{22,14},{9,1... | collective-permute-start | bytes 983048 | tf_op jit(solution)/shard_map/ppermute | solution.py:531
  36.5 24.0 %collective-permute-start.11 = (bf16[192,1024]{1,0:T(8,128)(2,1)S(1)}, bf16[192,1024]{1,0:T(8,128)(2,1)S(1)}, u32[]{:S(2)}, u32[]{:S(2)}) collective-permute-start(bf16[192,1024]{1,0:T(8,128)(2,1)S(1)} %collective-permute-done.refs_1_.refs_4_.refs_3_), channel_id=1, source_target_pairs={{0,1},{1,0},{2,3},{3,2},{4,5},{5,4},{6,7},{7,6},{8,9},{9,8},{10,11... | collective-permute-start | bytes 1179656 | tf_op jit(solution)/shard_map/ppermute | solution.py:536
  44.2 16.3 %collective-permute-start.12 = (bf16[192,1024]{1,0:T(8,128)(2,1)S(1)}, bf16[192,1024]{1,0:T(8,128)(2,1)S(1)}, u32[]{:S(2)}, u32[]{:S(2)}) collective-permute-start(bf16[192,1024]{1,0:T(8,128)(2,1)S(1)} %collective-permute-done.1.refs_2_.refs_6_.refs_4_), channel_id=1, source_target_pairs={{0,1},{1,0},{2,3},{3,2},{4,5},{5,4},{6,7},{7,6},{8,9},{9,8},{10,11... | collective-permute-start | bytes 1179656 | tf_op jit(solution)/shard_map/ppermute | solution.py:536
  44.2 16.2 %collective-permute-start.13 = (bf16[192,1024]{1,0:T(8,128)(2,1)S(1)}, bf16[192,1024]{1,0:T(8,128)(2,1)S(1)}, u32[]{:S(2)}, u32[]{:S(2)}) collective-permute-start(bf16[192,1024]{1,0:T(8,128)(2,1)S(1)} %collective-permute-done.2.refs_3_.refs_8_.refs_5_), channel_id=1, source_target_pairs={{0,1},{1,0},{2,3},{3,2},{4,5},{5,4},{6,7},{7,6},{8,9},{9,8},{10,11... | collective-permute-start | bytes 1179656 | tf_op jit(solution)/shard_map/ppermute | solution.py:536
  44.7 15.7 %collective-permute-start.17 = (bf16[320,512]{1,0:T(8,128)(2,1)S(1)}, bf16[320,512]{1,0:T(8,128)(2,1)S(1)}, u32[]{:S(2)}, u32[]{:S(2)}) collective-permute-start(bf16[320,512]{1,0:T(8,128)(2,1)S(1)} %get-tuple-element.57), channel_id=1, source_target_pairs={{8,0},{10,2},{12,4},{14,6},{16,24},{18,26},{20,28},{22,30},{9,1},{... | collective-permute-start | bytes 983048 | tf_op jit(solution)/shard_map/ppermute | solution.py:531
  46.7 22.1 %collective-permute-start.21 = (bf16[2,768,128]{2,1,0:T(8,128)(2,1)S(1)}, bf16[2,768,128]{2,1,0:T(8,128)(2,1)S(1)}, u32[]{:S(2)}, u32[]{:S(2)}) collective-permute-start(bf16[2,768,128]{2,1,0:T(8,128)(2,1)S(1)} %get-tuple-element.51.kv_ref), channel_id=1, source_target_pairs={{0,8},{2,10},{5,13},{7,15},{9,17},{11,19},{12,20},{14,22},{16,24},... | collective-permute-start | bytes 1179656 | tf_op jit(solution)/shard_map/ppermute | solution.py:546
  62.4 13.6 %collective-permute-start.19 = (bf16[768,128]{1,0:T(8,128)(2,1)S(1)}, bf16[768,128]{1,0:T(8,128)(2,1)S(1)}, u32[]{:S(2)}, u32[]{:S(2)}) collective-permute-start(bf16[768,128]{1,0:T(8,128)(2,1)S(1)} %get-tuple-element.60), channel_id=1, source_target_pairs={{0,4},{2,6},{4,0},{6,2},{8,12},{10,14},{12,8},{14,10},{16,20},{18,... | collective-permute-start | bytes 589832 | tf_op jit(solution)/shard_map/ppermute | solution.py:519
  64.2 12.5 %collective-permute-start.20 = (bf16[768,128]{1,0:T(8,128)(2,1)S(1)}, bf16[768,128]{1,0:T(8,128)(2,1)S(1)}, u32[]{:S(2)}, u32[]{:S(2)}) collective-permute-start(bf16[768,128]{1,0:T(8,128)(2,1)S(1)} %get-tuple-element.61), channel_id=1, source_target_pairs={{0,6},{2,4},{4,2},{6,0},{8,14},{10,12},{12,10},{14,8},{16,22},{18,... | collective-permute-start | bytes 589832 | tf_op jit(solution)/shard_map/ppermute | solution.py:519
  67.5 9.2 %collective-permute-start.18 = (bf16[768,128]{1,0:T(8,128)(2,1)S(1)}, bf16[768,128]{1,0:T(8,128)(2,1)S(1)}, u32[]{:S(2)}, u32[]{:S(2)}) collective-permute-start(bf16[768,128]{1,0:T(8,128)(2,1)S(1)} %get-tuple-element.59), channel_id=1, source_target_pairs={{0,2},{2,0},{4,6},{6,4},{8,10},{10,8},{12,14},{14,12},{16,18},{18,... | collective-permute-start | bytes 589832 | tf_op jit(solution)/shard_map/ppermute | solution.py:519
  69.8 1.5 %collective-permute-start.26 = (f32[384,64]{1,0:T(8,128)S(1)}, f32[384,64]{1,0:T(8,128)S(1)}, u32[]{:S(2)}, u32[]{:S(2)}) collective-permute-start(f32[384,64]{1,0:T(8,128)S(1)} %get-tuple-element.84), channel_id=1, source_target_pairs={{0,1},{1,0},{2,3},{3,2},{4,5},{5,4},{6,7},{7,6},{8,9},{9,8},{10,11... | collective-permute-start | bytes 294920 | tf_op jit(solution)/shard_map/ppermute | solution.py:536
  71.9 7.3 %collective-permute-start.29 = (bf16[384,128]{1,0:T(8,128)(2,1)S(1)}, bf16[384,128]{1,0:T(8,128)(2,1)S(1)}, u32[]{:S(2)}, u32[]{:S(2)}) collective-permute-start(bf16[384,128]{1,0:T(8,128)(2,1)S(1)} %shard_map.143.refs_0_), channel_id=1, source_target_pairs={{0,6},{2,4},{4,2},{6,0},{8,14},{10,12},{12,10},{14,8},{16,22},{18,... | collective-permute-start | bytes 294920 | tf_op jit(solution)/shard_map/ppermute | solution.py:519
  76.0 5.2 %collective-permute-start.28 = (bf16[384,128]{1,0:T(8,128)(2,1)S(1)}, bf16[384,128]{1,0:T(8,128)(2,1)S(1)}, u32[]{:S(2)}, u32[]{:S(2)}) collective-permute-start(bf16[384,128]{1,0:T(8,128)(2,1)S(1)} %shard_map.143.refs_0_), channel_id=1, source_target_pairs={{0,4},{2,6},{4,0},{6,2},{8,12},{10,14},{12,8},{14,10},{16,20},{18,... | collective-permute-start | bytes 294920 | tf_op jit(solution)/shard_map/ppermute | solution.py:519
  76.0 5.6 %collective-permute-start.27 = (bf16[384,128]{1,0:T(8,128)(2,1)S(1)}, bf16[384,128]{1,0:T(8,128)(2,1)S(1)}, u32[]{:S(2)}, u32[]{:S(2)}) collective-permute-start(bf16[384,128]{1,0:T(8,128)(2,1)S(1)} %shard_map.143.refs_0_), channel_id=1, source_target_pairs={{0,2},{2,0},{4,6},{6,4},{8,10},{10,8},{12,14},{14,12},{16,18},{18,... | collective-permute-start | bytes 294920 | tf_op jit(solution)/shard_map/ppermute | solution.py:519
  77.5 12.0 %collective-permute-start.22 = (bf16[2,768,128]{2,1,0:T(8,128)(2,1)S(1)}, bf16[2,768,128]{2,1,0:T(8,128)(2,1)S(1)}, u32[]{:S(2)}, u32[]{:S(2)}) collective-permute-start(bf16[2,768,128]{2,1,0:T(8,128)(2,1)S(1)} %get-tuple-element.75), channel_id=1, source_target_pairs={{8,0},{10,2},{13,5},{15,7},{17,9},{19,11},{20,12},{22,14},{24,16},... | collective-permute-start | bytes 1179656 | tf_op jit(solution)/shard_map/ppermute | solution.py:549
  81.7 1.4 %collective-permute-start.30 = (bf16[384,128]{1,0:T(8,128)(2,1)S(1)}, bf16[384,128]{1,0:T(8,128)(2,1)S(1)}, u32[]{:S(2)}, u32[]{:S(2)}) collective-permute-start(bf16[384,128]{1,0:T(8,128)(2,1)S(1)} %shard_map.144.refs_0_), channel_id=1, source_target_pairs={{0,1},{1,0},{2,3},{3,2},{4,5},{5,4},{6,7},{7,6},{8,9},{9,8},{10,11... | collective-permute-start | bytes 294920 | tf_op jit(solution)/shard_map/ppermute | solution.py:536
  84.7 12.4 %all-to-all-start = ((f32[16,4,768]{2,1,0:T(4,128)}), f32[16,4,768]{2,1,0:T(4,128)S(1)}, u32[]{:S(2)}, u32[]{:S(2)}) async-start(f32[16,4,768]{2,1,0:T(4,128)} %shard_map.145), calls=%async_computation | async-start | bytes 393216 | tf_op jit(solution)/shard_map/all_to_all | solution.py:687
  90.2 8.2 %collective-permute-start.23 = (bf16[3,192,128]{2,1,0:T(8,128)(2,1)S(1)}, bf16[3,192,128]{2,1,0:T(8,128)(2,1)S(1)}, u32[]{:S(2)}, u32[]{:S(2)}) collective-permute-start(bf16[3,192,128]{2,1,0:T(8,128)(2,1)S(1)} %get-tuple-element.77), channel_id=1, source_target_pairs={{0,2},{2,0},{4,6},{6,4},{8,10},{10,8},{12,14},{14,12},{16,18},{18,... | collective-permute-start | bytes 442376 | tf_op jit(solution)/shard_map/ppermute | solution.py:519
  92.0 8.0 %collective-permute-start.24 = (bf16[3,192,128]{2,1,0:T(8,128)(2,1)S(1)}, bf16[3,192,128]{2,1,0:T(8,128)(2,1)S(1)}, u32[]{:S(2)}, u32[]{:S(2)}) collective-permute-start(bf16[3,192,128]{2,1,0:T(8,128)(2,1)S(1)} %get-tuple-element.78), channel_id=1, source_target_pairs={{0,4},{2,6},{4,0},{6,2},{8,12},{10,14},{12,8},{14,10},{16,20},{18,... | collective-permute-start | bytes 442376 | tf_op jit(solution)/shard_map/ppermute | solution.py:519
  93.5 8.1 %collective-permute-start.25 = (bf16[3,192,128]{2,1,0:T(8,128)(2,1)S(1)}, bf16[3,192,128]{2,1,0:T(8,128)(2,1)S(1)}, u32[]{:S(2)}, u32[]{:S(2)}) collective-permute-start(bf16[3,192,128]{2,1,0:T(8,128)(2,1)S(1)} %get-tuple-element.79), channel_id=1, source_target_pairs={{0,6},{2,4},{4,2},{6,0},{8,14},{10,12},{12,10},{14,8},{16,22},{18,... | collective-permute-start | bytes 442376 | tf_op jit(solution)/shard_map/ppermute | solution.py:519
